TPU v7x, 32 devices: a whole 2x2x4 slice. The times are simulated.
32 devices in a mesh: gx: 8 (over z, y), gy: 4 (over x, core).
Axes of the slice: x: 2, y: 2, z: 4, core: 2. Of those that a mesh axis runs over, the one named last changes fastest.
Arguments:
- level_set: float32 [16, 512, 512], P(None, 'gx', 'gy'), may hold values from -6 to 6
- speed_x: float32 [16, 512, 512], P(None, 'gx', 'gy'), may hold values from -1 to 1
- speed_y: float32 [16, 512, 512], P(None, 'gx', 'gy'), may hold values from -1 to 1
- cotangent: float32 [16, 512, 512], P(None, 'gx', 'gy'), may hold values from -6 to 6
- blocks: bfloat16 [8, 4, 36, 4096], P('gx', 'gy'), may hold values from -0.75 to 0.75
- tile_count: int32 [8, 4], P('gx', 'gy'), may hold values from 1 to 36, as said below
- source_tile: int32 [8, 4, 36], P('gx', 'gy'), may hold values from 0 to 127, as said below
- dest_offset: int32 [8, 4, 36], P('gx', 'gy'), may hold values from 0 to 8, as said below
- dest_tile: int32 [8, 4, 36], P('gx', 'gy'), may hold values from 0 to 127
Outputs:
- grad_level_set: float32 [16, 512, 512], P(None, 'gx', 'gy')
- grad_blocks: float32 [8, 4, 36, 4096], P('gx', 'gy')
Inputs may be any that keep to these rules, and one draw needn't show every extreme that they name: `tile_count`: some device and its eight neighbours have all 36 slots live. `source_tile`: distinct within one device's list. `dest_offset`: each value occurs exactly 4 times among the 36 slots of one device.
All inputs are finite; a program needn't handle non-finite values.
Results may differ from a plain program's by a relative error of at most 0.0003.
Values sent between devices are 32-bit elements; how exact they have to be, the bound alone decides.
No kernel may reach another device: no remote copies, remote signals or barrier semaphores. Data moves between devices by JAX's collectives and lax.ppermute only.
A program may use at most 64 MiB of HBM per device.

v0:
```python
import jax
import jax.numpy as jnp
from jax import lax
from jax.sharding import PartitionSpec as P

TILE = 64
ROUTE_MOST = 4


COEFFICIENTS = (2.0 / 60.0, -13.0 / 60.0, 47.0 / 60.0, 27.0 / 60.0, -3.0 / 60.0)
UPWIND = (COEFFICIENTS[0], COEFFICIENTS[1], COEFFICIENTS[2], COEFFICIENTS[3], COEFFICIENTS[4], 0.0)
DOWNWIND = (
    0.0,
    COEFFICIENTS[4],
    COEFFICIENTS[3],
    COEFFICIENTS[2],
    COEFFICIENTS[1],
    COEFFICIENTS[0],
)
TIME_STEP = 0.3
PRECISE = lax.Precision.HIGHEST


def with_halo(block, sides, width):
    for axis, dim in sides:
        count = lax.axis_size(axis)
        forward = [(i, i + 1) for i in range(count - 1)]
        forward.append((count - 1, 0))
        backward = [(target, source) for source, target in forward]
        low = lax.ppermute(
            lax.slice_in_dim(block, block.shape[dim] - width, None, axis=dim), axis, forward
        )
        high = lax.ppermute(lax.slice_in_dim(block, 0, width, axis=dim), axis, backward)
        block = jnp.concatenate([low, block, high], axis=dim)
    return block


def shifted(block, axis, distance):
    devices = range(lax.axis_size(axis))
    route = [((i - distance) % len(devices), i) for i in devices]
    return lax.ppermute(block, axis, route)


def flux_faces(padded_view, face_speed, axis_dim, length):

    def neighbour(shift_by):
        return lax.slice_in_dim(padded_view, 2 + shift_by, 2 + shift_by + length, axis=axis_dim)

    upwind_part = (
        COEFFICIENTS[0] * neighbour(-2)
        + COEFFICIENTS[1] * neighbour(-1)
        + COEFFICIENTS[2] * neighbour(0)
        + COEFFICIENTS[3] * neighbour(1)
        + COEFFICIENTS[4] * neighbour(2)
    )
    downwind_part = (
        COEFFICIENTS[0] * neighbour(3)
        + COEFFICIENTS[1] * neighbour(2)
        + COEFFICIENTS[2] * neighbour(1)
        + COEFFICIENTS[3] * neighbour(0)
        + COEFFICIENTS[4] * neighbour(-1)
    )
    face_rate = lax.slice_in_dim(face_speed, 2, 2 + length, axis=axis_dim)
    return jnp.maximum(face_rate, 0.0) * upwind_part + jnp.minimum(face_rate, 0.0) * downwind_part


def advect(pad_field, pad_sx, pad_sy):
    extent_x = pad_field.shape[1] - 6
    extent_y = pad_field.shape[2] - 6
    flux_x = flux_faces(pad_field[:, :, 3:-3], pad_sx[:, :, 3:-3], 1, extent_x + 1)
    flux_y = flux_faces(pad_field[:, 3:-3, :], pad_sy[:, 3:-3, :], 2, extent_y + 1)
    return -(flux_x[:, 1:, :] - flux_x[:, :-1, :]) - (flux_y[:, :, 1:] - flux_y[:, :, :-1])


def adjoint_axis(padded_view, face_speed, axis_dim, extent):
    face_jump = lax.slice_in_dim(padded_view, 1, extent + 6, axis=axis_dim) - lax.slice_in_dim(
        padded_view, 0, extent + 5, axis=axis_dim
    )
    face_rate = lax.slice_in_dim(face_speed, 0, extent + 5, axis=axis_dim)
    upwind_part = jnp.maximum(face_rate, 0.0) * face_jump
    downwind_part = jnp.minimum(face_rate, 0.0) * face_jump
    summed = 0.0
    for number in range(6):
        offset_pos = 5 - number
        if UPWIND[number] != 0.0:
            summed = summed + UPWIND[number] * lax.slice_in_dim(
                upwind_part, offset_pos, offset_pos + extent, axis=axis_dim
            )
        if DOWNWIND[number] != 0.0:
            summed = summed + DOWNWIND[number] * lax.slice_in_dim(
                downwind_part, offset_pos, offset_pos + extent, axis=axis_dim
            )
    return summed


def adjoint_advect(pad_grad, pad_sx, pad_sy):
    extent_x = pad_grad.shape[1] - 6
    extent_y = pad_grad.shape[2] - 6
    part_x = adjoint_axis(pad_grad[:, :, 3:-3], pad_sx[:, :, 3:-3], 1, extent_x)
    part_y = adjoint_axis(pad_grad[:, 3:-3, :], pad_sy[:, 3:-3, :], 2, extent_y)
    return part_x + part_y


def rims(cotan_field):
    return with_halo(cotan_field, (("gx", 1), ("gy", 2)), 3)


def hop_x(members):
    moved_parts = []
    for offset in (1, -1):
        sent_parts = tuple((member[1 + offset] for member in members))
        moved_parts.append(shifted(sent_parts, "gx", offset))
    return tuple(
        (
            jnp.stack([moved_parts[0][number], member[1], moved_parts[1][number]], axis=0)
            for number, member in enumerate(members)
        )
    )


def hop_y(members):
    moved_parts = []
    for offset in (1, -1):
        sent_parts = tuple((member[:, 1 + offset] for member in members))
        moved_parts.append(shifted(sent_parts, "gy", offset))
    return tuple(
        (
            jnp.stack([moved_parts[0][number], member[:, 1], moved_parts[1][number]], axis=1)
            for number, member in enumerate(members)
        )
    )


def travel(members, outward):
    arrived = hop_y(hop_x(members)) if outward else hop_x(hop_y(members))
    return arrived


def shards(
    level_set, speed_x, speed_y, cotangent, blocks, tile_count, source_tile, dest_offset, dest_tile
):
    planes, extent_x, extent_y = level_set.shape
    slot_total = source_tile.shape[2]
    tile_total = extent_x * extent_y // TILE
    live_count = tile_count.reshape(())
    slot_index = jnp.arange(slot_total, dtype=jnp.int32)
    live_slots = slot_index < live_count
    live_weight = live_slots.astype(jnp.float32)
    heading = dest_offset.reshape(slot_total)
    source = source_tile.reshape(slot_total)
    target = dest_tile.reshape(slot_total)
    onehot = (
        (heading[:, None] == jnp.arange(9, dtype=jnp.int32)[None, :]) & live_slots[:, None]
    ).astype(jnp.int32)
    rank_counts = jnp.sum((jnp.cumsum(onehot, axis=0) - 1) * onehot, axis=1)
    lane_index = jnp.where(live_slots, heading, 9)
    rank_index = jnp.where(live_slots, rank_counts, ROUTE_MOST)

    def place(values, fill_value):
        empty_slots = jnp.full((9, ROUTE_MOST) + values.shape[1:], fill_value, values.dtype)
        packed = empty_slots.at[lane_index, rank_index].set(values, mode="drop")
        return packed.reshape((3, 3, ROUTE_MOST) + values.shape[1:])

    pad_phi, pad_sx, pad_sy = (
        with_halo(level_set, (("gx", 1), ("gy", 2)), 3),
        with_halo(speed_x, (("gx", 1), ("gy", 2)), 3),
        with_halo(speed_y, (("gx", 1), ("gy", 2)), 3),
    )
    pad_final = rims(cotangent)
    matrices = blocks.reshape(slot_total, TILE, TILE).astype(jnp.float32)
    start_tiles = level_set.reshape(planes, tile_total, TILE)
    picked_start = jnp.take(start_tiles, source, axis=1).transpose(1, 0, 2)
    ext_values = jnp.einsum("sab,szb->sza", matrices, picked_start, precision=PRECISE)
    landed_values, landed_index = travel(
        (place(ext_values, 0.0), place(target.astype(jnp.float32), float(tile_total))), True
    )
    arrival_index = landed_index.reshape(9 * ROUTE_MOST).astype(jnp.int32)
    arrived = (
        jnp.zeros((tile_total, planes, TILE), jnp.float32)
        .at[arrival_index]
        .add(landed_values.reshape(9 * ROUTE_MOST, planes, TILE), mode="drop")
    )
    ext_field = arrived.transpose(1, 0, 2).reshape(planes, extent_x, extent_y)
    section = level_set + TIME_STEP * (advect(pad_phi, pad_sx, pad_sy) + ext_field)
    picked_section = jnp.take(section.reshape(planes, tile_total, TILE), source, axis=1).transpose(
        1, 0, 2
    )
    safe_arrival = jnp.minimum(arrival_index, tile_total - 1)

    def pull(cotan_field, pad_cotan, picked_source):
        advected = adjoint_advect(pad_cotan, pad_sx, pad_sy)
        cotan_tiles = cotan_field.reshape(planes, tile_total, TILE)
        requested = jnp.take(cotan_tiles, safe_arrival, axis=1).transpose(1, 0, 2)
        requested = requested.reshape(3, 3, ROUTE_MOST, planes, TILE)
        returned = travel((requested,), False)[0]
        returned = returned.reshape(9, ROUTE_MOST, planes, TILE)[
            jnp.minimum(lane_index, 8), jnp.minimum(rank_index, ROUTE_MOST - 1)
        ]
        returned = returned * live_weight[:, None, None]
        back_values = jnp.einsum("sab,sza->szb", matrices, returned, precision=PRECISE)
        back_tiles = jnp.zeros((tile_total, planes, TILE), jnp.float32).at[source].add(back_values)
        block_grad = jnp.einsum("sza,szb->sab", returned, picked_source, precision=PRECISE)
        back_field = back_tiles.transpose(1, 0, 2).reshape(planes, extent_x, extent_y)
        return (advected + back_field, block_grad)

    final_pull, final_blocks = pull(cotangent, pad_final, picked_section)
    grad_section = 0.5 * cotangent + 0.5 * TIME_STEP * final_pull
    section_pull, section_blocks = pull(grad_section, rims(grad_section), picked_start)
    grad_level_set = 0.5 * cotangent + grad_section + TIME_STEP * section_pull
    grad_blocks = 0.5 * TIME_STEP * final_blocks + TIME_STEP * section_blocks
    return (grad_level_set, grad_blocks.reshape(1, 1, slot_total, TILE * TILE))


def solution(mesh):
    return jax.shard_map(
        shards,
        mesh=mesh,
        in_specs=(
            P(None, "gx", "gy"),
            P(None, "gx", "gy"),
            P(None, "gx", "gy"),
            P(None, "gx", "gy"),
            P("gx", "gy", None, None),
            P("gx", "gy"),
            P("gx", "gy", None),
            P("gx", "gy", None),
            P("gx", "gy", None),
        ),
        out_specs=(P(None, "gx", "gy"), P("gx", "gy", None, None)),
        check_vma=False,
    )
```

profile of v0, /device:TPU:0, one launch (start us, length us, event | category | flops | bytes accessed | tf_op | source)
XLA Modules:
  0.0 228.6 jit_solution(5095575138198693115)
XLA Ops:
  4.4 2.8 %scatter_fusion = f32[9,4]{0,1:T(4,128)S(1)} fusion(f32[9,4]{0,1:T(4,128)S(1)} %broadcast_in_dim.20, s32[36]{0:T(128)S(1)} %get-tuple-element.63, f32[36]{0:T(128)S(1)} %convert_bitcast_fusion), kind=kCustom, calls=%fused_computation.6 | custom fusion | bytes 720 | tf_op jit(solution)/shard_map/scatter | solution.py:161
  7.2 6.0 %collective-permute-start.11 = (f32[3,4]{0,1:T(4,128)S(1)}, f32[3,4]{0,1:T(4,128)S(1)}, u32[]{:S(2)}, u32[]{:S(2)}) collective-permute-start(f32[3,4]{0,1:T(4,128)S(1)} %get-tuple-element.60), channel_id=1, source_target_pairs={{4,0},{8,4},{12,8},{16,12},{20,16},{24,20},{28,24},{0,28},{5,1},{9... | collective-permute-start | bytes 152 | tf_op jit(solution)/shard_map/ppermute | solution.py:41
  13.3 4.8 %collective-permute-start.27 = (f32[16,3,128]{2,1,0:T(4,128)S(1)}, f32[16,3,128]{2,1,0:T(4,128)S(1)}, u32[]{:S(2)}, u32[]{:S(2)}) collective-permute-start(f32[16,3,128]{2,1,0:T(4,128)S(1)} %get-tuple-element.30), channel_id=1, source_target_pairs={{4,0},{8,4},{12,8},{16,12},{20,16},{24,20},{28,24},{0,28},{5,1},{9... | collective-permute-start | bytes 73736 | tf_op jit(solution)/shard_map/ppermute | solution.py:33
  22.4 2.8 %copy.87 = f32[16,128,64]{2,0,1:T(8,128)} copy(f32[16,128,64]{2,1,0:T(8,128)} %reshape.225) | data formatting | bytes 1048576 | tf_op jit(solution)/shard_map/reshape | solution.py:171
  25.9 2.0 gather_fusion.4
  30.5 5.3 %scatter_fusion.3 = f32[9,4,16,64]{3,2,1,0:T(8,128)} fusion(f32[9,4,16,64]{3,2,1,0:T(8,128)} %broadcast_in_dim.23, s32[36]{0:T(128)S(1)} %get-tuple-element.63, f32[36,16,64]{2,1,0:T(8,128)} %fusion.76), kind=kCustom, calls=%fused_computation.9 | custom fusion | bytes 442656 | tf_op jit(solution)/shard_map/scatter | solution.py:161
  39.1 2.8 %copy.66 = f32[16,128,64]{2,0,1:T(8,128)} copy(f32[16,128,64]{2,1,0:T(8,128)} %reshape.214) | data formatting | bytes 1048576 | tf_op jit(solution)/shard_map/reshape | solution.py:192
  42.0 5.5 %collective-permute-start.5 = (f32[16,3,128]{2,1,0:T(4,128)}, f32[16,3,128]{2,1,0:T(4,128)}, u32[]{:S(2)}, u32[]{:S(2)}) collective-permute-start(f32[16,3,128]{2,1,0:T(4,128)} %get-tuple-element.36), channel_id=1, source_target_pairs={{4,0},{8,4},{12,8},{16,12},{20,16},{24,20},{28,24},{0,28},{5,1},{9... | collective-permute-start | bytes 73736 | tf_op jit(solution)/shard_map/ppermute | solution.py:33
  47.7 3.0 %collective-permute-done.12 = f32[3,4]{1,0:T(4,128)S(1)} collective-permute-done((f32[3,4]{1,0:T(4,128)S(1)}, f32[3,4]{1,0:T(4,128)S(1)}, u32[]{:S(2)}, u32[]{:S(2)}) %collective-permute-start.12) | collective-permute-done | bytes 80 | tf_op jit(solution)/shard_map/ppermute | solution.py:41
  55.5 4.8 %collective-permute-start.3 = (f32[16,3,128]{2,1,0:T(4,128)}, f32[16,3,128]{2,1,0:T(4,128)}, u32[]{:S(2)}, u32[]{:S(2)}) collective-permute-start(f32[16,3,128]{2,1,0:T(4,128)} %get-tuple-element.38), channel_id=1, source_target_pairs={{4,0},{8,4},{12,8},{16,12},{20,16},{24,20},{28,24},{0,28},{5,1},{9... | collective-permute-start | bytes 73736 | tf_op jit(solution)/shard_map/ppermute | solution.py:33
  61.4 1.9 copy.83
  63.3 2.0 collective-permute-start.1
  68.2 1.9 copy.53
  73.9 1.9 copy.57
  76.8 2.3 fusion.20
  79.1 1.9 copy.58
  81.0 1.9 copy.54
  89.2 4.7 %collective-permute-start.31 = (f32[3,4,16,64]{3,2,1,0:T(8,128)}, f32[3,4,16,64]{3,2,1,0:T(8,128)}, u32[]{:S(2)}, u32[]{:S(2)}) collective-permute-start(f32[3,4,16,64]{3,2,1,0:T(8,128)} %get-tuple-element.43), channel_id=1, source_target_pairs={{4,0},{8,4},{12,8},{16,12},{20,16},{24,20},{28,24},{0,28},{5,1},{9... | collective-permute-start | bytes 147464 | tf_op jit(solution)/shard_map/ppermute | solution.py:41
  95.0 1.9 copy.59
  98.6 1.9 copy.60
  102.3 1.9 maximum_maximum_fusion
  105.7 3.4 %fusion.6 = f32[16,64,129]{2,1,0:T(8,128)} fusion(f32[16,70,131]{2,1,0:T(8,128)S(1)} %get-tuple-element.20, f32[16,70,131]{2,1,0:T(8,128)S(1)} %get-tuple-element.19, f32[16,3,128]{2,1,0:T(4,128)} %collective-permute-done.5, f32[16,64,128]{2,1,0:T(8,128)S(1)} %copy-done.6, f32[16,3,128]{2,1,0:T(4,128)} %collective-permute-done.4, f32[16,70,3]{2,1,0:T(8,128)S(1)} %copy.55), kind=kLoop, calls=%fused_computation.24 | loop fusion | flops 3434496 | bytes 4285568 | tf_op jit(solution)/shard_map/add | solution.py:64
  109.1 1.9 maximum_multiply_fusion.1
  116.9 4.7 %collective-permute-start.17 = (f32[3,4,16,64]{3,2,1,0:T(8,128)S(1)}, f32[3,4,16,64]{3,2,1,0:T(8,128)}, u32[]{:S(2)}, u32[]{:S(2)}) collective-permute-start(f32[3,4,16,64]{3,2,1,0:T(8,128)S(1)} %get-tuple-element.52), channel_id=1, source_target_pairs={{4,0},{8,4},{12,8},{16,12},{20,16},{24,20},{28,24},{0,28},{5,1},{9... | collective-permute-start | bytes 147464 | tf_op jit(solution)/shard_map/ppermute | solution.py:41
  123.4 6.3 %scatter_fusion.4 = f32[128,16,64]{2,1,0:T(8,128)} fusion(f32[128,16,64]{2,1,0:T(8,128)} %broadcast.245.clone.2, s32[36]{0:T(128)S(1)} %copy-done.28, f32[36,16,64]{2,1,0:T(8,128)} %bitcast.123), kind=kCustom, calls=%fused_computation.10 | custom fusion | flops 36864 | bytes 442512 | tf_op jit(solution)/shard_map/scatter-add | solution.py:181
  129.7 2.6 %copy.91 = f32[16,128,64]{2,1,0:T(8,128)} copy(f32[16,128,64]{2,0,1:T(8,128)} %bitcast.121) | data formatting | bytes 1048576 | tf_op jit(solution)/shard_map/transpose | solution.py:183
  132.3 2.2 reshape.228
  134.5 2.9 %fusion.29 = f32[16,64,128]{2,1,0:T(8,128)} fusion(f32[16,64,128]{2,1,0:T(8,128)S(1)} %copy-done, f32[16,64,128]{2,1,0:T(8,128)} %reshape.228, f32[16,64,129]{2,1,0:T(8,128)} %fusion.6, f32[16,65,128]{2,1,0:T(8,128)} %fusion.20), kind=kLoop, calls=%fused_computation.79 | loop fusion | flops 917504 | bytes 3670016 | tf_op jit(solution)/shard_map/add | solution.py:184
  137.4 2.2 reshape.229
  139.7 2.8 %copy.92 = f32[16,128,64]{2,0,1:T(8,128)} copy(f32[16,128,64]{2,1,0:T(8,128)} %reshape.229) | data formatting | bytes 1048576 | tf_op jit(solution)/shard_map/reshape | solution.py:185
  142.5 2.5 %gather_fusion.5 = f32[36,16,64]{2,1,0:T(8,128)} fusion(f32[16,128,64]{2,0,1:T(8,128)} %copy.92, s32[1024]{0:T(1024)S(1)} %pad_clamp_fusion), kind=kCustom, calls=%fused_computation.3.clone | custom fusion | bytes 295056 | tf_op jit(solution)/shard_map/jit(_take)/gather | solution.py:185
  148.4 2.5 %fusion.83 = f32[36,16,64]{2,1,0:T(8,128)} fusion(bf16[36,64,64]{2,1,0:T(8,128)(2,1)} %copy-done.2, f32[36,16,64]{2,1,0:T(8,128)S(1)} %gather_fusion, f32[36]{0:T(128)S(1)} %get-tuple-element.65), kind=kOutput, calls=%fused_computation.180 | convolution fusion | flops 28348416 | bytes 589968 | tf_op jit(solution)/shard_map/sab,sza->szb/dot_general | solution.py:200
  152.0 6.4 %scatter_fusion.1 = f32[128,16,64]{2,1,0:T(8,128)} fusion(f32[128,16,64]{2,1,0:T(8,128)} %broadcast.245.clone.1, s32[36]{0:T(128)S(1)} %copy-done.25, f32[36,16,64]{2,1,0:T(8,128)} %fusion.83), kind=kCustom, calls=%fused_computation.7 | custom fusion | flops 36864 | bytes 442512 | tf_op jit(solution)/shard_map/scatter-add | solution.py:201
  158.3 2.5 %copy.71 = f32[16,128,64]{2,1,0:T(8,128)} copy(f32[16,128,64]{2,0,1:T(8,128)} %bitcast.122) | data formatting | bytes 1048576 | tf_op jit(solution)/shard_map/transpose | solution.py:203
  160.9 2.2 reshape.220
  163.1 4.5 %fusion.57 = f32[16,64,128]{2,1,0:T(8,128)S(1)} fusion(f32[16,64,128]{2,1,0:T(8,128)} %reshape.220, f32[16,64,133]{2,1,0:T(8,128)} %minimum_multiply_fusion.1, f32[16,64,133]{2,1,0:T(8,128)S(1)} %get-tuple-element.9, f32[16,69,128]{2,1,0:T(8,128)S(1)} %get-tuple-element.18, f32[16,69,128]{2,1,0:T(8,128)S(1)} %get-tuple-element.17, ...), kind=kLoop, calls=%fused_computation.129 | loop fusion | flops 5636096 | bytes 12058624 | tf_op jit(solution)/shard_map/add | solution.py:207
  168.7 3.2 %convolution_multiply_fusion.1 = f32[36,64,64]{2,1,0:T(8,128)} fusion(f32[36,16,64]{2,1,0:T(8,128)S(1)} %copy-done.17, f32[36,16,64]{2,1,0:T(8,128)S(1)} %copy-done.13, f32[36]{0:T(128)S(1)} %get-tuple-element.65, pred[36]{0:T(512)(128)(4,1)S(1)} %copy-done.24), kind=kOutput, calls=%fused_computation.13 | convolution fusion | flops 28532736 | bytes 884916 | tf_op jit(solution)/shard_map/sza,szb->sab/dot_general | solution.py:202
  173.3 4.7 %collective-permute-start.19 = (f32[16,3,128]{2,1,0:T(4,128)S(1)}, f32[16,3,128]{2,1,0:T(4,128)S(1)}, u32[]{:S(2)}, u32[]{:S(2)}) collective-permute-start(f32[16,3,128]{2,1,0:T(4,128)S(1)} %get-tuple-element.32), channel_id=1, source_target_pairs={{4,0},{8,4},{12,8},{16,12},{20,16},{24,20},{28,24},{0,28},{5,1},{9... | collective-permute-start | bytes 73736 | tf_op jit(solution)/shard_map/ppermute | solution.py:33
  190.3 4.7 %collective-permute-start.25 = (f32[3,4,16,64]{3,2,1,0:T(8,128)S(1)}, f32[3,4,16,64]{3,2,1,0:T(8,128)S(1)}, u32[]{:S(2)}, u32[]{:S(2)}) collective-permute-start(f32[3,4,16,64]{3,2,1,0:T(8,128)S(1)} %get-tuple-element.46), channel_id=1, source_target_pairs={{4,0},{8,4},{12,8},{16,12},{20,16},{24,20},{28,24},{0,28},{5,1},{9... | collective-permute-start | bytes 147464 | tf_op jit(solution)/shard_map/ppermute | solution.py:41
  196.4 2.0 collective-permute-done.24
  199.2 2.5 %gather_fusion.1 = f32[36,16,64]{2,1,0:T(8,128)} fusion(f32[9,4,16,64]{3,2,1,0:T(8,128)} %bitcast.125, s32[36]{0:T(128)S(1)} %get-tuple-element.62), kind=kCustom, calls=%fused_computation.5 | custom fusion | bytes 295200 | tf_op jit(solution)/shard_map/gather | solution.py:196
  201.7 2.6 %fusion.80 = f32[36,16,64]{2,1,0:T(8,128)} fusion(bf16[36,64,64]{2,1,0:T(8,128)(2,1)} %copy-done.2, f32[36,16,64]{2,1,0:T(8,128)} %gather_fusion.1, f32[36]{0:T(128)S(1)} %get-tuple-element.65), kind=kOutput, calls=%fused_computation.177 | convolution fusion | flops 28348416 | bytes 589968 | tf_op jit(solution)/shard_map/sab,sza->szb/dot_general | solution.py:200
  204.3 4.2 %fusion = f32[36,64,64]{2,1,0:T(8,128)} fusion(f32[36,64,64]{2,1,0:T(8,128)S(1)} %copy-done.10, f32[36,16,64]{2,1,0:T(8,128)} %copy-done.11, f32[36,16,64]{2,1,0:T(8,128)} %gather_fusion.1, f32[36]{0:T(128)S(1)} %get-tuple-element.65, pred[36]{0:T(512)(128)(4,1)S(1)} %copy-done.24), kind=kOutput, calls=%fused_computation.12 | convolution fusion | flops 28680192 | bytes 1474740 | tf_op jit(solution)/shard_map/sza,szb->sab/dot_general | solution.py:202
  208.5 2.8 %reshape.323 = f32[1,1,36,4096]{3,1,2,0:T(1,128)} reshape(f32[36,64,64]{2,1,0:T(8,128)} %fusion) | data formatting | bytes 1179648 | tf_op jit(solution)/shard_map/reshape | solution.py:211
  212.5 6.4 %scatter_fusion.2 = f32[128,16,64]{2,1,0:T(8,128)} fusion(f32[128,16,64]{2,1,0:T(8,128)} %broadcast.245.clone, s32[36]{0:T(128)S(1)} %copy-done.25, f32[36,16,64]{2,1,0:T(8,128)} %fusion.80), kind=kCustom, calls=%fused_computation.8 | custom fusion | flops 36864 | bytes 442512 | tf_op jit(solution)/shard_map/scatter-add | solution.py:201
  218.8 2.5 %copy.81 = f32[16,128,64]{2,1,0:T(8,128)} copy(f32[16,128,64]{2,0,1:T(8,128)} %bitcast.120) | data formatting | bytes 1048576 | tf_op jit(solution)/shard_map/transpose | solution.py:203
  221.4 2.2 reshape.224
  223.6 5.0 %fusion.35 = f32[16,64,128]{2,1,0:T(8,128)} fusion(f32[16,64,128]{2,1,0:T(8,128)} %reshape.224, f32[16,64,133]{2,1,0:T(8,128)} %get-tuple-element.14, f32[16,64,133]{2,1,0:T(8,128)S(1)} %get-tuple-element.13, f32[16,69,128]{2,1,0:T(8,128)S(1)} %get-tuple-element.16, f32[16,69,128]{2,1,0:T(8,128)S(1)} %get-tuple-element.15, f32[16,64,128]{2,1,0:T(8,128)S(1)} %fusion.57, ...), kind=kLoop, calls=%fused_computation.87 | loop fusion | flops 5767168 | bytes 12582912 | tf_op jit(solution)/shard_map/add | solution.py:209
  (202 shorter events, 70.1 us)
Async XLA Ops:
  0.6 12.6 %copy-start = (f32[16,64,128]{2,1,0:T(8,128)S(1)}, f32[16,64,128]{2,1,0:T(8,128)}, u32[]{:S(2)}) copy-start(f32[16,64,128]{2,1,0:T(8,128)} %param.11) | copy-start | bytes 1572868
  0.6 17.5 %copy-start.6 = (f32[16,64,128]{2,1,0:T(8,128)S(1)}, f32[16,64,128]{2,1,0:T(8,128)}, u32[]{:S(2)}) copy-start(f32[16,64,128]{2,1,0:T(8,128)} %param.13) | copy-start | bytes 1572868
  7.2 12.8 %copy-start.29 = (s32[1,1,36]{2,1,0:T(1,128)S(1)}, s32[1,1,36]{2,1,0:T(1,128)}, u32[]{:S(2)}) copy-start(s32[1,1,36]{2,1,0:T(1,128)} %param.17) | copy-start | bytes 436
  7.2 34.7 %collective-permute-start.11 = (f32[3,4]{0,1:T(4,128)S(1)}, f32[3,4]{0,1:T(4,128)S(1)}, u32[]{:S(2)}, u32[]{:S(2)}) collective-permute-start(f32[3,4]{0,1:T(4,128)S(1)} %get-tuple-element.60), channel_id=1, source_target_pairs={{4,0},{8,4},{12,8},{16,12},{20,16},{24,20},{28,24},{0,28},{5,1},{9... | collective-permute-start | bytes 152 | tf_op jit(solution)/shard_map/ppermute | solution.py:41
  13.2 34.3 %collective-permute-start.10 = (f32[3,4]{0,1:T(4,128)S(1)}, f32[3,4]{0,1:T(4,128)S(1)}, u32[]{:S(2)}, u32[]{:S(2)}) collective-permute-start(f32[3,4]{0,1:T(4,128)S(1)} %get-tuple-element.59), channel_id=1, source_target_pairs={{28,0},{0,4},{4,8},{8,12},{12,16},{16,20},{20,24},{24,28},{29,1},{... | collective-permute-start | bytes 152 | tf_op jit(solution)/shard_map/ppermute | solution.py:41
  13.3 42.2 %collective-permute-start.26 = (f32[16,3,128]{2,1,0:T(4,128)S(1)}, f32[16,3,128]{2,1,0:T(4,128)S(1)}, u32[]{:S(2)}, u32[]{:S(2)}) collective-permute-start(f32[16,3,128]{2,1,0:T(4,128)S(1)} %get-tuple-element.29), channel_id=1, source_target_pairs={{0,4},{4,8},{8,12},{12,16},{16,20},{20,24},{24,28},{28,0},{1,5},{5... | collective-permute-start | bytes 73736 | tf_op jit(solution)/shard_map/ppermute | solution.py:30
  13.3 42.1 %collective-permute-start.27 = (f32[16,3,128]{2,1,0:T(4,128)S(1)}, f32[16,3,128]{2,1,0:T(4,128)S(1)}, u32[]{:S(2)}, u32[]{:S(2)}) collective-permute-start(f32[16,3,128]{2,1,0:T(4,128)S(1)} %get-tuple-element.30), channel_id=1, source_target_pairs={{4,0},{8,4},{12,8},{16,12},{20,16},{24,20},{28,24},{0,28},{5,1},{9... | collective-permute-start | bytes 73736 | tf_op jit(solution)/shard_map/ppermute | solution.py:33
  18.7 44.6 %collective-permute-start.4 = (f32[16,3,128]{2,1,0:T(4,128)}, f32[16,3,128]{2,1,0:T(4,128)}, u32[]{:S(2)}, u32[]{:S(2)}) collective-permute-start(f32[16,3,128]{2,1,0:T(4,128)} %get-tuple-element.35), channel_id=1, source_target_pairs={{0,4},{4,8},{8,12},{12,16},{16,20},{20,24},{24,28},{28,0},{1,5},{5... | collective-permute-start | bytes 73736 | tf_op jit(solution)/shard_map/ppermute | solution.py:30
  20.0 7.9 %copy-start.23 = (pred[36]{0:T(512)(128)(4,1)}, pred[36]{0:T(512)(128)(4,1)S(1)}, u32[]{:S(2)}) copy-start(pred[36]{0:T(512)(128)(4,1)S(1)} %compare_and_fusion) | copy-start | bytes 112
  25.9 9.9 %copy-start.2 = (bf16[36,64,64]{2,1,0:T(8,128)(2,1)}, bf16[36,64,64]{2,1,0:T(8,128)(2,1)S(1)}, u32[]{:S(2)}) copy-start(bf16[36,64,64]{2,1,0:T(8,128)(2,1)S(1)} %reshape.219) | copy-start | bytes 884740
  27.9 7.9 %copy-start.11 = (f32[36,16,64]{2,1,0:T(8,128)}, f32[36,16,64]{2,1,0:T(8,128)S(1)}, u32[]{:S(2)}) copy-start(f32[36,16,64]{2,1,0:T(8,128)S(1)} %gather_fusion.4) | copy-start | bytes 442372
  42.0 23.3 %collective-permute-start.5 = (f32[16,3,128]{2,1,0:T(4,128)}, f32[16,3,128]{2,1,0:T(4,128)}, u32[]{:S(2)}, u32[]{:S(2)}) collective-permute-start(f32[16,3,128]{2,1,0:T(4,128)} %get-tuple-element.36), channel_id=1, source_target_pairs={{4,0},{8,4},{12,8},{16,12},{20,16},{24,20},{28,24},{0,28},{5,1},{9... | collective-permute-start | bytes 73736 | tf_op jit(solution)/shard_map/ppermute | solution.py:33
  47.6 3.1 %collective-permute-start.12 = (f32[3,4]{1,0:T(4,128)S(1)}, f32[3,4]{1,0:T(4,128)S(1)}, u32[]{:S(2)}, u32[]{:S(2)}) collective-permute-start(f32[3,4]{1,0:T(4,128)S(1)} %bitcast.143), channel_id=1, source_target_pairs={{3,0},{0,1},{1,2},{2,3},{7,4},{4,5},{5,6},{6,7},{11,8},{8,9},{9,10... | collective-permute-start | bytes 152 | tf_op jit(solution)/shard_map/ppermute | solution.py:41
  50.7 1.3 collective-permute-start.13
  52.0 23.9 %collective-permute-start = (f32[16,3,128]{2,1,0:T(4,128)}, f32[16,3,128]{2,1,0:T(4,128)}, u32[]{:S(2)}, u32[]{:S(2)}) collective-permute-start(f32[16,3,128]{2,1,0:T(4,128)} %get-tuple-element.33), channel_id=1, source_target_pairs={{0,4},{4,8},{8,12},{12,16},{16,20},{20,24},{24,28},{28,0},{1,5},{5... | collective-permute-start | bytes 73736 | tf_op jit(solution)/shard_map/ppermute | solution.py:30
  55.4 4.8 %copy-start.19 = (f32[16,3,128]{2,1,0:T(4,128)}, f32[16,3,128]{2,1,0:T(4,128)S(1)}, u32[]{:S(2)}) copy-start(f32[16,3,128]{2,1,0:T(4,128)S(1)} %collective-permute-done.26) | copy-start | bytes 73732
  55.4 14.7 %collective-permute-start.2 = (f32[16,3,128]{2,1,0:T(4,128)}, f32[16,3,128]{2,1,0:T(4,128)}, u32[]{:S(2)}, u32[]{:S(2)}) collective-permute-start(f32[16,3,128]{2,1,0:T(4,128)} %get-tuple-element.37), channel_id=1, source_target_pairs={{0,4},{4,8},{8,12},{12,16},{16,20},{20,24},{24,28},{28,0},{1,5},{5... | collective-permute-start | bytes 73736 | tf_op jit(solution)/shard_map/ppermute | solution.py:30
  55.5 4.8 %copy-start.21 = (f32[16,3,128]{2,1,0:T(4,128)}, f32[16,3,128]{2,1,0:T(4,128)S(1)}, u32[]{:S(2)}) copy-start(f32[16,3,128]{2,1,0:T(4,128)S(1)} %collective-permute-done.27) | copy-start | bytes 73732
  55.5 16.4 %collective-permute-start.3 = (f32[16,3,128]{2,1,0:T(4,128)}, f32[16,3,128]{2,1,0:T(4,128)}, u32[]{:S(2)}, u32[]{:S(2)}) collective-permute-start(f32[16,3,128]{2,1,0:T(4,128)} %get-tuple-element.38), channel_id=1, source_target_pairs={{4,0},{8,4},{12,8},{16,12},{20,16},{24,20},{28,24},{0,28},{5,1},{9... | collective-permute-start | bytes 73736 | tf_op jit(solution)/shard_map/ppermute | solution.py:33
  63.3 19.6 %collective-permute-start.1 = (f32[16,3,128]{2,1,0:T(4,128)}, f32[16,3,128]{2,1,0:T(4,128)}, u32[]{:S(2)}, u32[]{:S(2)}) collective-permute-start(f32[16,3,128]{2,1,0:T(4,128)} %get-tuple-element.34), channel_id=1, source_target_pairs={{4,0},{8,4},{12,8},{16,12},{20,16},{24,20},{28,24},{0,28},{5,1},{9... | collective-permute-start | bytes 73736 | tf_op jit(solution)/shard_map/ppermute | solution.py:33
  65.3 18.5 %collective-permute-start.28 = (f32[16,70,3]{1,0,2:T(8,128)}, f32[16,70,3]{1,0,2:T(8,128)}, u32[]{:S(2)}, u32[]{:S(2)}) collective-permute-start(f32[16,70,3]{1,0,2:T(8,128)} %copy.83), channel_id=1, source_target_pairs={{0,1},{1,2},{2,3},{3,0},{4,5},{5,6},{6,7},{7,4},{8,9},{9,10},{10,1... | collective-permute-start | bytes 40328 | tf_op jit(solution)/shard_map/ppermute | solution.py:30
  70.1 17.2 %collective-permute-start.29 = (f32[16,70,3]{1,0,2:T(8,128)}, f32[16,70,3]{1,0,2:T(8,128)}, u32[]{:S(2)}, u32[]{:S(2)}) collective-permute-start(f32[16,70,3]{1,0,2:T(8,128)} %copy.85), channel_id=1, source_target_pairs={{1,0},{2,1},{3,2},{0,3},{5,4},{6,5},{7,6},{4,7},{9,8},{10,9},{11,1... | collective-permute-start | bytes 40328 | tf_op jit(solution)/shard_map/ppermute | solution.py:33
  71.8 17.4 %collective-permute-start.6 = (f32[16,70,3]{1,0,2:T(8,128)}, f32[16,70,3]{1,0,2:T(8,128)}, u32[]{:S(2)}, u32[]{:S(2)}) collective-permute-start(f32[16,70,3]{1,0,2:T(8,128)} %copy.53), channel_id=1, source_target_pairs={{0,1},{1,2},{2,3},{3,0},{4,5},{5,6},{6,7},{7,4},{8,9},{9,10},{10,1... | collective-permute-start | bytes 40328 | tf_op jit(solution)/shard_map/ppermute | solution.py:30
  72.7 4.1 %copy-start.8 = (f32[16,64,128]{2,1,0:T(8,128)S(1)}, f32[16,64,128]{2,1,0:T(8,128)}, u32[]{:S(2)}) copy-start(f32[16,64,128]{2,1,0:T(8,128)} %param.12) | copy-start | bytes 1572868
  72.7 4.1 %copy-start.20 = (f32[16,3,128]{2,1,0:T(4,128)S(1)}, f32[16,3,128]{2,1,0:T(4,128)}, u32[]{:S(2)}) copy-start(f32[16,3,128]{2,1,0:T(4,128)} %copy-done.19) | copy-start | bytes 73732
  75.9 19.1 %collective-permute-start.8 = (f32[16,70,3]{1,0,2:T(8,128)}, f32[16,70,3]{1,0,2:T(8,128)}, u32[]{:S(2)}, u32[]{:S(2)}) collective-permute-start(f32[16,70,3]{1,0,2:T(8,128)} %copy.57), channel_id=1, source_target_pairs={{0,1},{1,2},{2,3},{3,0},{4,5},{5,6},{6,7},{7,4},{8,9},{9,10},{10,1... | collective-permute-start | bytes 40328 | tf_op jit(solution)/shard_map/ppermute | solution.py:30
  82.9 14.0 %collective-permute-start.9 = (f32[16,70,3]{1,0,2:T(8,128)}, f32[16,70,3]{1,0,2:T(8,128)}, u32[]{:S(2)}, u32[]{:S(2)}) collective-permute-start(f32[16,70,3]{1,0,2:T(8,128)} %copy.58), channel_id=1, source_target_pairs={{1,0},{2,1},{3,2},{0,3},{5,4},{6,5},{7,6},{4,7},{9,8},{10,9},{11,1... | collective-permute-start | bytes 40328 | tf_op jit(solution)/shard_map/ppermute | solution.py:33
  83.7 16.8 %collective-permute-start.7 = (f32[16,70,3]{1,0,2:T(8,128)}, f32[16,70,3]{1,0,2:T(8,128)}, u32[]{:S(2)}, u32[]{:S(2)}) collective-permute-start(f32[16,70,3]{1,0,2:T(8,128)} %copy.54), channel_id=1, source_target_pairs={{1,0},{2,1},{3,2},{0,3},{5,4},{6,5},{7,6},{4,7},{9,8},{10,9},{11,1... | collective-permute-start | bytes 40328 | tf_op jit(solution)/shard_map/ppermute | solution.py:33
  87.3 25.1 %collective-permute-start.30 = (f32[3,4,16,64]{3,2,1,0:T(8,128)}, f32[3,4,16,64]{3,2,1,0:T(8,128)}, u32[]{:S(2)}, u32[]{:S(2)}) collective-permute-start(f32[3,4,16,64]{3,2,1,0:T(8,128)} %get-tuple-element.42), channel_id=1, source_target_pairs={{28,0},{0,4},{4,8},{8,12},{12,16},{16,20},{20,24},{24,28},{29,1},{... | collective-permute-start | bytes 147464 | tf_op jit(solution)/shard_map/ppermute | solution.py:41
  89.2 23.2 %collective-permute-start.31 = (f32[3,4,16,64]{3,2,1,0:T(8,128)}, f32[3,4,16,64]{3,2,1,0:T(8,128)}, u32[]{:S(2)}, u32[]{:S(2)}) collective-permute-start(f32[3,4,16,64]{3,2,1,0:T(8,128)} %get-tuple-element.43), channel_id=1, source_target_pairs={{4,0},{8,4},{12,8},{16,12},{20,16},{24,20},{28,24},{0,28},{5,1},{9... | collective-permute-start | bytes 147464 | tf_op jit(solution)/shard_map/ppermute | solution.py:41
  94.9 10.7 %copy-start.5 = (f32[16,70,3]{2,1,0:T(8,128)}, f32[16,70,3]{2,1,0:T(8,128)S(1)}, u32[]{:S(2)}) copy-start(f32[16,70,3]{2,1,0:T(8,128)S(1)} %copy.55) | copy-start | bytes 40324
  95.0 20.3 %collective-permute-start.14 = (f32[3,4,16,64]{3,2,1,0:T(8,128)}, f32[3,4,16,64]{3,2,1,0:T(8,128)}, u32[]{:S(2)}, u32[]{:S(2)}) collective-permute-start(f32[3,4,16,64]{3,2,1,0:T(8,128)} %get-tuple-element.54), channel_id=1, source_target_pairs={{3,0},{0,1},{1,2},{2,3},{7,4},{4,5},{5,6},{6,7},{11,8},{8,9},{9,10... | collective-permute-start | bytes 147464 | tf_op jit(solution)/shard_map/ppermute | solution.py:41
  96.9 18.3 %collective-permute-start.15 = (f32[3,4,16,64]{3,2,1,0:T(8,128)}, f32[3,4,16,64]{3,2,1,0:T(8,128)}, u32[]{:S(2)}, u32[]{:S(2)}) collective-permute-start(f32[3,4,16,64]{3,2,1,0:T(8,128)} %get-tuple-element.55), channel_id=1, source_target_pairs={{1,0},{2,1},{3,2},{0,3},{5,4},{6,5},{7,6},{4,7},{9,8},{10,9},{11,1... | collective-permute-start | bytes 147464 | tf_op jit(solution)/shard_map/ppermute | solution.py:41
  113.5 8.2 %collective-permute-start.32 = (f32[3,4,16,64]{3,2,1,0:T(8,128)S(1)}, f32[3,4,16,64]{3,2,1,0:T(8,128)S(1)}, u32[]{:S(2)}, u32[]{:S(2)}) collective-permute-start(f32[3,4,16,64]{3,2,1,0:T(8,128)S(1)} %get-tuple-element.39), channel_id=1, source_target_pairs={{3,0},{0,1},{1,2},{2,3},{7,4},{4,5},{5,6},{6,7},{11,8},{8,9},{9,10... | collective-permute-start | bytes 147464 | tf_op jit(solution)/shard_map/ppermute | solution.py:41
  113.5 8.1 %collective-permute-start.33 = (f32[3,4,16,64]{3,2,1,0:T(8,128)S(1)}, f32[3,4,16,64]{3,2,1,0:T(8,128)S(1)}, u32[]{:S(2)}, u32[]{:S(2)}) collective-permute-start(f32[3,4,16,64]{3,2,1,0:T(8,128)S(1)} %get-tuple-element.40), channel_id=1, source_target_pairs={{1,0},{2,1},{3,2},{0,3},{5,4},{6,5},{7,6},{4,7},{9,8},{10,9},{11,1... | collective-permute-start | bytes 147464 | tf_op jit(solution)/shard_map/ppermute | solution.py:41
  116.9 6.5 %copy-start.28 = (s32[36]{0:T(128)S(1)}, s32[36]{0:T(128)}, u32[]{:S(2)}) copy-start(s32[36]{0:T(128)} %fusion.108) | copy-start | bytes 436
  116.9 28.1 %collective-permute-start.16 = (f32[3,4,16,64]{3,2,1,0:T(8,128)}, f32[3,4,16,64]{3,2,1,0:T(8,128)}, u32[]{:S(2)}, u32[]{:S(2)}) collective-permute-start(f32[3,4,16,64]{3,2,1,0:T(8,128)} %get-tuple-element.51), channel_id=1, source_target_pairs={{28,0},{0,4},{4,8},{8,12},{12,16},{16,20},{20,24},{24,28},{29,1},{... | collective-permute-start | bytes 147464 | tf_op jit(solution)/shard_map/ppermute | solution.py:41
  116.9 28.1 %collective-permute-start.17 = (f32[3,4,16,64]{3,2,1,0:T(8,128)S(1)}, f32[3,4,16,64]{3,2,1,0:T(8,128)}, u32[]{:S(2)}, u32[]{:S(2)}) collective-permute-start(f32[3,4,16,64]{3,2,1,0:T(8,128)S(1)} %get-tuple-element.52), channel_id=1, source_target_pairs={{4,0},{8,4},{12,8},{16,12},{20,16},{24,20},{28,24},{0,28},{5,1},{9... | collective-permute-start | bytes 147464 | tf_op jit(solution)/shard_map/ppermute | solution.py:41
  148.4 10.0 %copy-start.12 = (f32[36,16,64]{2,1,0:T(8,128)}, f32[36,16,64]{2,1,0:T(8,128)S(1)}, u32[]{:S(2)}) copy-start(f32[36,16,64]{2,1,0:T(8,128)S(1)} %gather_fusion) | copy-start | bytes 442372
  173.2 7.2 %collective-permute-start.18 = (f32[16,3,128]{2,1,0:T(4,128)S(1)}, f32[16,3,128]{2,1,0:T(4,128)S(1)}, u32[]{:S(2)}, u32[]{:S(2)}) collective-permute-start(f32[16,3,128]{2,1,0:T(4,128)S(1)} %get-tuple-element.31), channel_id=1, source_target_pairs={{0,4},{4,8},{8,12},{12,16},{16,20},{20,24},{24,28},{28,0},{1,5},{5... | collective-permute-start | bytes 73736 | tf_op jit(solution)/shard_map/ppermute | solution.py:30
  173.3 7.1 %collective-permute-start.19 = (f32[16,3,128]{2,1,0:T(4,128)S(1)}, f32[16,3,128]{2,1,0:T(4,128)S(1)}, u32[]{:S(2)}, u32[]{:S(2)}) collective-permute-start(f32[16,3,128]{2,1,0:T(4,128)S(1)} %get-tuple-element.32), channel_id=1, source_target_pairs={{4,0},{8,4},{12,8},{16,12},{20,16},{24,20},{28,24},{0,28},{5,1},{9... | collective-permute-start | bytes 73736 | tf_op jit(solution)/shard_map/ppermute | solution.py:33
  178.6 10.5 %collective-permute-start.22 = (f32[3,4,16,64]{3,2,1,0:T(8,128)}, f32[3,4,16,64]{3,2,1,0:T(8,128)}, u32[]{:S(2)}, u32[]{:S(2)}) collective-permute-start(f32[3,4,16,64]{3,2,1,0:T(8,128)} %get-tuple-element.48), channel_id=1, source_target_pairs={{3,0},{0,1},{1,2},{2,3},{7,4},{4,5},{5,6},{6,7},{11,8},{8,9},{9,10... | collective-permute-start | bytes 147464 | tf_op jit(solution)/shard_map/ppermute | solution.py:41
  178.7 10.5 %collective-permute-start.23 = (f32[3,4,16,64]{3,2,1,0:T(8,128)}, f32[3,4,16,64]{3,2,1,0:T(8,128)}, u32[]{:S(2)}, u32[]{:S(2)}) collective-permute-start(f32[3,4,16,64]{3,2,1,0:T(8,128)} %get-tuple-element.49), channel_id=1, source_target_pairs={{1,0},{2,1},{3,2},{0,3},{5,4},{6,5},{7,6},{4,7},{9,8},{10,9},{11,1... | collective-permute-start | bytes 147464 | tf_op jit(solution)/shard_map/ppermute | solution.py:41
  180.9 3.6 %collective-permute-start.20 = (f32[16,70,3]{1,0,2:T(8,128)S(1)}, f32[16,70,3]{1,0,2:T(8,128)}, u32[]{:S(2)}, u32[]{:S(2)}) collective-permute-start(f32[16,70,3]{1,0,2:T(8,128)S(1)} %copy.72), channel_id=1, source_target_pairs={{0,1},{1,2},{2,3},{3,0},{4,5},{5,6},{6,7},{7,4},{8,9},{9,10},{10,1... | collective-permute-start | bytes 40328 | tf_op jit(solution)/shard_map/ppermute | solution.py:30
  181.8 3.8 %collective-permute-start.21 = (f32[16,70,3]{1,0,2:T(8,128)}, f32[16,70,3]{1,0,2:T(8,128)}, u32[]{:S(2)}, u32[]{:S(2)}) collective-permute-start(f32[16,70,3]{1,0,2:T(8,128)} %copy.73), channel_id=1, source_target_pairs={{1,0},{2,1},{3,2},{0,3},{5,4},{6,5},{7,6},{4,7},{9,8},{10,9},{11,1... | collective-permute-start | bytes 40328 | tf_op jit(solution)/shard_map/ppermute | solution.py:33
  189.1 5.9 %copy-start.4 = (f32[16,64,133]{2,1,0:T(8,128)S(1)}, f32[16,64,133]{2,1,0:T(8,128)}, u32[]{:S(2)}) copy-start(f32[16,64,133]{2,1,0:T(8,128)} %copy-done.3) | copy-start | bytes 1634308
  190.2 8.2 %collective-permute-start.24 = (f32[3,4,16,64]{3,2,1,0:T(8,128)S(1)}, f32[3,4,16,64]{3,2,1,0:T(8,128)S(1)}, u32[]{:S(2)}, u32[]{:S(2)}) collective-permute-start(f32[3,4,16,64]{3,2,1,0:T(8,128)S(1)} %get-tuple-element.45), channel_id=1, source_target_pairs={{28,0},{0,4},{4,8},{8,12},{12,16},{16,20},{20,24},{24,28},{29,1},{... | collective-permute-start | bytes 147464 | tf_op jit(solution)/shard_map/ppermute | solution.py:41
  190.3 8.1 %collective-permute-start.25 = (f32[3,4,16,64]{3,2,1,0:T(8,128)S(1)}, f32[3,4,16,64]{3,2,1,0:T(8,128)S(1)}, u32[]{:S(2)}, u32[]{:S(2)}) collective-permute-start(f32[3,4,16,64]{3,2,1,0:T(8,128)S(1)} %get-tuple-element.46), channel_id=1, source_target_pairs={{4,0},{8,4},{12,8},{16,12},{20,16},{24,20},{28,24},{0,28},{5,1},{9... | collective-permute-start | bytes 147464 | tf_op jit(solution)/shard_map/ppermute | solution.py:41
  (16 other events, 34.0 us)
where the time goes:
time: 231 us; the launch traced here: 229 us
  local copies, waits for them, and re-layouts  92.2 us (40%)
  other arithmetic  60.5 us (26%)
  starting transfers between devices  53.1 us (23%)
  matrix products  14.3 us (6%)
  waiting for transfers between devices  6.35 us (3%)
    ppermute x9, starting transfers between devices, with_halo(): lax.ppermute(lax.slice_in_dim(block, 0, width, axis=dim), axis, backward)  26.4 us
    ppermute x16, starting transfers between devices, shifted(): return lax.ppermute(block, axis, route)  25.6 us
    scatter-add x2, other arithmetic, pull(): jnp.zeros((tile_total, planes, TILE), jnp.float32).at[source]  12.7 us
    slice x13, local copies, waits for them, and re-layouts, with_halo(): lax.slice_in_dim(block, block.shape[dim] - width, None, axis=dim)  12.6 us
    scatter x2, local copies, waits for them, and re-layouts, place(): packed = empty_slots.at[lane_index, rank_index].set(values, mode='drop')  8.1 us
    dot_general x2, matrix products, pull(): jnp.einsum('sza,szb->sab', returned, picked_source, precision=PRECISE)  7.42 us
    ppermute x4, local copies, waits for them, and re-layouts, with_halo(): lax.ppermute(lax.slice_in_dim(block, 0, width, axis=dim), axis, backward)  7.39 us
    concatenate x7, other arithmetic, with_halo(): block = jnp.concatenate([low, block, high], axis=dim)  6.7 us
  transfers between devices with their start and end apart: 34, of which 3 were waited for; matrix products, arithmetic and copies ran while one was open for 45% of the time, Pallas kernels for 0%

commit v1 on v0

v1 whole, which is shorter than its diff:
```python
import functools

import jax
import jax.numpy as jnp
from jax import lax
from jax.experimental import pallas as pl
from jax.experimental.pallas import tpu as pltpu
from jax.sharding import PartitionSpec as P

TILE = 64
ROUTE_MOST = 4
TIME_STEP = 0.3
WEIGHTS = (2.0 / 60.0, -13.0 / 60.0, 47.0 / 60.0, 27.0 / 60.0, -3.0 / 60.0)
PAD = 80
VMEM_LIMIT = 56 << 20

A, B, S = 0, 1, 2


def matching(count, which):
    return [(i, (i + (1 if (i % 2 == 0) == (which == B) else -1)) % count) for i in range(count)]


def exchange(block, axis, which):
    return lax.ppermute(block, axis, matching(lax.axis_size(axis), which))


def lanes(shape):
    return lax.broadcasted_iota(jnp.int32, shape, len(shape) - 1)


def roll(value, shift):
    return pltpu.roll(value, shift % 128 if isinstance(shift, int) else shift, axis=value.ndim - 1)


def split(value):
    high = value.astype(jnp.bfloat16)
    return high, (value - high.astype(jnp.float32)).astype(jnp.bfloat16)


def pair_dot(value, matrix, over):
    high, low = split(value)
    both = lax.dot_general(
        jnp.concatenate([high, low], axis=0),
        matrix,
        (((1,), (over,)), ((), ())),
        preferred_element_type=jnp.float32,
    )
    rows = value.shape[0]
    return both[:rows] + both[rows:]


def row_of(ref, x, planes, stride):
    return ref[pl.ds(x, planes, stride), :]


def tile_pair(ref, first, second, planes, extent_x):
    one = row_of(ref, first // 2, planes, extent_x)
    two = row_of(ref, second // 2, planes, extent_x)
    lane = lanes(one.shape)
    one = jnp.where(first % 2 == 0, one, roll(one, TILE))
    two = jnp.where(second % 2 == 1, two, roll(two, TILE))
    return jnp.where(lane < TILE, one, two)


def add_tile_pair(ref, first, second, value, planes, extent_x):
    lane = lanes(value.shape)
    turned = roll(value, TILE)
    for tile, half in ((first, 0), (second, 1)):
        spot = pl.ds(tile // 2, planes, extent_x)
        placed = jnp.where(tile % 2 == half, value, turned)
        keep = (lane // TILE) == tile % 2
        ref[spot, :] = ref[spot, :] + jnp.where(keep, placed, 0.0)


def edge_pack(ref, planes, extent_x):
    lane = lanes((extent_x, 128))
    packed = jnp.zeros((extent_x, 128), jnp.float32)
    for z in range(planes):
        plane = ref[z * extent_x : (z + 1) * extent_x, :]
        packed = jnp.where(lane // 8 == z, roll(plane, 8 * z + 3), packed)
    return packed


def edge_rows(ref, start, planes, extent_x):
    return jnp.concatenate([row_of(ref, start + j, planes, extent_x) for j in range(3)], axis=0)


def upwind(face_rate):
    return jnp.maximum(face_rate, 0.0), jnp.minimum(face_rate, 0.0)


UP = {2: WEIGHTS[0], 1: WEIGHTS[1], 0: WEIGHTS[2], -1: WEIGHTS[3], -2: WEIGHTS[4]}
DOWN = {1: WEIGHTS[4], 0: WEIGHTS[3], -1: WEIGHTS[2], -2: WEIGHTS[1], -3: WEIGHTS[0]}


def combine(up_part, down_part, k):
    total = 0.0
    if k in UP:
        total = total + UP[k] * up_part
    if k in DOWN:
        total = total + DOWN[k] * down_part
    return total


def fill_padded(pad_ref, field_ref, rows_a, rows_b, even, planes, extent_x):
    high = 8 + extent_x
    at_a = jnp.where(even, 5, high)
    at_b = jnp.where(even, high, 5)
    for z in range(planes):
        pad_ref[z * PAD + 8 : z * PAD + high, :] = field_ref[z * extent_x : (z + 1) * extent_x, :]
    for j in range(3):
        part = slice(j * planes, (j + 1) * planes)
        pad_ref[pl.ds(at_a + j, planes, PAD), :] = rows_a[part]
        pad_ref[pl.ds(at_b + j, planes, PAD), :] = rows_b[part]


def edge_join(from_a, from_b, even):
    low = jnp.where(even, from_a, from_b)
    high = jnp.where(even, from_b, from_a)
    return jnp.where(lanes(low.shape) % 8 < 3, low, high)


def adjoint_edges(own, halo, own_rate, halo_rate):
    lane = lanes(own.shape) % 8
    after = roll(jnp.where(lane == 3, own, halo), -1)
    before = roll(jnp.where(lane == 2, own, halo), 1)
    jump = jnp.where(lane < 3, after - halo, halo - before)
    rate = jnp.where(lane < 3, halo_rate, roll(jnp.where(lane == 2, own_rate, halo_rate), 1))
    rate_up, rate_down = upwind(rate)
    up_part, down_part = rate_up * jump, rate_down * jump
    low_side = 0.0
    high_side = 0.0
    for k in (-1, -2, -3):
        part = jnp.where(lane < 3, combine(up_part, down_part, k), 0.0)
        low_side = low_side + roll(part, -k)
    for k in (0, 1, 2):
        part = jnp.where((lane >= 3) & (lane < 6), combine(up_part, down_part, k), 0.0)
        high_side = high_side + roll(part, -(k + 1))
    return jnp.where(lane < 3, high_side, jnp.where(lane < 6, low_side, 0.0))


def adjoint_plane(z, pad_ref, pad_rate_ref, rate_y_ref, edges, up_ref, down_ref, extent_x):
    base = pl.multiple_of(z * PAD, 8)
    here = pad_ref[pl.ds(base, PAD), :]
    jump = pad_ref[pl.ds(base + 1, PAD), :] - here
    rate_up, rate_down = upwind(pad_rate_ref[pl.ds(base, PAD), :])
    up_ref[pl.ds(base, PAD), :] = rate_up * jump
    down_ref[pl.ds(base, PAD), :] = rate_down * jump
    total = 0.0
    for k in range(-3, 3):
        if k in UP:
            total = total + UP[k] * up_ref[pl.ds(base + 8 + k, extent_x), :]
        if k in DOWN:
            total = total + DOWN[k] * down_ref[pl.ds(base + 8 + k, extent_x), :]
    field = pad_ref[pl.ds(base + 8, extent_x), :]
    lane = lanes(field.shape)
    jump = jnp.where(lane == 127, 0.0, roll(field, -1) - field)
    rate_up, rate_down = upwind(rate_y_ref[pl.ds(pl.multiple_of(z * extent_x, 8), extent_x), :])
    up_part, down_part = rate_up * jump, rate_down * jump
    ahead = combine(up_part, down_part, 2)
    for k in (1, 0):
        ahead = jnp.where(lane == 127, 0.0, roll(ahead, -1)) + combine(up_part, down_part, k)
    behind = combine(up_part, down_part, -3)
    for k in (-2, -1):
        behind = jnp.where(lane == 0, 0.0, roll(behind, 1)) + combine(up_part, down_part, k)
    behind = jnp.where(lane == 0, 0.0, roll(behind, 1))
    rim = roll(edges, 125 - 8 * z)
    return total + ahead + behind + jnp.where((lane < 3) | (lane >= 125), rim, 0.0)


def dim(ref):
    return ref.shape[0]


def begin_body(info, count, heading, target, source, field, cotan, rate_x, rate_y, order, rows_a, rows_b, packs, used, *, planes, extent_x):
    slots = heading.shape[0]
    for label in range(9):
        used[label] = 0
    lane = lanes((8, 128))

    def place(slot, asked):
        toward = heading[slot]
        flip_x = 1 - 2 * info[0]
        flip_y = 1 - 2 * info[1]
        ex = (toward // 3 - 1) * flip_x
        ey = (lax.rem(toward, 3) - 1) * flip_y
        lx = jnp.where(ex == 0, 2, (ex + 1) // 2)
        ly = jnp.where(ey == 0, 2, (ey + 1) // 2)
        label = ly * 3 + lx
        spot = label * ROUTE_MOST + used[label]
        used[label] = used[label] + 1
        alive = slot < count[0]
        order[0, spot] = slot
        order[1, spot] = source[slot]
        order[2, spot] = alive.astype(jnp.int32)
        wanted = jnp.where(alive, target[slot], 0)
        return jnp.where(lane == spot, wanted, asked)

    asked = lax.fori_loop(0, slots, place, jnp.zeros((8, 128), jnp.int32))
    asked = asked.astype(jnp.float32)
    even = info[0] == 0
    high = extent_x - 3
    for rows, start in ((rows_a, jnp.where(even, 0, high)), (rows_b, jnp.where(even, high, 0))):
        rows[0:8, :] = asked
        for number, ref in enumerate((cotan, rate_x, field)):
            first = 8 + number * 3 * planes
            rows[first : first + 3 * planes, :] = edge_rows(ref, start, planes, extent_x)
    for number, ref in enumerate((cotan, rate_y, field)):
        packs[number * extent_x : (number + 1) * extent_x, :] = edge_pack(ref, planes, extent_x)


def extend_body(order, field, blocks, pairs, picked, values, *, planes, extent_x):
    def one(number, carry):
        first, second = order[0, 2 * number], order[0, 2 * number + 1]
        one_block, two_block = blocks[first], blocks[second]
        zero = jnp.zeros_like(one_block)
        joined = jnp.concatenate(
            [jnp.concatenate([one_block, zero], axis=1), jnp.concatenate([zero, two_block], axis=1)], axis=0
        )
        pairs[number] = joined
        tiles = tile_pair(field, order[1, 2 * number], order[1, 2 * number + 1], planes, extent_x)
        picked[number] = tiles
        lane = lanes(tiles.shape)
        alive = jnp.where(lane < TILE, order[2, 2 * number], order[2, 2 * number + 1])
        values[number] = pair_dot(jnp.where(alive == 1, tiles, 0.0), joined, 1)
        return carry

    lax.fori_loop(0, pairs.shape[0], one, 0)


def gather_tiles(asked, field, outs, planes, extent_x):
    for ly in range(3):
        for lx in range(3):
            label = ly * 3 + lx
            for half in range(2):
                first = asked[label, label * ROUTE_MOST + 2 * half]
                second = asked[label, label * ROUTE_MOST + 2 * half + 1]
                outs[ly](lx, half, tile_pair(field, first, second, planes, extent_x))


def serve_body(asked, field, values, out_a, out_b, out_s, *, planes, extent_x):
    outs = (out_a, out_b, out_s)

    def writer(out):
        def write(lx, half, tiles):
            out[lx, half * planes : (half + 1) * planes, :] = tiles

        return write

    gather_tiles(asked, field, [writer(out) for out in outs], planes, extent_x)
    for ly, out in enumerate(outs):
        for lx in range(3):
            for half in range(2):
                out[3 + lx, half * planes : (half + 1) * planes, :] = values[(ly * 3 + lx) * 2 + half]


def landed(lx, ly, half, planes, shift, x_a, x_b, y_a, y_b, own):
    rows = slice(half * planes, (half + 1) * planes)
    if lx == S:
        return (y_a, y_b, own)[ly][shift + S, rows, :]
    return (x_a, x_b)[lx][shift + (1, 2, 0)[ly], rows, :]


def middle_body(
    info, order, asked, cotan, rate_x, rate_y, rows_a, rows_b, packs, packs_a, packs_b, x_a, x_b, y_a, y_b, own, pairs,
    grad, pad_grad_rate, edge_rate, returned, send_a, send_b, send_s, send_rows_a, send_rows_b,
    pad, up_ref, down_ref, *, planes, extent_x,
):
    even_x, even_y = info[0] == 0, info[1] == 0
    rows = 3 * planes
    fill_padded(pad, cotan, rows_a[8 : 8 + rows], rows_b[8 : 8 + rows], even_x, planes, extent_x)
    fill_padded(
        pad_grad_rate, rate_x, rows_a[8 + rows : 8 + 2 * rows], rows_b[8 + rows : 8 + 2 * rows], even_x, planes, extent_x
    )
    part = lambda ref, number, first: ref[first + number * extent_x : first + (number + 1) * extent_x]
    halo = edge_join(part(packs_a, 0, 24), part(packs_b, 0, 24), even_y)
    halo_rate = edge_join(part(packs_a, 1, 24), part(packs_b, 1, 24), even_y)
    edge_rate[...] = halo_rate
    edges = adjoint_edges(part(packs, 0, 0), halo, part(packs, 1, 0), halo_rate)

    def plane(z, carry):
        spot = pl.ds(pl.multiple_of(z * extent_x, 8), extent_x)
        pulled = adjoint_plane(z, pad, pad_grad_rate, rate_y, edges, up_ref, down_ref, extent_x)
        grad[spot, :] = 0.5 * cotan[spot, :] + (0.5 * TIME_STEP) * pulled
        return carry

    lax.fori_loop(0, planes, plane, 0)
    for ly in range(3):
        for lx in range(3):
            for half in range(2):
                number = (ly * 3 + lx) * 2 + half
                back = landed(lx, ly, half, planes, 0, x_a, x_b, y_a, y_b, own)
                lane = lanes(back.shape)
                alive = jnp.where(lane < TILE, order[2, 2 * number], order[2, 2 * number + 1])
                back = jnp.where(alive == 1, back, 0.0)
                returned[number] = back
                pulled = (0.5 * TIME_STEP) * pair_dot(back, pairs[number], 0)
                add_tile_pair(grad, order[1, 2 * number], order[1, 2 * number + 1], pulled, planes, extent_x)
    packed = edge_pack(grad, planes, extent_x)
    outs = (send_a, send_b, send_s)

    def writer(out):
        def write(lx, half, tiles):
            first = extent_x + (lx * 2 + half) * planes
            out[first : first + planes, :] = tiles

        return write

    for out in outs:
        out[0:extent_x, :] = packed
    gather_tiles(asked, grad, [writer(out) for out in outs], planes, extent_x)
    high = extent_x - 3
    send_rows_a[...] = edge_rows(grad, jnp.where(even_x, 0, high), planes, extent_x)
    send_rows_b[...] = edge_rows(grad, jnp.where(even_x, high, 0), planes, extent_x)


def section_body(
    info, order, asked, field, pad_rate, rate_y, packs, packs_a, packs_b, rows_a, rows_b, x_a, x_b, y_a, y_b, own,
    picked, pad, section, flux_ref, *, planes, extent_x,
):
    even_x, even_y = info[0] == 0, info[1] == 0
    rows = 3 * planes
    first = 8 + 2 * rows
    fill_padded(pad, field, rows_a[first : first + rows], rows_b[first : first + rows], even_x, planes, extent_x)
    part = lambda ref, number, first: ref[first + number * extent_x : first + (number + 1) * extent_x]
    halo = edge_join(part(packs_a, 2, 24), part(packs_b, 2, 24), even_y)
    own_edge = part(packs, 2, 0)
    halo_rate = edge_join(part(packs_a, 1, 24), part(packs_b, 1, 24), even_y)
    lane8 = lanes(halo.shape) % 8
    line = jnp.where(lane8 < 3, halo, own_edge)
    moved = {k: roll(line, -k) for k in range(-2, 4)}
    rate_up, rate_down = upwind(halo_rate)
    flux_low = rate_up * sum(WEIGHTS[j] * moved[j - 2] for j in range(5)) + rate_down * sum(
        WEIGHTS[j] * moved[3 - j] for j in range(5)
    )

    def plane(z, carry):
        base = pl.multiple_of(z * PAD, 8)
        spot = pl.ds(pl.multiple_of(z * extent_x, 8), extent_x)
        window = extent_x + 8
        near = {k: pad[pl.ds(base + 7 + k, window), :] for k in range(-2, 4)}
        rate_up, rate_down = upwind(pad_rate[pl.ds(base + 7, window), :])
        flux_ref[pl.ds(base, window), :] = rate_up * sum(WEIGHTS[j] * near[j - 2] for j in range(5)) + rate_down * sum(
            WEIGHTS[j] * near[3 - j] for j in range(5)
        )
        change = flux_ref[pl.ds(base, extent_x), :] - flux_ref[pl.ds(base + 1, extent_x), :]
        here = field[spot, :]
        lane = lanes(here.shape)
        turn = 125 - 8 * z
        rim = roll(halo, turn)
        near = {0: here}
        for k in (1, 2, 3):
            near[k] = roll(jnp.where(lane < k, rim, here), -k)
        for k in (1, 2):
            near[-k] = roll(jnp.where(lane >= 128 - k, rim, here), k)
        rate_up, rate_down = upwind(rate_y[spot, :])
        flux = rate_up * sum(WEIGHTS[j] * near[j - 2] for j in range(5)) + rate_down * sum(
            WEIGHTS[j] * near[3 - j] for j in range(5)
        )
        change = change + roll(jnp.where(lane == 127, roll(flux_low, turn), flux), 1) - flux
        section[spot, :] = here + TIME_STEP * change
        return carry

    lax.fori_loop(0, planes, plane, 0)
    for ly in range(3):
        for lx in range(3):
            label = ly * 3 + lx
            for half in range(2):
                came = landed(lx, ly, half, planes, 3, x_a, x_b, y_a, y_b, own)
                at = label * ROUTE_MOST + 2 * half
                add_tile_pair(section, asked[label, at], asked[label, at + 1], TIME_STEP * came, planes, extent_x)

    def pick(number, carry):
        picked[number] = tile_pair(section, order[1, 2 * number], order[1, 2 * number + 1], planes, extent_x)
        return carry

    lax.fori_loop(0, picked.shape[0], pick, 0)


def last_body(
    info, order, cotan, grad, pad_rate, rate_y, edge_rate, packs, own, y_a, y_b, x_a, x_b, pairs, returned,
    picked_start, picked_section, out, out_blocks,
    pad, up_ref, down_ref, work, *, planes, extent_x,
):
    even_x, even_y = info[0] == 0, info[1] == 0
    rows = 3 * planes
    fill_padded(pad, grad, x_a[0:rows], x_b[0:rows], even_x, planes, extent_x)
    halo = edge_join(y_a[0:extent_x], y_b[0:extent_x], even_y)
    edges = adjoint_edges(own[0:extent_x], halo, packs[extent_x : 2 * extent_x], edge_rate[...])

    def plane(z, carry):
        spot = pl.ds(pl.multiple_of(z * extent_x, 8), extent_x)
        pulled = adjoint_plane(z, pad, pad_rate, rate_y, edges, up_ref, down_ref, extent_x)
        out[spot, :] = 0.5 * cotan[spot, :] + grad[spot, :] + TIME_STEP * pulled
        return carry

    lax.fori_loop(0, planes, plane, 0)
    half_lane = lanes((TILE // 2, 128)) < TILE
    for ly in range(3):
        for lx in range(3):
            for half in range(2):
                number = (ly * 3 + lx) * 2 + half
                if lx == S:
                    ref, first = (y_a, y_b, own)[ly], extent_x + (S * 2 + half) * planes
                else:
                    ref, first = (x_a, x_b)[lx], rows + ((1, 2, 0)[ly] * 2 + half) * planes
                back = ref[first : first + planes, :]
                lane = lanes(back.shape)
                alive = jnp.where(lane < TILE, order[2, 2 * number], order[2, 2 * number + 1])
                back = jnp.where(alive == 1, back, 0.0)
                pulled = TIME_STEP * pair_dot(back, pairs[number], 0)
                add_tile_pair(out, order[1, 2 * number], order[1, 2 * number + 1], pulled, planes, extent_x)
                left = jnp.concatenate([(0.5 * TIME_STEP) * returned[number], TIME_STEP * back], axis=0)
                right = jnp.concatenate([picked_section[number], picked_start[number]], axis=0)
                left_high, left_low = split(left)
                right_high, right_low = split(right)
                outer = lax.dot_general(
                    jnp.concatenate([left_high, left_high, left_low], axis=0),
                    jnp.concatenate([right_high, right_low, right_high], axis=0),
                    (((0,), (0,)), ((), ())),
                    preferred_element_type=jnp.float32,
                )
                work[number] = outer
                for which in range(2):
                    slot = order[0, 2 * number + which]
                    even_rows = work[number, pl.ds(which * TILE, TILE // 2, 2), :]
                    odd_rows = work[number, pl.ds(which * TILE + 1, TILE // 2, 2), :]
                    if which == 0:
                        merged = jnp.where(half_lane, even_rows, roll(odd_rows, TILE))
                    else:
                        merged = jnp.where(half_lane, roll(even_rows, TILE), odd_rows)
                    out_blocks[pl.ds((slot // 8) * 256 + slot % 8, TILE // 2, 8), :] = merged


def call(body, ins, outs, scratch=(), smem_in=0, smem_out=0, **sizes):
    vmem = pl.BlockSpec(memory_space=pltpu.VMEM)
    smem = pl.BlockSpec(memory_space=pltpu.SMEM)
    return pl.pallas_call(
        functools.partial(body, **sizes),
        out_shape=tuple(jax.ShapeDtypeStruct(shape, kind) for shape, kind in outs),
        in_specs=[smem] * smem_in + [vmem] * (len(ins) - smem_in),
        out_specs=tuple([smem] * smem_out + [vmem] * (len(outs) - smem_out)),
        scratch_shapes=list(scratch),
        compiler_params=pltpu.CompilerParams(vmem_limit_bytes=VMEM_LIMIT),
        name=body.__name__,
    )(*ins)


def shards(
    level_set, speed_x, speed_y, cotangent, blocks, tile_count, source_tile, dest_offset, dest_tile
):
    planes, extent_x, extent_y = level_set.shape
    slots = source_tile.shape[2]
    cells = planes * extent_x
    f32, i32 = jnp.float32, jnp.int32
    field, rate_x, rate_y, cotan = (v.reshape(cells, extent_y) for v in (level_set, speed_x, speed_y, cotangent))
    info = jnp.stack([lax.axis_index("gx") % 2, lax.axis_index("gy") % 2]).astype(i32)
    sizes = dict(planes=planes, extent_x=extent_x)
    rows = 3 * planes
    pair_total = slots // 2
    padded = pltpu.VMEM((planes * PAD + 8, extent_y), f32)

    order, rows_a, rows_b, packs = call(
        begin_body,
        (info, tile_count.reshape(1), dest_offset.reshape(slots), dest_tile.reshape(slots), source_tile.reshape(slots),
         field, cotan, rate_x, rate_y),
        [((3, slots), i32), ((8 + 3 * rows, extent_y), f32), ((8 + 3 * rows, extent_y), f32), ((3 * extent_x, extent_y), f32)],
        scratch=(pltpu.SMEM((9,), i32),), smem_in=5, smem_out=1, **sizes,
    )
    got_rows_a = exchange(rows_a, "gx", A)
    got_rows_b = exchange(rows_b, "gx", B)
    column = jnp.concatenate([rows_a[:8], got_rows_a[:8], got_rows_b[:8], packs], axis=0)
    got_packs_a = exchange(column, "gy", A)
    got_packs_b = exchange(column, "gy", B)

    pairs, picked_start, values = call(
        extend_body,
        (order, field, blocks.reshape(slots, TILE, TILE)),
        [((pair_total, 128, 128), jnp.bfloat16), ((pair_total, planes, 128), f32), ((pair_total, planes, 128), f32)],
        smem_in=1, **sizes,
    )

    asked = jnp.concatenate(
        [got_packs_a[8:9], got_packs_a[16:17], got_packs_a[0:1],
         got_packs_b[8:9], got_packs_b[16:17], got_packs_b[0:1],
         column[8:9], column[16:17], column[0:1]], axis=0,
    ).astype(i32)
    box = ((6, 2 * planes, 128), f32)
    out_a, out_b, own = call(serve_body, (asked, cotan, values), [box, box, box], smem_in=1, **sizes)
    y_a = exchange(out_a, "gy", A)
    y_b = exchange(out_b, "gy", B)
    forward = lambda m: jnp.stack([own[m], y_a[m], y_b[m], own[3 + m], y_a[3 + m], y_b[3 + m]])
    x_a = exchange(forward(A), "gx", A)
    x_b = exchange(forward(B), "gx", B)

    send = ((extent_x + 6 * planes, 128), f32)
    grad, pad_rate, edge_rate, returned, send_a, send_b, send_s, send_rows_a, send_rows_b = call(
        middle_body,
        (info, order, asked, cotan, rate_x, rate_y, got_rows_a, got_rows_b, packs, got_packs_a, got_packs_b,
         x_a, x_b, y_a, y_b, own, pairs),
        [((cells, 128), f32), ((planes * PAD + 8, 128), f32), ((extent_x, 128), f32), ((pair_total, planes, 128), f32),
         send, send, send, ((rows, 128), f32), ((rows, 128), f32)],
        scratch=(padded, padded, padded), smem_in=3, **sizes,
    )
    last_y_a = exchange(send_a, "gy", A)
    last_y_b = exchange(send_b, "gy", B)

    def onward(edge, m):
        first = extent_x + m * 2 * planes
        part = slice(first, first + 2 * planes)
        return jnp.concatenate([edge, send_s[part], last_y_a[part], last_y_b[part]], axis=0)

    last_x_a = exchange(onward(send_rows_a, A), "gx", A)
    last_x_b = exchange(onward(send_rows_b, B), "gx", B)

    (picked_section,) = call(
        section_body,
        (info, order, asked, field, pad_rate, rate_y, packs, got_packs_a, got_packs_b, got_rows_a, got_rows_b,
         x_a, x_b, y_a, y_b, own),
        [((pair_total, planes, 128), f32)],
        scratch=(padded, pltpu.VMEM((cells, 128), f32), padded), smem_in=3, **sizes,
    )
    row_tiles = -(-slots // 8)
    grad_level_set, grad_blocks = call(
        last_body,
        (info, order, cotan, grad, pad_rate, rate_y, edge_rate, packs, send_s, last_y_a, last_y_b, last_x_a, last_x_b,
         pairs, returned, picked_start, picked_section),
        [((cells, 128), f32), ((row_tiles * 256, 128), f32)],
        scratch=(padded, padded, padded, pltpu.VMEM((pair_total, 128, 128), f32)), smem_in=2, **sizes,
    )
    grad_blocks = grad_blocks.reshape(row_tiles, TILE // 2, 8, 128).transpose(0, 2, 1, 3)
    grad_blocks = grad_blocks.reshape(row_tiles * 8, TILE * TILE)[:slots]
    return (grad_level_set.reshape(planes, extent_x, extent_y), grad_blocks.reshape(1, 1, slots, TILE * TILE))


def solution(mesh):
    return jax.shard_map(
        shards,
        mesh=mesh,
        in_specs=(
            P(None, "gx", "gy"),
            P(None, "gx", "gy"),
            P(None, "gx", "gy"),
            P(None, "gx", "gy"),
            P("gx", "gy", None, None),
            P("gx", "gy"),
            P("gx", "gy", None),
            P("gx", "gy", None),
            P("gx", "gy", None),
        ),
        out_specs=(P(None, "gx", "gy"), P("gx", "gy", None, None)),
        check_vma=False,
    )
```

time: 231 us -> 88.5 us (0.38)
  local copies, waits for them, and re-layouts: 92.2 us -> 10.4 us
  other arithmetic: 60.5 us -> 2.2 us
  Pallas kernels: 0 us -> 39.3 us
  starting transfers between devices: 53.1 us -> 18.8 us
  matrix products: 14.3 us -> 0 us
  waiting for transfers between devices: 6.35 us -> 15.4 us
    pallas_call x0 -> x6, Pallas kernels: none -> 39.3 us  [call(): pl.pallas_call(functools.partial(body, **sizes), out_shape=tuple((jax.Sha...]
    ppermute x34 -> x12, starting transfers between devices: 53.1 us -> 18.8 us  [exchange(): return lax.ppermute(block, axis, matching(lax.axis_size(axis), which))]
    reshape x13 -> x2, local copies, waits for them, and re-layouts: 24.1 us -> 4.01 us  [the longest x1 2.56 us: shards(): grad_blocks.reshape(1, 1, slots, TILE * TILE)]
    scatter-add x3 -> x0, other arithmetic: 19 us -> none  [the longest x2 12.7 us: pull(): jnp.zeros((tile_total, planes, TILE), jnp.float32).at[source]]
    add x5 -> x0, other arithmetic: 18.1 us -> none  [the longest x2 5.7 us: flux_faces(): jnp.maximum(face_rate, 0.0) * upwind_part]
    slice x20 -> x13, local copies, waits for them, and re-layouts: 19.9 us -> 2.77 us  [the longest x1 0.74 us: onward(): send_s[part]]
    dot_general x5 -> x0, matrix products: 14.3 us -> none  [the longest x2 7.42 us: pull(): jnp.einsum('sza,szb->sab', returned, picked_source, precision=PRECISE)]
    ppermute x10 -> x0, local copies, waits for them, and re-layouts: 13.4 us -> none  [the longest x4 7.39 us: with_halo(): lax.ppermute(lax.slice_in_dim(block, 0, width, axis=dim), axis, backward)]
  transfers between devices with their start and end apart: 34 -> 12, of which waited for: 3 -> 6; matrix products, arithmetic and copies ran while one was open for 45% -> 5% of each run, Pallas kernels for 0% -> 17%
where the time goes in v1:
time: 88.5 us; the launch traced here: 87.6 us
  Pallas kernels  39.3 us (44%)
  starting transfers between devices  18.8 us (21%)
  waiting for transfers between devices  15.4 us (17%)
  local copies, waits for them, and re-layouts  10.4 us (12%)
  other arithmetic  2.2 us (2%)
  between operations  1.49 us (2%)
    pallas_call x6, Pallas kernels, call(): pl.pallas_call(functools.partial(body, **sizes), out_shape=tuple((jax.Sha...  39.3 us
    ppermute x12, starting transfers between devices, exchange(): return lax.ppermute(block, axis, matching(lax.axis_size(axis), which))  18.8 us
    ppermute x12, waiting for transfers between devices, exchange(): return lax.ppermute(block, axis, matching(lax.axis_size(axis), which))  15.4 us
    unnamed x35, local copies, waits for them, and re-layouts  3.55 us
    reshape x1, local copies, waits for them, and re-layouts, shards(): grad_blocks.reshape(1, 1, slots, TILE * TILE)  2.56 us
  transfers between devices with their start and end apart: 12, of which 6 were waited for; matrix products, arithmetic and copies ran while one was open for 5% of the time, Pallas kernels for 17%

profile of v1, /device:TPU:0, one launch (start us, length us, event | category | flops | bytes accessed | tf_op | source)
XLA Modules:
  0.0 87.6 jit_solution(13490712074402462664)
XLA Ops:
  1.3 0.7 pad_add_fusion.info
  1.9 4.0 %begin_body.1 = (s32[3,36]{1,0:T(4,128)}, f32[152,128]{1,0:T(8,128)}, f32[152,128]{1,0:T(8,128)}, f32[192,128]{1,0:T(8,128)}) custom-call(s32[2]{0:T(128)} %pad_add_fusion.info, s32[1]{0:T(128)} %bitcast.17.count, s32[36]{0:T(128)} %bitcast.32, s32[36]{0:T(128)} %bitcast.33, s32[36]{0:T(128)} %bitcast.34, f32[1024,128]{1,0:T(8,128)} %bitcast.26, ...), custom_call_target="tpu_custom_call" | custom-call | tf_op jit(solution)/shard_map/begin_body/pallas_call | solution.py:439
  6.0 3.0 %collective-permute-start.1 = (f32[152,128]{1,0:T(8,128)}, f32[152,128]{1,0:T(8,128)S(1)}, u32[]{:S(2)}, u32[]{:S(2)}) collective-permute-start(f32[152,128]{1,0:T(8,128)} %get-tuple-element.25), channel_id=1, source_target_pairs={{0,4},{4,0},{8,12},{12,8},{16,20},{20,16},{24,28},{28,24},{1,5},{5... | collective-permute-start | bytes 233480 | tf_op jit(solution)/shard_map/ppermute | solution.py:25
  9.0 3.5 %collective-permute-start = (f32[152,128]{1,0:T(8,128)}, f32[152,128]{1,0:T(8,128)S(1)}, u32[]{:S(2)}, u32[]{:S(2)}) collective-permute-start(f32[152,128]{1,0:T(8,128)} %get-tuple-element.24), channel_id=1, source_target_pairs={{0,28},{4,8},{8,4},{12,16},{16,12},{20,24},{24,20},{28,0},{1,29},{... | collective-permute-start | bytes 233480 | tf_op jit(solution)/shard_map/ppermute | solution.py:25
  12.6 0.7 slice.96
  13.3 0.0 collective-permute-done.1.rows_b
  13.3 3.0 %collective-permute-done.rows_a = f32[152,128]{1,0:T(8,128)S(1)} collective-permute-done((f32[152,128]{1,0:T(8,128)}, f32[152,128]{1,0:T(8,128)S(1)}, u32[]{:S(2)}, u32[]{:S(2)}) %collective-permute-start) | collective-permute-done | bytes 77856 | tf_op jit(solution)/shard_map/ppermute | solution.py:25
  16.3 0.9 %pad_maximum_fusion = f32[216,128]{1,0:T(8,128)S(1)} fusion(f32[192,128]{1,0:T(8,128)} %get-tuple-element.26.packs, f32[8,128]{1,0:T(8,128)S(1)} %slice.128, f32[8,128]{1,0:T(8,128)S(1)} %slice.127, f32[8,128]{1,0:T(8,128)S(1)} %slice.96), kind=kLoop, calls=%fused_computation | loop fusion | flops 82944 | bytes 221184 | tf_op jit(solution)/shard_map/concatenate | solution.py:473
  17.3 0.0 collective-permute-start.3
  17.3 0.7 slice.107
  18.0 1.4 %reshape.51.blocks = bf16[36,64,64]{2,1,0:T(8,128)(2,1)} reshape(bf16[1,1,36,4096]{3,2,1,0:T(8,128)(2,1)S(1)} %copy-done.8) | data formatting | bytes 589824 | tf_op jit(solution)/shard_map/reshape | solution.py:479
  19.4 5.9 %extend_body.1 = (bf16[18,128,128]{2,1,0:T(8,128)(2,1)}, f32[18,16,128]{2,1,0:T(8,128)}, f32[18,16,128]{2,1,0:T(8,128)}) custom-call(s32[3,36]{1,0:T(4,128)} %get-tuple-element.23.order, f32[1024,128]{1,0:T(8,128)} %bitcast.27, bf16[36,64,64]{2,1,0:T(8,128)(2,1)} %reshape.51.blocks), custom_call_target="tpu_custom_call" | custom-call | tf_op jit(solution)/shard_map/extend_body/pallas_call | solution.py:439
  25.3 1.6 %collective-permute-start.2 = (f32[216,128]{1,0:T(8,128)S(1)}, f32[216,128]{1,0:T(8,128)S(1)}, u32[]{:S(2)}, u32[]{:S(2)}) collective-permute-start(f32[216,128]{1,0:T(8,128)S(1)} %pad_maximum_fusion), channel_id=1, source_target_pairs={{0,3},{1,2},{2,1},{3,0},{4,7},{5,6},{6,5},{7,4},{8,11},{9,10},{10,... | collective-permute-start | bytes 331784 | tf_op jit(solution)/shard_map/ppermute | solution.py:25
  26.9 0.0 copy-done.7
  26.9 0.0 collective-permute-done.3.packs_b
  26.9 0.0 copy-start.2
  26.9 3.1 %collective-permute-done.2.packs_a = f32[216,128]{1,0:T(8,128)S(1)} collective-permute-done((f32[216,128]{1,0:T(8,128)S(1)}, f32[216,128]{1,0:T(8,128)S(1)}, u32[]{:S(2)}, u32[]{:S(2)}) %collective-permute-start.2) | collective-permute-done | bytes 110624 | tf_op jit(solution)/shard_map/ppermute | solution.py:25
  30.0 0.6 slice-done
  30.6 0.0 slice-done.1
  30.7 0.6 convert_element_type.3.asked
  31.3 2.1 %serve_body.1 = (f32[6,32,128]{2,1,0:T(8,128)}, f32[6,32,128]{2,1,0:T(8,128)}, f32[6,32,128]{2,1,0:T(8,128)}) custom-call(s32[9,128]{1,0:T(8,128)} %convert_element_type.3.asked, f32[1024,128]{1,0:T(8,128)} %bitcast.19, f32[18,16,128]{2,1,0:T(8,128)} %get-tuple-element.27.values), custom_call_target="tpu_custom_call" | custom-call | tf_op jit(solution)/shard_map/serve_body/pallas_call | solution.py:439
  33.4 1.6 %collective-permute-start.4 = (f32[6,32,128]{2,1,0:T(8,128)}, f32[6,32,128]{2,1,0:T(8,128)S(1)}, u32[]{:S(2)}, u32[]{:S(2)}) collective-permute-start(f32[6,32,128]{2,1,0:T(8,128)} %get-tuple-element.29), channel_id=1, source_target_pairs={{0,3},{1,2},{2,1},{3,0},{4,7},{5,6},{6,5},{7,4},{8,11},{9,10},{10,... | collective-permute-start | bytes 294920 | tf_op jit(solution)/shard_map/ppermute | solution.py:25
  35.0 0.1 collective-permute-start.5
  35.1 0.7 constant_dynamic-update-slice_fusion.11
  35.8 2.4 %collective-permute-done.4.y_a = f32[6,32,128]{2,1,0:T(8,128)S(1)} collective-permute-done((f32[6,32,128]{2,1,0:T(8,128)}, f32[6,32,128]{2,1,0:T(8,128)S(1)}, u32[]{:S(2)}, u32[]{:S(2)}) %collective-permute-start.4) | collective-permute-done | bytes 98336 | tf_op jit(solution)/shard_map/ppermute | solution.py:25
  38.2 0.0 collective-permute-done.5.y_b
  38.2 0.8 constant_dynamic-update-slice_fusion.8
  39.0 0.1 collective-permute-start.7
  39.1 3.6 %collective-permute-start.6 = (f32[6,32,128]{2,1,0:T(8,128)S(1)}, f32[6,32,128]{2,1,0:T(8,128)S(1)}, u32[]{:S(2)}, u32[]{:S(2)}) collective-permute-start(f32[6,32,128]{2,1,0:T(8,128)S(1)} %get-tuple-element.51), channel_id=1, source_target_pairs={{0,28},{4,8},{8,4},{12,16},{16,12},{20,24},{24,20},{28,0},{1,29},{... | collective-permute-start | bytes 294920 | tf_op jit(solution)/shard_map/ppermute | solution.py:25
  42.7 1.5 %collective-permute-done.7.x_b = f32[6,32,128]{2,1,0:T(8,128)S(1)} collective-permute-done((f32[6,32,128]{2,1,0:T(8,128)S(1)}, f32[6,32,128]{2,1,0:T(8,128)S(1)}, u32[]{:S(2)}, u32[]{:S(2)}) %collective-permute-start.7) | collective-permute-done | bytes 98336 | tf_op jit(solution)/shard_map/ppermute | solution.py:25
  44.2 2.8 %collective-permute-done.6.x_a = f32[6,32,128]{2,1,0:T(8,128)S(1)} collective-permute-done((f32[6,32,128]{2,1,0:T(8,128)S(1)}, f32[6,32,128]{2,1,0:T(8,128)S(1)}, u32[]{:S(2)}, u32[]{:S(2)}) %collective-permute-start.6) | collective-permute-done | bytes 98336 | tf_op jit(solution)/shard_map/ppermute | solution.py:25
  47.0 0.6 copy-done.5
  47.7 9.2 %middle_body.1 = (f32[1024,128]{1,0:T(8,128)}, f32[1288,128]{1,0:T(8,128)}, f32[64,128]{1,0:T(8,128)}, f32[18,16,128]{2,1,0:T(8,128)}, f32[160,128]{1,0:T(8,128)...) custom-call(s32[2]{0:T(128)} %pad_add_fusion.info, ...), custom_call_target="tpu_custom_call" | custom-call | tf_op jit(solution)/shard_map/middle_body/pallas_call | solution.py:439
  56.9 0.8 collective-permute-start.8
  57.7 0.7 fusion.2
  58.4 0.9 collective-permute-start.9
  59.3 2.6 %collective-permute-done.8.y_a = f32[160,128]{1,0:T(8,128)S(1)} collective-permute-done((f32[160,128]{1,0:T(8,128)}, f32[160,128]{1,0:T(8,128)S(1)}, u32[]{:S(2)}, u32[]{:S(2)}) %collective-permute-start.8) | collective-permute-done | bytes 81952 | tf_op jit(solution)/shard_map/ppermute | solution.py:25
  61.9 0.0 collective-permute-done.9.y_b
  61.9 0.7 copy-done.14
  62.6 3.6 %collective-permute-start.10 = (f32[144,128]{1,0:T(8,128)S(1)}, f32[144,128]{1,0:T(8,128)S(1)}, u32[]{:S(2)}, u32[]{:S(2)}) collective-permute-start(f32[144,128]{1,0:T(8,128)S(1)} %pad_maximum_fusion.1), channel_id=1, source_target_pairs={{0,28},{4,8},{8,4},{12,16},{16,12},{20,24},{24,20},{28,0},{1,29},{... | collective-permute-start | bytes 221192 | tf_op jit(solution)/shard_map/ppermute | solution.py:25
  66.2 0.1 collective-permute-start.11
  66.3 9.1 %section_body.1.picked_section = f32[18,16,128]{2,1,0:T(8,128)} custom-call(s32[2]{0:T(128)} %pad_add_fusion.info, s32[3,36]{1,0:T(4,128)} %get-tuple-element.23.order, s32[9,128]{1,0:T(8,128)} %convert_element_type.3.asked, f32[1024,128]{1,0:T(8,128)} %bitcast.28, f32[1288,128]{1,0:T(8,128)} %get-tuple-element.33.pad_rate, f32[1024,128]{1,0:T(8,128)} %bitcast.24, ...), custom_call_target="tpu_custom_call" | custom-call | tf_op jit(solution)/shard_map/section_body/pallas_call | solution.py:439
  75.4 0.0 collective-permute-done.10.x_a
  75.4 0.0 collective-permute-done.11.x_b
  75.4 0.6 copy-done.11
  76.1 0.0 copy-done.12
  76.1 9.0 %last_body.1 = (f32[1024,128]{1,0:T(8,128)}, f32[1280,128]{1,0:T(8,128)}) custom-call(s32[2]{0:T(128)} %pad_add_fusion.info, s32[3,36]{1,0:T(4,128)} %get-tuple-element.23.order, f32[1024,128]{1,0:T(8,128)} %bitcast.21, f32[1024,128]{1,0:T(8,128)} %get-tuple-element.32.grad, f32[1288,128]{1,0:T(8,128)} %get-tuple-element.33.pad_rate, f32[1024,128]{1,0:T(8,128)} %bitcast.25, ...), custom_call_target="tpu_custom_call" | custom-call | tf_op jit(solution)/shard_map/last_body/pallas_call | solution.py:439
  85.1 2.6 %reshape.55 = f32[1,1,36,4096]{3,1,2,0:T(1,128)} reshape(f32[36,4096]{1,0:T(8,128)} %bitcast.31) | data formatting | bytes 1179648 | tf_op jit(solution)/shard_map/reshape | solution.py:534
  (39 shorter events, 0.1 us)
Async XLA Ops:
  1.9 16.0 %copy-start.8 = (bf16[1,1,36,4096]{3,2,1,0:T(8,128)(2,1)S(1)}, bf16[1,1,36,4096]{3,2,1,0:T(8,128)(2,1)}, u32[]{:S(2)}) copy-start(bf16[1,1,36,4096]{3,2,1,0:T(8,128)(2,1)} %param.13) | copy-start | bytes 884740
  6.0 7.3 %collective-permute-start.1 = (f32[152,128]{1,0:T(8,128)}, f32[152,128]{1,0:T(8,128)S(1)}, u32[]{:S(2)}, u32[]{:S(2)}) collective-permute-start(f32[152,128]{1,0:T(8,128)} %get-tuple-element.25), channel_id=1, source_target_pairs={{0,4},{4,0},{8,12},{12,8},{16,20},{20,16},{24,28},{28,24},{1,5},{5... | collective-permute-start | bytes 233480 | tf_op jit(solution)/shard_map/ppermute | solution.py:25
  9.0 7.3 %collective-permute-start = (f32[152,128]{1,0:T(8,128)}, f32[152,128]{1,0:T(8,128)S(1)}, u32[]{:S(2)}, u32[]{:S(2)}) collective-permute-start(f32[152,128]{1,0:T(8,128)} %get-tuple-element.24), channel_id=1, source_target_pairs={{0,28},{4,8},{8,4},{12,16},{16,12},{20,24},{24,20},{28,0},{1,29},{... | collective-permute-start | bytes 233480 | tf_op jit(solution)/shard_map/ppermute | solution.py:25
  13.3 13.6 %copy-start.6 = (f32[152,128]{1,0:T(8,128)}, f32[152,128]{1,0:T(8,128)S(1)}, u32[]{:S(2)}) copy-start(f32[152,128]{1,0:T(8,128)S(1)} %collective-permute-done.1.rows_b) | copy-start | bytes 233476
  16.3 10.6 %copy-start.7 = (f32[152,128]{1,0:T(8,128)}, f32[152,128]{1,0:T(8,128)S(1)}, u32[]{:S(2)}) copy-start(f32[152,128]{1,0:T(8,128)S(1)} %collective-permute-done.rows_a) | copy-start | bytes 233476
  17.3 9.6 %collective-permute-start.3 = (f32[216,128]{1,0:T(8,128)S(1)}, f32[216,128]{1,0:T(8,128)S(1)}, u32[]{:S(2)}, u32[]{:S(2)}) collective-permute-start(f32[216,128]{1,0:T(8,128)S(1)} %pad_maximum_fusion), channel_id=1, source_target_pairs={{0,1},{1,0},{2,3},{3,2},{4,5},{5,4},{6,7},{7,6},{8,9},{9,8},{10,11... | collective-permute-start | bytes 331784 | tf_op jit(solution)/shard_map/ppermute | solution.py:25
  25.3 4.7 %collective-permute-start.2 = (f32[216,128]{1,0:T(8,128)S(1)}, f32[216,128]{1,0:T(8,128)S(1)}, u32[]{:S(2)}, u32[]{:S(2)}) collective-permute-start(f32[216,128]{1,0:T(8,128)S(1)} %pad_maximum_fusion), channel_id=1, source_target_pairs={{0,3},{1,2},{2,1},{3,0},{4,7},{5,6},{6,5},{7,4},{8,11},{9,10},{10,... | collective-permute-start | bytes 331784 | tf_op jit(solution)/shard_map/ppermute | solution.py:25
  26.9 6.5 %copy-start.2 = (f32[216,128]{1,0:T(8,128)}, f32[216,128]{1,0:T(8,128)S(1)}, u32[]{:S(2)}) copy-start(f32[216,128]{1,0:T(8,128)S(1)} %collective-permute-done.3.packs_b) | copy-start | bytes 331780
  30.0 3.4 %copy-start.3 = (f32[216,128]{1,0:T(8,128)}, f32[216,128]{1,0:T(8,128)S(1)}, u32[]{:S(2)}) copy-start(f32[216,128]{1,0:T(8,128)S(1)} %collective-permute-done.2.packs_a) | copy-start | bytes 331780
  30.0 0.6 slice-start
  30.0 0.6 slice-start.1
  33.4 4.8 %collective-permute-start.4 = (f32[6,32,128]{2,1,0:T(8,128)}, f32[6,32,128]{2,1,0:T(8,128)S(1)}, u32[]{:S(2)}, u32[]{:S(2)}) collective-permute-start(f32[6,32,128]{2,1,0:T(8,128)} %get-tuple-element.29), channel_id=1, source_target_pairs={{0,3},{1,2},{2,1},{3,0},{4,7},{5,6},{6,5},{7,4},{8,11},{9,10},{10,... | collective-permute-start | bytes 294920 | tf_op jit(solution)/shard_map/ppermute | solution.py:25
  35.0 3.2 %collective-permute-start.5 = (f32[6,32,128]{2,1,0:T(8,128)}, f32[6,32,128]{2,1,0:T(8,128)S(1)}, u32[]{:S(2)}, u32[]{:S(2)}) collective-permute-start(f32[6,32,128]{2,1,0:T(8,128)} %get-tuple-element.30), channel_id=1, source_target_pairs={{0,1},{1,0},{2,3},{3,2},{4,5},{5,4},{6,7},{7,6},{8,9},{9,8},{10,11... | collective-permute-start | bytes 294920 | tf_op jit(solution)/shard_map/ppermute | solution.py:25
  38.2 0.8 copy-start
  38.2 0.8 copy-start.1
  39.0 5.2 %collective-permute-start.7 = (f32[6,32,128]{2,1,0:T(8,128)S(1)}, f32[6,32,128]{2,1,0:T(8,128)S(1)}, u32[]{:S(2)}, u32[]{:S(2)}) collective-permute-start(f32[6,32,128]{2,1,0:T(8,128)S(1)} %get-tuple-element.50), channel_id=1, source_target_pairs={{0,4},{4,0},{8,12},{12,8},{16,20},{20,16},{24,28},{28,24},{1,5},{5... | collective-permute-start | bytes 294920 | tf_op jit(solution)/shard_map/ppermute | solution.py:25
  39.1 7.9 %collective-permute-start.6 = (f32[6,32,128]{2,1,0:T(8,128)S(1)}, f32[6,32,128]{2,1,0:T(8,128)S(1)}, u32[]{:S(2)}, u32[]{:S(2)}) collective-permute-start(f32[6,32,128]{2,1,0:T(8,128)S(1)} %get-tuple-element.51), channel_id=1, source_target_pairs={{0,28},{4,8},{8,4},{12,16},{16,12},{20,24},{24,20},{28,0},{1,29},{... | collective-permute-start | bytes 294920 | tf_op jit(solution)/shard_map/ppermute | solution.py:25
  44.2 2.8 %copy-start.4 = (f32[6,32,128]{2,1,0:T(8,128)}, f32[6,32,128]{2,1,0:T(8,128)S(1)}, u32[]{:S(2)}) copy-start(f32[6,32,128]{2,1,0:T(8,128)S(1)} %collective-permute-done.7.x_b) | copy-start | bytes 294916
  47.0 0.6 copy-start.5
  56.9 5.0 %collective-permute-start.8 = (f32[160,128]{1,0:T(8,128)}, f32[160,128]{1,0:T(8,128)S(1)}, u32[]{:S(2)}, u32[]{:S(2)}) collective-permute-start(f32[160,128]{1,0:T(8,128)} %get-tuple-element.36), channel_id=1, source_target_pairs={{0,3},{1,2},{2,1},{3,0},{4,7},{5,6},{6,5},{7,4},{8,11},{9,10},{10,... | collective-permute-start | bytes 245768 | tf_op jit(solution)/shard_map/ppermute | solution.py:25
  58.4 3.5 %collective-permute-start.9 = (f32[160,128]{1,0:T(8,128)}, f32[160,128]{1,0:T(8,128)S(1)}, u32[]{:S(2)}, u32[]{:S(2)}) collective-permute-start(f32[160,128]{1,0:T(8,128)} %get-tuple-element.37), channel_id=1, source_target_pairs={{0,1},{1,0},{2,3},{3,2},{4,5},{5,4},{6,7},{7,6},{8,9},{9,8},{10,11... | collective-permute-start | bytes 245768 | tf_op jit(solution)/shard_map/ppermute | solution.py:25
  61.8 0.8 copy-start.9
  61.9 0.7 copy-start.14
  61.9 0.7 copy-start.10
  62.6 3.6 %copy-start.13 = (f32[48,128]{1,0:T(8,128)S(1)}, f32[48,128]{1,0:T(8,128)}, u32[]{:S(2)}) copy-start(f32[48,128]{1,0:T(8,128)} %get-tuple-element.39) | copy-start | bytes 73732
  62.6 12.8 %collective-permute-start.10 = (f32[144,128]{1,0:T(8,128)S(1)}, f32[144,128]{1,0:T(8,128)S(1)}, u32[]{:S(2)}, u32[]{:S(2)}) collective-permute-start(f32[144,128]{1,0:T(8,128)S(1)} %pad_maximum_fusion.1), channel_id=1, source_target_pairs={{0,28},{4,8},{8,4},{12,16},{16,12},{20,24},{24,20},{28,0},{1,29},{... | collective-permute-start | bytes 221192 | tf_op jit(solution)/shard_map/ppermute | solution.py:25
  66.2 9.2 %collective-permute-start.11 = (f32[144,128]{1,0:T(8,128)S(1)}, f32[144,128]{1,0:T(8,128)S(1)}, u32[]{:S(2)}, u32[]{:S(2)}) collective-permute-start(f32[144,128]{1,0:T(8,128)S(1)} %pad_maximum_fusion.2), channel_id=1, source_target_pairs={{0,4},{4,0},{8,12},{12,8},{16,20},{20,16},{24,28},{28,24},{1,5},{5... | collective-permute-start | bytes 221192 | tf_op jit(solution)/shard_map/ppermute | solution.py:25
  75.4 0.6 copy-start.11
  75.4 0.6 copy-start.12

commit v2 on v1

v2 whole, which is shorter than its diff:
```python
import functools

import jax
import jax.numpy as jnp
from jax import lax
from jax.experimental import pallas as pl
from jax.experimental.pallas import tpu as pltpu
from jax.sharding import PartitionSpec as P

TILE = 64
ROUTE_MOST = 4
TIME_STEP = 0.3
WEIGHTS = (2.0 / 60.0, -13.0 / 60.0, 47.0 / 60.0, 27.0 / 60.0, -3.0 / 60.0)
PAD = 80
VMEM_LIMIT = 16 << 20
UNROLL = 2

A, B, S = 0, 1, 2


def matching(count, which):
    return [(i, (i + (1 if (i % 2 == 0) == (which == B) else -1)) % count) for i in range(count)]


def exchange(block, axis, which):
    return lax.ppermute(block, axis, matching(lax.axis_size(axis), which))


def lanes(shape):
    return lax.broadcasted_iota(jnp.int32, shape, len(shape) - 1)


def roll(value, shift):
    return pltpu.roll(value, shift % 128 if isinstance(shift, int) else shift, axis=value.ndim - 1)


def split(value):
    high = value.astype(jnp.bfloat16)
    return high, (value - high.astype(jnp.float32)).astype(jnp.bfloat16)


def pair_dot(value, matrix, over):
    high, low = split(value)
    both = lax.dot_general(
        jnp.concatenate([high, low], axis=0),
        matrix,
        (((1,), (over,)), ((), ())),
        preferred_element_type=jnp.float32,
    )
    rows = value.shape[0]
    return both[:rows] + both[rows:]


def row_of(ref, x, planes, stride):
    return ref[pl.ds(x, planes, stride), :]


def tile_pair(ref, first, second, planes, extent_x):
    one = row_of(ref, first // 2, planes, extent_x)
    two = row_of(ref, second // 2, planes, extent_x)
    lane = lanes(one.shape)
    one = jnp.where(first % 2 == 0, one, roll(one, TILE))
    two = jnp.where(second % 2 == 1, two, roll(two, TILE))
    return jnp.where(lane < TILE, one, two)


def add_tile_pair(ref, first, second, value, planes, extent_x):
    lane = lanes(value.shape)
    turned = roll(value, TILE)
    for tile, half in ((first, 0), (second, 1)):
        spot = pl.ds(tile // 2, planes, extent_x)
        placed = jnp.where(tile % 2 == half, value, turned)
        keep = (lane // TILE) == tile % 2
        ref[spot, :] = ref[spot, :] + jnp.where(keep, placed, 0.0)


def edge_pack(ref, planes, extent_x):
    lane = lanes((extent_x, 128))
    packed = jnp.zeros((extent_x, 128), jnp.float32)
    for z in range(planes):
        plane = ref[z * extent_x : (z + 1) * extent_x, :]
        packed = jnp.where(lane // 8 == z, roll(plane, 8 * z + 3), packed)
    return packed


def edge_rows(ref, start, planes, extent_x):
    return jnp.concatenate([row_of(ref, start + j, planes, extent_x) for j in range(3)], axis=0)


def upwind(face_rate):
    return jnp.maximum(face_rate, 0.0), jnp.minimum(face_rate, 0.0)


UP = {2: WEIGHTS[0], 1: WEIGHTS[1], 0: WEIGHTS[2], -1: WEIGHTS[3], -2: WEIGHTS[4]}
DOWN = {1: WEIGHTS[4], 0: WEIGHTS[3], -1: WEIGHTS[2], -2: WEIGHTS[1], -3: WEIGHTS[0]}


def combine(up_part, down_part, k):
    total = 0.0
    if k in UP:
        total = total + UP[k] * up_part
    if k in DOWN:
        total = total + DOWN[k] * down_part
    return total


def fill_padded(pad_ref, field_ref, rows_a, rows_b, even, planes, extent_x):
    high = 8 + extent_x
    at_a = jnp.where(even, 5, high)
    at_b = jnp.where(even, high, 5)
    for z in range(planes):
        pad_ref[z * PAD + 8 : z * PAD + high, :] = field_ref[z * extent_x : (z + 1) * extent_x, :]
    for j in range(3):
        part = slice(j * planes, (j + 1) * planes)
        pad_ref[pl.ds(at_a + j, planes, PAD), :] = rows_a[part]
        pad_ref[pl.ds(at_b + j, planes, PAD), :] = rows_b[part]


def edge_join(from_a, from_b, even):
    low = jnp.where(even, from_a, from_b)
    high = jnp.where(even, from_b, from_a)
    return jnp.where(lanes(low.shape) % 8 < 3, low, high)


def adjoint_edges(own, halo, own_rate, halo_rate):
    lane = lanes(own.shape) % 8
    after = roll(jnp.where(lane == 3, own, halo), -1)
    before = roll(jnp.where(lane == 2, own, halo), 1)
    jump = jnp.where(lane < 3, after - halo, halo - before)
    rate = jnp.where(lane < 3, halo_rate, roll(jnp.where(lane == 2, own_rate, halo_rate), 1))
    rate_up, rate_down = upwind(rate)
    up_part, down_part = rate_up * jump, rate_down * jump
    low_side = 0.0
    high_side = 0.0
    for k in (-1, -2, -3):
        part = jnp.where(lane < 3, combine(up_part, down_part, k), 0.0)
        low_side = low_side + roll(part, -k)
    for k in (0, 1, 2):
        part = jnp.where((lane >= 3) & (lane < 6), combine(up_part, down_part, k), 0.0)
        high_side = high_side + roll(part, -(k + 1))
    return jnp.where(lane < 3, high_side, jnp.where(lane < 6, low_side, 0.0))


def adjoint_plane(z, pad_ref, pad_rate_ref, rate_y_ref, up_ref, down_ref, extent_x):
    base = pl.multiple_of(z * PAD, 8)
    here = pad_ref[pl.ds(base, PAD), :]
    jump = pad_ref[pl.ds(base + 1, PAD), :] - here
    rate_up, rate_down = upwind(pad_rate_ref[pl.ds(base, PAD), :])
    up_ref[pl.ds(base, PAD), :] = rate_up * jump
    down_ref[pl.ds(base, PAD), :] = rate_down * jump
    total = 0.0
    for k in range(-3, 3):
        if k in UP:
            total = total + UP[k] * up_ref[pl.ds(base + 8 + k, extent_x), :]
        if k in DOWN:
            total = total + DOWN[k] * down_ref[pl.ds(base + 8 + k, extent_x), :]
    field = pad_ref[pl.ds(base + 8, extent_x), :]
    lane = lanes(field.shape)
    jump = jnp.where(lane == 127, 0.0, roll(field, -1) - field)
    rate_up, rate_down = upwind(rate_y_ref[pl.ds(pl.multiple_of(z * extent_x, 8), extent_x), :])
    up_part, down_part = rate_up * jump, rate_down * jump
    ahead = combine(up_part, down_part, 2)
    for k in (1, 0):
        ahead = jnp.where(lane == 127, 0.0, roll(ahead, -1)) + combine(up_part, down_part, k)
    behind = combine(up_part, down_part, -3)
    for k in (-2, -1):
        behind = jnp.where(lane == 0, 0.0, roll(behind, 1)) + combine(up_part, down_part, k)
    behind = jnp.where(lane == 0, 0.0, roll(behind, 1))
    return total + ahead + behind


def parities():
    return lax.rem(lax.axis_index("gx"), 2), lax.rem(lax.axis_index("gy"), 2)


def alive_lanes(value, order, number):
    lane = lanes(value.shape)
    alive = jnp.where(lane < TILE, order[2, 2 * number], order[2, 2 * number + 1])
    return jnp.where(alive == 1, value, 0.0)


def part(ref, number, extent_x):
    return ref[number * extent_x : (number + 1) * extent_x]


def lists_body(count, heading, target, source, order, request, used, *, planes, extent_x):
    parity_x, parity_y = parities()
    for label in range(9):
        used[label] = 0
    lane = lanes((8, 128))

    def place(slot, asked):
        toward = heading[slot]
        ex = (toward // 3 - 1) * (1 - 2 * parity_x)
        ey = (lax.rem(toward, 3) - 1) * (1 - 2 * parity_y)
        lx = jnp.where(ex == 0, 2, (ex + 1) // 2)
        ly = jnp.where(ey == 0, 2, (ey + 1) // 2)
        label = ly * 3 + lx
        spot = label * ROUTE_MOST + used[label]
        used[label] = used[label] + 1
        alive = slot < count[0]
        order[0, spot] = slot
        order[1, spot] = source[slot]
        order[2, spot] = alive.astype(jnp.int32)
        wanted = jnp.where(alive, target[slot], 0)
        return jnp.where(lane == spot, wanted, asked)

    asked = lax.fori_loop(0, heading.shape[0], place, jnp.zeros((8, 128), jnp.int32), unroll=4)
    request[...] = asked.astype(jnp.float32)


def edges_body(field, cotan, rate_x, rate_y, rows_a, rows_b, late_a, late_b, packs, *, planes, extent_x):
    even = parities()[0] == 0
    high = extent_x - 3
    size = 3 * planes
    for rows, late, start in (
        (rows_a, late_a, jnp.where(even, 0, high)),
        (rows_b, late_b, jnp.where(even, high, 0)),
    ):
        rows[0:size, :] = edge_rows(cotan, start, planes, extent_x)
        rows[size : 2 * size, :] = edge_rows(rate_x, start, planes, extent_x)
        late[...] = edge_rows(field, start, planes, extent_x)
    for number, ref in enumerate((cotan, rate_y, field)):
        packs[number * extent_x : (number + 1) * extent_x, :] = edge_pack(ref, planes, extent_x)


def extend_body(order, field, blocks, pairs, picked, value_a, value_b, value_s, *, planes, extent_x):
    for ly, value in enumerate((value_a, value_b, value_s)):

        def one(inner, carry):
            number = ly * 6 + inner
            one_block, two_block = blocks[order[0, 2 * number]], blocks[order[0, 2 * number + 1]]
            zero = jnp.zeros_like(one_block)
            joined = jnp.concatenate(
                [jnp.concatenate([one_block, zero], axis=1), jnp.concatenate([zero, two_block], axis=1)], axis=0
            )
            pairs[number] = joined
            tiles = tile_pair(field, order[1, 2 * number], order[1, 2 * number + 1], planes, extent_x)
            picked[number] = tiles
            spot = pl.ds(pl.multiple_of(inner * planes, 8), planes)
            value[spot, :] = pair_dot(alive_lanes(tiles, order, number), joined, 1)
            return carry

        lax.fori_loop(0, 6, one, 0, unroll=UNROLL)


def gather_tiles(asked, field, outs, first, planes, extent_x):
    for ly in range(3):

        def one(inner, carry):
            at = ly * 12 + 2 * inner
            tiles = tile_pair(field, asked[ly, at], asked[ly, at + 1], planes, extent_x)
            outs[ly][pl.ds(pl.multiple_of(first + inner * planes, 8), planes), :] = tiles
            return carry

        lax.fori_loop(0, 6, one, 0, unroll=UNROLL)


def serve_body(request, got_a, got_b, from_a, from_b, cotan, asked, out_a, out_b, out_s, list_ref, sem, *, planes, extent_x):
    row = lax.broadcasted_iota(jnp.int32, (8, 128), 0)
    group = lax.rem(lanes((8, 128)), 12) // ROUTE_MOST
    merged = []
    for a, b, s in (
        (from_a[8:16], from_a[16:24], from_a[0:8]),
        (from_b[8:16], from_b[16:24], from_b[0:8]),
        (got_a[...], got_b[...], request[...]),
    ):
        merged.append(jnp.where(group == 0, a, jnp.where(group == 1, b, s))[0:1])
    spread = [jnp.broadcast_to(one, (8, 128)) for one in merged]
    joined = jnp.where(row == 0, spread[0], jnp.where(row == 1, spread[1], spread[2]))
    list_ref[...] = joined.astype(jnp.int32)
    copy = pltpu.make_async_copy(list_ref, asked, sem)
    copy.start()
    copy.wait()
    gather_tiles(asked, cotan, (out_a, out_b, out_s), 0, planes, extent_x)


def landed(lx, ly, half, planes, x_first, y_first, x_a, x_b, y_a, y_b, own):
    if lx == S:
        ref, first = (y_a, y_b, own)[ly], (0 if ly == S and own.shape[0] == 6 * planes else y_first) + (S * 2 + half) * planes
    else:
        ref, first = (x_a, x_b)[lx], x_first + ((1, 2, 0)[ly] * 2 + half) * planes
    return ref[first : first + planes, :]


LABELS = [(lx, ly, half) for ly in range(3) for lx in range(3) for half in range(2)]


def pull_body(cotan, rate_x, rate_y, rows_a, rows_b, packs, packs_a, packs_b, grad, pad_rate, edge_rate, pad, up_ref, down_ref, *, planes, extent_x):
    parity_x, parity_y = parities()
    even_x, even_y = parity_x == 0, parity_y == 0
    size = 3 * planes
    fill_padded(pad, cotan, rows_a[0:size], rows_b[0:size], even_x, planes, extent_x)
    fill_padded(pad_rate, rate_x, rows_a[size : 2 * size], rows_b[size : 2 * size], even_x, planes, extent_x)
    halo = edge_join(part(packs_a, 0, extent_x), part(packs_b, 0, extent_x), even_y)
    halo_rate = edge_join(part(packs_a, 1, extent_x), part(packs_b, 1, extent_x), even_y)
    edge_rate[...] = halo_rate
    edges = adjoint_edges(part(packs, 0, extent_x), halo, part(packs, 1, extent_x), halo_rate)

    def plane(z, carry):
        spot = pl.ds(pl.multiple_of(z * extent_x, 8), extent_x)
        pulled = adjoint_plane(z, pad, pad_rate, rate_y, up_ref, down_ref, extent_x)
        rim = roll(edges, 125 - 8 * z)
        lane = lanes(rim.shape)
        pulled = pulled + jnp.where((lane < 3) | (lane >= 125), rim, 0.0)
        grad[spot, :] = 0.5 * cotan[spot, :] + (0.5 * TIME_STEP) * pulled
        return carry

    lax.fori_loop(0, planes, plane, 0)


def push_body(field, pad_rate, rate_y, edge_rate, late_a, late_b, packs, packs_a, packs_b, section, pad, flux_ref, *, planes, extent_x):
    parity_x, parity_y = parities()
    even_x, even_y = parity_x == 0, parity_y == 0
    fill_padded(pad, field, late_a[...], late_b[...], even_x, planes, extent_x)
    halo = edge_join(part(packs_a, 2, extent_x), part(packs_b, 2, extent_x), even_y)
    line = jnp.where(lanes(halo.shape) % 8 < 3, halo, part(packs, 2, extent_x))
    moved = {k: roll(line, -k) for k in range(-2, 4)}
    rate_up, rate_down = upwind(edge_rate[...])
    flux_low = rate_up * sum(WEIGHTS[j] * moved[j - 2] for j in range(5)) + rate_down * sum(
        WEIGHTS[j] * moved[3 - j] for j in range(5)
    )

    def plane(z, carry):
        base = pl.multiple_of(z * PAD, 8)
        spot = pl.ds(pl.multiple_of(z * extent_x, 8), extent_x)
        window = extent_x + 8
        near = {k: pad[pl.ds(base + 7 + k, window), :] for k in range(-2, 4)}
        rate_up, rate_down = upwind(pad_rate[pl.ds(base + 7, window), :])
        flux_ref[pl.ds(base, window), :] = rate_up * sum(WEIGHTS[j] * near[j - 2] for j in range(5)) + rate_down * sum(
            WEIGHTS[j] * near[3 - j] for j in range(5)
        )
        change = flux_ref[pl.ds(base, extent_x), :] - flux_ref[pl.ds(base + 1, extent_x), :]
        here = field[spot, :]
        lane = lanes(here.shape)
        turn = 125 - 8 * z
        rim = roll(halo, turn)
        near = {0: here}
        for k in (1, 2, 3):
            near[k] = roll(jnp.where(lane < k, rim, here), -k)
        for k in (1, 2):
            near[-k] = roll(jnp.where(lane >= 128 - k, rim, here), k)
        rate_up, rate_down = upwind(rate_y[spot, :])
        flux = rate_up * sum(WEIGHTS[j] * near[j - 2] for j in range(5)) + rate_down * sum(
            WEIGHTS[j] * near[3 - j] for j in range(5)
        )
        change = change + roll(jnp.where(lane == 127, roll(flux_low, turn), flux), 1) - flux
        section[spot, :] = here + TIME_STEP * change
        return carry

    lax.fori_loop(0, planes, plane, 0)


def middle_body(order, asked, early, pairs, x_a, x_b, y_a, y_b, own, grad, returned, send_a, send_b, send_s, rows_a, rows_b, *, planes, extent_x):
    even_x = parities()[0] == 0
    for number, label in enumerate(LABELS):
        back = alive_lanes(landed(*label, planes, 0, 0, x_a, x_b, y_a, y_b, own), order, number)
        returned[number] = back
        pulled = (0.5 * TIME_STEP) * pair_dot(back, pairs[number], 0)
        add_tile_pair(grad, order[1, 2 * number], order[1, 2 * number + 1], pulled, planes, extent_x)
    packed = edge_pack(grad, planes, extent_x)
    for out in (send_a, send_b, send_s):
        out[0:extent_x, :] = packed
    gather_tiles(asked, grad, (send_a, send_b, send_s), extent_x, planes, extent_x)
    high = extent_x - 3
    rows_a[...] = edge_rows(grad, jnp.where(even_x, 0, high), planes, extent_x)
    rows_b[...] = edge_rows(grad, jnp.where(even_x, high, 0), planes, extent_x)


def inner_body(cotan, grad, pad_rate, rate_y, out, pad, up_ref, down_ref, *, planes, extent_x):
    high = 8 + extent_x
    for z in range(planes):
        pad[z * PAD + 8 : z * PAD + high, :] = grad[z * extent_x : (z + 1) * extent_x, :]
    for j in range(3):
        pad[pl.ds(5 + j, planes, PAD), :] = row_of(grad, 0, planes, extent_x)
        pad[pl.ds(high + j, planes, PAD), :] = row_of(grad, extent_x - 1, planes, extent_x)

    def plane(z, carry):
        spot = pl.ds(pl.multiple_of(z * extent_x, 8), extent_x)
        pulled = adjoint_plane(z, pad, pad_rate, rate_y, up_ref, down_ref, extent_x)
        out[spot, :] = 0.5 * cotan[spot, :] + grad[spot, :] + TIME_STEP * pulled
        return carry

    lax.fori_loop(0, planes, plane, 0)


def outer(left, right):
    left_high, left_low = split(left)
    right_high, right_low = split(right)
    return lax.dot_general(
        jnp.concatenate([left_high, left_high, left_low], axis=0),
        jnp.concatenate([right_high, right_low, right_high], axis=0),
        (((0,), (0,)), ((), ())),
        preferred_element_type=jnp.float32,
    )


def section_body(order, asked, early, returned, x_a, x_b, y_a, y_b, own, section, first_outer, *, planes, extent_x):
    for number, (lx, ly, half) in enumerate(LABELS):
        came = TIME_STEP * landed(lx, ly, half, planes, 0, 3 * extent_x, x_a, x_b, y_a, y_b, own)
        at = ly * 12 + lx * ROUTE_MOST + 2 * half
        add_tile_pair(section, asked[ly, at], asked[ly, at + 1], came, planes, extent_x)

    def pick(number, carry):
        picked = tile_pair(section, order[1, 2 * number], order[1, 2 * number + 1], planes, extent_x)
        first_outer[number] = outer((0.5 * TIME_STEP) * returned[number], picked)
        return carry

    lax.fori_loop(0, first_outer.shape[0], pick, 0, unroll=UNROLL)


def last_body(
    order, early, grad, pad_rate, edge_rate, packs, own, y_a, y_b, x_a, x_b, pairs, first_outer, picked, out, out_blocks, work, total,
    *, planes, extent_x,
):
    parity_x, parity_y = parities()
    even_x, even_y = parity_x == 0, parity_y == 0
    size = 3 * planes
    halo = edge_join(y_a[0:extent_x], y_b[0:extent_x], even_y)
    edges = adjoint_edges(own[0:extent_x], halo, part(packs, 1, extent_x), edge_rate[...])

    def plane(z, carry):
        spot = pl.ds(pl.multiple_of(z * extent_x, 8), extent_x)
        rim = roll(edges, 125 - 8 * z)
        lane = lanes(rim.shape)
        total[spot, :] = early[spot, :] + TIME_STEP * jnp.where((lane < 3) | (lane >= 125), rim, 0.0)
        return carry

    lax.fori_loop(0, planes, plane, 0, unroll=2)
    low_rows = [jnp.where(even_x, x_a[j * planes : (j + 1) * planes], x_b[j * planes : (j + 1) * planes]) for j in range(3)]
    high_rows = [jnp.where(even_x, x_b[j * planes : (j + 1) * planes], x_a[j * planes : (j + 1) * planes]) for j in range(3)]
    first_cell = row_of(grad, 0, planes, extent_x)
    last_cell = row_of(grad, extent_x - 1, planes, extent_x)
    for line, low_face in ((low_rows + [first_cell], -3), ([last_cell] + high_rows, extent_x - 1)):
        faces = []
        for j in range(3):
            rate_up, rate_down = upwind(row_of(pad_rate, 8 + low_face + j, planes, PAD))
            jump = line[j + 1] - line[j]
            faces.append((rate_up * jump, rate_down * jump))
        cells = range(0, 3) if low_face < 0 else range(extent_x - 3, extent_x)
        for cell in cells:
            added = 0.0
            for j in range(3):
                k = low_face + j - cell
                if -3 <= k <= 2:
                    added = added + combine(*faces[j], k)
            spot = pl.ds(cell, planes, extent_x)
            total[spot, :] = total[spot, :] + TIME_STEP * added
    half_lane = lanes((TILE // 2, 128)) < TILE
    for number, label in enumerate(LABELS):
        back = alive_lanes(landed(*label, planes, size, extent_x, x_a, x_b, y_a, y_b, own), order, number)
        pulled = TIME_STEP * pair_dot(back, pairs[number], 0)
        add_tile_pair(total, order[1, 2 * number], order[1, 2 * number + 1], pulled, planes, extent_x)
        work[number] = first_outer[number] + outer(TIME_STEP * back, picked[number])
        for which in range(2):
            slot = order[0, 2 * number + which]
            even_rows = work[number, pl.ds(which * TILE, TILE // 2, 2), :]
            odd_rows = work[number, pl.ds(which * TILE + 1, TILE // 2, 2), :]
            if which == 0:
                merged = jnp.where(half_lane, even_rows, roll(odd_rows, TILE))
            else:
                merged = jnp.where(half_lane, roll(even_rows, TILE), odd_rows)
            out_blocks[pl.ds(pl.multiple_of(slot * (TILE // 2), 8), TILE // 2), :] = merged
    out[...] = total[...]


SPACE = {"v": pltpu.VMEM, "s": pltpu.SMEM}


def call(body, smem, vmem, outs, scratch=(), alias=None, **sizes):
    ins, specs, shapes, out_specs = [], [], [], []
    for value, kind in [(v, "s") for v in smem] + [(v, "v") for v in vmem]:
        if isinstance(value, tuple):
            value = value[0]
        else:
            value = pltpu.with_memory_space_constraint(value, SPACE[kind])
        ins.append(value)
        specs.append(pl.BlockSpec(memory_space=SPACE[kind]))
    for shape, dtype, kind in outs:
        shapes.append(jax.ShapeDtypeStruct(shape, dtype) if kind == "h" else SPACE[kind](shape, dtype))
        out_specs.append(pl.BlockSpec(memory_space=SPACE["s" if kind == "s" else "v"]))
    return pl.pallas_call(
        functools.partial(body, **sizes),
        out_shape=tuple(shapes),
        in_specs=specs,
        out_specs=tuple(out_specs),
        scratch_shapes=list(scratch),
        input_output_aliases=alias or {},
        compiler_params=pltpu.CompilerParams(vmem_limit_bytes=VMEM_LIMIT),
        name=body.__name__,
    )(*ins)


def shards(
    level_set, speed_x, speed_y, cotangent, blocks, tile_count, source_tile, dest_offset, dest_tile
):
    planes, extent_x, extent_y = level_set.shape
    slots = source_tile.shape[2]
    cells = planes * extent_x
    f32, i32 = jnp.float32, jnp.int32
    field, rate_x, rate_y, cotan = (v.reshape(cells, extent_y) for v in (level_set, speed_x, speed_y, cotangent))
    sizes = dict(planes=planes, extent_x=extent_x)
    size = 3 * planes
    pair_total = slots // 2
    box = ((2 * size, 128), f32, "v")
    padded = ((planes * PAD + 8, extent_y), f32)
    pad_scratch = pltpu.VMEM(*padded)
    whole = ((cells, 128), f32, "v")

    order, request = call(
        lists_body,
        [(tile_count.reshape(1),), (dest_offset.reshape(slots),), (dest_tile.reshape(slots),), (source_tile.reshape(slots),)], [],
        [((3, slots), i32, "s"), ((8, 128), f32, "v")],
        scratch=(pltpu.SMEM((9,), i32),), **sizes,
    )
    got_b = exchange(request, "gx", B)
    got_a = exchange(request, "gx", A)
    rows_a, rows_b, late_a, late_b, packs = call(
        edges_body, [], [field, cotan, rate_x, rate_y],
        [box, box, ((size, 128), f32, "v"), ((size, 128), f32, "v"), ((3 * extent_x, 128), f32, "v")], **sizes,
    )
    rows_b = exchange(rows_b, "gx", B)
    rows_a = exchange(rows_a, "gx", A)
    column = jnp.concatenate([request, got_a, got_b], axis=0)
    from_b = exchange(column, "gy", B)
    from_a = exchange(column, "gy", A)
    pairs, picked, value_a, value_b, value_s = call(
        extend_body, [order], [field, blocks.reshape(slots, TILE, TILE)],
        [((pair_total, 128, 128), jnp.bfloat16, "v"), ((pair_total, planes, 128), f32, "v"), box, box, box], **sizes,
    )
    packs_b = exchange(jnp.concatenate([packs, value_b], axis=0), "gy", B)
    packs_a = exchange(jnp.concatenate([packs, value_a], axis=0), "gy", A)

    asked, tiles_a, tiles_b, tiles_s = call(
        serve_body, [], [request, got_a, got_b, from_a, from_b, cotan],
        [((8, 128), i32, "s"), box, box, box], scratch=(pltpu.VMEM((8, 128), i32), pltpu.SemaphoreType.DMA(())), **sizes,
    )
    y_b = exchange(tiles_b, "gy", B)
    y_a = exchange(tiles_a, "gy", A)

    def onward(own, a, b, own_first, first, m):
        cut = lambda v, start: v[start + m * 2 * planes : start + (m + 1) * 2 * planes]
        return [cut(own, own_first), cut(a, first), cut(b, first)]

    x_b = exchange(jnp.concatenate(onward(tiles_s, y_a, y_b, 0, 0, B), axis=0), "gx", B)
    x_a = exchange(jnp.concatenate(onward(tiles_s, y_a, y_b, 0, 0, A), axis=0), "gx", A)
    early, pad_rate, edge_rate = call(
        pull_body, [], [cotan, rate_x, rate_y, rows_a, rows_b, packs, packs_a, packs_b],
        [whole, padded + ("v",), ((extent_x, 128), f32, "v")], scratch=(pad_scratch,) * 3, **sizes,
    )
    extra = 3 * extent_x
    z_b = exchange(jnp.concatenate(onward(value_s, packs_a, packs_b, 0, extra, B) + [late_b], axis=0), "gx", B)
    z_a = exchange(jnp.concatenate(onward(value_s, packs_a, packs_b, 0, extra, A) + [late_a], axis=0), "gx", A)
    grad, returned, send_a, send_b, send_s, edge_a, edge_b = call(
        middle_body, [order, asked], [early, pairs, x_a, x_b, y_a, y_b, tiles_s],
        [whole, ((pair_total, planes, 128), f32, "v")] + [((extent_x + 2 * size, 128), f32, "v")] * 3 + [((size, 128), f32, "v")] * 2,
        alias={2: 0}, **sizes,
    )
    last_y_b = exchange(send_b, "gy", B)
    last_y_a = exchange(send_a, "gy", A)
    last_x_b = exchange(jnp.concatenate([edge_b] + onward(send_s, last_y_a, last_y_b, extent_x, extent_x, B), axis=0), "gx", B)
    last_x_a = exchange(jnp.concatenate([edge_a] + onward(send_s, last_y_a, last_y_b, extent_x, extent_x, A), axis=0), "gx", A)
    (pushed,) = call(
        push_body, [], [field, pad_rate, rate_y, edge_rate, z_a[2 * size :], z_b[2 * size :], packs, packs_a, packs_b],
        [whole], scratch=(pad_scratch,) * 2, **sizes,
    )
    (inner,) = call(
        inner_body, [], [cotan, grad, pad_rate, rate_y], [whole], scratch=(pad_scratch,) * 3, **sizes,
    )
    section, first_outer = call(
        section_body, [order, asked], [pushed, returned, z_a, z_b, packs_a, packs_b, value_s],
        [whole, ((pair_total, 128, 128), f32, "v")], alias={2: 0}, **sizes,
    )
    grad_level_set, grad_blocks = call(
        last_body, [order],
        [inner, grad, pad_rate, edge_rate, packs, send_s, last_y_a, last_y_b, last_x_a, last_x_b, pairs, first_outer, picked],
        [((cells, 128), f32, "h"), ((slots * TILE // 2, 128), f32, "h")],
        scratch=(pltpu.VMEM((pair_total, 128, 128), f32), pltpu.VMEM((cells, 128), f32)), **sizes,
    )
    return (grad_level_set.reshape(planes, extent_x, extent_y), grad_blocks.reshape(1, 1, slots, TILE * TILE))


def solution(mesh):
    return jax.shard_map(
        shards,
        mesh=mesh,
        in_specs=(
            P(None, "gx", "gy"),
            P(None, "gx", "gy"),
            P(None, "gx", "gy"),
            P(None, "gx", "gy"),
            P("gx", "gy", None, None),
            P("gx", "gy"),
            P("gx", "gy", None),
            P("gx", "gy", None),
            P("gx", "gy", None),
        ),
        out_specs=(P(None, "gx", "gy"), P("gx", "gy", None, None)),
        check_vma=False,
    )
```

time: 88.5 us -> 66.5 us (0.75)
  Pallas kernels: 39.3 us -> 27.7 us
  local copies, waits for them, and re-layouts: 10.4 us -> 4.62 us
  waiting for transfers between devices: 15.4 us -> 10.8 us
  starting transfers between devices: 18.8 us -> 21.4 us
  other arithmetic: 2.2 us -> 0.06 us
    pallas_call x6 -> x10, Pallas kernels: 39.3 us -> 27.7 us  [call(): pl.pallas_call(functools.partial(body, **sizes), out_shape=tuple(shapes),...]
    ppermute x12 -> x18, waiting for transfers between devices: 15.4 us -> 10.8 us  [exchange(): return lax.ppermute(block, axis, matching(lax.axis_size(axis), which))]
    slice x13 -> x11, local copies, waits for them, and re-layouts: 2.77 us -> 0.04 us  [the longest x9 0.03 us: onward(): v[start + m * 2 * planes:start + (m + 1) * 2 * planes]]
    ppermute x12 -> x18, starting transfers between devices: 18.8 us -> 21.4 us  [exchange(): return lax.ppermute(block, axis, matching(lax.axis_size(axis), which))]
    reshape x1 -> x0, local copies, waits for them, and re-layouts: 2.56 us -> none  [shards(): grad_blocks.reshape(1, 1, slots, TILE * TILE)]
    unnamed x35 -> x18, local copies, waits for them, and re-layouts: 3.55 us -> 3.02 us
  transfers between devices with their start and end apart: 12 -> 18, of which waited for: 6 -> 4; matrix products, arithmetic and copies ran while one was open for 5% -> 3% of each run, Pallas kernels for 17% -> 35%
where the time goes in v2:
time: 66.5 us; the launch traced here: 66.2 us
  Pallas kernels  27.7 us (42%)
  starting transfers between devices  21.4 us (32%)
  waiting for transfers between devices  10.8 us (16%)
  local copies, waits for them, and re-layouts  4.62 us (7%)
  between operations  1.68 us (3%)
    pallas_call x10, Pallas kernels, call(): pl.pallas_call(functools.partial(body, **sizes), out_shape=tuple(shapes),...  27.7 us
    ppermute x18, starting transfers between devices, exchange(): return lax.ppermute(block, axis, matching(lax.axis_size(axis), which))  21.4 us
    ppermute x18, waiting for transfers between devices, exchange(): return lax.ppermute(block, axis, matching(lax.axis_size(axis), which))  10.8 us
    unnamed x18, local copies, waits for them, and re-layouts  3.02 us
    reshape x1, local copies, waits for them, and re-layouts, shards(): blocks.reshape(slots, TILE, TILE)  1.56 us
  transfers between devices with their start and end apart: 18, of which 4 were waited for; matrix products, arithmetic and copies ran while one was open for 3% of the time, Pallas kernels for 35%

profile of v2, /device:TPU:0, one launch (start us, length us, event | category | flops | bytes accessed | tf_op | source)
XLA Modules:
  0.0 66.2 jit_solution(79829592626681901)
XLA Ops:
  1.4 0.6 copy-done.5
  2.1 0.7 copy-done.6
  2.7 0.7 copy-done.7
  3.4 1.5 %lists_body.1 = (s32[3,36]{1,0:T(4,128)S(4)}, f32[8,128]{1,0:T(8,128)S(1)}) custom-call(s32[1]{0:T(128)} %bitcast.10.count, s32[36]{0:T(128)S(1)} %bitcast.24, s32[36]{0:T(128)S(1)} %bitcast.25, s32[36]{0:T(128)S(1)} %bitcast.26), custom_call_target="tpu_custom_call" | custom-call | tf_op jit(solution)/shard_map/lists_body/pallas_call | solution.py:482
  4.9 6.1 %collective-permute-start = (f32[8,128]{1,0:T(8,128)S(1)}, f32[8,128]{1,0:T(8,128)S(1)}, u32[]{:S(2)}, u32[]{:S(2)}) collective-permute-start(f32[8,128]{1,0:T(8,128)S(1)} %get-tuple-element.32.request), channel_id=1, source_target_pairs={{0,28},{4,8},{8,4},{12,16},{16,12},{20,24},{24,20},{28,0},{1,29},{... | collective-permute-start | bytes 12296 | tf_op jit(solution)/shard_map/ppermute | solution.py:26
  10.9 1.6 %reshape.45.blocks = bf16[36,64,64]{2,1,0:T(8,128)(2,1)S(1)} reshape(bf16[1,1,36,4096]{3,2,1,0:T(8,128)(2,1)} %param.13) | data formatting | bytes 589824 | tf_op jit(solution)/shard_map/reshape | solution.py:528
  12.5 2.1 %extend_body.1 = (bf16[18,128,128]{2,1,0:T(8,128)(2,1)S(1)}, f32[18,16,128]{2,1,0:T(8,128)S(1)}, f32[96,128]{1,0:T(8,128)S(1)}, f32[96,128]{1,0:T(8,128)S(1)}, f32[96,128]{1,0:T(8,128)S(1)}) custom-call(s32[3,36]{1,0:T(4,128)S(4)} %get-tuple-element.31.order, f32[1024,128]{1,0:T(8,128)S(1)} %bitcast.19, bf16[36,64,64]{2,1,0:T(8,128)(2,1)S(1)} %reshape.45.blocks), custom_call_target="tpu_custom_call" | custom-call | tf_op jit(solution)/shard_map/extend_body/pallas_call | solution.py:482
  14.6 0.0 copy-start.3
  14.7 1.0 %copy-done.3 = f32[16,64,128]{2,1,0:T(8,128)S(1)} copy-done((f32[16,64,128]{2,1,0:T(8,128)S(1)}, f32[16,64,128]{2,1,0:T(8,128)}, u32[]{:S(2)}) %copy-start.3) | copy-done | bytes 524312
  15.7 0.5 edges_body.1
  16.2 0.0 copy-start.4
  16.2 0.7 %collective-permute-start.6 = (f32[288,128]{1,0:T(8,128)S(1)}, f32[288,128]{1,0:T(8,128)S(1)}, u32[]{:S(2)}, u32[]{:S(2)}) collective-permute-start(f32[288,128]{1,0:T(8,128)S(1)} %get-tuple-element.69), channel_id=1, source_target_pairs={{0,3},{1,2},{2,1},{3,0},{4,7},{5,6},{6,5},{7,4},{8,11},{9,10},{10,... | collective-permute-start | bytes 442376 | tf_op jit(solution)/shard_map/ppermute | solution.py:26
  16.9 1.0 %collective-permute-start.7 = (f32[288,128]{1,0:T(8,128)S(1)}, f32[288,128]{1,0:T(8,128)S(1)}, u32[]{:S(2)}, u32[]{:S(2)}) collective-permute-start(f32[288,128]{1,0:T(8,128)S(1)} %get-tuple-element.68), channel_id=1, source_target_pairs={{0,1},{1,0},{2,3},{3,2},{4,5},{5,4},{6,7},{7,6},{8,9},{9,8},{10,11... | collective-permute-start | bytes 442376 | tf_op jit(solution)/shard_map/ppermute | solution.py:26
  17.9 1.9 %collective-permute-start.4 = (f32[96,128]{1,0:T(8,128)S(1)}, f32[96,128]{1,0:T(8,128)S(1)}, u32[]{:S(2)}, u32[]{:S(2)}) collective-permute-start(f32[96,128]{1,0:T(8,128)S(1)} %get-tuple-element.34), channel_id=1, source_target_pairs={{0,28},{4,8},{8,4},{12,16},{16,12},{20,24},{24,20},{28,0},{1,29},{... | collective-permute-start | bytes 147464 | tf_op jit(solution)/shard_map/ppermute | solution.py:26
  19.8 0.0 collective-permute-done.got_a
  19.8 0.0 collective-permute-done.1.got_b
  19.8 0.1 collective-permute-start.2
  19.9 0.6 collective-permute-start.3
  20.5 2.5 %collective-permute-done.2.from_a = f32[24,128]{1,0:T(8,128)S(1)} collective-permute-done((f32[24,128]{1,0:T(8,128)S(1)}, f32[24,128]{1,0:T(8,128)S(1)}, u32[]{:S(2)}, u32[]{:S(2)}) %collective-permute-start.2) | collective-permute-done | bytes 12320 | tf_op jit(solution)/shard_map/ppermute | solution.py:26
  23.0 1.6 %collective-permute-start.5 = (f32[96,128]{1,0:T(8,128)S(1)}, f32[96,128]{1,0:T(8,128)S(1)}, u32[]{:S(2)}, u32[]{:S(2)}) collective-permute-start(f32[96,128]{1,0:T(8,128)S(1)} %get-tuple-element.35), channel_id=1, source_target_pairs={{0,4},{4,0},{8,12},{12,8},{16,20},{20,16},{24,28},{28,24},{1,5},{5... | collective-permute-start | bytes 147464 | tf_op jit(solution)/shard_map/ppermute | solution.py:26
  24.7 0.0 collective-permute-done.3.from_b
  24.7 1.6 %serve_body.1 = (s32[8,128]{1,0:T(8,128)S(4)}, f32[96,128]{1,0:T(8,128)S(1)}, f32[96,128]{1,0:T(8,128)S(1)}, f32[96,128]{1,0:T(8,128)S(1)}) custom-call(f32[8,128]{1,0:T(8,128)S(1)} %get-tuple-element.32.request, f32[8,128]{1,0:T(8,128)S(1)} %collective-permute-done.got_a, f32[8,128]{1,0:T(8,128)S(1)} %collective-permute-done.1.got_b, ...), custom_call_target="tpu_custom_call" | custom-call | tf_op jit(solution)/shard_map/serve_body/pallas_call | solution.py:482
  26.3 0.1 collective-permute-start.8
  26.4 4.0 %collective-permute-done.8.y_a = f32[96,128]{1,0:T(8,128)S(1)} collective-permute-done((f32[96,128]{1,0:T(8,128)S(1)}, f32[96,128]{1,0:T(8,128)S(1)}, u32[]{:S(2)}, u32[]{:S(2)}) %collective-permute-start.8) | collective-permute-done | bytes 49184 | tf_op jit(solution)/shard_map/ppermute | solution.py:26
  30.3 0.1 collective-permute-start.9
  30.4 1.1 %collective-permute-done.9.y_b = f32[96,128]{1,0:T(8,128)S(1)} collective-permute-done((f32[96,128]{1,0:T(8,128)S(1)}, f32[96,128]{1,0:T(8,128)S(1)}, u32[]{:S(2)}, u32[]{:S(2)}) %collective-permute-start.9) | collective-permute-done | bytes 49184 | tf_op jit(solution)/shard_map/ppermute | solution.py:26
  31.6 1.1 %collective-permute-start.10 = (f32[96,128]{1,0:T(8,128)S(1)}, f32[96,128]{1,0:T(8,128)S(1)}, u32[]{:S(2)}, u32[]{:S(2)}) collective-permute-start(f32[96,128]{1,0:T(8,128)S(1)} %pad_maximum_fusion.6), channel_id=1, source_target_pairs={{0,28},{4,8},{8,4},{12,16},{16,12},{20,24},{24,20},{28,0},{1,29},{... | collective-permute-start | bytes 147464 | tf_op jit(solution)/shard_map/ppermute | solution.py:26
  32.7 0.3 collective-permute-start.11
  33.0 0.0 collective-permute-done.7.packs_b.y_b
  33.0 1.9 %collective-permute-start.17 = (f32[144,128]{1,0:T(8,128)S(1)}, f32[144,128]{1,0:T(8,128)S(1)}, u32[]{:S(2)}, u32[]{:S(2)}) collective-permute-start(f32[144,128]{1,0:T(8,128)S(1)} %pad_maximum_fusion.5), channel_id=1, source_target_pairs={{0,4},{4,0},{8,12},{12,8},{16,20},{20,16},{24,28},{28,24},{1,5},{5... | collective-permute-start | bytes 221192 | tf_op jit(solution)/shard_map/ppermute | solution.py:26
  34.9 3.7 %collective-permute-start.16 = (f32[144,128]{1,0:T(8,128)S(1)}, f32[144,128]{1,0:T(8,128)S(1)}, u32[]{:S(2)}, u32[]{:S(2)}) collective-permute-start(f32[144,128]{1,0:T(8,128)S(1)} %pad_maximum_fusion.4), channel_id=1, source_target_pairs={{0,28},{4,8},{8,4},{12,16},{16,12},{20,24},{24,20},{28,0},{1,29},{... | collective-permute-start | bytes 221192 | tf_op jit(solution)/shard_map/ppermute | solution.py:26
  38.6 0.0 collective-permute-done.5.rows_b
  38.6 5.0 %pull_body.1 = (f32[1024,128]{1,0:T(8,128)S(1)}, f32[1288,128]{1,0:T(8,128)S(1)}, f32[64,128]{1,0:T(8,128)S(1)}) custom-call(f32[1024,128]{1,0:T(8,128)S(1)} %bitcast.13, f32[1024,128]{1,0:T(8,128)S(1)} %bitcast.23, f32[1024,128]{1,0:T(8,128)S(1)} %bitcast.16, f32[96,128]{1,0:T(8,128)S(1)} %collective-permute-done.4.rows_a, ...), custom_call_target="tpu_custom_call" | custom-call | tf_op jit(solution)/shard_map/pull_body/pallas_call | solution.py:482
  43.6 0.0 collective-permute-done.11.x_b
  43.6 2.0 %middle_body.1 = (f32[1024,128]{1,0:T(8,128)S(1)}, f32[18,16,128]{2,1,0:T(8,128)S(1)}, f32[160,128]{1,0:T(8,128)S(1)}, f32[160,128]{1,0:T(8,128)S(1)}, f32[160,1...) custom-call(s32[3,36]{1,0:T(4,128)S(4)} %get-tuple-element.31.order, ...), custom_call_target="tpu_custom_call", output_to_operand_aliasing={{0}: (2, {})} | custom-call | tf_op jit(solution)/shard_map/middle_body/pallas_call | solution.py:482
  45.6 0.1 collective-permute-start.12
  45.7 0.7 %collective-permute-start.13 = (f32[160,128]{1,0:T(8,128)S(1)}, f32[160,128]{1,0:T(8,128)S(1)}, u32[]{:S(2)}, u32[]{:S(2)}) collective-permute-start(f32[160,128]{1,0:T(8,128)S(1)} %get-tuple-element.49), channel_id=1, source_target_pairs={{0,1},{1,0},{2,3},{3,2},{4,5},{5,4},{6,7},{7,6},{8,9},{9,8},{10,11... | collective-permute-start | bytes 245768 | tf_op jit(solution)/shard_map/ppermute | solution.py:26
  46.5 3.2 %collective-permute-done.12.y_a = f32[160,128]{1,0:T(8,128)S(1)} collective-permute-done((f32[160,128]{1,0:T(8,128)S(1)}, f32[160,128]{1,0:T(8,128)S(1)}, u32[]{:S(2)}, u32[]{:S(2)}) %collective-permute-start.12) | collective-permute-done | bytes 81952 | tf_op jit(solution)/shard_map/ppermute | solution.py:26
  49.7 0.0 collective-permute-done.13.y_b
  49.7 0.1 collective-permute-start.15
  49.8 1.4 %collective-permute-start.14 = (f32[144,128]{1,0:T(8,128)S(1)}, f32[144,128]{1,0:T(8,128)S(1)}, u32[]{:S(2)}, u32[]{:S(2)}) collective-permute-start(f32[144,128]{1,0:T(8,128)S(1)} %pad_maximum_fusion.2), channel_id=1, source_target_pairs={{0,28},{4,8},{8,4},{12,16},{16,12},{20,24},{24,20},{28,0},{1,29},{... | collective-permute-start | bytes 221192 | tf_op jit(solution)/shard_map/ppermute | solution.py:26
  51.1 4.7 %inner_body.1.early = f32[1024,128]{1,0:T(8,128)S(1)} custom-call(f32[1024,128]{1,0:T(8,128)S(1)} %bitcast.14, f32[1024,128]{1,0:T(8,128)S(1)} %get-tuple-element.44.grad, f32[1288,128]{1,0:T(8,128)S(1)} %get-tuple-element.45.pad_rate, f32[1024,128]{1,0:T(8,128)S(1)} %bitcast.17), custom_call_target="tpu_custom_call" | custom-call | tf_op jit(solution)/shard_map/inner_body/pallas_call | solution.py:482
  55.9 0.0 collective-permute-done.16.x_a
  55.9 4.4 %push_body.1.early = f32[1024,128]{1,0:T(8,128)S(1)} custom-call(f32[1024,128]{1,0:T(8,128)S(1)} %bitcast.21, f32[1288,128]{1,0:T(8,128)S(1)} %get-tuple-element.45.pad_rate, f32[1024,128]{1,0:T(8,128)S(1)} %bitcast.18, f32[64,128]{1,0:T(8,128)S(1)} %get-tuple-element.46.edge_rate, f32[48,128]{1,0:T(8,128)S(1)} %slice.90.late_a, ...), custom_call_target="tpu_custom_call" | custom-call | tf_op jit(solution)/shard_map/push_body/pallas_call | solution.py:482
  60.3 3.0 %section_body.1 = (f32[1024,128]{1,0:T(8,128)S(1)}, f32[18,128,128]{2,1,0:T(8,128)S(1)}) custom-call(s32[3,36]{1,0:T(4,128)S(4)} %get-tuple-element.31.order, s32[8,128]{1,0:T(8,128)S(4)} %get-tuple-element.33.asked, f32[1024,128]{1,0:T(8,128)S(1)} %push_body.1.early, ...), custom_call_target="tpu_custom_call", output_to_operand_aliasing={{0}: (2, {})} | custom-call | tf_op jit(solution)/shard_map/section_body/pallas_call | solution.py:482
  63.3 0.0 collective-permute-done.15.x_b
  63.3 0.0 collective-permute-done.14.x_a
  63.3 2.9 %last_body.1 = (f32[1024,128]{1,0:T(8,128)}, f32[1152,128]{1,0:T(8,128)}) custom-call(s32[3,36]{1,0:T(4,128)S(4)} %get-tuple-element.31.order, f32[1024,128]{1,0:T(8,128)S(1)} %inner_body.1.early, f32[1024,128]{1,0:T(8,128)S(1)} %get-tuple-element.44.grad, f32[1288,128]{1,0:T(8,128)S(1)} %get-tuple-element.45.pad_rate, ...), custom_call_target="tpu_custom_call" | custom-call | tf_op jit(solution)/shard_map/last_body/pallas_call | solution.py:482
  (36 shorter events, 0.1 us)
Async XLA Ops:
  0.6 11.9 %copy-start.2 = (f32[16,64,128]{2,1,0:T(8,128)S(1)}, f32[16,64,128]{2,1,0:T(8,128)}, u32[]{:S(2)}) copy-start(f32[16,64,128]{2,1,0:T(8,128)} %param.9) | copy-start | bytes 1572868
  0.6 14.0 %copy-start = (f32[16,64,128]{2,1,0:T(8,128)S(1)}, f32[16,64,128]{2,1,0:T(8,128)}, u32[]{:S(2)}) copy-start(f32[16,64,128]{2,1,0:T(8,128)} %param.12) | copy-start | bytes 1572868
  0.7 14.0 %copy-start.1 = (f32[16,64,128]{2,1,0:T(8,128)S(1)}, f32[16,64,128]{2,1,0:T(8,128)}, u32[]{:S(2)}) copy-start(f32[16,64,128]{2,1,0:T(8,128)} %param.11) | copy-start | bytes 1572868
  1.4 0.7 copy-start.5
  2.1 0.7 copy-start.6
  2.7 0.7 copy-start.7
  4.9 14.9 %collective-permute-start = (f32[8,128]{1,0:T(8,128)S(1)}, f32[8,128]{1,0:T(8,128)S(1)}, u32[]{:S(2)}, u32[]{:S(2)}) collective-permute-start(f32[8,128]{1,0:T(8,128)S(1)} %get-tuple-element.32.request), channel_id=1, source_target_pairs={{0,28},{4,8},{8,4},{12,16},{16,12},{20,24},{24,20},{28,0},{1,29},{... | collective-permute-start | bytes 12296 | tf_op jit(solution)/shard_map/ppermute | solution.py:26
  10.9 8.9 %collective-permute-start.1 = (f32[8,128]{1,0:T(8,128)S(1)}, f32[8,128]{1,0:T(8,128)S(1)}, u32[]{:S(2)}, u32[]{:S(2)}) collective-permute-start(f32[8,128]{1,0:T(8,128)S(1)} %get-tuple-element.32.request), channel_id=1, source_target_pairs={{0,4},{4,0},{8,12},{12,8},{16,20},{20,16},{24,28},{28,24},{1,5},{5... | collective-permute-start | bytes 12296 | tf_op jit(solution)/shard_map/ppermute | solution.py:26
  14.6 1.0 %copy-start.3 = (f32[16,64,128]{2,1,0:T(8,128)S(1)}, f32[16,64,128]{2,1,0:T(8,128)}, u32[]{:S(2)}) copy-start(f32[16,64,128]{2,1,0:T(8,128)} %param.10) | copy-start | bytes 1572868
  16.2 22.4 %copy-start.4 = (f32[16,64,128]{2,1,0:T(8,128)S(1)}, f32[16,64,128]{2,1,0:T(8,128)}, u32[]{:S(2)}) copy-start(f32[16,64,128]{2,1,0:T(8,128)} %param.10) | copy-start | bytes 1572868
  16.2 16.5 %collective-permute-start.6 = (f32[288,128]{1,0:T(8,128)S(1)}, f32[288,128]{1,0:T(8,128)S(1)}, u32[]{:S(2)}, u32[]{:S(2)}) collective-permute-start(f32[288,128]{1,0:T(8,128)S(1)} %get-tuple-element.69), channel_id=1, source_target_pairs={{0,3},{1,2},{2,1},{3,0},{4,7},{5,6},{6,5},{7,4},{8,11},{9,10},{10,... | collective-permute-start | bytes 442376 | tf_op jit(solution)/shard_map/ppermute | solution.py:26
  16.9 16.0 %collective-permute-start.7 = (f32[288,128]{1,0:T(8,128)S(1)}, f32[288,128]{1,0:T(8,128)S(1)}, u32[]{:S(2)}, u32[]{:S(2)}) collective-permute-start(f32[288,128]{1,0:T(8,128)S(1)} %get-tuple-element.68), channel_id=1, source_target_pairs={{0,1},{1,0},{2,3},{3,2},{4,5},{5,4},{6,7},{7,6},{8,9},{9,8},{10,11... | collective-permute-start | bytes 442376 | tf_op jit(solution)/shard_map/ppermute | solution.py:26
  17.9 17.0 %collective-permute-start.4 = (f32[96,128]{1,0:T(8,128)S(1)}, f32[96,128]{1,0:T(8,128)S(1)}, u32[]{:S(2)}, u32[]{:S(2)}) collective-permute-start(f32[96,128]{1,0:T(8,128)S(1)} %get-tuple-element.34), channel_id=1, source_target_pairs={{0,28},{4,8},{8,4},{12,16},{16,12},{20,24},{24,20},{28,0},{1,29},{... | collective-permute-start | bytes 147464 | tf_op jit(solution)/shard_map/ppermute | solution.py:26
  19.8 3.2 %collective-permute-start.2 = (f32[24,128]{1,0:T(8,128)S(1)}, f32[24,128]{1,0:T(8,128)S(1)}, u32[]{:S(2)}, u32[]{:S(2)}) collective-permute-start(f32[24,128]{1,0:T(8,128)S(1)} %constant_dynamic-update-slice_fusion), channel_id=1, source_target_pairs={{0,3},{1,2},{2,1},{3,0},{4,7},{5,6},{6,5},{7,4},{8,11},{9,10},{10,... | collective-permute-start | bytes 36872 | tf_op jit(solution)/shard_map/ppermute | solution.py:26
  19.9 4.8 %collective-permute-start.3 = (f32[24,128]{1,0:T(8,128)S(1)}, f32[24,128]{1,0:T(8,128)S(1)}, u32[]{:S(2)}, u32[]{:S(2)}) collective-permute-start(f32[24,128]{1,0:T(8,128)S(1)} %constant_dynamic-update-slice_fusion), channel_id=1, source_target_pairs={{0,1},{1,0},{2,3},{3,2},{4,5},{5,4},{6,7},{7,6},{8,9},{9,8},{10,11... | collective-permute-start | bytes 36872 | tf_op jit(solution)/shard_map/ppermute | solution.py:26
  23.0 15.6 %collective-permute-start.5 = (f32[96,128]{1,0:T(8,128)S(1)}, f32[96,128]{1,0:T(8,128)S(1)}, u32[]{:S(2)}, u32[]{:S(2)}) collective-permute-start(f32[96,128]{1,0:T(8,128)S(1)} %get-tuple-element.35), channel_id=1, source_target_pairs={{0,4},{4,0},{8,12},{12,8},{16,20},{20,16},{24,28},{28,24},{1,5},{5... | collective-permute-start | bytes 147464 | tf_op jit(solution)/shard_map/ppermute | solution.py:26
  26.3 4.0 %collective-permute-start.8 = (f32[96,128]{1,0:T(8,128)S(1)}, f32[96,128]{1,0:T(8,128)S(1)}, u32[]{:S(2)}, u32[]{:S(2)}) collective-permute-start(f32[96,128]{1,0:T(8,128)S(1)} %get-tuple-element.42), channel_id=1, source_target_pairs={{0,3},{1,2},{2,1},{3,0},{4,7},{5,6},{6,5},{7,4},{8,11},{9,10},{10,... | collective-permute-start | bytes 147464 | tf_op jit(solution)/shard_map/ppermute | solution.py:26
  30.3 1.2 %collective-permute-start.9 = (f32[96,128]{1,0:T(8,128)S(1)}, f32[96,128]{1,0:T(8,128)S(1)}, u32[]{:S(2)}, u32[]{:S(2)}) collective-permute-start(f32[96,128]{1,0:T(8,128)S(1)} %get-tuple-element.43), channel_id=1, source_target_pairs={{0,1},{1,0},{2,3},{3,2},{4,5},{5,4},{6,7},{7,6},{8,9},{9,8},{10,11... | collective-permute-start | bytes 147464 | tf_op jit(solution)/shard_map/ppermute | solution.py:26
  31.6 12.1 %collective-permute-start.10 = (f32[96,128]{1,0:T(8,128)S(1)}, f32[96,128]{1,0:T(8,128)S(1)}, u32[]{:S(2)}, u32[]{:S(2)}) collective-permute-start(f32[96,128]{1,0:T(8,128)S(1)} %pad_maximum_fusion.6), channel_id=1, source_target_pairs={{0,28},{4,8},{8,4},{12,16},{16,12},{20,24},{24,20},{28,0},{1,29},{... | collective-permute-start | bytes 147464 | tf_op jit(solution)/shard_map/ppermute | solution.py:26
  32.7 10.9 %collective-permute-start.11 = (f32[96,128]{1,0:T(8,128)S(1)}, f32[96,128]{1,0:T(8,128)S(1)}, u32[]{:S(2)}, u32[]{:S(2)}) collective-permute-start(f32[96,128]{1,0:T(8,128)S(1)} %pad_maximum_fusion.7), channel_id=1, source_target_pairs={{0,4},{4,0},{8,12},{12,8},{16,20},{20,16},{24,28},{28,24},{1,5},{5... | collective-permute-start | bytes 147464 | tf_op jit(solution)/shard_map/ppermute | solution.py:26
  33.0 22.9 %collective-permute-start.17 = (f32[144,128]{1,0:T(8,128)S(1)}, f32[144,128]{1,0:T(8,128)S(1)}, u32[]{:S(2)}, u32[]{:S(2)}) collective-permute-start(f32[144,128]{1,0:T(8,128)S(1)} %pad_maximum_fusion.5), channel_id=1, source_target_pairs={{0,4},{4,0},{8,12},{12,8},{16,20},{20,16},{24,28},{28,24},{1,5},{5... | collective-permute-start | bytes 221192 | tf_op jit(solution)/shard_map/ppermute | solution.py:26
  34.9 21.0 %collective-permute-start.16 = (f32[144,128]{1,0:T(8,128)S(1)}, f32[144,128]{1,0:T(8,128)S(1)}, u32[]{:S(2)}, u32[]{:S(2)}) collective-permute-start(f32[144,128]{1,0:T(8,128)S(1)} %pad_maximum_fusion.4), channel_id=1, source_target_pairs={{0,28},{4,8},{8,4},{12,16},{16,12},{20,24},{24,20},{28,0},{1,29},{... | collective-permute-start | bytes 221192 | tf_op jit(solution)/shard_map/ppermute | solution.py:26
  45.6 4.0 %collective-permute-start.12 = (f32[160,128]{1,0:T(8,128)S(1)}, f32[160,128]{1,0:T(8,128)S(1)}, u32[]{:S(2)}, u32[]{:S(2)}) collective-permute-start(f32[160,128]{1,0:T(8,128)S(1)} %get-tuple-element.48), channel_id=1, source_target_pairs={{0,3},{1,2},{2,1},{3,0},{4,7},{5,6},{6,5},{7,4},{8,11},{9,10},{10,... | collective-permute-start | bytes 245768 | tf_op jit(solution)/shard_map/ppermute | solution.py:26
  45.7 4.0 %collective-permute-start.13 = (f32[160,128]{1,0:T(8,128)S(1)}, f32[160,128]{1,0:T(8,128)S(1)}, u32[]{:S(2)}, u32[]{:S(2)}) collective-permute-start(f32[160,128]{1,0:T(8,128)S(1)} %get-tuple-element.49), channel_id=1, source_target_pairs={{0,1},{1,0},{2,3},{3,2},{4,5},{5,4},{6,7},{7,6},{8,9},{9,8},{10,11... | collective-permute-start | bytes 245768 | tf_op jit(solution)/shard_map/ppermute | solution.py:26
  49.7 13.6 %collective-permute-start.15 = (f32[144,128]{1,0:T(8,128)S(1)}, f32[144,128]{1,0:T(8,128)S(1)}, u32[]{:S(2)}, u32[]{:S(2)}) collective-permute-start(f32[144,128]{1,0:T(8,128)S(1)} %pad_maximum_fusion.3), channel_id=1, source_target_pairs={{0,4},{4,0},{8,12},{12,8},{16,20},{20,16},{24,28},{28,24},{1,5},{5... | collective-permute-start | bytes 221192 | tf_op jit(solution)/shard_map/ppermute | solution.py:26
  49.8 13.5 %collective-permute-start.14 = (f32[144,128]{1,0:T(8,128)S(1)}, f32[144,128]{1,0:T(8,128)S(1)}, u32[]{:S(2)}, u32[]{:S(2)}) collective-permute-start(f32[144,128]{1,0:T(8,128)S(1)} %pad_maximum_fusion.2), channel_id=1, source_target_pairs={{0,28},{4,8},{8,4},{12,16},{16,12},{20,24},{24,20},{28,0},{1,29},{... | collective-permute-start | bytes 221192 | tf_op jit(solution)/shard_map/ppermute | solution.py:26

commit v3 on v2

--- a/solution.py
+++ b/solution.py
@@ -13,7 +13,6 @@
 WEIGHTS = (2.0 / 60.0, -13.0 / 60.0, 47.0 / 60.0, 27.0 / 60.0, -3.0 / 60.0)
 PAD = 80
 VMEM_LIMIT = 16 << 20
-UNROLL = 2
 
 A, B, S = 0, 1, 2
 
@@ -142,7 +141,7 @@
 
 
 def adjoint_plane(z, pad_ref, pad_rate_ref, rate_y_ref, up_ref, down_ref, extent_x):
-    base = pl.multiple_of(z * PAD, 8)
+    base = z * PAD
     here = pad_ref[pl.ds(base, PAD), :]
     jump = pad_ref[pl.ds(base + 1, PAD), :] - here
     rate_up, rate_down = upwind(pad_rate_ref[pl.ds(base, PAD), :])
@@ -157,7 +156,7 @@
     field = pad_ref[pl.ds(base + 8, extent_x), :]
     lane = lanes(field.shape)
     jump = jnp.where(lane == 127, 0.0, roll(field, -1) - field)
-    rate_up, rate_down = upwind(rate_y_ref[pl.ds(pl.multiple_of(z * extent_x, 8), extent_x), :])
+    rate_up, rate_down = upwind(rate_y_ref[pl.ds(z * extent_x, extent_x), :])
     up_part, down_part = rate_up * jump, rate_down * jump
     ahead = combine(up_part, down_part, 2)
     for k in (1, 0):
@@ -183,77 +182,82 @@
     return ref[number * extent_x : (number + 1) * extent_x]
 
 
-def lists_body(count, heading, target, source, order, request, used, *, planes, extent_x):
+def begin_body(
+    count, heading, target, source, field, cotan, rate_x, rate_y,
+    order, send_a, send_b, field_out, cotan_out, rate_x_out, rate_y_out,
+    heading_in, target_in, source_in, used, sems, *, planes, extent_x,
+):
+    pairs = (
+        (heading, heading_in), (target, target_in), (source, source_in),
+        (cotan, cotan_out), (rate_x, rate_x_out), (field, field_out), (rate_y, rate_y_out),
+    )
+    copies = [pltpu.make_async_copy(a, b, sems.at[number]) for number, (a, b) in enumerate(pairs)]
+    for copy in copies:
+        copy.start()
     parity_x, parity_y = parities()
     for label in range(9):
         used[label] = 0
     lane = lanes((8, 128))
-
-    def place(slot, asked):
-        toward = heading[slot]
-        ex = (toward // 3 - 1) * (1 - 2 * parity_x)
-        ey = (lax.rem(toward, 3) - 1) * (1 - 2 * parity_y)
+    for copy in copies[:3]:
+        copy.wait()
+    total = count[0, 0]
+    asked = jnp.zeros((8, 128), jnp.int32)
+    for slot in range(heading.shape[0]):
+        toward = heading_in[slot]
+        across = (toward >= 3).astype(jnp.int32) + (toward >= 6).astype(jnp.int32)
+        ex = (across - 1) * (1 - 2 * parity_x)
+        ey = (toward - 3 * across - 1) * (1 - 2 * parity_y)
         lx = jnp.where(ex == 0, 2, (ex + 1) // 2)
         ly = jnp.where(ey == 0, 2, (ey + 1) // 2)
         label = ly * 3 + lx
         spot = label * ROUTE_MOST + used[label]
         used[label] = used[label] + 1
-        alive = slot < count[0]
         order[0, spot] = slot
-        order[1, spot] = source[slot]
-        order[2, spot] = alive.astype(jnp.int32)
-        wanted = jnp.where(alive, target[slot], 0)
-        return jnp.where(lane == spot, wanted, asked)
-
-    asked = lax.fori_loop(0, heading.shape[0], place, jnp.zeros((8, 128), jnp.int32), unroll=4)
-    request[...] = asked.astype(jnp.float32)
-
-
-def edges_body(field, cotan, rate_x, rate_y, rows_a, rows_b, late_a, late_b, packs, *, planes, extent_x):
-    even = parities()[0] == 0
+        order[1, spot] = source_in[slot]
+        order[2, spot] = (slot < total).astype(jnp.int32)
+        wanted = jnp.where(slot < total, target_in[slot], 0)
+        asked = jnp.where(lane == spot, wanted, asked)
+    even = parity_x == 0
     high = extent_x - 3
     size = 3 * planes
-    for rows, late, start in (
-        (rows_a, late_a, jnp.where(even, 0, high)),
-        (rows_b, late_b, jnp.where(even, high, 0)),
-    ):
-        rows[0:size, :] = edge_rows(cotan, start, planes, extent_x)
-        rows[size : 2 * size, :] = edge_rows(rate_x, start, planes, extent_x)
-        late[...] = edge_rows(field, start, planes, extent_x)
+    for out in (send_a, send_b):
+        out[0:8, :] = asked.astype(jnp.float32)
+    for number, ref in enumerate((cotan_out, rate_x_out, field_out)):
+        copies[3 + number].wait()
+        first = 8 + number * size
+        send_a[first : first + size, :] = edge_rows(ref, jnp.where(even, 0, high), planes, extent_x)
+        send_b[first : first + size, :] = edge_rows(ref, jnp.where(even, high, 0), planes, extent_x)
+    copies[6].wait()
+
+
+def extend_body(order, field, cotan, rate_y, blocks, pairs, picked, send_a, send_b, value_s, *, planes, extent_x):
+    extra = 3 * extent_x
     for number, ref in enumerate((cotan, rate_y, field)):
-        packs[number * extent_x : (number + 1) * extent_x, :] = edge_pack(ref, planes, extent_x)
-
-
-def extend_body(order, field, blocks, pairs, picked, value_a, value_b, value_s, *, planes, extent_x):
-    for ly, value in enumerate((value_a, value_b, value_s)):
-
-        def one(inner, carry):
-            number = ly * 6 + inner
-            one_block, two_block = blocks[order[0, 2 * number]], blocks[order[0, 2 * number + 1]]
-            zero = jnp.zeros_like(one_block)
-            joined = jnp.concatenate(
-                [jnp.concatenate([one_block, zero], axis=1), jnp.concatenate([zero, two_block], axis=1)], axis=0
-            )
-            pairs[number] = joined
-            tiles = tile_pair(field, order[1, 2 * number], order[1, 2 * number + 1], planes, extent_x)
-            picked[number] = tiles
-            spot = pl.ds(pl.multiple_of(inner * planes, 8), planes)
-            value[spot, :] = pair_dot(alive_lanes(tiles, order, number), joined, 1)
-            return carry
-
-        lax.fori_loop(0, 6, one, 0, unroll=UNROLL)
+        packed = edge_pack(ref, planes, extent_x)
+        for out in (send_a, send_b):
+            out[number * extent_x : (number + 1) * extent_x, :] = packed
+    for number in range(18):
+        one_block, two_block = blocks[order[0, 2 * number]], blocks[order[0, 2 * number + 1]]
+        zero = jnp.zeros_like(one_block)
+        joined = jnp.concatenate(
+            [jnp.concatenate([one_block, zero], axis=1), jnp.concatenate([zero, two_block], axis=1)], axis=0
+        )
+        pairs[number] = joined
+        tiles = tile_pair(field, order[1, 2 * number], order[1, 2 * number + 1], planes, extent_x)
+        picked[number] = tiles
+        value = pair_dot(alive_lanes(tiles, order, number), joined, 1)
+        out, first = ((send_a, extra), (send_b, extra), (value_s, 0))[number // 6]
+        first = first + number % 6 * planes
+        out[first : first + planes, :] = value
 
 
 def gather_tiles(asked, field, outs, first, planes, extent_x):
     for ly in range(3):
 
-        def one(inner, carry):
+        for inner in range(6):
             at = ly * 12 + 2 * inner
             tiles = tile_pair(field, asked[ly, at], asked[ly, at + 1], planes, extent_x)
-            outs[ly][pl.ds(pl.multiple_of(first + inner * planes, 8), planes), :] = tiles
-            return carry
-
-        lax.fori_loop(0, 6, one, 0, unroll=UNROLL)
+            outs[ly][first + inner * planes : first + (inner + 1) * planes, :] = tiles
 
 
 def serve_body(request, got_a, got_b, from_a, from_b, cotan, asked, out_a, out_b, out_s, list_ref, sem, *, planes, extent_x):
@@ -263,7 +267,7 @@
     for a, b, s in (
         (from_a[8:16], from_a[16:24], from_a[0:8]),
         (from_b[8:16], from_b[16:24], from_b[0:8]),
-        (got_a[...], got_b[...], request[...]),
+        (got_a[0:8], got_b[0:8], request[0:8]),
     ):
         merged.append(jnp.where(group == 0, a, jnp.where(group == 1, b, s))[0:1])
     spread = [jnp.broadcast_to(one, (8, 128)) for one in merged]
@@ -290,29 +294,27 @@
     parity_x, parity_y = parities()
     even_x, even_y = parity_x == 0, parity_y == 0
     size = 3 * planes
-    fill_padded(pad, cotan, rows_a[0:size], rows_b[0:size], even_x, planes, extent_x)
-    fill_padded(pad_rate, rate_x, rows_a[size : 2 * size], rows_b[size : 2 * size], even_x, planes, extent_x)
+    fill_padded(pad, cotan, rows_a[8 : 8 + size], rows_b[8 : 8 + size], even_x, planes, extent_x)
+    fill_padded(pad_rate, rate_x, rows_a[8 + size : 8 + 2 * size], rows_b[8 + size : 8 + 2 * size], even_x, planes, extent_x)
     halo = edge_join(part(packs_a, 0, extent_x), part(packs_b, 0, extent_x), even_y)
     halo_rate = edge_join(part(packs_a, 1, extent_x), part(packs_b, 1, extent_x), even_y)
     edge_rate[...] = halo_rate
     edges = adjoint_edges(part(packs, 0, extent_x), halo, part(packs, 1, extent_x), halo_rate)
 
-    def plane(z, carry):
-        spot = pl.ds(pl.multiple_of(z * extent_x, 8), extent_x)
+    for z in range(planes):
+        spot = pl.ds(z * extent_x, extent_x)
         pulled = adjoint_plane(z, pad, pad_rate, rate_y, up_ref, down_ref, extent_x)
         rim = roll(edges, 125 - 8 * z)
         lane = lanes(rim.shape)
         pulled = pulled + jnp.where((lane < 3) | (lane >= 125), rim, 0.0)
         grad[spot, :] = 0.5 * cotan[spot, :] + (0.5 * TIME_STEP) * pulled
-        return carry
-
-    lax.fori_loop(0, planes, plane, 0)
-
-
-def push_body(field, pad_rate, rate_y, edge_rate, late_a, late_b, packs, packs_a, packs_b, section, pad, flux_ref, *, planes, extent_x):
+
+
+def push_body(field, pad_rate, rate_y, edge_rate, rows_a, rows_b, packs, packs_a, packs_b, section, pad, flux_ref, *, planes, extent_x):
     parity_x, parity_y = parities()
     even_x, even_y = parity_x == 0, parity_y == 0
-    fill_padded(pad, field, late_a[...], late_b[...], even_x, planes, extent_x)
+    first = 8 + 6 * planes
+    fill_padded(pad, field, rows_a[first : first + 3 * planes], rows_b[first : first + 3 * planes], even_x, planes, extent_x)
     halo = edge_join(part(packs_a, 2, extent_x), part(packs_b, 2, extent_x), even_y)
     line = jnp.where(lanes(halo.shape) % 8 < 3, halo, part(packs, 2, extent_x))
     moved = {k: roll(line, -k) for k in range(-2, 4)}
@@ -321,9 +323,9 @@
         WEIGHTS[j] * moved[3 - j] for j in range(5)
     )
 
-    def plane(z, carry):
-        base = pl.multiple_of(z * PAD, 8)
-        spot = pl.ds(pl.multiple_of(z * extent_x, 8), extent_x)
+    for z in range(planes):
+        base = z * PAD
+        spot = pl.ds(z * extent_x, extent_x)
         window = extent_x + 8
         near = {k: pad[pl.ds(base + 7 + k, window), :] for k in range(-2, 4)}
         rate_up, rate_down = upwind(pad_rate[pl.ds(base + 7, window), :])
@@ -346,9 +348,6 @@
         )
         change = change + roll(jnp.where(lane == 127, roll(flux_low, turn), flux), 1) - flux
         section[spot, :] = here + TIME_STEP * change
-        return carry
-
-    lax.fori_loop(0, planes, plane, 0)
 
 
 def middle_body(order, asked, early, pairs, x_a, x_b, y_a, y_b, own, grad, returned, send_a, send_b, send_s, rows_a, rows_b, *, planes, extent_x):
@@ -375,13 +374,10 @@
         pad[pl.ds(5 + j, planes, PAD), :] = row_of(grad, 0, planes, extent_x)
         pad[pl.ds(high + j, planes, PAD), :] = row_of(grad, extent_x - 1, planes, extent_x)
 
-    def plane(z, carry):
-        spot = pl.ds(pl.multiple_of(z * extent_x, 8), extent_x)
+    for z in range(planes):
+        spot = pl.ds(z * extent_x, extent_x)
         pulled = adjoint_plane(z, pad, pad_rate, rate_y, up_ref, down_ref, extent_x)
         out[spot, :] = 0.5 * cotan[spot, :] + grad[spot, :] + TIME_STEP * pulled
-        return carry
-
-    lax.fori_loop(0, planes, plane, 0)
 
 
 def outer(left, right):
@@ -401,12 +397,9 @@
         at = ly * 12 + lx * ROUTE_MOST + 2 * half
         add_tile_pair(section, asked[ly, at], asked[ly, at + 1], came, planes, extent_x)
 
-    def pick(number, carry):
+    for number in range(first_outer.shape[0]):
         picked = tile_pair(section, order[1, 2 * number], order[1, 2 * number + 1], planes, extent_x)
         first_outer[number] = outer((0.5 * TIME_STEP) * returned[number], picked)
-        return carry
-
-    lax.fori_loop(0, first_outer.shape[0], pick, 0, unroll=UNROLL)
 
 
 def last_body(
@@ -419,14 +412,11 @@
     halo = edge_join(y_a[0:extent_x], y_b[0:extent_x], even_y)
     edges = adjoint_edges(own[0:extent_x], halo, part(packs, 1, extent_x), edge_rate[...])
 
-    def plane(z, carry):
-        spot = pl.ds(pl.multiple_of(z * extent_x, 8), extent_x)
+    for z in range(planes):
+        spot = pl.ds(z * extent_x, extent_x)
         rim = roll(edges, 125 - 8 * z)
         lane = lanes(rim.shape)
         total[spot, :] = early[spot, :] + TIME_STEP * jnp.where((lane < 3) | (lane >= 125), rim, 0.0)
-        return carry
-
-    lax.fori_loop(0, planes, plane, 0, unroll=2)
     low_rows = [jnp.where(even_x, x_a[j * planes : (j + 1) * planes], x_b[j * planes : (j + 1) * planes]) for j in range(3)]
     high_rows = [jnp.where(even_x, x_b[j * planes : (j + 1) * planes], x_a[j * planes : (j + 1) * planes]) for j in range(3)]
     first_cell = row_of(grad, 0, planes, extent_x)
@@ -464,18 +454,15 @@
     out[...] = total[...]
 
 
-SPACE = {"v": pltpu.VMEM, "s": pltpu.SMEM}
-
-
-def call(body, smem, vmem, outs, scratch=(), alias=None, **sizes):
-    ins, specs, shapes, out_specs = [], [], [], []
-    for value, kind in [(v, "s") for v in smem] + [(v, "v") for v in vmem]:
-        if isinstance(value, tuple):
-            value = value[0]
-        else:
-            value = pltpu.with_memory_space_constraint(value, SPACE[kind])
-        ins.append(value)
-        specs.append(pl.BlockSpec(memory_space=SPACE[kind]))
+SPACE = {"v": pltpu.VMEM, "s": pltpu.SMEM, "h": pltpu.HBM}
+
+
+def call(body, ins, outs, scratch=(), alias=None, **sizes):
+    values, specs, shapes, out_specs = [], [], [], []
+    for kind, group in ins:
+        for value in group:
+            values.append(value if kind == "r" else pltpu.with_memory_space_constraint(value, SPACE[kind]))
+            specs.append(pl.BlockSpec(memory_space=SPACE["s" if kind == "r" else kind]))
     for shape, dtype, kind in outs:
         shapes.append(jax.ShapeDtypeStruct(shape, dtype) if kind == "h" else SPACE[kind](shape, dtype))
         out_specs.append(pl.BlockSpec(memory_space=SPACE["s" if kind == "s" else "v"]))
@@ -488,7 +475,7 @@
         input_output_aliases=alias or {},
         compiler_params=pltpu.CompilerParams(vmem_limit_bytes=VMEM_LIMIT),
         name=body.__name__,
-    )(*ins)
+    )(*values)
 
 
 def shards(
@@ -507,36 +494,39 @@
     pad_scratch = pltpu.VMEM(*padded)
     whole = ((cells, 128), f32, "v")
 
-    order, request = call(
-        lists_body,
-        [(tile_count.reshape(1),), (dest_offset.reshape(slots),), (dest_tile.reshape(slots),), (source_tile.reshape(slots),)], [],
-        [((3, slots), i32, "s"), ((8, 128), f32, "v")],
-        scratch=(pltpu.SMEM((9,), i32),), **sizes,
-    )
-    got_b = exchange(request, "gx", B)
-    got_a = exchange(request, "gx", A)
-    rows_a, rows_b, late_a, late_b, packs = call(
-        edges_body, [], [field, cotan, rate_x, rate_y],
-        [box, box, ((size, 128), f32, "v"), ((size, 128), f32, "v"), ((3 * extent_x, 128), f32, "v")], **sizes,
-    )
-    rows_b = exchange(rows_b, "gx", B)
-    rows_a = exchange(rows_a, "gx", A)
-    column = jnp.concatenate([request, got_a, got_b], axis=0)
+    order, send_a, send_b, field, cotan, rate_x, rate_y = call(
+        begin_body,
+        [("r", [tile_count]), ("h", [v.reshape(slots) for v in (dest_offset, dest_tile, source_tile)] + [field, cotan, rate_x, rate_y])],
+        [((3, slots), i32, "s")] + [((8 + 3 * size, 128), f32, "v")] * 2 + [whole] * 4,
+        scratch=[pltpu.SMEM((slots,), i32)] * 3 + [pltpu.SMEM((9,), i32), pltpu.SemaphoreType.DMA((7,))],
+        **sizes,
+    )
+    rows_b = exchange(send_b, "gx", B)
+    rows_a = exchange(send_a, "gx", A)
+    column = jnp.concatenate([send_a[:8], rows_a[:8], rows_b[:8]], axis=0)
+    extra = 3 * extent_x
+    pairs, picked, wide_a, wide_b, value_s = call(
+        extend_body, [("s", [order]), ("v", [field, cotan, rate_y, blocks.reshape(slots, TILE, TILE)])],
+        [((pair_total, 128, 128), jnp.bfloat16, "v"), ((pair_total, planes, 128), f32, "v")]
+        + [((extra + 2 * size, 128), f32, "v")] * 2 + [box], **sizes,
+    )
+    column, wide_a, wide_b = lax.optimization_barrier((column, wide_a, wide_b))
     from_b = exchange(column, "gy", B)
     from_a = exchange(column, "gy", A)
-    pairs, picked, value_a, value_b, value_s = call(
-        extend_body, [order], [field, blocks.reshape(slots, TILE, TILE)],
-        [((pair_total, 128, 128), jnp.bfloat16, "v"), ((pair_total, planes, 128), f32, "v"), box, box, box], **sizes,
-    )
-    packs_b = exchange(jnp.concatenate([packs, value_b], axis=0), "gy", B)
-    packs_a = exchange(jnp.concatenate([packs, value_a], axis=0), "gy", A)
+    packs_b = exchange(wide_b, "gy", B)
+    packs_a = exchange(wide_a, "gy", A)
 
     asked, tiles_a, tiles_b, tiles_s = call(
-        serve_body, [], [request, got_a, got_b, from_a, from_b, cotan],
+        serve_body, [("v", [send_a, rows_a, rows_b, from_a, from_b, cotan])],
         [((8, 128), i32, "s"), box, box, box], scratch=(pltpu.VMEM((8, 128), i32), pltpu.SemaphoreType.DMA(())), **sizes,
     )
     y_b = exchange(tiles_b, "gy", B)
     y_a = exchange(tiles_a, "gy", A)
+    early, pad_rate, edge_rate = call(
+        pull_body, [("v", [cotan, rate_x, rate_y, rows_a, rows_b, wide_a, packs_a, packs_b])],
+        [whole, padded + ("v",), ((extent_x, 128), f32, "v")], scratch=(pad_scratch,) * 3, **sizes,
+    )
+    y_a, y_b, early = lax.optimization_barrier((y_a, y_b, early))
 
     def onward(own, a, b, own_first, first, m):
         cut = lambda v, start: v[start + m * 2 * planes : start + (m + 1) * 2 * planes]
@@ -544,36 +534,32 @@
 
     x_b = exchange(jnp.concatenate(onward(tiles_s, y_a, y_b, 0, 0, B), axis=0), "gx", B)
     x_a = exchange(jnp.concatenate(onward(tiles_s, y_a, y_b, 0, 0, A), axis=0), "gx", A)
-    early, pad_rate, edge_rate = call(
-        pull_body, [], [cotan, rate_x, rate_y, rows_a, rows_b, packs, packs_a, packs_b],
-        [whole, padded + ("v",), ((extent_x, 128), f32, "v")], scratch=(pad_scratch,) * 3, **sizes,
-    )
-    extra = 3 * extent_x
-    z_b = exchange(jnp.concatenate(onward(value_s, packs_a, packs_b, 0, extra, B) + [late_b], axis=0), "gx", B)
-    z_a = exchange(jnp.concatenate(onward(value_s, packs_a, packs_b, 0, extra, A) + [late_a], axis=0), "gx", A)
+    z_b = exchange(jnp.concatenate(onward(value_s, packs_a, packs_b, 0, extra, B), axis=0), "gx", B)
+    z_a = exchange(jnp.concatenate(onward(value_s, packs_a, packs_b, 0, extra, A), axis=0), "gx", A)
     grad, returned, send_a, send_b, send_s, edge_a, edge_b = call(
-        middle_body, [order, asked], [early, pairs, x_a, x_b, y_a, y_b, tiles_s],
+        middle_body, [("s", [order, asked]), ("v", [early, pairs, x_a, x_b, y_a, y_b, tiles_s])],
         [whole, ((pair_total, planes, 128), f32, "v")] + [((extent_x + 2 * size, 128), f32, "v")] * 3 + [((size, 128), f32, "v")] * 2,
         alias={2: 0}, **sizes,
     )
     last_y_b = exchange(send_b, "gy", B)
     last_y_a = exchange(send_a, "gy", A)
+    (pushed,) = call(
+        push_body, [("v", [field, pad_rate, rate_y, edge_rate, rows_a, rows_b, wide_a, packs_a, packs_b])],
+        [whole], scratch=(pad_scratch,) * 2, **sizes,
+    )
+    last_y_a, last_y_b, pushed = lax.optimization_barrier((last_y_a, last_y_b, pushed))
     last_x_b = exchange(jnp.concatenate([edge_b] + onward(send_s, last_y_a, last_y_b, extent_x, extent_x, B), axis=0), "gx", B)
     last_x_a = exchange(jnp.concatenate([edge_a] + onward(send_s, last_y_a, last_y_b, extent_x, extent_x, A), axis=0), "gx", A)
-    (pushed,) = call(
-        push_body, [], [field, pad_rate, rate_y, edge_rate, z_a[2 * size :], z_b[2 * size :], packs, packs_a, packs_b],
-        [whole], scratch=(pad_scratch,) * 2, **sizes,
-    )
     (inner,) = call(
-        inner_body, [], [cotan, grad, pad_rate, rate_y], [whole], scratch=(pad_scratch,) * 3, **sizes,
+        inner_body, [("v", [cotan, grad, pad_rate, rate_y])], [whole], scratch=(pad_scratch,) * 3, **sizes,
     )
     section, first_outer = call(
-        section_body, [order, asked], [pushed, returned, z_a, z_b, packs_a, packs_b, value_s],
+        section_body, [("s", [order, asked]), ("v", [pushed, returned, z_a, z_b, packs_a, packs_b, value_s])],
         [whole, ((pair_total, 128, 128), f32, "v")], alias={2: 0}, **sizes,
     )
     grad_level_set, grad_blocks = call(
-        last_body, [order],
-        [inner, grad, pad_rate, edge_rate, packs, send_s, last_y_a, last_y_b, last_x_a, last_x_b, pairs, first_outer, picked],
+        last_body,
+        [("s", [order]), ("v", [inner, grad, pad_rate, edge_rate, wide_a, send_s, last_y_a, last_y_b, last_x_a, last_x_b, pairs, first_outer, picked])],
         [((cells, 128), f32, "h"), ((slots * TILE // 2, 128), f32, "h")],
         scratch=(pltpu.VMEM((pair_total, 128, 128), f32), pltpu.VMEM((cells, 128), f32)), **sizes,
     )

time: 66.5 us -> 52.5 us (0.79)
  Pallas kernels: 27.7 us -> 19.3 us
  local copies, waits for them, and re-layouts: 4.62 us -> 0.68 us
  waiting for transfers between devices: 10.8 us -> 9.83 us
    pallas_call x10 -> x9, Pallas kernels: 27.7 us -> 19.3 us  [call(): pl.pallas_call(functools.partial(body, **sizes), out_shape=tuple(shapes),...]
    unnamed x18 -> x2, local copies, waits for them, and re-layouts: 3.02 us -> 0.01 us
    ppermute x18 -> x16, waiting for transfers between devices: 10.8 us -> 9.83 us  [exchange(): return lax.ppermute(block, axis, matching(lax.axis_size(axis), which))]
    reshape x1, local copies, waits for them, and re-layouts: 1.56 us -> 0.64 us  [shards(): blocks.reshape(slots, TILE, TILE)]
    ppermute x18 -> x16, starting transfers between devices: 21.4 us -> 21 us  [exchange(): return lax.ppermute(block, axis, matching(lax.axis_size(axis), which))]
  transfers between devices with their start and end apart: 18 -> 16, of which waited for: 4 -> 6; matrix products, arithmetic and copies ran while one was open for 3% -> 1% of each run, Pallas kernels for 35% -> 29%
where the time goes in v3:
time: 52.5 us; the launch traced here: 52.4 us
  starting transfers between devices  21 us (40%)
  Pallas kernels  19.3 us (37%)
  waiting for transfers between devices  9.83 us (19%)
  between operations  1.52 us (3%)
  local copies, waits for them, and re-layouts  0.68 us (1%)
    ppermute x16, starting transfers between devices, exchange(): return lax.ppermute(block, axis, matching(lax.axis_size(axis), which))  21 us
    pallas_call x9, Pallas kernels, call(): pl.pallas_call(functools.partial(body, **sizes), out_shape=tuple(shapes),...  19.3 us
    ppermute x16, waiting for transfers between devices, exchange(): return lax.ppermute(block, axis, matching(lax.axis_size(axis), which))  9.83 us
  transfers between devices with their start and end apart: 16, of which 6 were waited for; matrix products, arithmetic and copies ran while one was open for 1% of the time, Pallas kernels for 29%

profile of v3, /device:TPU:0, one launch (start us, length us, event | category | flops | bytes accessed | tf_op | source)
XLA Modules:
  0.0 52.4 jit_solution(15855503115791783107)
XLA Ops:
  0.6 0.0 copy-start
  1.3 1.6 %begin_body.1 = (s32[3,36]{1,0:T(4,128)S(4)}, f32[152,128]{1,0:T(8,128)S(1)}, f32[152,128]{1,0:T(8,128)S(1)}, f32[1024,128]{1,0:T(8,128)S(1)}, f32[1024,128]{1,0...) custom-call(s32[1,1]{1,0:T(1,128)S(6)} %copy.17.count, s32[36]{0:T(128)} %bitcast.13, s32[36]{0:T(128)} %bitcast.14, ...), custom_call_target="tpu_custom_call" | custom-call | tf_op jit(solution)/shard_map/begin_body/pallas_call | solution.py:469
  3.0 3.0 %collective-permute-start.1 = (f32[152,128]{1,0:T(8,128)S(1)}, f32[152,128]{1,0:T(8,128)S(1)}, u32[]{:S(2)}, u32[]{:S(2)}) collective-permute-start(f32[152,128]{1,0:T(8,128)S(1)} %get-tuple-element.43), channel_id=1, source_target_pairs={{0,4},{4,0},{8,12},{12,8},{16,20},{20,16},{24,28},{28,24},{1,5},{5... | collective-permute-start | bytes 233480 | tf_op jit(solution)/shard_map/ppermute | solution.py:25
  6.0 3.5 %collective-permute-start = (f32[152,128]{1,0:T(8,128)S(1)}, f32[152,128]{1,0:T(8,128)S(1)}, u32[]{:S(2)}, u32[]{:S(2)}) collective-permute-start(f32[152,128]{1,0:T(8,128)S(1)} %get-tuple-element.42.request), channel_id=1, source_target_pairs={{0,28},{4,8},{8,4},{12,16},{16,12},{20,24},{24,20},{28,0},{1,29},{... | collective-permute-start | bytes 233480 | tf_op jit(solution)/shard_map/ppermute | solution.py:25
  9.5 0.0 copy-done
  9.5 0.6 %reshape.41.blocks = bf16[36,64,64]{2,1,0:T(8,128)(2,1)S(1)} reshape(bf16[1,1,36,4096]{3,2,1,0:T(8,128)(2,1)S(1)} %copy-done) | data formatting | bytes 589824 | tf_op jit(solution)/shard_map/reshape | solution.py:509
  10.2 0.8 %extend_body.1 = (bf16[18,128,128]{2,1,0:T(8,128)(2,1)S(1)}, f32[18,16,128]{2,1,0:T(8,128)S(1)}, f32[288,128]{1,0:T(8,128)S(1)}, f32[288,128]{1,0:T(8,128)S(1)}, f32[96,128]{1,0:T(8,128)S(1)}) custom-call(s32[3,36]{1,0:T(4,128)S(4)} %get-tuple-element.40.order, f32[1024,128]{1,0:T(8,128)S(1)} %get-tuple-element.44.field, ...), custom_call_target="tpu_custom_call" | custom-call | tf_op jit(solution)/shard_map/extend_body/pallas_call | solution.py:469
  11.0 0.0 collective-permute-done.1.got_b.rows_b
  11.0 2.1 %collective-permute-done.got_a.rows_a = f32[152,128]{1,0:T(8,128)S(1)} collective-permute-done((f32[152,128]{1,0:T(8,128)S(1)}, f32[152,128]{1,0:T(8,128)S(1)}, u32[]{:S(2)}, u32[]{:S(2)}) %collective-permute-start) | collective-permute-done | bytes 77856 | tf_op jit(solution)/shard_map/ppermute | solution.py:25
  13.1 0.0 collective-permute-start.3
  13.1 1.6 %collective-permute-start.2 = (f32[24,128]{1,0:T(8,128)S(1)}, f32[24,128]{1,0:T(8,128)S(1)}, u32[]{:S(2)}, u32[]{:S(2)}) collective-permute-start(f32[24,128]{1,0:T(8,128)S(1)} %pad_maximum_fusion.6), channel_id=1, source_target_pairs={{0,3},{1,2},{2,1},{3,0},{4,7},{5,6},{6,5},{7,4},{8,11},{9,10},{10,... | collective-permute-start | bytes 36872 | tf_op jit(solution)/shard_map/ppermute | solution.py:25
  14.7 0.1 collective-permute-start.7
  14.8 0.6 %collective-permute-start.6 = (f32[288,128]{1,0:T(8,128)S(1)}, f32[288,128]{1,0:T(8,128)S(1)}, u32[]{:S(2)}, u32[]{:S(2)}) collective-permute-start(f32[288,128]{1,0:T(8,128)S(1)} %get-tuple-element.53.packs), channel_id=1, source_target_pairs={{0,3},{1,2},{2,1},{3,0},{4,7},{5,6},{6,5},{7,4},{8,11},{9,10},{10,... | collective-permute-start | bytes 442376 | tf_op jit(solution)/shard_map/ppermute | solution.py:25
  15.3 0.0 collective-permute-done.3.from_b
  15.4 0.9 %collective-permute-done.2.from_a = f32[24,128]{1,0:T(8,128)S(1)} collective-permute-done((f32[24,128]{1,0:T(8,128)S(1)}, f32[24,128]{1,0:T(8,128)S(1)}, u32[]{:S(2)}, u32[]{:S(2)}) %collective-permute-start.2) | collective-permute-done | bytes 12320 | tf_op jit(solution)/shard_map/ppermute | solution.py:25
  16.3 1.0 %serve_body.1 = (s32[8,128]{1,0:T(8,128)S(4)}, f32[96,128]{1,0:T(8,128)S(1)}, f32[96,128]{1,0:T(8,128)S(1)}, f32[96,128]{1,0:T(8,128)S(1)}) custom-call(f32[152,128]{1,0:T(8,128)S(1)} %get-tuple-element.42.request, f32[152,128]{1,0:T(8,128)S(1)} %collective-permute-done.got_a.rows_a, f32[152,128]{1,0:T(8,128)S(1)} %collective-permute-done.1.got_b.rows_b, ...), custom_call_target="tpu_custom_call" | custom-call | tf_op jit(solution)/shard_map/serve_body/pallas_call | solution.py:469
  17.3 2.0 %collective-permute-start.4 = (f32[96,128]{1,0:T(8,128)S(1)}, f32[96,128]{1,0:T(8,128)S(1)}, u32[]{:S(2)}, u32[]{:S(2)}) collective-permute-start(f32[96,128]{1,0:T(8,128)S(1)} %get-tuple-element.50), channel_id=1, source_target_pairs={{0,3},{1,2},{2,1},{3,0},{4,7},{5,6},{6,5},{7,4},{8,11},{9,10},{10,... | collective-permute-start | bytes 147464 | tf_op jit(solution)/shard_map/ppermute | solution.py:25
  19.3 0.0 collective-permute-start.5
  19.3 0.0 collective-permute-done.7.packs_b.y_b
  19.3 1.0 %collective-permute-done.6.packs_a.y_a = f32[288,128]{1,0:T(8,128)S(1)} collective-permute-done((f32[288,128]{1,0:T(8,128)S(1)}, f32[288,128]{1,0:T(8,128)S(1)}, u32[]{:S(2)}, u32[]{:S(2)}) %collective-permute-start.6) | collective-permute-done | bytes 147488 | tf_op jit(solution)/shard_map/ppermute | solution.py:25
  20.3 4.3 %pull_body.1 = (f32[1024,128]{1,0:T(8,128)S(1)}, f32[1288,128]{1,0:T(8,128)S(1)}, f32[64,128]{1,0:T(8,128)S(1)}) custom-call(f32[1024,128]{1,0:T(8,128)S(1)} %get-tuple-element.41.cotan, f32[1024,128]{1,0:T(8,128)S(1)} %get-tuple-element.52.rate_x, f32[1024,128]{1,0:T(8,128)S(1)} %get-tuple-element.45.rate_y, ...), custom_call_target="tpu_custom_call" | custom-call | tf_op jit(solution)/shard_map/pull_body/pallas_call | solution.py:469
  24.7 0.0 collective-permute-done.4.y_a
  24.7 0.0 collective-permute-done.5.y_b
  24.7 3.6 %collective-permute-start.8 = (f32[96,128]{1,0:T(8,128)S(1)}, f32[96,128]{1,0:T(8,128)S(1)}, u32[]{:S(2)}, u32[]{:S(2)}) collective-permute-start(f32[96,128]{1,0:T(8,128)S(1)} %pad_maximum_fusion.2), channel_id=1, source_target_pairs={{0,28},{4,8},{8,4},{12,16},{16,12},{20,24},{24,20},{28,0},{1,29},{... | collective-permute-start | bytes 147464 | tf_op jit(solution)/shard_map/ppermute | solution.py:25
  28.4 0.0 collective-permute-start.9
  28.4 1.2 %collective-permute-start.14 = (f32[96,128]{1,0:T(8,128)S(1)}, f32[96,128]{1,0:T(8,128)S(1)}, u32[]{:S(2)}, u32[]{:S(2)}) collective-permute-start(f32[96,128]{1,0:T(8,128)S(1)} %pad_maximum_fusion.4), channel_id=1, source_target_pairs={{0,28},{4,8},{8,4},{12,16},{16,12},{20,24},{24,20},{28,0},{1,29},{... | collective-permute-start | bytes 147464 | tf_op jit(solution)/shard_map/ppermute | solution.py:25
  29.6 3.0 %push_body.1.early = f32[1024,128]{1,0:T(8,128)S(1)} custom-call(f32[1024,128]{1,0:T(8,128)S(1)} %get-tuple-element.44.field, f32[1288,128]{1,0:T(8,128)S(1)} %get-tuple-element.62.pad_rate, f32[1024,128]{1,0:T(8,128)S(1)} %get-tuple-element.45.rate_y, f32[64,128]{1,0:T(8,128)S(1)} %get-tuple-element.63.edge_rate, ...), custom_call_target="tpu_custom_call" | custom-call | tf_op jit(solution)/shard_map/push_body/pallas_call | solution.py:469
  32.7 0.0 collective-permute-done.8.x_a
  32.7 0.5 collective-permute-done.9.x_b
  33.2 1.3 %middle_body.1 = (f32[1024,128]{1,0:T(8,128)S(1)}, f32[18,16,128]{2,1,0:T(8,128)S(1)}, f32[160,128]{1,0:T(8,128)S(1)}, f32[160,128]{1,0:T(8,128)S(1)}, f32[160,1...) custom-call(s32[3,36]{1,0:T(4,128)S(4)} %get-tuple-element.40.order, ...), custom_call_target="tpu_custom_call", output_to_operand_aliasing={{0}: (2, {})} | custom-call | tf_op jit(solution)/shard_map/middle_body/pallas_call | solution.py:469
  34.5 0.1 collective-permute-start.10
  34.6 0.4 collective-permute-start.11
  34.9 4.1 %collective-permute-done.10.y_a = f32[160,128]{1,0:T(8,128)S(1)} collective-permute-done((f32[160,128]{1,0:T(8,128)S(1)}, f32[160,128]{1,0:T(8,128)S(1)}, u32[]{:S(2)}, u32[]{:S(2)}) %collective-permute-start.10) | collective-permute-done | bytes 81952 | tf_op jit(solution)/shard_map/ppermute | solution.py:25
  39.0 0.0 collective-permute-done.11.y_b
  39.1 2.9 %collective-permute-start.12 = (f32[144,128]{1,0:T(8,128)S(1)}, f32[144,128]{1,0:T(8,128)S(1)}, u32[]{:S(2)}, u32[]{:S(2)}) collective-permute-start(f32[144,128]{1,0:T(8,128)S(1)} %pad_maximum_fusion), channel_id=1, source_target_pairs={{0,28},{4,8},{8,4},{12,16},{16,12},{20,24},{24,20},{28,0},{1,29},{... | collective-permute-start | bytes 221192 | tf_op jit(solution)/shard_map/ppermute | solution.py:25
  41.9 0.4 collective-permute-start.13
  42.4 1.6 %collective-permute-start.15 = (f32[96,128]{1,0:T(8,128)S(1)}, f32[96,128]{1,0:T(8,128)S(1)}, u32[]{:S(2)}, u32[]{:S(2)}) collective-permute-start(f32[96,128]{1,0:T(8,128)S(1)} %pad_maximum_fusion.5), channel_id=1, source_target_pairs={{0,4},{4,0},{8,12},{12,8},{16,20},{20,16},{24,28},{28,24},{1,5},{5... | collective-permute-start | bytes 147464 | tf_op jit(solution)/shard_map/ppermute | solution.py:25
  44.0 3.5 %inner_body.1.early = f32[1024,128]{1,0:T(8,128)S(1)} custom-call(f32[1024,128]{1,0:T(8,128)S(1)} %get-tuple-element.41.cotan, f32[1024,128]{1,0:T(8,128)S(1)} %get-tuple-element.61.grad, f32[1288,128]{1,0:T(8,128)S(1)} %get-tuple-element.62.pad_rate, f32[1024,128]{1,0:T(8,128)S(1)} %get-tuple-element.45.rate_y), custom_call_target="tpu_custom_call" | custom-call | tf_op jit(solution)/shard_map/inner_body/pallas_call | solution.py:469
  47.5 0.0 collective-permute-done.14.x_a
  47.5 1.2 %collective-permute-done.15.x_b = f32[96,128]{1,0:T(8,128)S(1)} collective-permute-done((f32[96,128]{1,0:T(8,128)S(1)}, f32[96,128]{1,0:T(8,128)S(1)}, u32[]{:S(2)}, u32[]{:S(2)}) %collective-permute-start.15) | collective-permute-done | bytes 49184 | tf_op jit(solution)/shard_map/ppermute | solution.py:25
  48.7 1.3 %section_body.1 = (f32[1024,128]{1,0:T(8,128)S(1)}, f32[18,128,128]{2,1,0:T(8,128)S(1)}) custom-call(s32[3,36]{1,0:T(4,128)S(4)} %get-tuple-element.40.order, s32[8,128]{1,0:T(8,128)S(4)} %get-tuple-element.49.asked, f32[1024,128]{1,0:T(8,128)S(1)} %push_body.1.early, ...), custom_call_target="tpu_custom_call", output_to_operand_aliasing={{0}: (2, {})} | custom-call | tf_op jit(solution)/shard_map/section_body/pallas_call | solution.py:469
  50.0 0.0 collective-permute-done.12.x_a
  50.0 0.0 collective-permute-done.13.x_b
  50.0 2.3 %last_body.1 = (f32[1024,128]{1,0:T(8,128)}, f32[1152,128]{1,0:T(8,128)}) custom-call(s32[3,36]{1,0:T(4,128)S(4)} %get-tuple-element.40.order, f32[1024,128]{1,0:T(8,128)S(1)} %inner_body.1.early, f32[1024,128]{1,0:T(8,128)S(1)} %get-tuple-element.61.grad, f32[1288,128]{1,0:T(8,128)S(1)} %get-tuple-element.62.pad_rate, ...), custom_call_target="tpu_custom_call" | custom-call | tf_op jit(solution)/shard_map/last_body/pallas_call | solution.py:469
  (18 shorter events, 0.1 us)
Async XLA Ops:
  0.6 8.9 %copy-start = (bf16[1,1,36,4096]{3,2,1,0:T(8,128)(2,1)S(1)}, bf16[1,1,36,4096]{3,2,1,0:T(8,128)(2,1)}, u32[]{:S(2)}) copy-start(bf16[1,1,36,4096]{3,2,1,0:T(8,128)(2,1)} %param.13) | copy-start | bytes 884740
  3.0 8.0 %collective-permute-start.1 = (f32[152,128]{1,0:T(8,128)S(1)}, f32[152,128]{1,0:T(8,128)S(1)}, u32[]{:S(2)}, u32[]{:S(2)}) collective-permute-start(f32[152,128]{1,0:T(8,128)S(1)} %get-tuple-element.43), channel_id=1, source_target_pairs={{0,4},{4,0},{8,12},{12,8},{16,20},{20,16},{24,28},{28,24},{1,5},{5... | collective-permute-start | bytes 233480 | tf_op jit(solution)/shard_map/ppermute | solution.py:25
  6.0 7.1 %collective-permute-start = (f32[152,128]{1,0:T(8,128)S(1)}, f32[152,128]{1,0:T(8,128)S(1)}, u32[]{:S(2)}, u32[]{:S(2)}) collective-permute-start(f32[152,128]{1,0:T(8,128)S(1)} %get-tuple-element.42.request), channel_id=1, source_target_pairs={{0,28},{4,8},{8,4},{12,16},{16,12},{20,24},{24,20},{28,0},{1,29},{... | collective-permute-start | bytes 233480 | tf_op jit(solution)/shard_map/ppermute | solution.py:25
  13.1 2.3 %collective-permute-start.3 = (f32[24,128]{1,0:T(8,128)S(1)}, f32[24,128]{1,0:T(8,128)S(1)}, u32[]{:S(2)}, u32[]{:S(2)}) collective-permute-start(f32[24,128]{1,0:T(8,128)S(1)} %pad_maximum_fusion.6), channel_id=1, source_target_pairs={{0,1},{1,0},{2,3},{3,2},{4,5},{5,4},{6,7},{7,6},{8,9},{9,8},{10,11... | collective-permute-start | bytes 36872 | tf_op jit(solution)/shard_map/ppermute | solution.py:25
  13.1 3.2 %collective-permute-start.2 = (f32[24,128]{1,0:T(8,128)S(1)}, f32[24,128]{1,0:T(8,128)S(1)}, u32[]{:S(2)}, u32[]{:S(2)}) collective-permute-start(f32[24,128]{1,0:T(8,128)S(1)} %pad_maximum_fusion.6), channel_id=1, source_target_pairs={{0,3},{1,2},{2,1},{3,0},{4,7},{5,6},{6,5},{7,4},{8,11},{9,10},{10,... | collective-permute-start | bytes 36872 | tf_op jit(solution)/shard_map/ppermute | solution.py:25
  14.7 4.6 %collective-permute-start.7 = (f32[288,128]{1,0:T(8,128)S(1)}, f32[288,128]{1,0:T(8,128)S(1)}, u32[]{:S(2)}, u32[]{:S(2)}) collective-permute-start(f32[288,128]{1,0:T(8,128)S(1)} %get-tuple-element.54), channel_id=1, source_target_pairs={{0,1},{1,0},{2,3},{3,2},{4,5},{5,4},{6,7},{7,6},{8,9},{9,8},{10,11... | collective-permute-start | bytes 442376 | tf_op jit(solution)/shard_map/ppermute | solution.py:25
  14.8 5.6 %collective-permute-start.6 = (f32[288,128]{1,0:T(8,128)S(1)}, f32[288,128]{1,0:T(8,128)S(1)}, u32[]{:S(2)}, u32[]{:S(2)}) collective-permute-start(f32[288,128]{1,0:T(8,128)S(1)} %get-tuple-element.53.packs), channel_id=1, source_target_pairs={{0,3},{1,2},{2,1},{3,0},{4,7},{5,6},{6,5},{7,4},{8,11},{9,10},{10,... | collective-permute-start | bytes 442376 | tf_op jit(solution)/shard_map/ppermute | solution.py:25
  17.3 7.4 %collective-permute-start.4 = (f32[96,128]{1,0:T(8,128)S(1)}, f32[96,128]{1,0:T(8,128)S(1)}, u32[]{:S(2)}, u32[]{:S(2)}) collective-permute-start(f32[96,128]{1,0:T(8,128)S(1)} %get-tuple-element.50), channel_id=1, source_target_pairs={{0,3},{1,2},{2,1},{3,0},{4,7},{5,6},{6,5},{7,4},{8,11},{9,10},{10,... | collective-permute-start | bytes 147464 | tf_op jit(solution)/shard_map/ppermute | solution.py:25
  19.3 5.4 %collective-permute-start.5 = (f32[96,128]{1,0:T(8,128)S(1)}, f32[96,128]{1,0:T(8,128)S(1)}, u32[]{:S(2)}, u32[]{:S(2)}) collective-permute-start(f32[96,128]{1,0:T(8,128)S(1)} %get-tuple-element.51), channel_id=1, source_target_pairs={{0,1},{1,0},{2,3},{3,2},{4,5},{5,4},{6,7},{7,6},{8,9},{9,8},{10,11... | collective-permute-start | bytes 147464 | tf_op jit(solution)/shard_map/ppermute | solution.py:25
  24.7 8.0 %collective-permute-start.8 = (f32[96,128]{1,0:T(8,128)S(1)}, f32[96,128]{1,0:T(8,128)S(1)}, u32[]{:S(2)}, u32[]{:S(2)}) collective-permute-start(f32[96,128]{1,0:T(8,128)S(1)} %pad_maximum_fusion.2), channel_id=1, source_target_pairs={{0,28},{4,8},{8,4},{12,16},{16,12},{20,24},{24,20},{28,0},{1,29},{... | collective-permute-start | bytes 147464 | tf_op jit(solution)/shard_map/ppermute | solution.py:25
  28.4 4.8 %collective-permute-start.9 = (f32[96,128]{1,0:T(8,128)S(1)}, f32[96,128]{1,0:T(8,128)S(1)}, u32[]{:S(2)}, u32[]{:S(2)}) collective-permute-start(f32[96,128]{1,0:T(8,128)S(1)} %pad_maximum_fusion.3), channel_id=1, source_target_pairs={{0,4},{4,0},{8,12},{12,8},{16,20},{20,16},{24,28},{28,24},{1,5},{5... | collective-permute-start | bytes 147464 | tf_op jit(solution)/shard_map/ppermute | solution.py:25
  28.4 19.1 %collective-permute-start.14 = (f32[96,128]{1,0:T(8,128)S(1)}, f32[96,128]{1,0:T(8,128)S(1)}, u32[]{:S(2)}, u32[]{:S(2)}) collective-permute-start(f32[96,128]{1,0:T(8,128)S(1)} %pad_maximum_fusion.4), channel_id=1, source_target_pairs={{0,28},{4,8},{8,4},{12,16},{16,12},{20,24},{24,20},{28,0},{1,29},{... | collective-permute-start | bytes 147464 | tf_op jit(solution)/shard_map/ppermute | solution.py:25
  34.5 4.5 %collective-permute-start.10 = (f32[160,128]{1,0:T(8,128)S(1)}, f32[160,128]{1,0:T(8,128)S(1)}, u32[]{:S(2)}, u32[]{:S(2)}) collective-permute-start(f32[160,128]{1,0:T(8,128)S(1)} %get-tuple-element.65), channel_id=1, source_target_pairs={{0,3},{1,2},{2,1},{3,0},{4,7},{5,6},{6,5},{7,4},{8,11},{9,10},{10,... | collective-permute-start | bytes 245768 | tf_op jit(solution)/shard_map/ppermute | solution.py:25
  34.6 4.5 %collective-permute-start.11 = (f32[160,128]{1,0:T(8,128)S(1)}, f32[160,128]{1,0:T(8,128)S(1)}, u32[]{:S(2)}, u32[]{:S(2)}) collective-permute-start(f32[160,128]{1,0:T(8,128)S(1)} %get-tuple-element.66), channel_id=1, source_target_pairs={{0,1},{1,0},{2,3},{3,2},{4,5},{5,4},{6,7},{7,6},{8,9},{9,8},{10,11... | collective-permute-start | bytes 245768 | tf_op jit(solution)/shard_map/ppermute | solution.py:25
  39.1 11.0 %collective-permute-start.12 = (f32[144,128]{1,0:T(8,128)S(1)}, f32[144,128]{1,0:T(8,128)S(1)}, u32[]{:S(2)}, u32[]{:S(2)}) collective-permute-start(f32[144,128]{1,0:T(8,128)S(1)} %pad_maximum_fusion), channel_id=1, source_target_pairs={{0,28},{4,8},{8,4},{12,16},{16,12},{20,24},{24,20},{28,0},{1,29},{... | collective-permute-start | bytes 221192 | tf_op jit(solution)/shard_map/ppermute | solution.py:25
  41.9 8.1 %collective-permute-start.13 = (f32[144,128]{1,0:T(8,128)S(1)}, f32[144,128]{1,0:T(8,128)S(1)}, u32[]{:S(2)}, u32[]{:S(2)}) collective-permute-start(f32[144,128]{1,0:T(8,128)S(1)} %pad_maximum_fusion.1), channel_id=1, source_target_pairs={{0,4},{4,0},{8,12},{12,8},{16,20},{20,16},{24,28},{28,24},{1,5},{5... | collective-permute-start | bytes 221192 | tf_op jit(solution)/shard_map/ppermute | solution.py:25
  42.4 6.4 %collective-permute-start.15 = (f32[96,128]{1,0:T(8,128)S(1)}, f32[96,128]{1,0:T(8,128)S(1)}, u32[]{:S(2)}, u32[]{:S(2)}) collective-permute-start(f32[96,128]{1,0:T(8,128)S(1)} %pad_maximum_fusion.5), channel_id=1, source_target_pairs={{0,4},{4,0},{8,12},{12,8},{16,20},{20,16},{24,28},{28,24},{1,5},{5... | collective-permute-start | bytes 147464 | tf_op jit(solution)/shard_map/ppermute | solution.py:25

commit v4 on v3

--- a/solution.py
+++ b/solution.py
@@ -140,7 +140,7 @@
     return jnp.where(lane < 3, high_side, jnp.where(lane < 6, low_side, 0.0))
 
 
-def adjoint_plane(z, pad_ref, pad_rate_ref, rate_y_ref, up_ref, down_ref, extent_x):
+def adjoint_x(z, pad_ref, pad_rate_ref, up_ref, down_ref, extent_x):
     base = z * PAD
     here = pad_ref[pl.ds(base, PAD), :]
     jump = pad_ref[pl.ds(base + 1, PAD), :] - here
@@ -153,19 +153,34 @@
             total = total + UP[k] * up_ref[pl.ds(base + 8 + k, extent_x), :]
         if k in DOWN:
             total = total + DOWN[k] * down_ref[pl.ds(base + 8 + k, extent_x), :]
-    field = pad_ref[pl.ds(base + 8, extent_x), :]
-    lane = lanes(field.shape)
-    jump = jnp.where(lane == 127, 0.0, roll(field, -1) - field)
-    rate_up, rate_down = upwind(rate_y_ref[pl.ds(z * extent_x, extent_x), :])
-    up_part, down_part = rate_up * jump, rate_down * jump
-    ahead = combine(up_part, down_part, 2)
-    for k in (1, 0):
-        ahead = jnp.where(lane == 127, 0.0, roll(ahead, -1)) + combine(up_part, down_part, k)
-    behind = combine(up_part, down_part, -3)
-    for k in (-2, -1):
-        behind = jnp.where(lane == 0, 0.0, roll(behind, 1)) + combine(up_part, down_part, k)
-    behind = jnp.where(lane == 0, 0.0, roll(behind, 1))
-    return total + ahead + behind
+    return total
+
+
+def band(weights, first_lost):
+    row = lax.broadcasted_iota(jnp.int32, (128, 128), 0)
+    gap = row - lax.broadcasted_iota(jnp.int32, (128, 128), 1)
+    matrix = jnp.zeros((128, 128), jnp.float32)
+    for k, weight in weights.items():
+        matrix = jnp.where(gap == k, float(round(60.0 * weight)), matrix)
+    return jnp.where(row >= first_lost, 0.0, matrix).astype(jnp.bfloat16)
+
+
+def mix(left, matrix):
+    return lax.dot_general(left, matrix, (((1,), (0,)), ((), ())), preferred_element_type=jnp.float32)
+
+
+def adjoint_y(field_ref, rate_y_ref, planes, extent_x):
+    up_matrix, down_matrix = band(UP, 127), band(DOWN, 127)
+    matrix = jnp.concatenate([up_matrix, up_matrix, down_matrix, down_matrix], axis=0)
+    rows = 4 * extent_x
+    results = []
+    for chunk in range(planes // 4):
+        field = field_ref[chunk * rows : (chunk + 1) * rows, :]
+        jump = roll(field, -1) - field
+        rate_up, rate_down = upwind(rate_y_ref[chunk * rows : (chunk + 1) * rows, :])
+        left = jnp.concatenate(split(rate_up * jump) + split(rate_down * jump), axis=1)
+        results.append(mix(left, matrix))
+    return results
 
 
 def parities():
@@ -200,7 +215,7 @@
     lane = lanes((8, 128))
     for copy in copies[:3]:
         copy.wait()
-    total = count[0, 0]
+    total = jnp.max(count[...]).astype(jnp.int32)
     asked = jnp.zeros((8, 128), jnp.int32)
     for slot in range(heading.shape[0]):
         toward = heading_in[slot]
@@ -290,24 +305,30 @@
 LABELS = [(lx, ly, half) for ly in range(3) for lx in range(3) for half in range(2)]
 
 
-def pull_body(cotan, rate_x, rate_y, rows_a, rows_b, packs, packs_a, packs_b, grad, pad_rate, edge_rate, pad, up_ref, down_ref, *, planes, extent_x):
-    parity_x, parity_y = parities()
-    even_x, even_y = parity_x == 0, parity_y == 0
-    size = 3 * planes
-    fill_padded(pad, cotan, rows_a[8 : 8 + size], rows_b[8 : 8 + size], even_x, planes, extent_x)
-    fill_padded(pad_rate, rate_x, rows_a[8 + size : 8 + 2 * size], rows_b[8 + size : 8 + 2 * size], even_x, planes, extent_x)
+def pull_y_body(cotan, rate_y, packs, packs_a, packs_b, grad, edge_rate, *, planes, extent_x):
+    even_y = parities()[1] == 0
     halo = edge_join(part(packs_a, 0, extent_x), part(packs_b, 0, extent_x), even_y)
     halo_rate = edge_join(part(packs_a, 1, extent_x), part(packs_b, 1, extent_x), even_y)
     edge_rate[...] = halo_rate
     edges = adjoint_edges(part(packs, 0, extent_x), halo, part(packs, 1, extent_x), halo_rate)
-
+    pulled = adjoint_y(cotan, rate_y, planes, extent_x)
     for z in range(planes):
         spot = pl.ds(z * extent_x, extent_x)
-        pulled = adjoint_plane(z, pad, pad_rate, rate_y, up_ref, down_ref, extent_x)
         rim = roll(edges, 125 - 8 * z)
         lane = lanes(rim.shape)
-        pulled = pulled + jnp.where((lane < 3) | (lane >= 125), rim, 0.0)
-        grad[spot, :] = 0.5 * cotan[spot, :] + (0.5 * TIME_STEP) * pulled
+        rim = jnp.where((lane < 3) | (lane >= 125), rim, 0.0)
+        main = pulled[z // 4][z % 4 * extent_x : (z % 4 + 1) * extent_x]
+        grad[spot, :] = 0.5 * cotan[spot, :] + (0.5 * TIME_STEP) * (main * (1.0 / 60.0) + rim)
+
+
+def pull_x_body(early, cotan, rate_x, rows_a, rows_b, grad, pad_rate, pad, up_ref, down_ref, *, planes, extent_x):
+    even_x = parities()[0] == 0
+    size = 3 * planes
+    fill_padded(pad, cotan, rows_a[8 : 8 + size], rows_b[8 : 8 + size], even_x, planes, extent_x)
+    fill_padded(pad_rate, rate_x, rows_a[8 + size : 8 + 2 * size], rows_b[8 + size : 8 + 2 * size], even_x, planes, extent_x)
+    for z in range(planes):
+        spot = pl.ds(z * extent_x, extent_x)
+        grad[spot, :] = early[spot, :] + (0.5 * TIME_STEP) * adjoint_x(z, pad, pad_rate, up_ref, down_ref, extent_x)
 
 
 def push_body(field, pad_rate, rate_y, edge_rate, rows_a, rows_b, packs, packs_a, packs_b, section, pad, flux_ref, *, planes, extent_x):
@@ -316,13 +337,37 @@
     first = 8 + 6 * planes
     fill_padded(pad, field, rows_a[first : first + 3 * planes], rows_b[first : first + 3 * planes], even_x, planes, extent_x)
     halo = edge_join(part(packs_a, 2, extent_x), part(packs_b, 2, extent_x), even_y)
-    line = jnp.where(lanes(halo.shape) % 8 < 3, halo, part(packs, 2, extent_x))
-    moved = {k: roll(line, -k) for k in range(-2, 4)}
+    own_rate = part(packs, 1, extent_x)
+    lane8 = lanes(halo.shape) % 8
+
+    def shifted_by(value, k):
+        return roll(value, -k) if k else value
+
+    def stencils(value):
+        up_part = sum(WEIGHTS[j] * shifted_by(value, j - 2) for j in range(5))
+        down_part = sum(WEIGHTS[j] * shifted_by(value, 3 - j) for j in range(5))
+        return up_part, down_part
+
+    up_part, down_part = stencils(jnp.where(lane8 < 3, halo, jnp.where(lane8 < 6, part(packs, 2, extent_x), 0.0)))
     rate_up, rate_down = upwind(edge_rate[...])
-    flux_low = rate_up * sum(WEIGHTS[j] * moved[j - 2] for j in range(5)) + rate_down * sum(
-        WEIGHTS[j] * moved[3 - j] for j in range(5)
-    )
-
+    flux_low = roll(rate_up * up_part + rate_down * down_part, 1)
+    rate_up, rate_down = upwind(own_rate)
+    up_part, down_part = stencils(jnp.where((lane8 >= 3) & (lane8 < 6), halo, 0.0))
+    flux_high = jnp.where(lane8 < 3, rate_up * up_part + rate_down * down_part, 0.0)
+    up_part, down_part = stencils(jnp.where(lane8 < 3, halo, 0.0))
+    flux_first = jnp.where((lane8 >= 3) & (lane8 < 5), rate_up * up_part + rate_down * down_part, 0.0)
+    change_edge = roll(flux_high, 1) - flux_high
+    before = jnp.where(lane8 == 3, flux_low, roll(flux_first, 1))
+    change_edge = jnp.where(lane8 < 3, change_edge, jnp.where(lane8 < 6, before - flux_first, 0.0))
+    both = jnp.concatenate([band({k: WEIGHTS[k + 2] for k in range(-2, 3)}, 128), band({k: WEIGHTS[3 - k] for k in range(-1, 4)}, 128)], axis=1)
+    both = jnp.concatenate([both, both], axis=0)
+    chunk_rows = 4 * extent_x
+    fluxes = []
+    for chunk in range(planes // 4):
+        rows = slice(chunk * chunk_rows, (chunk + 1) * chunk_rows)
+        parts = mix(jnp.concatenate(split(field[rows, :]), axis=1), both) * (1.0 / 60.0)
+        rate_up, rate_down = upwind(rate_y[rows, :])
+        fluxes.append(rate_up * parts[:, :128] + rate_down * parts[:, 128:])
     for z in range(planes):
         base = z * PAD
         spot = pl.ds(z * extent_x, extent_x)
@@ -333,21 +378,12 @@
             WEIGHTS[j] * near[3 - j] for j in range(5)
         )
         change = flux_ref[pl.ds(base, extent_x), :] - flux_ref[pl.ds(base + 1, extent_x), :]
-        here = field[spot, :]
-        lane = lanes(here.shape)
-        turn = 125 - 8 * z
-        rim = roll(halo, turn)
-        near = {0: here}
-        for k in (1, 2, 3):
-            near[k] = roll(jnp.where(lane < k, rim, here), -k)
-        for k in (1, 2):
-            near[-k] = roll(jnp.where(lane >= 128 - k, rim, here), k)
-        rate_up, rate_down = upwind(rate_y[spot, :])
-        flux = rate_up * sum(WEIGHTS[j] * near[j - 2] for j in range(5)) + rate_down * sum(
-            WEIGHTS[j] * near[3 - j] for j in range(5)
-        )
-        change = change + roll(jnp.where(lane == 127, roll(flux_low, turn), flux), 1) - flux
-        section[spot, :] = here + TIME_STEP * change
+        flux = fluxes[z // 4][z % 4 * extent_x : (z % 4 + 1) * extent_x]
+        lane = lanes(flux.shape)
+        rim = roll(change_edge, 125 - 8 * z)
+        rim = jnp.where((lane < 3) | (lane >= 125), rim, 0.0)
+        change = change + jnp.where(lane == 0, 0.0, roll(flux, 1)) - flux + rim
+        section[spot, :] = field[spot, :] + TIME_STEP * change
 
 
 def middle_body(order, asked, early, pairs, x_a, x_b, y_a, y_b, own, grad, returned, send_a, send_b, send_s, rows_a, rows_b, *, planes, extent_x):
@@ -374,9 +410,11 @@
         pad[pl.ds(5 + j, planes, PAD), :] = row_of(grad, 0, planes, extent_x)
         pad[pl.ds(high + j, planes, PAD), :] = row_of(grad, extent_x - 1, planes, extent_x)
 
+    along_y = adjoint_y(grad, rate_y, planes, extent_x)
     for z in range(planes):
         spot = pl.ds(z * extent_x, extent_x)
-        pulled = adjoint_plane(z, pad, pad_rate, rate_y, up_ref, down_ref, extent_x)
+        pulled = along_y[z // 4][z % 4 * extent_x : (z % 4 + 1) * extent_x] * (1.0 / 60.0)
+        pulled = pulled + adjoint_x(z, pad, pad_rate, up_ref, down_ref, extent_x)
         out[spot, :] = 0.5 * cotan[spot, :] + grad[spot, :] + TIME_STEP * pulled
 
 
@@ -393,7 +431,7 @@
 
 def section_body(order, asked, early, returned, x_a, x_b, y_a, y_b, own, section, first_outer, *, planes, extent_x):
     for number, (lx, ly, half) in enumerate(LABELS):
-        came = TIME_STEP * landed(lx, ly, half, planes, 0, 3 * extent_x, x_a, x_b, y_a, y_b, own)
+        came = TIME_STEP * landed(lx, ly, half, planes, 6 * planes, 3 * extent_x, x_a, x_b, y_a, y_b, own)
         at = ly * 12 + lx * ROUTE_MOST + 2 * half
         add_tile_pair(section, asked[ly, at], asked[ly, at + 1], came, planes, extent_x)
 
@@ -403,7 +441,7 @@
 
 
 def last_body(
-    order, early, grad, pad_rate, edge_rate, packs, own, y_a, y_b, x_a, x_b, pairs, first_outer, picked, out, out_blocks, work, total,
+    order, early, grad, pad_rate, edge_rate, packs, own, y_a, y_b, x_a, x_b, pairs, first_outer, picked, out, out_blocks, work, total, blocks, sems,
     *, planes, extent_x,
 ):
     parity_x, parity_y = parities()
@@ -436,11 +474,16 @@
                     added = added + combine(*faces[j], k)
             spot = pl.ds(cell, planes, extent_x)
             total[spot, :] = total[spot, :] + TIME_STEP * added
-    half_lane = lanes((TILE // 2, 128)) < TILE
+    backs = []
     for number, label in enumerate(LABELS):
         back = alive_lanes(landed(*label, planes, size, extent_x, x_a, x_b, y_a, y_b, own), order, number)
+        backs.append(back)
         pulled = TIME_STEP * pair_dot(back, pairs[number], 0)
         add_tile_pair(total, order[1, 2 * number], order[1, 2 * number + 1], pulled, planes, extent_x)
+    copies = [pltpu.make_async_copy(total, out, sems.at[0]), pltpu.make_async_copy(blocks, out_blocks, sems.at[1])]
+    copies[0].start()
+    half_lane = lanes((TILE // 2, 128)) < TILE
+    for number, back in enumerate(backs):
         work[number] = first_outer[number] + outer(TIME_STEP * back, picked[number])
         for which in range(2):
             slot = order[0, 2 * number + which]
@@ -450,8 +493,10 @@
                 merged = jnp.where(half_lane, even_rows, roll(odd_rows, TILE))
             else:
                 merged = jnp.where(half_lane, roll(even_rows, TILE), odd_rows)
-            out_blocks[pl.ds(pl.multiple_of(slot * (TILE // 2), 8), TILE // 2), :] = merged
-    out[...] = total[...]
+            blocks[pl.ds(pl.multiple_of(slot * (TILE // 2), 8), TILE // 2), :] = merged
+    copies[1].start()
+    for copy in copies:
+        copy.wait()
 
 
 SPACE = {"v": pltpu.VMEM, "s": pltpu.SMEM, "h": pltpu.HBM}
@@ -464,8 +509,8 @@
             values.append(value if kind == "r" else pltpu.with_memory_space_constraint(value, SPACE[kind]))
             specs.append(pl.BlockSpec(memory_space=SPACE["s" if kind == "r" else kind]))
     for shape, dtype, kind in outs:
-        shapes.append(jax.ShapeDtypeStruct(shape, dtype) if kind == "h" else SPACE[kind](shape, dtype))
-        out_specs.append(pl.BlockSpec(memory_space=SPACE["s" if kind == "s" else "v"]))
+        shapes.append(SPACE[kind](shape, dtype))
+        out_specs.append(pl.BlockSpec(memory_space=SPACE[kind]))
     return pl.pallas_call(
         functools.partial(body, **sizes),
         out_shape=tuple(shapes),
@@ -496,13 +541,13 @@
 
     order, send_a, send_b, field, cotan, rate_x, rate_y = call(
         begin_body,
-        [("r", [tile_count]), ("h", [v.reshape(slots) for v in (dest_offset, dest_tile, source_tile)] + [field, cotan, rate_x, rate_y])],
+        [("v", [jnp.broadcast_to(tile_count.reshape(1, 1), (8, 128)).astype(f32)]), ("h", [v.reshape(slots) for v in (dest_offset, dest_tile, source_tile)] + [field, cotan, rate_x, rate_y])],
         [((3, slots), i32, "s")] + [((8 + 3 * size, 128), f32, "v")] * 2 + [whole] * 4,
         scratch=[pltpu.SMEM((slots,), i32)] * 3 + [pltpu.SMEM((9,), i32), pltpu.SemaphoreType.DMA((7,))],
         **sizes,
     )
+    rows_a = exchange(send_a, "gx", A)
     rows_b = exchange(send_b, "gx", B)
-    rows_a = exchange(send_a, "gx", A)
     column = jnp.concatenate([send_a[:8], rows_a[:8], rows_b[:8]], axis=0)
     extra = 3 * extent_x
     pairs, picked, wide_a, wide_b, value_s = call(
@@ -522,9 +567,8 @@
     )
     y_b = exchange(tiles_b, "gy", B)
     y_a = exchange(tiles_a, "gy", A)
-    early, pad_rate, edge_rate = call(
-        pull_body, [("v", [cotan, rate_x, rate_y, rows_a, rows_b, wide_a, packs_a, packs_b])],
-        [whole, padded + ("v",), ((extent_x, 128), f32, "v")], scratch=(pad_scratch,) * 3, **sizes,
+    early, edge_rate = call(
+        pull_y_body, [("v", [cotan, rate_y, wide_a, packs_a, packs_b])], [whole, ((extent_x, 128), f32, "v")], **sizes,
     )
     y_a, y_b, early = lax.optimization_barrier((y_a, y_b, early))
 
@@ -532,15 +576,19 @@
         cut = lambda v, start: v[start + m * 2 * planes : start + (m + 1) * 2 * planes]
         return [cut(own, own_first), cut(a, first), cut(b, first)]
 
-    x_b = exchange(jnp.concatenate(onward(tiles_s, y_a, y_b, 0, 0, B), axis=0), "gx", B)
-    x_a = exchange(jnp.concatenate(onward(tiles_s, y_a, y_b, 0, 0, A), axis=0), "gx", A)
-    z_b = exchange(jnp.concatenate(onward(value_s, packs_a, packs_b, 0, extra, B), axis=0), "gx", B)
-    z_a = exchange(jnp.concatenate(onward(value_s, packs_a, packs_b, 0, extra, A), axis=0), "gx", A)
+    both = lambda m: jnp.concatenate(onward(tiles_s, y_a, y_b, 0, 0, m) + onward(value_s, packs_a, packs_b, 0, extra, m), axis=0)
+    x_b = exchange(both(B), "gx", B)
+    x_a = exchange(both(A), "gx", A)
+    early, pad_rate = call(
+        pull_x_body, [("v", [early, cotan, rate_x, rows_a, rows_b])], [whole, padded + ("v",)],
+        scratch=(pad_scratch,) * 3, alias={0: 0}, **sizes,
+    )
     grad, returned, send_a, send_b, send_s, edge_a, edge_b = call(
         middle_body, [("s", [order, asked]), ("v", [early, pairs, x_a, x_b, y_a, y_b, tiles_s])],
         [whole, ((pair_total, planes, 128), f32, "v")] + [((extent_x + 2 * size, 128), f32, "v")] * 3 + [((size, 128), f32, "v")] * 2,
         alias={2: 0}, **sizes,
     )
+    send_a, send_b, field = lax.optimization_barrier((send_a, send_b, field))
     last_y_b = exchange(send_b, "gy", B)
     last_y_a = exchange(send_a, "gy", A)
     (pushed,) = call(
@@ -554,14 +602,15 @@
         inner_body, [("v", [cotan, grad, pad_rate, rate_y])], [whole], scratch=(pad_scratch,) * 3, **sizes,
     )
     section, first_outer = call(
-        section_body, [("s", [order, asked]), ("v", [pushed, returned, z_a, z_b, packs_a, packs_b, value_s])],
+        section_body, [("s", [order, asked]), ("v", [pushed, returned, x_a, x_b, packs_a, packs_b, value_s])],
         [whole, ((pair_total, 128, 128), f32, "v")], alias={2: 0}, **sizes,
     )
     grad_level_set, grad_blocks = call(
         last_body,
         [("s", [order]), ("v", [inner, grad, pad_rate, edge_rate, wide_a, send_s, last_y_a, last_y_b, last_x_a, last_x_b, pairs, first_outer, picked])],
         [((cells, 128), f32, "h"), ((slots * TILE // 2, 128), f32, "h")],
-        scratch=(pltpu.VMEM((pair_total, 128, 128), f32), pltpu.VMEM((cells, 128), f32)), **sizes,
+        scratch=(pltpu.VMEM((pair_total, 128, 128), f32), pltpu.VMEM((cells, 128), f32),
+                 pltpu.VMEM((slots * TILE // 2, 128), f32), pltpu.SemaphoreType.DMA((2,))), **sizes,
     )
     return (grad_level_set.reshape(planes, extent_x, extent_y), grad_blocks.reshape(1, 1, slots, TILE * TILE))
 

time: 52.5 us -> 46.4 us (0.88)
  Pallas kernels: 19.3 us -> 11.8 us
  waiting for transfers between devices: 9.83 us -> 12.6 us
  starting transfers between devices: 21 us -> 19.6 us
    pallas_call x9 -> x10, Pallas kernels: 19.3 us -> 11.8 us  [call(): pl.pallas_call(functools.partial(body, **sizes), out_shape=tuple(shapes),...]
    ppermute x16 -> x14, waiting for transfers between devices: 9.83 us -> 12.6 us  [exchange(): return lax.ppermute(block, axis, matching(lax.axis_size(axis), which))]
    ppermute x16 -> x14, starting transfers between devices: 21 us -> 19.6 us  [exchange(): return lax.ppermute(block, axis, matching(lax.axis_size(axis), which))]
  transfers between devices with their start and end apart: 16 -> 14, of which waited for: 6 -> 9; matrix products, arithmetic and copies ran while one was open for 1% -> 1% of each run, Pallas kernels for 29% -> 14%
where the time goes in v4:
time: 46.4 us; the launch traced here: 46.2 us
  starting transfers between devices  19.6 us (42%)
  waiting for transfers between devices  12.6 us (27%)
  Pallas kernels  11.8 us (25%)
  between operations  1.49 us (3%)
  local copies, waits for them, and re-layouts  0.69 us (1%)
    ppermute x14, starting transfers between devices, exchange(): return lax.ppermute(block, axis, matching(lax.axis_size(axis), which))  19.6 us
    ppermute x14, waiting for transfers between devices, exchange(): return lax.ppermute(block, axis, matching(lax.axis_size(axis), which))  12.6 us
    pallas_call x10, Pallas kernels, call(): pl.pallas_call(functools.partial(body, **sizes), out_shape=tuple(shapes),...  11.8 us
  transfers between devices with their start and end apart: 14, of which 9 were waited for; matrix products, arithmetic and copies ran while one was open for 1% of the time, Pallas kernels for 14%

profile of v4, /device:TPU:0, one launch (start us, length us, event | category | flops | bytes accessed | tf_op | source)
XLA Modules:
  0.0 46.2 jit_solution(204126835734846003)
XLA Ops:
  0.6 0.0 copy-start
  1.3 1.6 %begin_body.1 = (s32[3,36]{1,0:T(4,128)S(4)}, f32[152,128]{1,0:T(8,128)S(1)}, f32[152,128]{1,0:T(8,128)S(1)}, f32[1024,128]{1,0:T(8,128)S(1)}, f32[1024,128]{1,0...) custom-call(f32[8,128]{1,0:T(8,128)S(1)} %broadcast_in_dim.2.count, s32[36]{0:T(128)} %bitcast.14, ...), custom_call_target="tpu_custom_call" | custom-call | tf_op jit(solution)/shard_map/begin_body/pallas_call | solution.py:514
  3.0 3.0 %collective-permute-start.1 = (f32[152,128]{1,0:T(8,128)S(1)}, f32[152,128]{1,0:T(8,128)S(1)}, u32[]{:S(2)}, u32[]{:S(2)}) collective-permute-start(f32[152,128]{1,0:T(8,128)S(1)} %get-tuple-element.47), channel_id=1, source_target_pairs={{0,4},{4,0},{8,12},{12,8},{16,20},{20,16},{24,28},{28,24},{1,5},{5... | collective-permute-start | bytes 233480 | tf_op jit(solution)/shard_map/ppermute | solution.py:25
  6.0 3.5 %collective-permute-start = (f32[152,128]{1,0:T(8,128)S(1)}, f32[152,128]{1,0:T(8,128)S(1)}, u32[]{:S(2)}, u32[]{:S(2)}) collective-permute-start(f32[152,128]{1,0:T(8,128)S(1)} %get-tuple-element.46.request), channel_id=1, source_target_pairs={{0,28},{4,8},{8,4},{12,16},{16,12},{20,24},{24,20},{28,0},{1,29},{... | collective-permute-start | bytes 233480 | tf_op jit(solution)/shard_map/ppermute | solution.py:25
  9.6 0.0 copy-done
  9.6 0.6 %reshape.42.blocks = bf16[36,64,64]{2,1,0:T(8,128)(2,1)S(1)} reshape(bf16[1,1,36,4096]{3,2,1,0:T(8,128)(2,1)S(1)} %copy-done) | data formatting | bytes 589824 | tf_op jit(solution)/shard_map/reshape | solution.py:554
  10.2 0.8 %extend_body.1 = (bf16[18,128,128]{2,1,0:T(8,128)(2,1)S(1)}, f32[18,16,128]{2,1,0:T(8,128)S(1)}, f32[288,128]{1,0:T(8,128)S(1)}, f32[288,128]{1,0:T(8,128)S(1)}, f32[96,128]{1,0:T(8,128)S(1)}) custom-call(s32[3,36]{1,0:T(4,128)S(4)} %get-tuple-element.44.order, f32[1024,128]{1,0:T(8,128)S(1)} %get-tuple-element.75.field, ...), custom_call_target="tpu_custom_call" | custom-call | tf_op jit(solution)/shard_map/extend_body/pallas_call | solution.py:514
  11.0 0.0 collective-permute-done.1.got_b.rows_b
  11.0 2.1 %collective-permute-done.got_a.rows_a = f32[152,128]{1,0:T(8,128)S(1)} collective-permute-done((f32[152,128]{1,0:T(8,128)S(1)}, f32[152,128]{1,0:T(8,128)S(1)}, u32[]{:S(2)}, u32[]{:S(2)}) %collective-permute-start) | collective-permute-done | bytes 77856 | tf_op jit(solution)/shard_map/ppermute | solution.py:25
  13.1 0.0 collective-permute-start.3
  13.1 1.6 %collective-permute-start.2 = (f32[24,128]{1,0:T(8,128)S(1)}, f32[24,128]{1,0:T(8,128)S(1)}, u32[]{:S(2)}, u32[]{:S(2)}) collective-permute-start(f32[24,128]{1,0:T(8,128)S(1)} %pad_maximum_fusion.2), channel_id=1, source_target_pairs={{0,3},{1,2},{2,1},{3,0},{4,7},{5,6},{6,5},{7,4},{8,11},{9,10},{10,... | collective-permute-start | bytes 36872 | tf_op jit(solution)/shard_map/ppermute | solution.py:25
  14.7 0.1 collective-permute-start.7
  14.8 0.6 %collective-permute-start.6 = (f32[288,128]{1,0:T(8,128)S(1)}, f32[288,128]{1,0:T(8,128)S(1)}, u32[]{:S(2)}, u32[]{:S(2)}) collective-permute-start(f32[288,128]{1,0:T(8,128)S(1)} %get-tuple-element.56.packs), channel_id=1, source_target_pairs={{0,3},{1,2},{2,1},{3,0},{4,7},{5,6},{6,5},{7,4},{8,11},{9,10},{10,... | collective-permute-start | bytes 442376 | tf_op jit(solution)/shard_map/ppermute | solution.py:25
  15.4 0.0 collective-permute-done.3.from_b
  15.4 0.9 %collective-permute-done.2.from_a = f32[24,128]{1,0:T(8,128)S(1)} collective-permute-done((f32[24,128]{1,0:T(8,128)S(1)}, f32[24,128]{1,0:T(8,128)S(1)}, u32[]{:S(2)}, u32[]{:S(2)}) %collective-permute-start.2) | collective-permute-done | bytes 12320 | tf_op jit(solution)/shard_map/ppermute | solution.py:25
  16.3 1.0 %serve_body.1 = (s32[8,128]{1,0:T(8,128)S(4)}, f32[96,128]{1,0:T(8,128)S(1)}, f32[96,128]{1,0:T(8,128)S(1)}, f32[96,128]{1,0:T(8,128)S(1)}) custom-call(f32[152,128]{1,0:T(8,128)S(1)} %get-tuple-element.46.request, f32[152,128]{1,0:T(8,128)S(1)} %collective-permute-done.got_a.rows_a, f32[152,128]{1,0:T(8,128)S(1)} %collective-permute-done.1.got_b.rows_b, ...), custom_call_target="tpu_custom_call" | custom-call | tf_op jit(solution)/shard_map/serve_body/pallas_call | solution.py:514
  17.3 2.0 %collective-permute-start.4 = (f32[96,128]{1,0:T(8,128)S(1)}, f32[96,128]{1,0:T(8,128)S(1)}, u32[]{:S(2)}, u32[]{:S(2)}) collective-permute-start(f32[96,128]{1,0:T(8,128)S(1)} %get-tuple-element.54), channel_id=1, source_target_pairs={{0,3},{1,2},{2,1},{3,0},{4,7},{5,6},{6,5},{7,4},{8,11},{9,10},{10,... | collective-permute-start | bytes 147464 | tf_op jit(solution)/shard_map/ppermute | solution.py:25
  19.3 0.0 collective-permute-start.5
  19.3 0.0 collective-permute-done.7.packs_b.y_b
  19.3 1.0 %collective-permute-done.6.packs_a.y_a = f32[288,128]{1,0:T(8,128)S(1)} collective-permute-done((f32[288,128]{1,0:T(8,128)S(1)}, f32[288,128]{1,0:T(8,128)S(1)}, u32[]{:S(2)}, u32[]{:S(2)}) %collective-permute-start.6) | collective-permute-done | bytes 147488 | tf_op jit(solution)/shard_map/ppermute | solution.py:25
  20.4 0.6 %pull_y_body.1 = (f32[1024,128]{1,0:T(8,128)S(1)}, f32[64,128]{1,0:T(8,128)S(1)}) custom-call(f32[1024,128]{1,0:T(8,128)S(1)} %get-tuple-element.45.cotan, f32[1024,128]{1,0:T(8,128)S(1)} %get-tuple-element.49.rate_y, f32[288,128]{1,0:T(8,128)S(1)} %get-tuple-element.56.packs, f32[288,128]{1,0:T(8,128)S(1)} %collective-permute-done.6.packs_a.y_a, ...), custom_call_target="tpu_custom_call" | custom-call | tf_op jit(solution)/shard_map/pull_y_body/pallas_call | solution.py:514
  21.0 0.7 %collective-permute-done.4.y_a = f32[96,128]{1,0:T(8,128)S(1)} collective-permute-done((f32[96,128]{1,0:T(8,128)S(1)}, f32[96,128]{1,0:T(8,128)S(1)}, u32[]{:S(2)}, u32[]{:S(2)}) %collective-permute-start.4) | collective-permute-done | bytes 49184 | tf_op jit(solution)/shard_map/ppermute | solution.py:25
  21.7 0.0 collective-permute-done.5.y_b
  21.7 0.1 collective-permute-start.9
  21.8 3.6 %collective-permute-start.8 = (f32[192,128]{1,0:T(8,128)S(1)}, f32[192,128]{1,0:T(8,128)S(1)}, u32[]{:S(2)}, u32[]{:S(2)}) collective-permute-start(f32[192,128]{1,0:T(8,128)S(1)} %get-tuple-element.91), channel_id=1, source_target_pairs={{0,28},{4,8},{8,4},{12,16},{16,12},{20,24},{24,20},{28,0},{1,29},{... | collective-permute-start | bytes 294920 | tf_op jit(solution)/shard_map/ppermute | solution.py:25
  25.4 0.7 %pull_x_body.1 = (f32[1024,128]{1,0:T(8,128)S(1)}, f32[1288,128]{1,0:T(8,128)S(1)}) custom-call(f32[1024,128]{1,0:T(8,128)S(1)} %get-tuple-element.59.early, f32[1024,128]{1,0:T(8,128)S(1)} %get-tuple-element.45.cotan, f32[1024,128]{1,0:T(8,128)S(1)} %get-tuple-element.60.rate_x, ...), custom_call_target="tpu_custom_call", output_to_operand_aliasing={{0}: (0, {})} | custom-call | tf_op jit(solution)/shard_map/pull_x_body/pallas_call | solution.py:514
  26.1 0.7 %collective-permute-done.9.x_b = f32[192,128]{1,0:T(8,128)S(1)} collective-permute-done((f32[192,128]{1,0:T(8,128)S(1)}, f32[192,128]{1,0:T(8,128)S(1)}, u32[]{:S(2)}, u32[]{:S(2)}) %collective-permute-start.9) | collective-permute-done | bytes 98336 | tf_op jit(solution)/shard_map/ppermute | solution.py:25
  26.8 2.8 %collective-permute-done.8.x_a = f32[192,128]{1,0:T(8,128)S(1)} collective-permute-done((f32[192,128]{1,0:T(8,128)S(1)}, f32[192,128]{1,0:T(8,128)S(1)}, u32[]{:S(2)}, u32[]{:S(2)}) %collective-permute-start.8) | collective-permute-done | bytes 98336 | tf_op jit(solution)/shard_map/ppermute | solution.py:25
  29.6 1.3 %middle_body.1 = (f32[1024,128]{1,0:T(8,128)S(1)}, f32[18,16,128]{2,1,0:T(8,128)S(1)}, f32[160,128]{1,0:T(8,128)S(1)}, f32[160,128]{1,0:T(8,128)S(1)}, f32[160,1...) custom-call(s32[3,36]{1,0:T(4,128)S(4)} %get-tuple-element.44.order, ...), custom_call_target="tpu_custom_call", output_to_operand_aliasing={{0}: (2, {})} | custom-call | tf_op jit(solution)/shard_map/middle_body/pallas_call | solution.py:514
  30.9 0.9 %collective-permute-start.10 = (f32[160,128]{1,0:T(8,128)S(1)}, f32[160,128]{1,0:T(8,128)S(1)}, u32[]{:S(2)}, u32[]{:S(2)}) collective-permute-start(f32[160,128]{1,0:T(8,128)S(1)} %get-tuple-element.73), channel_id=1, source_target_pairs={{0,3},{1,2},{2,1},{3,0},{4,7},{5,6},{6,5},{7,4},{8,11},{9,10},{10,... | collective-permute-start | bytes 245768 | tf_op jit(solution)/shard_map/ppermute | solution.py:25
  31.8 0.5 %collective-permute-start.11 = (f32[160,128]{1,0:T(8,128)S(1)}, f32[160,128]{1,0:T(8,128)S(1)}, u32[]{:S(2)}, u32[]{:S(2)}) collective-permute-start(f32[160,128]{1,0:T(8,128)S(1)} %get-tuple-element.74), channel_id=1, source_target_pairs={{0,1},{1,0},{2,3},{3,2},{4,5},{5,4},{6,7},{7,6},{8,9},{9,8},{10,11... | collective-permute-start | bytes 245768 | tf_op jit(solution)/shard_map/ppermute | solution.py:25
  32.3 1.2 %push_body.1.early = f32[1024,128]{1,0:T(8,128)S(1)} custom-call(f32[1024,128]{1,0:T(8,128)S(1)} %get-tuple-element.75.field, f32[1288,128]{1,0:T(8,128)S(1)} %get-tuple-element.68.pad_rate, f32[1024,128]{1,0:T(8,128)S(1)} %get-tuple-element.49.rate_y, f32[64,128]{1,0:T(8,128)S(1)} %get-tuple-element.69.edge_rate, ...), custom_call_target="tpu_custom_call" | custom-call | tf_op jit(solution)/shard_map/push_body/pallas_call | solution.py:514
  33.5 2.0 %collective-permute-done.10.y_a = f32[160,128]{1,0:T(8,128)S(1)} collective-permute-done((f32[160,128]{1,0:T(8,128)S(1)}, f32[160,128]{1,0:T(8,128)S(1)}, u32[]{:S(2)}, u32[]{:S(2)}) %collective-permute-start.10) | collective-permute-done | bytes 81952 | tf_op jit(solution)/shard_map/ppermute | solution.py:25
  35.5 0.0 collective-permute-done.11.y_b
  35.5 3.6 %collective-permute-start.12 = (f32[144,128]{1,0:T(8,128)S(1)}, f32[144,128]{1,0:T(8,128)S(1)}, u32[]{:S(2)}, u32[]{:S(2)}) collective-permute-start(f32[144,128]{1,0:T(8,128)S(1)} %pad_maximum_fusion), channel_id=1, source_target_pairs={{0,28},{4,8},{8,4},{12,16},{16,12},{20,24},{24,20},{28,0},{1,29},{... | collective-permute-start | bytes 221192 | tf_op jit(solution)/shard_map/ppermute | solution.py:25
  39.1 0.0 collective-permute-start.13
  39.2 1.1 %inner_body.1.early = f32[1024,128]{1,0:T(8,128)S(1)} custom-call(f32[1024,128]{1,0:T(8,128)S(1)} %get-tuple-element.45.cotan, f32[1024,128]{1,0:T(8,128)S(1)} %get-tuple-element.67.grad, f32[1288,128]{1,0:T(8,128)S(1)} %get-tuple-element.68.pad_rate, f32[1024,128]{1,0:T(8,128)S(1)} %get-tuple-element.49.rate_y), custom_call_target="tpu_custom_call" | custom-call | tf_op jit(solution)/shard_map/inner_body/pallas_call | solution.py:514
  40.3 1.2 %section_body.1 = (f32[1024,128]{1,0:T(8,128)S(1)}, f32[18,128,128]{2,1,0:T(8,128)S(1)}) custom-call(s32[3,36]{1,0:T(4,128)S(4)} %get-tuple-element.44.order, s32[8,128]{1,0:T(8,128)S(4)} %get-tuple-element.53.asked, f32[1024,128]{1,0:T(8,128)S(1)} %push_body.1.early, ...), custom_call_target="tpu_custom_call", output_to_operand_aliasing={{0}: (2, {})} | custom-call | tf_op jit(solution)/shard_map/section_body/pallas_call | solution.py:514
  41.5 1.2 %collective-permute-done.12.x_a = f32[144,128]{1,0:T(8,128)S(1)} collective-permute-done((f32[144,128]{1,0:T(8,128)S(1)}, f32[144,128]{1,0:T(8,128)S(1)}, u32[]{:S(2)}, u32[]{:S(2)}) %collective-permute-start.12) | collective-permute-done | bytes 73760 | tf_op jit(solution)/shard_map/ppermute | solution.py:25
  42.7 1.3 %collective-permute-done.13.x_b = f32[144,128]{1,0:T(8,128)S(1)} collective-permute-done((f32[144,128]{1,0:T(8,128)S(1)}, f32[144,128]{1,0:T(8,128)S(1)}, u32[]{:S(2)}, u32[]{:S(2)}) %collective-permute-start.13) | collective-permute-done | bytes 73760 | tf_op jit(solution)/shard_map/ppermute | solution.py:25
  44.0 2.2 %last_body.1 = (f32[1024,128]{1,0:T(8,128)}, f32[1152,128]{1,0:T(8,128)}) custom-call(s32[3,36]{1,0:T(4,128)S(4)} %get-tuple-element.44.order, f32[1024,128]{1,0:T(8,128)S(1)} %inner_body.1.early, f32[1024,128]{1,0:T(8,128)S(1)} %get-tuple-element.67.grad, f32[1288,128]{1,0:T(8,128)S(1)} %get-tuple-element.68.pad_rate, ...), custom_call_target="tpu_custom_call" | custom-call | tf_op jit(solution)/shard_map/last_body/pallas_call | solution.py:514
  (15 shorter events, 0.1 us)
Async XLA Ops:
  0.6 8.9 %copy-start = (bf16[1,1,36,4096]{3,2,1,0:T(8,128)(2,1)S(1)}, bf16[1,1,36,4096]{3,2,1,0:T(8,128)(2,1)}, u32[]{:S(2)}) copy-start(bf16[1,1,36,4096]{3,2,1,0:T(8,128)(2,1)} %param.13) | copy-start | bytes 884740
  3.0 8.0 %collective-permute-start.1 = (f32[152,128]{1,0:T(8,128)S(1)}, f32[152,128]{1,0:T(8,128)S(1)}, u32[]{:S(2)}, u32[]{:S(2)}) collective-permute-start(f32[152,128]{1,0:T(8,128)S(1)} %get-tuple-element.47), channel_id=1, source_target_pairs={{0,4},{4,0},{8,12},{12,8},{16,20},{20,16},{24,28},{28,24},{1,5},{5... | collective-permute-start | bytes 233480 | tf_op jit(solution)/shard_map/ppermute | solution.py:25
  6.0 7.1 %collective-permute-start = (f32[152,128]{1,0:T(8,128)S(1)}, f32[152,128]{1,0:T(8,128)S(1)}, u32[]{:S(2)}, u32[]{:S(2)}) collective-permute-start(f32[152,128]{1,0:T(8,128)S(1)} %get-tuple-element.46.request), channel_id=1, source_target_pairs={{0,28},{4,8},{8,4},{12,16},{16,12},{20,24},{24,20},{28,0},{1,29},{... | collective-permute-start | bytes 233480 | tf_op jit(solution)/shard_map/ppermute | solution.py:25
  13.1 2.3 %collective-permute-start.3 = (f32[24,128]{1,0:T(8,128)S(1)}, f32[24,128]{1,0:T(8,128)S(1)}, u32[]{:S(2)}, u32[]{:S(2)}) collective-permute-start(f32[24,128]{1,0:T(8,128)S(1)} %pad_maximum_fusion.2), channel_id=1, source_target_pairs={{0,1},{1,0},{2,3},{3,2},{4,5},{5,4},{6,7},{7,6},{8,9},{9,8},{10,11... | collective-permute-start | bytes 36872 | tf_op jit(solution)/shard_map/ppermute | solution.py:25
  13.1 3.2 %collective-permute-start.2 = (f32[24,128]{1,0:T(8,128)S(1)}, f32[24,128]{1,0:T(8,128)S(1)}, u32[]{:S(2)}, u32[]{:S(2)}) collective-permute-start(f32[24,128]{1,0:T(8,128)S(1)} %pad_maximum_fusion.2), channel_id=1, source_target_pairs={{0,3},{1,2},{2,1},{3,0},{4,7},{5,6},{6,5},{7,4},{8,11},{9,10},{10,... | collective-permute-start | bytes 36872 | tf_op jit(solution)/shard_map/ppermute | solution.py:25
  14.7 4.6 %collective-permute-start.7 = (f32[288,128]{1,0:T(8,128)S(1)}, f32[288,128]{1,0:T(8,128)S(1)}, u32[]{:S(2)}, u32[]{:S(2)}) collective-permute-start(f32[288,128]{1,0:T(8,128)S(1)} %get-tuple-element.57), channel_id=1, source_target_pairs={{0,1},{1,0},{2,3},{3,2},{4,5},{5,4},{6,7},{7,6},{8,9},{9,8},{10,11... | collective-permute-start | bytes 442376 | tf_op jit(solution)/shard_map/ppermute | solution.py:25
  14.8 5.6 %collective-permute-start.6 = (f32[288,128]{1,0:T(8,128)S(1)}, f32[288,128]{1,0:T(8,128)S(1)}, u32[]{:S(2)}, u32[]{:S(2)}) collective-permute-start(f32[288,128]{1,0:T(8,128)S(1)} %get-tuple-element.56.packs), channel_id=1, source_target_pairs={{0,3},{1,2},{2,1},{3,0},{4,7},{5,6},{6,5},{7,4},{8,11},{9,10},{10,... | collective-permute-start | bytes 442376 | tf_op jit(solution)/shard_map/ppermute | solution.py:25
  17.3 4.4 %collective-permute-start.4 = (f32[96,128]{1,0:T(8,128)S(1)}, f32[96,128]{1,0:T(8,128)S(1)}, u32[]{:S(2)}, u32[]{:S(2)}) collective-permute-start(f32[96,128]{1,0:T(8,128)S(1)} %get-tuple-element.54), channel_id=1, source_target_pairs={{0,3},{1,2},{2,1},{3,0},{4,7},{5,6},{6,5},{7,4},{8,11},{9,10},{10,... | collective-permute-start | bytes 147464 | tf_op jit(solution)/shard_map/ppermute | solution.py:25
  19.3 2.4 %collective-permute-start.5 = (f32[96,128]{1,0:T(8,128)S(1)}, f32[96,128]{1,0:T(8,128)S(1)}, u32[]{:S(2)}, u32[]{:S(2)}) collective-permute-start(f32[96,128]{1,0:T(8,128)S(1)} %get-tuple-element.55), channel_id=1, source_target_pairs={{0,1},{1,0},{2,3},{3,2},{4,5},{5,4},{6,7},{7,6},{8,9},{9,8},{10,11... | collective-permute-start | bytes 147464 | tf_op jit(solution)/shard_map/ppermute | solution.py:25
  21.7 5.0 %collective-permute-start.9 = (f32[192,128]{1,0:T(8,128)S(1)}, f32[192,128]{1,0:T(8,128)S(1)}, u32[]{:S(2)}, u32[]{:S(2)}) collective-permute-start(f32[192,128]{1,0:T(8,128)S(1)} %get-tuple-element.90), channel_id=1, source_target_pairs={{0,4},{4,0},{8,12},{12,8},{16,20},{20,16},{24,28},{28,24},{1,5},{5... | collective-permute-start | bytes 294920 | tf_op jit(solution)/shard_map/ppermute | solution.py:25
  21.8 7.7 %collective-permute-start.8 = (f32[192,128]{1,0:T(8,128)S(1)}, f32[192,128]{1,0:T(8,128)S(1)}, u32[]{:S(2)}, u32[]{:S(2)}) collective-permute-start(f32[192,128]{1,0:T(8,128)S(1)} %get-tuple-element.91), channel_id=1, source_target_pairs={{0,28},{4,8},{8,4},{12,16},{16,12},{20,24},{24,20},{28,0},{1,29},{... | collective-permute-start | bytes 294920 | tf_op jit(solution)/shard_map/ppermute | solution.py:25
  30.9 4.6 %collective-permute-start.10 = (f32[160,128]{1,0:T(8,128)S(1)}, f32[160,128]{1,0:T(8,128)S(1)}, u32[]{:S(2)}, u32[]{:S(2)}) collective-permute-start(f32[160,128]{1,0:T(8,128)S(1)} %get-tuple-element.73), channel_id=1, source_target_pairs={{0,3},{1,2},{2,1},{3,0},{4,7},{5,6},{6,5},{7,4},{8,11},{9,10},{10,... | collective-permute-start | bytes 245768 | tf_op jit(solution)/shard_map/ppermute | solution.py:25
  31.8 3.7 %collective-permute-start.11 = (f32[160,128]{1,0:T(8,128)S(1)}, f32[160,128]{1,0:T(8,128)S(1)}, u32[]{:S(2)}, u32[]{:S(2)}) collective-permute-start(f32[160,128]{1,0:T(8,128)S(1)} %get-tuple-element.74), channel_id=1, source_target_pairs={{0,1},{1,0},{2,3},{3,2},{4,5},{5,4},{6,7},{7,6},{8,9},{9,8},{10,11... | collective-permute-start | bytes 245768 | tf_op jit(solution)/shard_map/ppermute | solution.py:25
  35.5 7.2 %collective-permute-start.12 = (f32[144,128]{1,0:T(8,128)S(1)}, f32[144,128]{1,0:T(8,128)S(1)}, u32[]{:S(2)}, u32[]{:S(2)}) collective-permute-start(f32[144,128]{1,0:T(8,128)S(1)} %pad_maximum_fusion), channel_id=1, source_target_pairs={{0,28},{4,8},{8,4},{12,16},{16,12},{20,24},{24,20},{28,0},{1,29},{... | collective-permute-start | bytes 221192 | tf_op jit(solution)/shard_map/ppermute | solution.py:25
  39.1 4.8 %collective-permute-start.13 = (f32[144,128]{1,0:T(8,128)S(1)}, f32[144,128]{1,0:T(8,128)S(1)}, u32[]{:S(2)}, u32[]{:S(2)}) collective-permute-start(f32[144,128]{1,0:T(8,128)S(1)} %pad_maximum_fusion.1), channel_id=1, source_target_pairs={{0,4},{4,0},{8,12},{12,8},{16,20},{20,16},{24,28},{28,24},{1,5},{5... | collective-permute-start | bytes 221192 | tf_op jit(solution)/shard_map/ppermute | solution.py:25

commit v5 on v4

--- a/solution.py
+++ b/solution.py
@@ -183,14 +183,16 @@
     return results
 
 
+LABELS = [(lx, ly, half) for ly in range(3) for lx in range(3) for half in range(2)]
+
+
 def parities():
     return lax.rem(lax.axis_index("gx"), 2), lax.rem(lax.axis_index("gy"), 2)
 
 
-def alive_lanes(value, order, number):
+def alive_lanes(value, order, number, total):
     lane = lanes(value.shape)
-    alive = jnp.where(lane < TILE, order[2, 2 * number], order[2, 2 * number + 1])
-    return jnp.where(alive == 1, value, 0.0)
+    return jnp.where(jnp.where(lane < TILE, order[0, 2 * number], order[0, 2 * number + 1]) < total, value, 0.0)
 
 
 def part(ref, number, extent_x):
@@ -198,7 +200,7 @@
 
 
 def begin_body(
-    count, heading, target, source, field, cotan, rate_x, rate_y,
+    heading, target, source, field, cotan, rate_x, rate_y,
     order, send_a, send_b, field_out, cotan_out, rate_x_out, rate_y_out,
     heading_in, target_in, source_in, used, sems, *, planes, extent_x,
 ):
@@ -215,7 +217,6 @@
     lane = lanes((8, 128))
     for copy in copies[:3]:
         copy.wait()
-    total = jnp.max(count[...]).astype(jnp.int32)
     asked = jnp.zeros((8, 128), jnp.int32)
     for slot in range(heading.shape[0]):
         toward = heading_in[slot]
@@ -229,9 +230,7 @@
         used[label] = used[label] + 1
         order[0, spot] = slot
         order[1, spot] = source_in[slot]
-        order[2, spot] = (slot < total).astype(jnp.int32)
-        wanted = jnp.where(slot < total, target_in[slot], 0)
-        asked = jnp.where(lane == spot, wanted, asked)
+        asked = jnp.where(lane == spot, target_in[slot], asked)
     even = parity_x == 0
     high = extent_x - 3
     size = 3 * planes
@@ -245,13 +244,11 @@
     copies[6].wait()
 
 
-def extend_body(order, field, cotan, rate_y, blocks, pairs, picked, send_a, send_b, value_s, *, planes, extent_x):
-    extra = 3 * extent_x
-    for number, ref in enumerate((cotan, rate_y, field)):
-        packed = edge_pack(ref, planes, extent_x)
-        for out in (send_a, send_b):
-            out[number * extent_x : (number + 1) * extent_x, :] = packed
-    for number in range(18):
+def extend_body(order, count, field, cotan, rate_y, blocks, pairs, picked, packs, value_a, value_b, value_s, *, planes, extent_x):
+    for number, ref in enumerate((rate_y, field, cotan)):
+        packs[number * extent_x : (number + 1) * extent_x, :] = edge_pack(ref, planes, extent_x)
+    total = count[0, 0]
+    for number, (lx, ly, half) in enumerate(LABELS):
         one_block, two_block = blocks[order[0, 2 * number]], blocks[order[0, 2 * number + 1]]
         zero = jnp.zeros_like(one_block)
         joined = jnp.concatenate(
@@ -260,65 +257,78 @@
         pairs[number] = joined
         tiles = tile_pair(field, order[1, 2 * number], order[1, 2 * number + 1], planes, extent_x)
         picked[number] = tiles
-        value = pair_dot(alive_lanes(tiles, order, number), joined, 1)
-        out, first = ((send_a, extra), (send_b, extra), (value_s, 0))[number // 6]
-        first = first + number % 6 * planes
-        out[first : first + planes, :] = value
+        first = (ly * 2 + half) * planes
+        value = pair_dot(alive_lanes(tiles, order, number, total), joined, 1)
+        (value_a, value_b, value_s)[lx][first : first + planes, :] = value
+
+
+def merge_lists(a, b, s):
+    group = lax.rem(lanes((8, 128)), 12) // ROUTE_MOST
+    return jnp.where(group == 0, a, jnp.where(group == 1, b, s)).astype(jnp.int32)
+
+
+def to_scalars(value, list_ref, asked, sem):
+    list_ref[...] = value
+    copy = pltpu.make_async_copy(list_ref, asked, sem)
+    copy.start()
+    copy.wait()
+
+
+def serve_body(request, got_a, got_b, cotan_a, cotan_b, cotan, out_a, out_b, out_s, list_ref, asked, sem, *, planes, extent_x):
+    to_scalars(merge_lists(got_a[0:8], got_b[0:8], request[0:8]), list_ref, asked, sem)
+    for lx, ly, half in LABELS:
+        at = ly * 12 + lx * ROUTE_MOST + 2 * half
+        tiles = tile_pair((cotan_a, cotan_b, cotan)[ly], asked[0, at], asked[0, at + 1], planes, extent_x)
+        first = (ly * 2 + half) * planes
+        (out_a, out_b, out_s)[lx][first : first + planes, :] = tiles
 
 
 def gather_tiles(asked, field, outs, first, planes, extent_x):
     for ly in range(3):
-
         for inner in range(6):
             at = ly * 12 + 2 * inner
             tiles = tile_pair(field, asked[ly, at], asked[ly, at + 1], planes, extent_x)
             outs[ly][first + inner * planes : first + (inner + 1) * planes, :] = tiles
 
 
-def serve_body(request, got_a, got_b, from_a, from_b, cotan, asked, out_a, out_b, out_s, list_ref, sem, *, planes, extent_x):
+def rows_at(ref, first, planes):
+    return ref[first : first + planes, :]
+
+
+def pull_y_body(
+    cotan, cotan_a, cotan_b, rate_y, packs, request, got_a, got_b, from_a, from_b, grad, edge_rate, asked, list_ref, joined, sem,
+    *, planes, extent_x,
+):
     row = lax.broadcasted_iota(jnp.int32, (8, 128), 0)
-    group = lax.rem(lanes((8, 128)), 12) // ROUTE_MOST
-    merged = []
-    for a, b, s in (
-        (from_a[8:16], from_a[16:24], from_a[0:8]),
-        (from_b[8:16], from_b[16:24], from_b[0:8]),
-        (got_a[0:8], got_b[0:8], request[0:8]),
-    ):
-        merged.append(jnp.where(group == 0, a, jnp.where(group == 1, b, s))[0:1])
-    spread = [jnp.broadcast_to(one, (8, 128)) for one in merged]
-    joined = jnp.where(row == 0, spread[0], jnp.where(row == 1, spread[1], spread[2]))
-    list_ref[...] = joined.astype(jnp.int32)
+    spread = [
+        jnp.broadcast_to(merge_lists(a, b, c)[0:1], (8, 128))
+        for a, b, c in (
+            (from_a[8:16], from_a[16:24], from_a[0:8]),
+            (from_b[8:16], from_b[16:24], from_b[0:8]),
+            (got_a[0:8], got_b[0:8], request[0:8]),
+        )
+    ]
+    list_ref[...] = jnp.where(row == 0, spread[0], jnp.where(row == 1, spread[1], spread[2]))
     copy = pltpu.make_async_copy(list_ref, asked, sem)
     copy.start()
-    copy.wait()
-    gather_tiles(asked, cotan, (out_a, out_b, out_s), 0, planes, extent_x)
-
-
-def landed(lx, ly, half, planes, x_first, y_first, x_a, x_b, y_a, y_b, own):
-    if lx == S:
-        ref, first = (y_a, y_b, own)[ly], (0 if ly == S and own.shape[0] == 6 * planes else y_first) + (S * 2 + half) * planes
-    else:
-        ref, first = (x_a, x_b)[lx], x_first + ((1, 2, 0)[ly] * 2 + half) * planes
-    return ref[first : first + planes, :]
-
-
-LABELS = [(lx, ly, half) for ly in range(3) for lx in range(3) for half in range(2)]
-
-
-def pull_y_body(cotan, rate_y, packs, packs_a, packs_b, grad, edge_rate, *, planes, extent_x):
     even_y = parities()[1] == 0
-    halo = edge_join(part(packs_a, 0, extent_x), part(packs_b, 0, extent_x), even_y)
-    halo_rate = edge_join(part(packs_a, 1, extent_x), part(packs_b, 1, extent_x), even_y)
+    lane = lanes((extent_x, 128))
+    upper = jnp.where(even_y, lane, 127 - lane) >= TILE
+    for z in range(planes):
+        plane = slice(z * extent_x, (z + 1) * extent_x)
+        joined[plane, :] = jnp.where(upper, cotan_a[plane, :], cotan_b[plane, :])
+    halo = edge_pack(joined, planes, extent_x)
+    halo_rate = edge_join(from_a[24 : 24 + extent_x], from_b[24 : 24 + extent_x], even_y)
     edge_rate[...] = halo_rate
-    edges = adjoint_edges(part(packs, 0, extent_x), halo, part(packs, 1, extent_x), halo_rate)
+    edges = adjoint_edges(part(packs, 2, extent_x), halo, part(packs, 0, extent_x), halo_rate)
     pulled = adjoint_y(cotan, rate_y, planes, extent_x)
     for z in range(planes):
         spot = pl.ds(z * extent_x, extent_x)
         rim = roll(edges, 125 - 8 * z)
-        lane = lanes(rim.shape)
         rim = jnp.where((lane < 3) | (lane >= 125), rim, 0.0)
         main = pulled[z // 4][z % 4 * extent_x : (z % 4 + 1) * extent_x]
         grad[spot, :] = 0.5 * cotan[spot, :] + (0.5 * TIME_STEP) * (main * (1.0 / 60.0) + rim)
+    copy.wait()
 
 
 def pull_x_body(early, cotan, rate_x, rows_a, rows_b, grad, pad_rate, pad, up_ref, down_ref, *, planes, extent_x):
@@ -336,8 +346,9 @@
     even_x, even_y = parity_x == 0, parity_y == 0
     first = 8 + 6 * planes
     fill_padded(pad, field, rows_a[first : first + 3 * planes], rows_b[first : first + 3 * planes], even_x, planes, extent_x)
-    halo = edge_join(part(packs_a, 2, extent_x), part(packs_b, 2, extent_x), even_y)
-    own_rate = part(packs, 1, extent_x)
+    second = slice(24 + extent_x, 24 + 2 * extent_x)
+    halo = edge_join(packs_a[second], packs_b[second], even_y)
+    own_rate = part(packs, 0, extent_x)
     lane8 = lanes(halo.shape) % 8
 
     def shifted_by(value, k):
@@ -348,7 +359,7 @@
         down_part = sum(WEIGHTS[j] * shifted_by(value, 3 - j) for j in range(5))
         return up_part, down_part
 
-    up_part, down_part = stencils(jnp.where(lane8 < 3, halo, jnp.where(lane8 < 6, part(packs, 2, extent_x), 0.0)))
+    up_part, down_part = stencils(jnp.where(lane8 < 3, halo, jnp.where(lane8 < 6, part(packs, 1, extent_x), 0.0)))
     rate_up, rate_down = upwind(edge_rate[...])
     flux_low = roll(rate_up * up_part + rate_down * down_part, 1)
     rate_up, rate_down = upwind(own_rate)
@@ -386,10 +397,12 @@
         section[spot, :] = field[spot, :] + TIME_STEP * change
 
 
-def middle_body(order, asked, early, pairs, x_a, x_b, y_a, y_b, own, grad, returned, send_a, send_b, send_s, rows_a, rows_b, *, planes, extent_x):
+def middle_body(order, asked, count, early, pairs, x_a, x_b, own, grad, returned, send_a, send_b, send_s, rows_a, rows_b, *, planes, extent_x):
     even_x = parities()[0] == 0
-    for number, label in enumerate(LABELS):
-        back = alive_lanes(landed(*label, planes, 0, 0, x_a, x_b, y_a, y_b, own), order, number)
+    alive = count[0, 0]
+    for number, (lx, ly, half) in enumerate(LABELS):
+        back = rows_at((x_a, x_b, own)[lx], (ly * 2 + half) * planes, planes)
+        back = alive_lanes(back, order, number, alive)
         returned[number] = back
         pulled = (0.5 * TIME_STEP) * pair_dot(back, pairs[number], 0)
         add_tile_pair(grad, order[1, 2 * number], order[1, 2 * number + 1], pulled, planes, extent_x)
@@ -431,7 +444,11 @@
 
 def section_body(order, asked, early, returned, x_a, x_b, y_a, y_b, own, section, first_outer, *, planes, extent_x):
     for number, (lx, ly, half) in enumerate(LABELS):
-        came = TIME_STEP * landed(lx, ly, half, planes, 6 * planes, 3 * extent_x, x_a, x_b, y_a, y_b, own)
+        if ly == S:
+            came = rows_at((x_a, x_b, own)[lx], (0 if lx == S else 6 * planes) + (S * 2 + half) * planes, planes)
+        else:
+            came = rows_at((y_a, y_b)[ly], ((1, 2, 0)[lx] * 2 + half) * planes, planes)
+        came = TIME_STEP * came
         at = ly * 12 + lx * ROUTE_MOST + 2 * half
         add_tile_pair(section, asked[ly, at], asked[ly, at + 1], came, planes, extent_x)
 
@@ -441,14 +458,14 @@
 
 
 def last_body(
-    order, early, grad, pad_rate, edge_rate, packs, own, y_a, y_b, x_a, x_b, pairs, first_outer, picked, out, out_blocks, work, total, blocks, sems,
+    order, count, early, grad, pad_rate, edge_rate, packs, own, y_a, y_b, x_a, x_b, pairs, first_outer, picked, out, out_blocks, work, total, blocks, sems,
     *, planes, extent_x,
 ):
     parity_x, parity_y = parities()
     even_x, even_y = parity_x == 0, parity_y == 0
     size = 3 * planes
     halo = edge_join(y_a[0:extent_x], y_b[0:extent_x], even_y)
-    edges = adjoint_edges(own[0:extent_x], halo, part(packs, 1, extent_x), edge_rate[...])
+    edges = adjoint_edges(own[0:extent_x], halo, part(packs, 0, extent_x), edge_rate[...])
 
     for z in range(planes):
         spot = pl.ds(z * extent_x, extent_x)
@@ -476,7 +493,12 @@
             total[spot, :] = total[spot, :] + TIME_STEP * added
     backs = []
     for number, label in enumerate(LABELS):
-        back = alive_lanes(landed(*label, planes, size, extent_x, x_a, x_b, y_a, y_b, own), order, number)
+        lx, ly, half = label
+        if lx == S:
+            back = rows_at((y_a, y_b, own)[ly], extent_x + (S * 2 + half) * planes, planes)
+        else:
+            back = rows_at((x_a, x_b)[lx], size + ((1, 2, 0)[ly] * 2 + half) * planes, planes)
+        back = alive_lanes(back, order, number, count[0, 0])
         backs.append(back)
         pulled = TIME_STEP * pair_dot(back, pairs[number], 0)
         add_tile_pair(total, order[1, 2 * number], order[1, 2 * number + 1], pulled, planes, extent_x)
@@ -539,60 +561,61 @@
     pad_scratch = pltpu.VMEM(*padded)
     whole = ((cells, 128), f32, "v")
 
+    cotan_b = exchange(cotan, "gy", B)
+    cotan_a = exchange(cotan, "gy", A)
     order, send_a, send_b, field, cotan, rate_x, rate_y = call(
         begin_body,
-        [("v", [jnp.broadcast_to(tile_count.reshape(1, 1), (8, 128)).astype(f32)]), ("h", [v.reshape(slots) for v in (dest_offset, dest_tile, source_tile)] + [field, cotan, rate_x, rate_y])],
-        [((3, slots), i32, "s")] + [((8 + 3 * size, 128), f32, "v")] * 2 + [whole] * 4,
+        [("h", [v.reshape(slots) for v in (dest_offset, dest_tile, source_tile)] + [field, cotan, rate_x, rate_y])],
+        [((2, slots), i32, "s")] + [((8 + 3 * size, 128), f32, "v")] * 2 + [whole] * 4,
         scratch=[pltpu.SMEM((slots,), i32)] * 3 + [pltpu.SMEM((9,), i32), pltpu.SemaphoreType.DMA((7,))],
         **sizes,
     )
+    request = send_a
     rows_a = exchange(send_a, "gx", A)
     rows_b = exchange(send_b, "gx", B)
-    column = jnp.concatenate([send_a[:8], rows_a[:8], rows_b[:8]], axis=0)
-    extra = 3 * extent_x
-    pairs, picked, wide_a, wide_b, value_s = call(
-        extend_body, [("s", [order]), ("v", [field, cotan, rate_y, blocks.reshape(slots, TILE, TILE)])],
-        [((pair_total, 128, 128), jnp.bfloat16, "v"), ((pair_total, planes, 128), f32, "v")]
-        + [((extra + 2 * size, 128), f32, "v")] * 2 + [box], **sizes,
-    )
-    column, wide_a, wide_b = lax.optimization_barrier((column, wide_a, wide_b))
-    from_b = exchange(column, "gy", B)
-    from_a = exchange(column, "gy", A)
-    packs_b = exchange(wide_b, "gy", B)
-    packs_a = exchange(wide_a, "gy", A)
-
-    asked, tiles_a, tiles_b, tiles_s = call(
-        serve_body, [("v", [send_a, rows_a, rows_b, from_a, from_b, cotan])],
-        [((8, 128), i32, "s"), box, box, box], scratch=(pltpu.VMEM((8, 128), i32), pltpu.SemaphoreType.DMA(())), **sizes,
-    )
-    y_b = exchange(tiles_b, "gy", B)
-    y_a = exchange(tiles_a, "gy", A)
-    early, edge_rate = call(
-        pull_y_body, [("v", [cotan, rate_y, wide_a, packs_a, packs_b])], [whole, ((extent_x, 128), f32, "v")], **sizes,
-    )
-    y_a, y_b, early = lax.optimization_barrier((y_a, y_b, early))
+    pairs, picked, packs, value_a, value_b, value_s = call(
+        extend_body, [("s", [order]), ("r", [tile_count]), ("v", [field, cotan, rate_y, blocks.reshape(slots, TILE, TILE)])],
+        [((pair_total, 128, 128), jnp.bfloat16, "v"), ((pair_total, planes, 128), f32, "v"), ((3 * extent_x, 128), f32, "v")]
+        + [box] * 3, **sizes,
+    )
+    tiles_a, tiles_b, tiles_s = call(
+        serve_body, [("v", [request, rows_a, rows_b, cotan_a, cotan_b, cotan])], [box, box, box],
+        scratch=(pltpu.VMEM((8, 128), i32), pltpu.SMEM((8, 128), i32), pltpu.SemaphoreType.DMA(())), **sizes,
+    )
+    wide = jnp.concatenate([request[:8], rows_a[:8], rows_b[:8], packs[: 2 * extent_x]], axis=0)
+    wide, tiles_a, tiles_b = lax.optimization_barrier((wide, tiles_a, tiles_b))
+    x_b = exchange(jnp.concatenate([tiles_b, value_b], axis=0), "gx", B)
+    x_a = exchange(jnp.concatenate([tiles_a, value_a], axis=0), "gx", A)
+    packs_b = exchange(wide, "gy", B)
+    packs_a = exchange(wide, "gy", A)
+    early, edge_rate, asked = call(
+        pull_y_body, [("v", [cotan, cotan_a, cotan_b, rate_y, packs, request, rows_a, rows_b, packs_a, packs_b])],
+        [whole, ((extent_x, 128), f32, "v"), ((8, 128), i32, "s")],
+        scratch=(pltpu.VMEM((8, 128), i32), pltpu.VMEM((cells, 128), f32), pltpu.SemaphoreType.DMA(())), **sizes,
+    )
+    early, pad_rate = call(
+        pull_x_body, [("v", [early, cotan, rate_x, rows_a, rows_b])], [whole, padded + ("v",)],
+        scratch=(pad_scratch,) * 3, alias={0: 0}, **sizes,
+    )
+    grad, returned, send_a, send_b, send_s, edge_a, edge_b = call(
+        middle_body, [("s", [order, asked]), ("r", [tile_count]), ("v", [early, pairs, x_a, x_b, tiles_s])],
+        [whole, ((pair_total, planes, 128), f32, "v")] + [((extent_x + 2 * size, 128), f32, "v")] * 3 + [((size, 128), f32, "v")] * 2,
+        alias={3: 0}, **sizes,
+    )
 
     def onward(own, a, b, own_first, first, m):
         cut = lambda v, start: v[start + m * 2 * planes : start + (m + 1) * 2 * planes]
         return [cut(own, own_first), cut(a, first), cut(b, first)]
 
-    both = lambda m: jnp.concatenate(onward(tiles_s, y_a, y_b, 0, 0, m) + onward(value_s, packs_a, packs_b, 0, extra, m), axis=0)
-    x_b = exchange(both(B), "gx", B)
-    x_a = exchange(both(A), "gx", A)
-    early, pad_rate = call(
-        pull_x_body, [("v", [early, cotan, rate_x, rows_a, rows_b])], [whole, padded + ("v",)],
-        scratch=(pad_scratch,) * 3, alias={0: 0}, **sizes,
-    )
-    grad, returned, send_a, send_b, send_s, edge_a, edge_b = call(
-        middle_body, [("s", [order, asked]), ("v", [early, pairs, x_a, x_b, y_a, y_b, tiles_s])],
-        [whole, ((pair_total, planes, 128), f32, "v")] + [((extent_x + 2 * size, 128), f32, "v")] * 3 + [((size, 128), f32, "v")] * 2,
-        alias={2: 0}, **sizes,
-    )
-    send_a, send_b, field = lax.optimization_barrier((send_a, send_b, field))
+    ext_a = jnp.concatenate(onward(value_s, x_a, x_b, 0, 2 * size, A), axis=0)
+    ext_b = jnp.concatenate(onward(value_s, x_a, x_b, 0, 2 * size, B), axis=0)
+    send_a, send_b, field, ext_a, ext_b = lax.optimization_barrier((send_a, send_b, field, ext_a, ext_b))
     last_y_b = exchange(send_b, "gy", B)
     last_y_a = exchange(send_a, "gy", A)
+    ext_b = exchange(ext_b, "gy", B)
+    ext_a = exchange(ext_a, "gy", A)
     (pushed,) = call(
-        push_body, [("v", [field, pad_rate, rate_y, edge_rate, rows_a, rows_b, wide_a, packs_a, packs_b])],
+        push_body, [("v", [field, pad_rate, rate_y, edge_rate, rows_a, rows_b, packs, packs_a, packs_b])],
         [whole], scratch=(pad_scratch,) * 2, **sizes,
     )
     last_y_a, last_y_b, pushed = lax.optimization_barrier((last_y_a, last_y_b, pushed))
@@ -602,12 +625,12 @@
         inner_body, [("v", [cotan, grad, pad_rate, rate_y])], [whole], scratch=(pad_scratch,) * 3, **sizes,
     )
     section, first_outer = call(
-        section_body, [("s", [order, asked]), ("v", [pushed, returned, x_a, x_b, packs_a, packs_b, value_s])],
+        section_body, [("s", [order, asked]), ("v", [pushed, returned, x_a, x_b, ext_a, ext_b, value_s])],
         [whole, ((pair_total, 128, 128), f32, "v")], alias={2: 0}, **sizes,
     )
     grad_level_set, grad_blocks = call(
         last_body,
-        [("s", [order]), ("v", [inner, grad, pad_rate, edge_rate, wide_a, send_s, last_y_a, last_y_b, last_x_a, last_x_b, pairs, first_outer, picked])],
+        [("s", [order]), ("r", [tile_count]), ("v", [inner, grad, pad_rate, edge_rate, packs, send_s, last_y_a, last_y_b, last_x_a, last_x_b, pairs, first_outer, picked])],
         [((cells, 128), f32, "h"), ((slots * TILE // 2, 128), f32, "h")],
         scratch=(pltpu.VMEM((pair_total, 128, 128), f32), pltpu.VMEM((cells, 128), f32),
                  pltpu.VMEM((slots * TILE // 2, 128), f32), pltpu.SemaphoreType.DMA((2,))), **sizes,

time: 46.4 us -> 44.7 us (0.963)
  waiting for transfers between devices: 12.6 us -> 7.53 us
  local copies, waits for them, and re-layouts: 0.69 us -> 2.39 us
  Pallas kernels: 11.8 us -> 12.6 us
  starting transfers between devices: 19.6 us -> 20.4 us
    ppermute x14, waiting for transfers between devices: 12.6 us -> 7.53 us  [exchange(): return lax.ppermute(block, axis, matching(lax.axis_size(axis), which))]
    reshape x1, local copies, waits for them, and re-layouts: 0.64 us -> 1.56 us  [shards(): blocks.reshape(slots, TILE, TILE)]
    ppermute x14, starting transfers between devices: 19.6 us -> 20.4 us  [exchange(): return lax.ppermute(block, axis, matching(lax.axis_size(axis), which))]
    pallas_call x10, Pallas kernels: 11.8 us -> 12.6 us  [call(): pl.pallas_call(functools.partial(body, **sizes), out_shape=tuple(shapes),...]
    unnamed x7 -> x4, local copies, waits for them, and re-layouts: 0.03 us -> 0.79 us
  transfers between devices with their start and end apart: 14 -> 14, of which waited for: 9 -> 5; matrix products, arithmetic and copies ran while one was open for 1% -> 4% of each run, Pallas kernels for 14% -> 18%
where the time goes in v5:
time: 44.7 us; the launch traced here: 44.5 us
  starting transfers between devices  20.4 us (46%)
  Pallas kernels  12.6 us (28%)
  waiting for transfers between devices  7.53 us (17%)
  local copies, waits for them, and re-layouts  2.39 us (5%)
  between operations  1.49 us (3%)
    ppermute x14, starting transfers between devices, exchange(): return lax.ppermute(block, axis, matching(lax.axis_size(axis), which))  20.4 us
    pallas_call x10, Pallas kernels, call(): pl.pallas_call(functools.partial(body, **sizes), out_shape=tuple(shapes),...  12.6 us
    ppermute x14, waiting for transfers between devices, exchange(): return lax.ppermute(block, axis, matching(lax.axis_size(axis), which))  7.53 us
    reshape x1, local copies, waits for them, and re-layouts, shards(): blocks.reshape(slots, TILE, TILE)  1.56 us
  transfers between devices with their start and end apart: 14, of which 5 were waited for; matrix products, arithmetic and copies ran while one was open for 4% of the time, Pallas kernels for 18%

profile of v5, /device:TPU:0, one launch (start us, length us, event | category | flops | bytes accessed | tf_op | source)
XLA Modules:
  0.0 44.5 jit_solution(17048515910547376645)
XLA Ops:
  0.6 0.5 %collective-permute-start.1 = (f32[1024,128]{1,0:T(8,128)}, f32[1024,128]{1,0:T(8,128)S(1)}, u32[]{:S(2)}, u32[]{:S(2)}) collective-permute-start(f32[1024,128]{1,0:T(8,128)} %bitcast.12), channel_id=1, source_target_pairs={{0,1},{1,0},{2,3},{3,2},{4,5},{5,4},{6,7},{7,6},{8,9},{9,8},{10,11... | collective-permute-start | bytes 1572872 | tf_op jit(solution)/shard_map/ppermute | solution.py:25
  1.1 2.6 %collective-permute-start = (f32[1024,128]{1,0:T(8,128)}, f32[1024,128]{1,0:T(8,128)S(1)}, u32[]{:S(2)}, u32[]{:S(2)}) collective-permute-start(f32[1024,128]{1,0:T(8,128)} %bitcast.13), channel_id=1, source_target_pairs={{0,3},{1,2},{2,1},{3,0},{4,7},{5,6},{6,5},{7,4},{8,11},{9,10},{10,... | collective-permute-start | bytes 1572872 | tf_op jit(solution)/shard_map/ppermute | solution.py:25
  3.8 1.6 %begin_body.1 = (s32[2,36]{1,0:T(2,128)S(4)}, f32[152,128]{1,0:T(8,128)S(1)}, f32[152,128]{1,0:T(8,128)S(1)}, f32[1024,128]{1,0:T(8,128)S(1)}, f32[1024,128]{1,0...) custom-call(s32[36]{0:T(128)} %bitcast.15, s32[36]{0:T(128)} %bitcast.16, s32[36]{0:T(128)} %bitcast.17, ...), custom_call_target="tpu_custom_call" | custom-call | tf_op jit(solution)/shard_map/begin_body/pallas_call | solution.py:536
  5.4 0.0 copy-start
  5.4 0.8 %copy-done = f32[1024,128]{1,0:T(8,128)} copy-done((f32[1024,128]{1,0:T(8,128)}, f32[1024,128]{1,0:T(8,128)S(1)}, u32[]{:S(2)}) %copy-start) | copy-done | bytes 524312
  6.1 1.5 %collective-permute-start.3 = (f32[152,128]{1,0:T(8,128)S(1)}, f32[152,128]{1,0:T(8,128)S(1)}, u32[]{:S(2)}, u32[]{:S(2)}) collective-permute-start(f32[152,128]{1,0:T(8,128)S(1)} %get-tuple-element.50), channel_id=1, source_target_pairs={{0,4},{4,0},{8,12},{12,8},{16,20},{20,16},{24,28},{28,24},{1,5},{5... | collective-permute-start | bytes 233480 | tf_op jit(solution)/shard_map/ppermute | solution.py:25
  7.7 3.5 %collective-permute-start.2 = (f32[152,128]{1,0:T(8,128)S(1)}, f32[152,128]{1,0:T(8,128)S(1)}, u32[]{:S(2)}, u32[]{:S(2)}) collective-permute-start(f32[152,128]{1,0:T(8,128)S(1)} %get-tuple-element.49.request), channel_id=1, source_target_pairs={{0,28},{4,8},{8,4},{12,16},{16,12},{20,24},{24,20},{28,0},{1,29},{... | collective-permute-start | bytes 233480 | tf_op jit(solution)/shard_map/ppermute | solution.py:25
  11.9 1.6 %reshape.41.blocks = bf16[36,64,64]{2,1,0:T(8,128)(2,1)S(1)} reshape(bf16[1,1,36,4096]{3,2,1,0:T(8,128)(2,1)} %param.13) | data formatting | bytes 589824 | tf_op jit(solution)/shard_map/reshape | solution.py:577
  13.4 0.8 %extend_body.1 = (bf16[18,128,128]{2,1,0:T(8,128)(2,1)S(1)}, f32[18,16,128]{2,1,0:T(8,128)S(1)}, f32[192,128]{1,0:T(8,128)S(1)}, f32[96,128]{1,0:T(8,128)S(1)}, ...) custom-call(s32[2,36]{1,0:T(2,128)S(4)} %get-tuple-element.44.order, s32[1,1]{1,0:T(1,128)S(6)} %copy.19.count, ...), custom_call_target="tpu_custom_call" | custom-call | tf_op jit(solution)/shard_map/extend_body/pallas_call | solution.py:536
  14.3 0.0 collective-permute-done.3.got_b.rows_b
  14.3 0.5 %collective-permute-done.2.got_a.rows_a = f32[152,128]{1,0:T(8,128)S(1)} collective-permute-done((f32[152,128]{1,0:T(8,128)S(1)}, f32[152,128]{1,0:T(8,128)S(1)}, u32[]{:S(2)}, u32[]{:S(2)}) %collective-permute-start.2) | collective-permute-done | bytes 77856 | tf_op jit(solution)/shard_map/ppermute | solution.py:25
  14.8 0.0 collective-permute-done.1.cotan_b
  14.8 1.4 %collective-permute-done.cotan_a = f32[1024,128]{1,0:T(8,128)S(1)} collective-permute-done((f32[1024,128]{1,0:T(8,128)}, f32[1024,128]{1,0:T(8,128)S(1)}, u32[]{:S(2)}, u32[]{:S(2)}) %collective-permute-start) | collective-permute-done | bytes 524320 | tf_op jit(solution)/shard_map/ppermute | solution.py:25
  16.2 1.0 %serve_body.1 = (f32[96,128]{1,0:T(8,128)S(1)}, f32[96,128]{1,0:T(8,128)S(1)}, f32[96,128]{1,0:T(8,128)S(1)}) custom-call(f32[152,128]{1,0:T(8,128)S(1)} %get-tuple-element.49.request, f32[152,128]{1,0:T(8,128)S(1)} %collective-permute-done.2.got_a.rows_a, f32[152,128]{1,0:T(8,128)S(1)} %collective-permute-done.3.got_b.rows_b, ...), custom_call_target="tpu_custom_call" | custom-call | tf_op jit(solution)/shard_map/serve_body/pallas_call | solution.py:536
  17.2 0.2 collective-permute-start.5
  17.4 1.4 %collective-permute-start.4 = (f32[152,128]{1,0:T(8,128)S(1)}, f32[152,128]{1,0:T(8,128)S(1)}, u32[]{:S(2)}, u32[]{:S(2)}) collective-permute-start(f32[152,128]{1,0:T(8,128)S(1)} %pad_maximum_fusion.2), channel_id=1, source_target_pairs={{0,3},{1,2},{2,1},{3,0},{4,7},{5,6},{6,5},{7,4},{8,11},{9,10},{10,... | collective-permute-start | bytes 233480 | tf_op jit(solution)/shard_map/ppermute | solution.py:25
  18.8 1.6 %collective-permute-start.7 = (f32[192,128]{1,0:T(8,128)S(1)}, f32[192,128]{1,0:T(8,128)S(1)}, u32[]{:S(2)}, u32[]{:S(2)}) collective-permute-start(f32[192,128]{1,0:T(8,128)S(1)} %pad_maximum_fusion.1), channel_id=1, source_target_pairs={{0,4},{4,0},{8,12},{12,8},{16,20},{20,16},{24,28},{28,24},{1,5},{5... | collective-permute-start | bytes 294920 | tf_op jit(solution)/shard_map/ppermute | solution.py:25
  20.4 0.0 copy-start.1
  20.4 3.6 %collective-permute-start.6 = (f32[192,128]{1,0:T(8,128)S(1)}, f32[192,128]{1,0:T(8,128)S(1)}, u32[]{:S(2)}, u32[]{:S(2)}) collective-permute-start(f32[192,128]{1,0:T(8,128)S(1)} %pad_maximum_fusion), channel_id=1, source_target_pairs={{0,28},{4,8},{8,4},{12,16},{16,12},{20,24},{24,20},{28,0},{1,29},{... | collective-permute-start | bytes 294920 | tf_op jit(solution)/shard_map/ppermute | solution.py:25
  24.0 0.0 collective-permute-done.5.from_b.packs_b
  24.0 0.0 collective-permute-done.4.from_a.packs_a
  24.0 1.4 %pull_y_body.1 = (f32[1024,128]{1,0:T(8,128)S(1)}, f32[64,128]{1,0:T(8,128)S(1)}, s32[8,128]{1,0:T(8,128)S(4)}) custom-call(f32[1024,128]{1,0:T(8,128)S(1)} %get-tuple-element.45.cotan, f32[1024,128]{1,0:T(8,128)S(1)} %collective-permute-done.cotan_a, f32[1024,128]{1,0:T(8,128)S(1)} %collective-permute-done.1.cotan_b, ...), custom_call_target="tpu_custom_call" | custom-call | tf_op jit(solution)/shard_map/pull_y_body/pallas_call | solution.py:536
  25.4 0.0 copy-done.1
  25.4 0.7 %pull_x_body.1 = (f32[1024,128]{1,0:T(8,128)S(1)}, f32[1288,128]{1,0:T(8,128)S(1)}) custom-call(f32[1024,128]{1,0:T(8,128)S(1)} %get-tuple-element.55.early, f32[1024,128]{1,0:T(8,128)S(1)} %get-tuple-element.45.cotan, f32[1024,128]{1,0:T(8,128)S(1)} %copy-done.1, ...), custom_call_target="tpu_custom_call", output_to_operand_aliasing={{0}: (0, {})} | custom-call | tf_op jit(solution)/shard_map/pull_x_body/pallas_call | solution.py:536
  26.1 0.0 collective-permute-done.7.x_b
  26.1 1.9 %collective-permute-done.6.x_a = f32[192,128]{1,0:T(8,128)S(1)} collective-permute-done((f32[192,128]{1,0:T(8,128)S(1)}, f32[192,128]{1,0:T(8,128)S(1)}, u32[]{:S(2)}, u32[]{:S(2)}) %collective-permute-start.6) | collective-permute-done | bytes 98336 | tf_op jit(solution)/shard_map/ppermute | solution.py:25
  28.0 1.3 %middle_body.1 = (f32[1024,128]{1,0:T(8,128)S(1)}, f32[18,16,128]{2,1,0:T(8,128)S(1)}, f32[160,128]{1,0:T(8,128)S(1)}, f32[160,128]{1,0:T(8,128)S(1)}, f32[160,1...) custom-call(s32[2,36]{1,0:T(2,128)S(4)} %get-tuple-element.44.order, ...), custom_call_target="tpu_custom_call", output_to_operand_aliasing={{0}: (3, {})} | custom-call | tf_op jit(solution)/shard_map/middle_body/pallas_call | solution.py:536
  29.3 0.1 collective-permute-start.8
  29.4 0.6 %collective-permute-start.9 = (f32[160,128]{1,0:T(8,128)S(1)}, f32[160,128]{1,0:T(8,128)S(1)}, u32[]{:S(2)}, u32[]{:S(2)}) collective-permute-start(f32[160,128]{1,0:T(8,128)S(1)} %get-tuple-element.72), channel_id=1, source_target_pairs={{0,1},{1,0},{2,3},{3,2},{4,5},{5,4},{6,7},{7,6},{8,9},{9,8},{10,11... | collective-permute-start | bytes 245768 | tf_op jit(solution)/shard_map/ppermute | solution.py:25
  30.0 1.2 %push_body.1.early = f32[1024,128]{1,0:T(8,128)S(1)} custom-call(f32[1024,128]{1,0:T(8,128)S(1)} %get-tuple-element.73.field, f32[1288,128]{1,0:T(8,128)S(1)} %get-tuple-element.65.pad_rate, f32[1024,128]{1,0:T(8,128)S(1)} %get-tuple-element.46.rate_y, f32[64,128]{1,0:T(8,128)S(1)} %get-tuple-element.66.edge_rate, ...), custom_call_target="tpu_custom_call" | custom-call | tf_op jit(solution)/shard_map/push_body/pallas_call | solution.py:536
  31.2 2.4 %collective-permute-done.8.y_a = f32[160,128]{1,0:T(8,128)S(1)} collective-permute-done((f32[160,128]{1,0:T(8,128)S(1)}, f32[160,128]{1,0:T(8,128)S(1)}, u32[]{:S(2)}, u32[]{:S(2)}) %collective-permute-start.8) | collective-permute-done | bytes 81952 | tf_op jit(solution)/shard_map/ppermute | solution.py:25
  33.6 0.0 collective-permute-done.9.y_b
  33.7 3.6 %collective-permute-start.10 = (f32[144,128]{1,0:T(8,128)S(1)}, f32[144,128]{1,0:T(8,128)S(1)}, u32[]{:S(2)}, u32[]{:S(2)}) collective-permute-start(f32[144,128]{1,0:T(8,128)S(1)} %pad_maximum_fusion.3), channel_id=1, source_target_pairs={{0,28},{4,8},{8,4},{12,16},{16,12},{20,24},{24,20},{28,0},{1,29},{... | collective-permute-start | bytes 221192 | tf_op jit(solution)/shard_map/ppermute | solution.py:25
  37.3 0.0 collective-permute-start.11
  37.3 0.5 %collective-permute-start.12 = (f32[96,128]{1,0:T(8,128)S(1)}, f32[96,128]{1,0:T(8,128)S(1)}, u32[]{:S(2)}, u32[]{:S(2)}) collective-permute-start(f32[96,128]{1,0:T(8,128)S(1)} %get-tuple-element.80), channel_id=1, source_target_pairs={{0,3},{1,2},{2,1},{3,0},{4,7},{5,6},{6,5},{7,4},{8,11},{9,10},{10,... | collective-permute-start | bytes 147464 | tf_op jit(solution)/shard_map/ppermute | solution.py:25
  37.8 0.7 %collective-permute-start.13 = (f32[96,128]{1,0:T(8,128)S(1)}, f32[96,128]{1,0:T(8,128)S(1)}, u32[]{:S(2)}, u32[]{:S(2)}) collective-permute-start(f32[96,128]{1,0:T(8,128)S(1)} %get-tuple-element.81), channel_id=1, source_target_pairs={{0,1},{1,0},{2,3},{3,2},{4,5},{5,4},{6,7},{7,6},{8,9},{9,8},{10,11... | collective-permute-start | bytes 147464 | tf_op jit(solution)/shard_map/ppermute | solution.py:25
  38.5 1.1 %inner_body.1.early = f32[1024,128]{1,0:T(8,128)S(1)} custom-call(f32[1024,128]{1,0:T(8,128)S(1)} %get-tuple-element.45.cotan, f32[1024,128]{1,0:T(8,128)S(1)} %get-tuple-element.64.grad, f32[1288,128]{1,0:T(8,128)S(1)} %get-tuple-element.65.pad_rate, f32[1024,128]{1,0:T(8,128)S(1)} %get-tuple-element.46.rate_y), custom_call_target="tpu_custom_call" | custom-call | tf_op jit(solution)/shard_map/inner_body/pallas_call | solution.py:536
  39.6 1.4 %collective-permute-done.12.y_a = f32[96,128]{1,0:T(8,128)S(1)} collective-permute-done((f32[96,128]{1,0:T(8,128)S(1)}, f32[96,128]{1,0:T(8,128)S(1)}, u32[]{:S(2)}, u32[]{:S(2)}) %collective-permute-start.12) | collective-permute-done | bytes 49184 | tf_op jit(solution)/shard_map/ppermute | solution.py:25
  41.0 0.0 collective-permute-done.13.y_b
  41.0 1.2 %section_body.1 = (f32[1024,128]{1,0:T(8,128)S(1)}, f32[18,128,128]{2,1,0:T(8,128)S(1)}) custom-call(s32[2,36]{1,0:T(2,128)S(4)} %get-tuple-element.44.order, s32[8,128]{1,0:T(8,128)S(4)} %get-tuple-element.54.asked, f32[1024,128]{1,0:T(8,128)S(1)} %push_body.1.early, ...), custom_call_target="tpu_custom_call", output_to_operand_aliasing={{0}: (2, {})} | custom-call | tf_op jit(solution)/shard_map/section_body/pallas_call | solution.py:536
  42.2 0.0 collective-permute-done.10.x_a
  42.2 0.0 collective-permute-done.11.x_b
  42.2 2.3 %last_body.1 = (f32[1024,128]{1,0:T(8,128)}, f32[1152,128]{1,0:T(8,128)}) custom-call(s32[2,36]{1,0:T(2,128)S(4)} %get-tuple-element.44.order, s32[1,1]{1,0:T(1,128)S(6)} %copy.19.count, f32[1024,128]{1,0:T(8,128)S(1)} %inner_body.1.early, f32[1024,128]{1,0:T(8,128)S(1)} %get-tuple-element.64.grad, f32[1288,128]{1,0:T(8,128)S(1)} %get-tuple-element.65.pad_rate, ...), custom_call_target="tpu_custom_call" | custom-call | tf_op jit(solution)/shard_map/last_body/pallas_call | solution.py:536
  (16 shorter events, 0.1 us)
Async XLA Ops:
  0.6 14.1 %collective-permute-start.1 = (f32[1024,128]{1,0:T(8,128)}, f32[1024,128]{1,0:T(8,128)S(1)}, u32[]{:S(2)}, u32[]{:S(2)}) collective-permute-start(f32[1024,128]{1,0:T(8,128)} %bitcast.12), channel_id=1, source_target_pairs={{0,1},{1,0},{2,3},{3,2},{4,5},{5,4},{6,7},{7,6},{8,9},{9,8},{10,11... | collective-permute-start | bytes 1572872 | tf_op jit(solution)/shard_map/ppermute | solution.py:25
  1.1 15.0 %collective-permute-start = (f32[1024,128]{1,0:T(8,128)}, f32[1024,128]{1,0:T(8,128)S(1)}, u32[]{:S(2)}, u32[]{:S(2)}) collective-permute-start(f32[1024,128]{1,0:T(8,128)} %bitcast.13), channel_id=1, source_target_pairs={{0,3},{1,2},{2,1},{3,0},{4,7},{5,6},{6,5},{7,4},{8,11},{9,10},{10,... | collective-permute-start | bytes 1572872 | tf_op jit(solution)/shard_map/ppermute | solution.py:25
  5.4 0.8 %copy-start = (f32[1024,128]{1,0:T(8,128)}, f32[1024,128]{1,0:T(8,128)S(1)}, u32[]{:S(2)}) copy-start(f32[1024,128]{1,0:T(8,128)S(1)} %get-tuple-element.56.rate_x) | copy-start | bytes 1572868
  6.1 8.1 %collective-permute-start.3 = (f32[152,128]{1,0:T(8,128)S(1)}, f32[152,128]{1,0:T(8,128)S(1)}, u32[]{:S(2)}, u32[]{:S(2)}) collective-permute-start(f32[152,128]{1,0:T(8,128)S(1)} %get-tuple-element.50), channel_id=1, source_target_pairs={{0,4},{4,0},{8,12},{12,8},{16,20},{20,16},{24,28},{28,24},{1,5},{5... | collective-permute-start | bytes 233480 | tf_op jit(solution)/shard_map/ppermute | solution.py:25
  7.7 7.1 %collective-permute-start.2 = (f32[152,128]{1,0:T(8,128)S(1)}, f32[152,128]{1,0:T(8,128)S(1)}, u32[]{:S(2)}, u32[]{:S(2)}) collective-permute-start(f32[152,128]{1,0:T(8,128)S(1)} %get-tuple-element.49.request), channel_id=1, source_target_pairs={{0,28},{4,8},{8,4},{12,16},{16,12},{20,24},{24,20},{28,0},{1,29},{... | collective-permute-start | bytes 233480 | tf_op jit(solution)/shard_map/ppermute | solution.py:25
  17.2 6.8 %collective-permute-start.5 = (f32[152,128]{1,0:T(8,128)S(1)}, f32[152,128]{1,0:T(8,128)S(1)}, u32[]{:S(2)}, u32[]{:S(2)}) collective-permute-start(f32[152,128]{1,0:T(8,128)S(1)} %pad_maximum_fusion.2), channel_id=1, source_target_pairs={{0,1},{1,0},{2,3},{3,2},{4,5},{5,4},{6,7},{7,6},{8,9},{9,8},{10,11... | collective-permute-start | bytes 233480 | tf_op jit(solution)/shard_map/ppermute | solution.py:25
  17.4 6.6 %collective-permute-start.4 = (f32[152,128]{1,0:T(8,128)S(1)}, f32[152,128]{1,0:T(8,128)S(1)}, u32[]{:S(2)}, u32[]{:S(2)}) collective-permute-start(f32[152,128]{1,0:T(8,128)S(1)} %pad_maximum_fusion.2), channel_id=1, source_target_pairs={{0,3},{1,2},{2,1},{3,0},{4,7},{5,6},{6,5},{7,4},{8,11},{9,10},{10,... | collective-permute-start | bytes 233480 | tf_op jit(solution)/shard_map/ppermute | solution.py:25
  18.8 7.3 %collective-permute-start.7 = (f32[192,128]{1,0:T(8,128)S(1)}, f32[192,128]{1,0:T(8,128)S(1)}, u32[]{:S(2)}, u32[]{:S(2)}) collective-permute-start(f32[192,128]{1,0:T(8,128)S(1)} %pad_maximum_fusion.1), channel_id=1, source_target_pairs={{0,4},{4,0},{8,12},{12,8},{16,20},{20,16},{24,28},{28,24},{1,5},{5... | collective-permute-start | bytes 294920 | tf_op jit(solution)/shard_map/ppermute | solution.py:25
  20.4 5.0 %copy-start.1 = (f32[1024,128]{1,0:T(8,128)S(1)}, f32[1024,128]{1,0:T(8,128)}, u32[]{:S(2)}) copy-start(f32[1024,128]{1,0:T(8,128)} %copy-done) | copy-start | bytes 1572868
  20.4 7.6 %collective-permute-start.6 = (f32[192,128]{1,0:T(8,128)S(1)}, f32[192,128]{1,0:T(8,128)S(1)}, u32[]{:S(2)}, u32[]{:S(2)}) collective-permute-start(f32[192,128]{1,0:T(8,128)S(1)} %pad_maximum_fusion), channel_id=1, source_target_pairs={{0,28},{4,8},{8,4},{12,16},{16,12},{20,24},{24,20},{28,0},{1,29},{... | collective-permute-start | bytes 294920 | tf_op jit(solution)/shard_map/ppermute | solution.py:25
  29.3 4.3 %collective-permute-start.8 = (f32[160,128]{1,0:T(8,128)S(1)}, f32[160,128]{1,0:T(8,128)S(1)}, u32[]{:S(2)}, u32[]{:S(2)}) collective-permute-start(f32[160,128]{1,0:T(8,128)S(1)} %get-tuple-element.71), channel_id=1, source_target_pairs={{0,3},{1,2},{2,1},{3,0},{4,7},{5,6},{6,5},{7,4},{8,11},{9,10},{10,... | collective-permute-start | bytes 245768 | tf_op jit(solution)/shard_map/ppermute | solution.py:25
  29.4 4.2 %collective-permute-start.9 = (f32[160,128]{1,0:T(8,128)S(1)}, f32[160,128]{1,0:T(8,128)S(1)}, u32[]{:S(2)}, u32[]{:S(2)}) collective-permute-start(f32[160,128]{1,0:T(8,128)S(1)} %get-tuple-element.72), channel_id=1, source_target_pairs={{0,1},{1,0},{2,3},{3,2},{4,5},{5,4},{6,7},{7,6},{8,9},{9,8},{10,11... | collective-permute-start | bytes 245768 | tf_op jit(solution)/shard_map/ppermute | solution.py:25
  33.7 8.5 %collective-permute-start.10 = (f32[144,128]{1,0:T(8,128)S(1)}, f32[144,128]{1,0:T(8,128)S(1)}, u32[]{:S(2)}, u32[]{:S(2)}) collective-permute-start(f32[144,128]{1,0:T(8,128)S(1)} %pad_maximum_fusion.3), channel_id=1, source_target_pairs={{0,28},{4,8},{8,4},{12,16},{16,12},{20,24},{24,20},{28,0},{1,29},{... | collective-permute-start | bytes 221192 | tf_op jit(solution)/shard_map/ppermute | solution.py:25
  37.3 4.9 %collective-permute-start.11 = (f32[144,128]{1,0:T(8,128)S(1)}, f32[144,128]{1,0:T(8,128)S(1)}, u32[]{:S(2)}, u32[]{:S(2)}) collective-permute-start(f32[144,128]{1,0:T(8,128)S(1)} %pad_maximum_fusion.4), channel_id=1, source_target_pairs={{0,4},{4,0},{8,12},{12,8},{16,20},{20,16},{24,28},{28,24},{1,5},{5... | collective-permute-start | bytes 221192 | tf_op jit(solution)/shard_map/ppermute | solution.py:25
  37.3 3.7 %collective-permute-start.12 = (f32[96,128]{1,0:T(8,128)S(1)}, f32[96,128]{1,0:T(8,128)S(1)}, u32[]{:S(2)}, u32[]{:S(2)}) collective-permute-start(f32[96,128]{1,0:T(8,128)S(1)} %get-tuple-element.80), channel_id=1, source_target_pairs={{0,3},{1,2},{2,1},{3,0},{4,7},{5,6},{6,5},{7,4},{8,11},{9,10},{10,... | collective-permute-start | bytes 147464 | tf_op jit(solution)/shard_map/ppermute | solution.py:25
  37.8 3.2 %collective-permute-start.13 = (f32[96,128]{1,0:T(8,128)S(1)}, f32[96,128]{1,0:T(8,128)S(1)}, u32[]{:S(2)}, u32[]{:S(2)}) collective-permute-start(f32[96,128]{1,0:T(8,128)S(1)} %get-tuple-element.81), channel_id=1, source_target_pairs={{0,1},{1,0},{2,3},{3,2},{4,5},{5,4},{6,7},{7,6},{8,9},{9,8},{10,11... | collective-permute-start | bytes 147464 | tf_op jit(solution)/shard_map/ppermute | solution.py:25

commit v6 on v5

--- a/solution.py
+++ b/solution.py
@@ -200,15 +200,15 @@
 
 
 def begin_body(
-    heading, target, source, field, cotan, rate_x, rate_y,
-    order, send_a, send_b, field_out, cotan_out, rate_x_out, rate_y_out,
-    heading_in, target_in, source_in, used, sems, *, planes, extent_x,
+    heading, target, source, field, cotan, rate_x, rate_y, blocks, count,
+    order, send_a, send_b, value_s, late_a, late_b, pairs, picked, field_out, cotan_out, rate_y_out,
+    rate_x_out, blocks_in, flat, square, heading_in, target_in, source_in, used, sems, *, planes, extent_x,
 ):
-    pairs = (
+    moves = (
         (heading, heading_in), (target, target_in), (source, source_in),
-        (cotan, cotan_out), (rate_x, rate_x_out), (field, field_out), (rate_y, rate_y_out),
-    )
-    copies = [pltpu.make_async_copy(a, b, sems.at[number]) for number, (a, b) in enumerate(pairs)]
+        (blocks, blocks_in), (field, field_out), (cotan, cotan_out), (rate_x, rate_x_out), (rate_y, rate_y_out),
+    )
+    copies = [pltpu.make_async_copy(a, b, sems.at[number]) for number, (a, b) in enumerate(moves)]
     for copy in copies:
         copy.start()
     parity_x, parity_y = parities()
@@ -218,7 +218,8 @@
     for copy in copies[:3]:
         copy.wait()
     asked = jnp.zeros((8, 128), jnp.int32)
-    for slot in range(heading.shape[0]):
+    slots = heading.shape[0]
+    for slot in range(slots):
         toward = heading_in[slot]
         across = (toward >= 3).astype(jnp.int32) + (toward >= 6).astype(jnp.int32)
         ex = (across - 1) * (1 - 2 * parity_x)
@@ -231,35 +232,48 @@
         order[0, spot] = slot
         order[1, spot] = source_in[slot]
         asked = jnp.where(lane == spot, target_in[slot], asked)
+    for out in (send_a, send_b):
+        out[0:8, :] = asked.astype(jnp.float32)
+    copies[3].wait()
+    half = TILE // 2
+    for row in range(half):
+        flat[pl.ds(row, slots, half), :] = blocks_in[:, row * 128 : (row + 1) * 128].astype(jnp.float32)
+    copies[4].wait()
+    total = count[0, 0]
+    size = 3 * planes
+    first_half = lanes((half, 128)) < TILE
+    for number, (lx, ly, side) in enumerate(LABELS):
+        one = flat[pl.ds(pl.multiple_of(order[0, 2 * number] * half, 8), half), :]
+        two = flat[pl.ds(pl.multiple_of(order[0, 2 * number + 1] * half, 8), half), :]
+        square[number, pl.ds(0, half, 2), :] = jnp.where(first_half, one, 0.0)
+        square[number, pl.ds(1, half, 2), :] = jnp.where(first_half, roll(one, TILE), 0.0)
+        square[number, pl.ds(TILE, half, 2), :] = jnp.where(first_half, 0.0, roll(two, TILE))
+        square[number, pl.ds(TILE + 1, half, 2), :] = jnp.where(first_half, 0.0, two)
+        joined = square[number].astype(jnp.bfloat16)
+        pairs[number] = joined
+        tiles = tile_pair(field_out, order[1, 2 * number], order[1, 2 * number + 1], planes, extent_x)
+        picked[number] = tiles
+        value = pair_dot(alive_lanes(tiles, order, number, total), joined, 1)
+        first = (0 if lx == S else 8 + 2 * size) + (ly * 2 + side) * planes
+        (send_a, send_b, value_s)[lx][first : first + planes, :] = value
     even = parity_x == 0
     high = extent_x - 3
-    size = 3 * planes
-    for out in (send_a, send_b):
-        out[0:8, :] = asked.astype(jnp.float32)
     for number, ref in enumerate((cotan_out, rate_x_out, field_out)):
-        copies[3 + number].wait()
-        first = 8 + number * size
-        send_a[first : first + size, :] = edge_rows(ref, jnp.where(even, 0, high), planes, extent_x)
-        send_b[first : first + size, :] = edge_rows(ref, jnp.where(even, high, 0), planes, extent_x)
-    copies[6].wait()
-
-
-def extend_body(order, count, field, cotan, rate_y, blocks, pairs, picked, packs, value_a, value_b, value_s, *, planes, extent_x):
+        if number < 2:
+            copies[5 + number].wait()
+        to_a = edge_rows(ref, jnp.where(even, 0, high), planes, extent_x)
+        to_b = edge_rows(ref, jnp.where(even, high, 0), planes, extent_x)
+        if number < 2:
+            spot = slice(8 + number * size, 8 + (number + 1) * size)
+            send_a[spot, :], send_b[spot, :] = to_a, to_b
+        else:
+            late_a[...], late_b[...] = to_a, to_b
+    copies[7].wait()
+
+
+def edges_body(field, cotan, rate_y, packs, *, planes, extent_x):
     for number, ref in enumerate((rate_y, field, cotan)):
         packs[number * extent_x : (number + 1) * extent_x, :] = edge_pack(ref, planes, extent_x)
-    total = count[0, 0]
-    for number, (lx, ly, half) in enumerate(LABELS):
-        one_block, two_block = blocks[order[0, 2 * number]], blocks[order[0, 2 * number + 1]]
-        zero = jnp.zeros_like(one_block)
-        joined = jnp.concatenate(
-            [jnp.concatenate([one_block, zero], axis=1), jnp.concatenate([zero, two_block], axis=1)], axis=0
-        )
-        pairs[number] = joined
-        tiles = tile_pair(field, order[1, 2 * number], order[1, 2 * number + 1], planes, extent_x)
-        picked[number] = tiles
-        first = (ly * 2 + half) * planes
-        value = pair_dot(alive_lanes(tiles, order, number, total), joined, 1)
-        (value_a, value_b, value_s)[lx][first : first + planes, :] = value
 
 
 def merge_lists(a, b, s):
@@ -274,7 +288,7 @@
     copy.wait()
 
 
-def serve_body(request, got_a, got_b, cotan_a, cotan_b, cotan, out_a, out_b, out_s, list_ref, asked, sem, *, planes, extent_x):
+def serve_body(request, got_b, got_a, cotan_a, cotan_b, cotan, out_a, out_b, out_s, list_ref, asked, sem, *, planes, extent_x):
     to_scalars(merge_lists(got_a[0:8], got_b[0:8], request[0:8]), list_ref, asked, sem)
     for lx, ly, half in LABELS:
         at = ly * 12 + lx * ROUTE_MOST + 2 * half
@@ -344,7 +358,7 @@
 def push_body(field, pad_rate, rate_y, edge_rate, rows_a, rows_b, packs, packs_a, packs_b, section, pad, flux_ref, *, planes, extent_x):
     parity_x, parity_y = parities()
     even_x, even_y = parity_x == 0, parity_y == 0
-    first = 8 + 6 * planes
+    first = 6 * planes
     fill_padded(pad, field, rows_a[first : first + 3 * planes], rows_b[first : first + 3 * planes], even_x, planes, extent_x)
     second = slice(24 + extent_x, 24 + 2 * extent_x)
     halo = edge_join(packs_a[second], packs_b[second], even_y)
@@ -445,9 +459,9 @@
 def section_body(order, asked, early, returned, x_a, x_b, y_a, y_b, own, section, first_outer, *, planes, extent_x):
     for number, (lx, ly, half) in enumerate(LABELS):
         if ly == S:
-            came = rows_at((x_a, x_b, own)[lx], (0 if lx == S else 6 * planes) + (S * 2 + half) * planes, planes)
+            came = rows_at((x_a, x_b, own)[lx], (0 if lx == S else 8 + 6 * planes) + (S * 2 + half) * planes, planes)
         else:
-            came = rows_at((y_a, y_b)[ly], ((1, 2, 0)[lx] * 2 + half) * planes, planes)
+            came = rows_at((y_a, y_b)[ly], 24 + 2 * extent_x + ((1, 2, 0)[lx] * 2 + half) * planes, planes)
         came = TIME_STEP * came
         at = ly * 12 + lx * ROUTE_MOST + 2 * half
         add_tile_pair(section, asked[ly, at], asked[ly, at + 1], came, planes, extent_x)
@@ -457,21 +471,46 @@
         first_outer[number] = outer((0.5 * TIME_STEP) * returned[number], picked)
 
 
+def finish(number, back, order, pairs, first_outer, picked, total, work, blocks, planes, extent_x):
+    pulled = TIME_STEP * pair_dot(back, pairs[number], 0)
+    add_tile_pair(total, order[1, 2 * number], order[1, 2 * number + 1], pulled, planes, extent_x)
+    work[number] = first_outer[number] + outer(TIME_STEP * back, picked[number])
+    half_lane = lanes((TILE // 2, 128)) < TILE
+    for which in range(2):
+        slot = order[0, 2 * number + which]
+        even_rows = work[number, pl.ds(which * TILE, TILE // 2, 2), :]
+        odd_rows = work[number, pl.ds(which * TILE + 1, TILE // 2, 2), :]
+        if which == 0:
+            merged = jnp.where(half_lane, even_rows, roll(odd_rows, TILE))
+        else:
+            merged = jnp.where(half_lane, roll(even_rows, TILE), odd_rows)
+        blocks[pl.ds(pl.multiple_of(slot * (TILE // 2), 8), TILE // 2), :] = merged
+
+
+def rest_body(
+    order, count, early, rate_edge, packs, own, y_a, y_b, pairs, first_outer, picked, total, blocks, work, *, planes, extent_x,
+):
+    even_y = parities()[1] == 0
+    halo = edge_join(y_a[0:extent_x], y_b[0:extent_x], even_y)
+    edges = adjoint_edges(own[0:extent_x], halo, part(packs, 0, extent_x), rate_edge[...])
+    lane = lanes((extent_x, 128))
+    for z in range(planes):
+        spot = pl.ds(z * extent_x, extent_x)
+        rim = roll(edges, 125 - 8 * z)
+        total[spot, :] = total[spot, :] + TIME_STEP * jnp.where((lane < 3) | (lane >= 125), rim, 0.0)
+    for number, (lx, ly, half) in enumerate(LABELS):
+        if lx == S:
+            back = rows_at((y_a, y_b, own)[ly], extent_x + (S * 2 + half) * planes, planes)
+            back = alive_lanes(back, order, number, count[0, 0])
+            finish(number, back, order, pairs, first_outer, picked, total, work, blocks, planes, extent_x)
+
+
 def last_body(
-    order, count, early, grad, pad_rate, edge_rate, packs, own, y_a, y_b, x_a, x_b, pairs, first_outer, picked, out, out_blocks, work, total, blocks, sems,
+    order, count, early, blocks_early, grad, pad_rate, x_b, x_a, pairs, first_outer, picked, out, out_blocks, total, blocks, work, sems,
     *, planes, extent_x,
 ):
-    parity_x, parity_y = parities()
-    even_x, even_y = parity_x == 0, parity_y == 0
+    even_x = parities()[0] == 0
     size = 3 * planes
-    halo = edge_join(y_a[0:extent_x], y_b[0:extent_x], even_y)
-    edges = adjoint_edges(own[0:extent_x], halo, part(packs, 0, extent_x), edge_rate[...])
-
-    for z in range(planes):
-        spot = pl.ds(z * extent_x, extent_x)
-        rim = roll(edges, 125 - 8 * z)
-        lane = lanes(rim.shape)
-        total[spot, :] = early[spot, :] + TIME_STEP * jnp.where((lane < 3) | (lane >= 125), rim, 0.0)
     low_rows = [jnp.where(even_x, x_a[j * planes : (j + 1) * planes], x_b[j * planes : (j + 1) * planes]) for j in range(3)]
     high_rows = [jnp.where(even_x, x_b[j * planes : (j + 1) * planes], x_a[j * planes : (j + 1) * planes]) for j in range(3)]
     first_cell = row_of(grad, 0, planes, extent_x)
@@ -491,32 +530,14 @@
                     added = added + combine(*faces[j], k)
             spot = pl.ds(cell, planes, extent_x)
             total[spot, :] = total[spot, :] + TIME_STEP * added
-    backs = []
-    for number, label in enumerate(LABELS):
-        lx, ly, half = label
-        if lx == S:
-            back = rows_at((y_a, y_b, own)[ly], extent_x + (S * 2 + half) * planes, planes)
-        else:
+    for number, (lx, ly, half) in enumerate(LABELS):
+        if lx != S:
             back = rows_at((x_a, x_b)[lx], size + ((1, 2, 0)[ly] * 2 + half) * planes, planes)
-        back = alive_lanes(back, order, number, count[0, 0])
-        backs.append(back)
-        pulled = TIME_STEP * pair_dot(back, pairs[number], 0)
-        add_tile_pair(total, order[1, 2 * number], order[1, 2 * number + 1], pulled, planes, extent_x)
+            back = alive_lanes(back, order, number, count[0, 0])
+            finish(number, back, order, pairs, first_outer, picked, total, work, blocks, planes, extent_x)
     copies = [pltpu.make_async_copy(total, out, sems.at[0]), pltpu.make_async_copy(blocks, out_blocks, sems.at[1])]
-    copies[0].start()
-    half_lane = lanes((TILE // 2, 128)) < TILE
-    for number, back in enumerate(backs):
-        work[number] = first_outer[number] + outer(TIME_STEP * back, picked[number])
-        for which in range(2):
-            slot = order[0, 2 * number + which]
-            even_rows = work[number, pl.ds(which * TILE, TILE // 2, 2), :]
-            odd_rows = work[number, pl.ds(which * TILE + 1, TILE // 2, 2), :]
-            if which == 0:
-                merged = jnp.where(half_lane, even_rows, roll(odd_rows, TILE))
-            else:
-                merged = jnp.where(half_lane, roll(even_rows, TILE), odd_rows)
-            blocks[pl.ds(pl.multiple_of(slot * (TILE // 2), 8), TILE // 2), :] = merged
-    copies[1].start()
+    for copy in copies:
+        copy.start()
     for copy in copies:
         copy.wait()
 
@@ -561,33 +582,42 @@
     pad_scratch = pltpu.VMEM(*padded)
     whole = ((cells, 128), f32, "v")
 
+    cotan_a = exchange(cotan, "gy", A)
     cotan_b = exchange(cotan, "gy", B)
-    cotan_a = exchange(cotan, "gy", A)
-    order, send_a, send_b, field, cotan, rate_x, rate_y = call(
+    head = 8 + 2 * size
+    head = 8 + 2 * size
+    sent = ((head + 2 * size, 128), f32, "v")
+    tall = ((slots * TILE // 2, 128), f32)
+    order, send_a, send_b, value_s, late_a, late_b, pairs, picked, field, cotan, rate_y = call(
         begin_body,
-        [("h", [v.reshape(slots) for v in (dest_offset, dest_tile, source_tile)] + [field, cotan, rate_x, rate_y])],
-        [((2, slots), i32, "s")] + [((8 + 3 * size, 128), f32, "v")] * 2 + [whole] * 4,
-        scratch=[pltpu.SMEM((slots,), i32)] * 3 + [pltpu.SMEM((9,), i32), pltpu.SemaphoreType.DMA((7,))],
+        [("h", [v.reshape(slots) for v in (dest_offset, dest_tile, source_tile)] + [field, cotan, rate_x, rate_y, blocks.reshape(slots, TILE * TILE)]),
+         ("r", [tile_count])],
+        [((2, slots), i32, "s"), sent, sent, box] + [((size, 128), f32, "v")] * 2
+        + [((pair_total, 128, 128), jnp.bfloat16, "v"), ((pair_total, planes, 128), f32, "v")] + [whole] * 3,
+        scratch=[pltpu.VMEM((cells, 128), f32), pltpu.VMEM((slots, TILE * TILE), jnp.bfloat16), pltpu.VMEM(*tall), pltpu.VMEM((pair_total, 128, 128), f32)]
+        + [pltpu.SMEM((slots,), i32)] * 3 + [pltpu.SMEM((9,), i32), pltpu.SemaphoreType.DMA((8,))],
         **sizes,
     )
     request = send_a
     rows_a = exchange(send_a, "gx", A)
     rows_b = exchange(send_b, "gx", B)
-    pairs, picked, packs, value_a, value_b, value_s = call(
-        extend_body, [("s", [order]), ("r", [tile_count]), ("v", [field, cotan, rate_y, blocks.reshape(slots, TILE, TILE)])],
-        [((pair_total, 128, 128), jnp.bfloat16, "v"), ((pair_total, planes, 128), f32, "v"), ((3 * extent_x, 128), f32, "v")]
-        + [box] * 3, **sizes,
-    )
+    (packs,) = call(edges_body, [("v", [field, cotan, rate_y])], [((3 * extent_x, 128), f32, "v")], **sizes)
+
+    def onward(own, a, b, own_first, first, m):
+        cut = lambda v, start: v[start + m * 2 * planes : start + (m + 1) * 2 * planes]
+        return [cut(own, own_first), cut(a, first), cut(b, first)]
+
+    wide = lambda m: jnp.concatenate(
+        [request[:8], rows_a[:8], rows_b[:8], packs[: 2 * extent_x]] + onward(value_s, rows_a, rows_b, 0, head, m), axis=0
+    )
+    packs_b = exchange(wide(B), "gy", B)
+    packs_a = exchange(wide(A), "gy", A)
     tiles_a, tiles_b, tiles_s = call(
-        serve_body, [("v", [request, rows_a, rows_b, cotan_a, cotan_b, cotan])], [box, box, box],
+        serve_body, [("v", [request, rows_b, rows_a, cotan_a, cotan_b, cotan])], [box, box, box],
         scratch=(pltpu.VMEM((8, 128), i32), pltpu.SMEM((8, 128), i32), pltpu.SemaphoreType.DMA(())), **sizes,
     )
-    wide = jnp.concatenate([request[:8], rows_a[:8], rows_b[:8], packs[: 2 * extent_x]], axis=0)
-    wide, tiles_a, tiles_b = lax.optimization_barrier((wide, tiles_a, tiles_b))
-    x_b = exchange(jnp.concatenate([tiles_b, value_b], axis=0), "gx", B)
-    x_a = exchange(jnp.concatenate([tiles_a, value_a], axis=0), "gx", A)
-    packs_b = exchange(wide, "gy", B)
-    packs_a = exchange(wide, "gy", A)
+    x_b = exchange(jnp.concatenate([tiles_b, late_b], axis=0), "gx", B)
+    x_a = exchange(jnp.concatenate([tiles_a, late_a], axis=0), "gx", A)
     early, edge_rate, asked = call(
         pull_y_body, [("v", [cotan, cotan_a, cotan_b, rate_y, packs, request, rows_a, rows_b, packs_a, packs_b])],
         [whole, ((extent_x, 128), f32, "v"), ((8, 128), i32, "s")],
@@ -603,37 +633,35 @@
         alias={3: 0}, **sizes,
     )
 
-    def onward(own, a, b, own_first, first, m):
-        cut = lambda v, start: v[start + m * 2 * planes : start + (m + 1) * 2 * planes]
-        return [cut(own, own_first), cut(a, first), cut(b, first)]
-
-    ext_a = jnp.concatenate(onward(value_s, x_a, x_b, 0, 2 * size, A), axis=0)
-    ext_b = jnp.concatenate(onward(value_s, x_a, x_b, 0, 2 * size, B), axis=0)
-    send_a, send_b, field, ext_a, ext_b = lax.optimization_barrier((send_a, send_b, field, ext_a, ext_b))
+    send_a, send_b, field = lax.optimization_barrier((send_a, send_b, field))
     last_y_b = exchange(send_b, "gy", B)
     last_y_a = exchange(send_a, "gy", A)
-    ext_b = exchange(ext_b, "gy", B)
-    ext_a = exchange(ext_a, "gy", A)
     (pushed,) = call(
-        push_body, [("v", [field, pad_rate, rate_y, edge_rate, rows_a, rows_b, packs, packs_a, packs_b])],
+        push_body, [("v", [field, pad_rate, rate_y, edge_rate, x_a, x_b, packs, packs_a, packs_b])],
         [whole], scratch=(pad_scratch,) * 2, **sizes,
     )
     last_y_a, last_y_b, pushed = lax.optimization_barrier((last_y_a, last_y_b, pushed))
+    last_x_a = exchange(jnp.concatenate([edge_a] + onward(send_s, last_y_a, last_y_b, extent_x, extent_x, A), axis=0), "gx", A)
     last_x_b = exchange(jnp.concatenate([edge_b] + onward(send_s, last_y_a, last_y_b, extent_x, extent_x, B), axis=0), "gx", B)
-    last_x_a = exchange(jnp.concatenate([edge_a] + onward(send_s, last_y_a, last_y_b, extent_x, extent_x, A), axis=0), "gx", A)
     (inner,) = call(
         inner_body, [("v", [cotan, grad, pad_rate, rate_y])], [whole], scratch=(pad_scratch,) * 3, **sizes,
     )
     section, first_outer = call(
-        section_body, [("s", [order, asked]), ("v", [pushed, returned, x_a, x_b, ext_a, ext_b, value_s])],
+        section_body, [("s", [order, asked]), ("v", [pushed, returned, rows_a, rows_b, packs_a, packs_b, value_s])],
         [whole, ((pair_total, 128, 128), f32, "v")], alias={2: 0}, **sizes,
     )
-    grad_level_set, grad_blocks = call(
+    work = pltpu.VMEM((pair_total, 128, 128), f32)
+    flat = ((slots * TILE // 2, 128), f32)
+    total, early_blocks = call(
+        rest_body,
+        [("s", [order]), ("r", [tile_count]), ("v", [inner, edge_rate, packs, send_s, last_y_a, last_y_b, pairs, first_outer, picked])],
+        [whole, flat + ("v",)], scratch=(work,), alias={2: 0}, **sizes,
+    )
+    grad_level_set, grad_blocks, _, _ = call(
         last_body,
-        [("s", [order]), ("r", [tile_count]), ("v", [inner, grad, pad_rate, edge_rate, packs, send_s, last_y_a, last_y_b, last_x_a, last_x_b, pairs, first_outer, picked])],
-        [((cells, 128), f32, "h"), ((slots * TILE // 2, 128), f32, "h")],
-        scratch=(pltpu.VMEM((pair_total, 128, 128), f32), pltpu.VMEM((cells, 128), f32),
-                 pltpu.VMEM((slots * TILE // 2, 128), f32), pltpu.SemaphoreType.DMA((2,))), **sizes,
+        [("s", [order]), ("r", [tile_count]), ("v", [total, early_blocks, grad, pad_rate, last_x_b, last_x_a, pairs, first_outer, picked])],
+        [((cells, 128), f32, "h"), flat + ("h",), whole, flat + ("v",)],
+        scratch=(work, pltpu.SemaphoreType.DMA((2,))), alias={2: 2, 3: 3}, **sizes,
     )
     return (grad_level_set.reshape(planes, extent_x, extent_y), grad_blocks.reshape(1, 1, slots, TILE * TILE))
 

time: 44.7 us -> 41.1 us (0.919)
  local copies, waits for them, and re-layouts: 2.39 us -> 0.05 us
  starting transfers between devices: 20.4 us -> 18.6 us
  Pallas kernels: 12.6 us -> 13.8 us
  waiting for transfers between devices: 7.53 us -> 7.03 us
    ppermute x14 -> x12, starting transfers between devices: 20.4 us -> 18.6 us  [exchange(): return lax.ppermute(block, axis, matching(lax.axis_size(axis), which))]
    reshape x1 -> x0, local copies, waits for them, and re-layouts: 1.56 us -> none  [shards(): blocks.reshape(slots, TILE, TILE)]
    pallas_call x10 -> x11, Pallas kernels: 12.6 us -> 13.8 us  [call(): pl.pallas_call(functools.partial(body, **sizes), out_shape=tuple(shapes),...]
    unnamed x4 -> x10, local copies, waits for them, and re-layouts: 0.79 us -> 0.04 us
    ppermute x14 -> x12, waiting for transfers between devices: 7.53 us -> 7.03 us  [exchange(): return lax.ppermute(block, axis, matching(lax.axis_size(axis), which))]
  transfers between devices with their start and end apart: 14 -> 12, of which waited for: 5 -> 4; matrix products, arithmetic and copies ran while one was open for 4% -> 0% of each run, Pallas kernels for 18% -> 26%
where the time goes in v6:
time: 41.1 us; the launch traced here: 40.9 us
  starting transfers between devices  18.6 us (45%)
  Pallas kernels  13.8 us (34%)
  waiting for transfers between devices  7.03 us (17%)
  between operations  1.47 us (4%)
    ppermute x12, starting transfers between devices, exchange(): return lax.ppermute(block, axis, matching(lax.axis_size(axis), which))  18.6 us
    pallas_call x11, Pallas kernels, call(): pl.pallas_call(functools.partial(body, **sizes), out_shape=tuple(shapes),...  13.8 us
    ppermute x12, waiting for transfers between devices, exchange(): return lax.ppermute(block, axis, matching(lax.axis_size(axis), which))  7.03 us
  transfers between devices with their start and end apart: 12, of which 4 were waited for; matrix products, arithmetic and copies ran while one was open for 0% of the time, Pallas kernels for 26%

profile of v6, /device:TPU:0, one launch (start us, length us, event | category | flops | bytes accessed | tf_op | source)
XLA Modules:
  0.0 40.9 jit_solution(9169709349528886908)
XLA Ops:
  0.6 0.5 %collective-permute-start.1 = (f32[1024,128]{1,0:T(8,128)}, f32[1024,128]{1,0:T(8,128)S(1)}, u32[]{:S(2)}, u32[]{:S(2)}) collective-permute-start(f32[1024,128]{1,0:T(8,128)} %bitcast.14), channel_id=1, source_target_pairs={{0,1},{1,0},{2,3},{3,2},{4,5},{5,4},{6,7},{7,6},{8,9},{9,8},{10,11... | collective-permute-start | bytes 1572872 | tf_op jit(solution)/shard_map/ppermute | solution.py:25
  1.2 2.6 %collective-permute-start = (f32[1024,128]{1,0:T(8,128)}, f32[1024,128]{1,0:T(8,128)S(1)}, u32[]{:S(2)}, u32[]{:S(2)}) collective-permute-start(f32[1024,128]{1,0:T(8,128)} %bitcast.15), channel_id=1, source_target_pairs={{0,3},{1,2},{2,1},{3,0},{4,7},{5,6},{6,5},{7,4},{8,11},{9,10},{10,... | collective-permute-start | bytes 1572872 | tf_op jit(solution)/shard_map/ppermute | solution.py:25
  4.4 2.8 %begin_body.1 = (s32[2,36]{1,0:T(2,128)S(4)}, f32[200,128]{1,0:T(8,128)S(1)}, f32[200,128]{1,0:T(8,128)S(1)}, f32[96,128]{1,0:T(8,128)S(1)}, f32[48,128]{1,0:T(8...) custom-call(s32[36]{0:T(128)} %bitcast.18, ...), custom_call_target="tpu_custom_call" | custom-call | tf_op jit(solution)/shard_map/begin_body/pallas_call | solution.py:557
  7.2 1.6 %collective-permute-start.3 = (f32[200,128]{1,0:T(8,128)S(1)}, f32[200,128]{1,0:T(8,128)S(1)}, u32[]{:S(2)}, u32[]{:S(2)}) collective-permute-start(f32[200,128]{1,0:T(8,128)S(1)} %get-tuple-element.44), channel_id=1, source_target_pairs={{0,4},{4,0},{8,12},{12,8},{16,20},{20,16},{24,28},{28,24},{1,5},{5... | collective-permute-start | bytes 307208 | tf_op jit(solution)/shard_map/ppermute | solution.py:25
  8.8 3.5 %collective-permute-start.2 = (f32[200,128]{1,0:T(8,128)S(1)}, f32[200,128]{1,0:T(8,128)S(1)}, u32[]{:S(2)}, u32[]{:S(2)}) collective-permute-start(f32[200,128]{1,0:T(8,128)S(1)} %get-tuple-element.43.request), channel_id=1, source_target_pairs={{0,28},{4,8},{8,4},{12,16},{16,12},{20,24},{24,20},{28,0},{1,29},{... | collective-permute-start | bytes 307208 | tf_op jit(solution)/shard_map/ppermute | solution.py:25
  12.4 0.5 %edges_body.1.packs = f32[192,128]{1,0:T(8,128)S(1)} custom-call(f32[1024,128]{1,0:T(8,128)S(1)} %get-tuple-element.63.field, f32[1024,128]{1,0:T(8,128)S(1)} %get-tuple-element.40.cotan, f32[1024,128]{1,0:T(8,128)S(1)} %get-tuple-element.41.rate_y), custom_call_target="tpu_custom_call" | custom-call | tf_op jit(solution)/shard_map/edges_body/pallas_call | solution.py:557
  12.8 3.3 %collective-permute-done.2.got_a.rows_a.x_a = f32[200,128]{1,0:T(8,128)S(1)} collective-permute-done((f32[200,128]{1,0:T(8,128)S(1)}, f32[200,128]{1,0:T(8,128)S(1)}, u32[]{:S(2)}, u32[]{:S(2)}) %collective-permute-start.2) | collective-permute-done | bytes 102432 | tf_op jit(solution)/shard_map/ppermute | solution.py:25
  16.2 0.0 collective-permute-done.3.got_b.rows_b.x_b
  16.3 0.1 collective-permute-start.5
  16.3 0.7 %collective-permute-start.4 = (f32[248,128]{1,0:T(8,128)S(1)}, f32[248,128]{1,0:T(8,128)S(1)}, u32[]{:S(2)}, u32[]{:S(2)}) collective-permute-start(f32[248,128]{1,0:T(8,128)S(1)} %get-tuple-element.81), channel_id=1, source_target_pairs={{0,3},{1,2},{2,1},{3,0},{4,7},{5,6},{6,5},{7,4},{8,11},{9,10},{10,... | collective-permute-start | bytes 380936 | tf_op jit(solution)/shard_map/ppermute | solution.py:25
  17.0 0.0 collective-permute-done.1.cotan_b
  17.0 0.0 collective-permute-done.cotan_a
  17.0 1.0 %serve_body.1 = (f32[96,128]{1,0:T(8,128)S(1)}, f32[96,128]{1,0:T(8,128)S(1)}, f32[96,128]{1,0:T(8,128)S(1)}) custom-call(f32[200,128]{1,0:T(8,128)S(1)} %get-tuple-element.43.request, f32[200,128]{1,0:T(8,128)S(1)} %collective-permute-done.3.got_b.rows_b.x_b, f32[200,128]{1,0:T(8,128)S(1)} %collective-permute-done.2.got_a.rows_a.x_a, ...), custom_call_target="tpu_custom_call" | custom-call | tf_op jit(solution)/shard_map/serve_body/pallas_call | solution.py:557
  18.0 0.7 %collective-permute-start.7 = (f32[144,128]{1,0:T(8,128)S(1)}, f32[144,128]{1,0:T(8,128)S(1)}, u32[]{:S(2)}, u32[]{:S(2)}) collective-permute-start(f32[144,128]{1,0:T(8,128)S(1)} %pad_maximum_fusion.1), channel_id=1, source_target_pairs={{0,4},{4,0},{8,12},{12,8},{16,20},{20,16},{24,28},{28,24},{1,5},{5... | collective-permute-start | bytes 221192 | tf_op jit(solution)/shard_map/ppermute | solution.py:25
  18.7 0.0 copy-start
  18.7 3.6 %collective-permute-start.6 = (f32[144,128]{1,0:T(8,128)S(1)}, f32[144,128]{1,0:T(8,128)S(1)}, u32[]{:S(2)}, u32[]{:S(2)}) collective-permute-start(f32[144,128]{1,0:T(8,128)S(1)} %pad_maximum_fusion), channel_id=1, source_target_pairs={{0,28},{4,8},{8,4},{12,16},{16,12},{20,24},{24,20},{28,0},{1,29},{... | collective-permute-start | bytes 221192 | tf_op jit(solution)/shard_map/ppermute | solution.py:25
  22.3 0.0 collective-permute-done.5.from_b.packs_b.y_b
  22.3 0.0 collective-permute-done.4.from_a.packs_a.y_a
  22.3 1.4 %pull_y_body.1 = (f32[1024,128]{1,0:T(8,128)S(1)}, f32[64,128]{1,0:T(8,128)S(1)}, s32[8,128]{1,0:T(8,128)S(4)}) custom-call(f32[1024,128]{1,0:T(8,128)S(1)} %get-tuple-element.40.cotan, f32[1024,128]{1,0:T(8,128)S(1)} %collective-permute-done.cotan_a, f32[1024,128]{1,0:T(8,128)S(1)} %collective-permute-done.1.cotan_b, ...), custom_call_target="tpu_custom_call" | custom-call | tf_op jit(solution)/shard_map/pull_y_body/pallas_call | solution.py:557
  23.7 0.0 copy-done
  23.8 0.7 %pull_x_body.1 = (f32[1024,128]{1,0:T(8,128)S(1)}, f32[1288,128]{1,0:T(8,128)S(1)}) custom-call(f32[1024,128]{1,0:T(8,128)S(1)} %get-tuple-element.47.early, f32[1024,128]{1,0:T(8,128)S(1)} %get-tuple-element.40.cotan, f32[1024,128]{1,0:T(8,128)S(1)} %bitcast.11, ...), custom_call_target="tpu_custom_call", output_to_operand_aliasing={{0}: (0, {})} | custom-call | tf_op jit(solution)/shard_map/pull_x_body/pallas_call | solution.py:557
  24.4 0.0 collective-permute-done.7.x_b.rows_b
  24.5 1.4 %collective-permute-done.6.x_a.rows_a = f32[144,128]{1,0:T(8,128)S(1)} collective-permute-done((f32[144,128]{1,0:T(8,128)S(1)}, f32[144,128]{1,0:T(8,128)S(1)}, u32[]{:S(2)}, u32[]{:S(2)}) %collective-permute-start.6) | collective-permute-done | bytes 73760 | tf_op jit(solution)/shard_map/ppermute | solution.py:25
  25.8 1.3 %middle_body.1 = (f32[1024,128]{1,0:T(8,128)S(1)}, f32[18,16,128]{2,1,0:T(8,128)S(1)}, f32[160,128]{1,0:T(8,128)S(1)}, f32[160,128]{1,0:T(8,128)S(1)}, f32[160,1...) custom-call(s32[2,36]{1,0:T(2,128)S(4)} %get-tuple-element.39.order, ...), custom_call_target="tpu_custom_call", output_to_operand_aliasing={{0}: (3, {})} | custom-call | tf_op jit(solution)/shard_map/middle_body/pallas_call | solution.py:557
  27.1 0.2 collective-permute-start.8
  27.3 1.5 %collective-permute-start.9 = (f32[160,128]{1,0:T(8,128)S(1)}, f32[160,128]{1,0:T(8,128)S(1)}, u32[]{:S(2)}, u32[]{:S(2)}) collective-permute-start(f32[160,128]{1,0:T(8,128)S(1)} %get-tuple-element.62), channel_id=1, source_target_pairs={{0,1},{1,0},{2,3},{3,2},{4,5},{5,4},{6,7},{7,6},{8,9},{9,8},{10,11... | collective-permute-start | bytes 245768 | tf_op jit(solution)/shard_map/ppermute | solution.py:25
  28.8 1.2 %push_body.1.early = f32[1024,128]{1,0:T(8,128)S(1)} custom-call(f32[1024,128]{1,0:T(8,128)S(1)} %get-tuple-element.63.field, f32[1288,128]{1,0:T(8,128)S(1)} %get-tuple-element.56.pad_rate, f32[1024,128]{1,0:T(8,128)S(1)} %get-tuple-element.41.rate_y, f32[64,128]{1,0:T(8,128)S(1)} %get-tuple-element.57.edge_rate.rate_edge, ...), custom_call_target="tpu_custom_call" | custom-call | tf_op jit(solution)/shard_map/push_body/pallas_call | solution.py:557
  30.0 1.9 %collective-permute-done.8.y_a = f32[160,128]{1,0:T(8,128)S(1)} collective-permute-done((f32[160,128]{1,0:T(8,128)S(1)}, f32[160,128]{1,0:T(8,128)S(1)}, u32[]{:S(2)}, u32[]{:S(2)}) %collective-permute-start.8) | collective-permute-done | bytes 81952 | tf_op jit(solution)/shard_map/ppermute | solution.py:25
  31.9 0.0 collective-permute-done.9.y_b
  31.9 0.1 collective-permute-start.10
  32.0 3.6 %collective-permute-start.11 = (f32[144,128]{1,0:T(8,128)S(1)}, f32[144,128]{1,0:T(8,128)S(1)}, u32[]{:S(2)}, u32[]{:S(2)}) collective-permute-start(f32[144,128]{1,0:T(8,128)S(1)} %pad_maximum_fusion.3), channel_id=1, source_target_pairs={{0,28},{4,8},{8,4},{12,16},{16,12},{20,24},{24,20},{28,0},{1,29},{... | collective-permute-start | bytes 221192 | tf_op jit(solution)/shard_map/ppermute | solution.py:25
  35.6 1.1 %inner_body.1.early = f32[1024,128]{1,0:T(8,128)S(1)} custom-call(f32[1024,128]{1,0:T(8,128)S(1)} %get-tuple-element.40.cotan, f32[1024,128]{1,0:T(8,128)S(1)} %get-tuple-element.55.grad, f32[1288,128]{1,0:T(8,128)S(1)} %get-tuple-element.56.pad_rate, f32[1024,128]{1,0:T(8,128)S(1)} %get-tuple-element.41.rate_y), custom_call_target="tpu_custom_call" | custom-call | tf_op jit(solution)/shard_map/inner_body/pallas_call | solution.py:557
  36.8 1.2 %section_body.1 = (f32[1024,128]{1,0:T(8,128)S(1)}, f32[18,128,128]{2,1,0:T(8,128)S(1)}) custom-call(s32[2,36]{1,0:T(2,128)S(4)} %get-tuple-element.39.order, s32[8,128]{1,0:T(8,128)S(4)} %get-tuple-element.46.asked, f32[1024,128]{1,0:T(8,128)S(1)} %push_body.1.early, ...), custom_call_target="tpu_custom_call", output_to_operand_aliasing={{0}: (2, {})} | custom-call | tf_op jit(solution)/shard_map/section_body/pallas_call | solution.py:557
  38.0 0.7 %rest_body.1 = (f32[1024,128]{1,0:T(8,128)S(1)}, f32[1152,128]{1,0:T(8,128)S(1)}) custom-call(s32[2,36]{1,0:T(2,128)S(4)} %get-tuple-element.39.order, s32[1,1]{1,0:T(1,128)S(6)} %copy.34.count, f32[1024,128]{1,0:T(8,128)S(1)} %inner_body.1.early, f32[64,128]{1,0:T(8,128)S(1)} %get-tuple-element.57.edge_rate.rate_edge, ...), custom_call_target="tpu_custom_call", output_to_operand_aliasing={{0}: (2, {})} | custom-call | tf_op jit(solution)/shard_map/rest_body/pallas_call | solution.py:557
  38.7 0.0 collective-permute-done.10.x_b
  38.7 0.4 %collective-permute-done.11.x_a = f32[144,128]{1,0:T(8,128)S(1)} collective-permute-done((f32[144,128]{1,0:T(8,128)S(1)}, f32[144,128]{1,0:T(8,128)S(1)}, u32[]{:S(2)}, u32[]{:S(2)}) %collective-permute-start.11) | collective-permute-done | bytes 73760 | tf_op jit(solution)/shard_map/ppermute | solution.py:25
  39.1 1.8 %last_body.1 = (f32[1024,128]{1,0:T(8,128)}, f32[1152,128]{1,0:T(8,128)}, f32[1024,128]{1,0:T(8,128)S(1)}, f32[1152,128]{1,0:T(8,128)S(1)}) custom-call(s32[2,36]{1,0:T(2,128)S(4)} %get-tuple-element.39.order, s32[1,1]{1,0:T(1,128)S(6)} %copy.34.count, f32[1024,128]{1,0:T(8,128)S(1)} %get-tuple-element.70.early, ...), custom_call_target="tpu_custom_call", output_to_operand_aliasing={{2}: (2, {}), {3}: (3, {})} | custom-call | tf_op jit(solution)/shard_map/last_body/pallas_call | solution.py:557
  (15 shorter events, 0.1 us)
Async XLA Ops:
  0.6 16.4 %collective-permute-start.1 = (f32[1024,128]{1,0:T(8,128)}, f32[1024,128]{1,0:T(8,128)S(1)}, u32[]{:S(2)}, u32[]{:S(2)}) collective-permute-start(f32[1024,128]{1,0:T(8,128)} %bitcast.14), channel_id=1, source_target_pairs={{0,1},{1,0},{2,3},{3,2},{4,5},{5,4},{6,7},{7,6},{8,9},{9,8},{10,11... | collective-permute-start | bytes 1572872 | tf_op jit(solution)/shard_map/ppermute | solution.py:25
  1.2 15.9 %collective-permute-start = (f32[1024,128]{1,0:T(8,128)}, f32[1024,128]{1,0:T(8,128)S(1)}, u32[]{:S(2)}, u32[]{:S(2)}) collective-permute-start(f32[1024,128]{1,0:T(8,128)} %bitcast.15), channel_id=1, source_target_pairs={{0,3},{1,2},{2,1},{3,0},{4,7},{5,6},{6,5},{7,4},{8,11},{9,10},{10,... | collective-permute-start | bytes 1572872 | tf_op jit(solution)/shard_map/ppermute | solution.py:25
  7.2 8.9 %collective-permute-start.3 = (f32[200,128]{1,0:T(8,128)S(1)}, f32[200,128]{1,0:T(8,128)S(1)}, u32[]{:S(2)}, u32[]{:S(2)}) collective-permute-start(f32[200,128]{1,0:T(8,128)S(1)} %get-tuple-element.44), channel_id=1, source_target_pairs={{0,4},{4,0},{8,12},{12,8},{16,20},{20,16},{24,28},{28,24},{1,5},{5... | collective-permute-start | bytes 307208 | tf_op jit(solution)/shard_map/ppermute | solution.py:25
  8.8 7.4 %collective-permute-start.2 = (f32[200,128]{1,0:T(8,128)S(1)}, f32[200,128]{1,0:T(8,128)S(1)}, u32[]{:S(2)}, u32[]{:S(2)}) collective-permute-start(f32[200,128]{1,0:T(8,128)S(1)} %get-tuple-element.43.request), channel_id=1, source_target_pairs={{0,28},{4,8},{8,4},{12,16},{16,12},{20,24},{24,20},{28,0},{1,29},{... | collective-permute-start | bytes 307208 | tf_op jit(solution)/shard_map/ppermute | solution.py:25
  16.3 6.1 %collective-permute-start.5 = (f32[248,128]{1,0:T(8,128)S(1)}, f32[248,128]{1,0:T(8,128)S(1)}, u32[]{:S(2)}, u32[]{:S(2)}) collective-permute-start(f32[248,128]{1,0:T(8,128)S(1)} %get-tuple-element.80), channel_id=1, source_target_pairs={{0,1},{1,0},{2,3},{3,2},{4,5},{5,4},{6,7},{7,6},{8,9},{9,8},{10,11... | collective-permute-start | bytes 380936 | tf_op jit(solution)/shard_map/ppermute | solution.py:25
  16.3 6.0 %collective-permute-start.4 = (f32[248,128]{1,0:T(8,128)S(1)}, f32[248,128]{1,0:T(8,128)S(1)}, u32[]{:S(2)}, u32[]{:S(2)}) collective-permute-start(f32[248,128]{1,0:T(8,128)S(1)} %get-tuple-element.81), channel_id=1, source_target_pairs={{0,3},{1,2},{2,1},{3,0},{4,7},{5,6},{6,5},{7,4},{8,11},{9,10},{10,... | collective-permute-start | bytes 380936 | tf_op jit(solution)/shard_map/ppermute | solution.py:25
  18.0 6.4 %collective-permute-start.7 = (f32[144,128]{1,0:T(8,128)S(1)}, f32[144,128]{1,0:T(8,128)S(1)}, u32[]{:S(2)}, u32[]{:S(2)}) collective-permute-start(f32[144,128]{1,0:T(8,128)S(1)} %pad_maximum_fusion.1), channel_id=1, source_target_pairs={{0,4},{4,0},{8,12},{12,8},{16,20},{20,16},{24,28},{28,24},{1,5},{5... | collective-permute-start | bytes 221192 | tf_op jit(solution)/shard_map/ppermute | solution.py:25
  18.7 5.0 %copy-start = (f32[16,64,128]{2,1,0:T(8,128)S(1)}, f32[16,64,128]{2,1,0:T(8,128)}, u32[]{:S(2)}) copy-start(f32[16,64,128]{2,1,0:T(8,128)} %param.10) | copy-start | bytes 1572868
  18.7 7.1 %collective-permute-start.6 = (f32[144,128]{1,0:T(8,128)S(1)}, f32[144,128]{1,0:T(8,128)S(1)}, u32[]{:S(2)}, u32[]{:S(2)}) collective-permute-start(f32[144,128]{1,0:T(8,128)S(1)} %pad_maximum_fusion), channel_id=1, source_target_pairs={{0,28},{4,8},{8,4},{12,16},{16,12},{20,24},{24,20},{28,0},{1,29},{... | collective-permute-start | bytes 221192 | tf_op jit(solution)/shard_map/ppermute | solution.py:25
  27.1 4.8 %collective-permute-start.8 = (f32[160,128]{1,0:T(8,128)S(1)}, f32[160,128]{1,0:T(8,128)S(1)}, u32[]{:S(2)}, u32[]{:S(2)}) collective-permute-start(f32[160,128]{1,0:T(8,128)S(1)} %get-tuple-element.61), channel_id=1, source_target_pairs={{0,3},{1,2},{2,1},{3,0},{4,7},{5,6},{6,5},{7,4},{8,11},{9,10},{10,... | collective-permute-start | bytes 245768 | tf_op jit(solution)/shard_map/ppermute | solution.py:25
  27.3 4.6 %collective-permute-start.9 = (f32[160,128]{1,0:T(8,128)S(1)}, f32[160,128]{1,0:T(8,128)S(1)}, u32[]{:S(2)}, u32[]{:S(2)}) collective-permute-start(f32[160,128]{1,0:T(8,128)S(1)} %get-tuple-element.62), channel_id=1, source_target_pairs={{0,1},{1,0},{2,3},{3,2},{4,5},{5,4},{6,7},{7,6},{8,9},{9,8},{10,11... | collective-permute-start | bytes 245768 | tf_op jit(solution)/shard_map/ppermute | solution.py:25
  31.9 6.8 %collective-permute-start.10 = (f32[144,128]{1,0:T(8,128)S(1)}, f32[144,128]{1,0:T(8,128)S(1)}, u32[]{:S(2)}, u32[]{:S(2)}) collective-permute-start(f32[144,128]{1,0:T(8,128)S(1)} %pad_maximum_fusion.2), channel_id=1, source_target_pairs={{0,4},{4,0},{8,12},{12,8},{16,20},{20,16},{24,28},{28,24},{1,5},{5... | collective-permute-start | bytes 221192 | tf_op jit(solution)/shard_map/ppermute | solution.py:25
  32.0 7.1 %collective-permute-start.11 = (f32[144,128]{1,0:T(8,128)S(1)}, f32[144,128]{1,0:T(8,128)S(1)}, u32[]{:S(2)}, u32[]{:S(2)}) collective-permute-start(f32[144,128]{1,0:T(8,128)S(1)} %pad_maximum_fusion.3), channel_id=1, source_target_pairs={{0,28},{4,8},{8,4},{12,16},{16,12},{20,24},{24,20},{28,0},{1,29},{... | collective-permute-start | bytes 221192 | tf_op jit(solution)/shard_map/ppermute | solution.py:25

commit v7 on v6

--- a/solution.py
+++ b/solution.py
@@ -12,6 +12,7 @@
 TIME_STEP = 0.3
 WEIGHTS = (2.0 / 60.0, -13.0 / 60.0, 47.0 / 60.0, 27.0 / 60.0, -3.0 / 60.0)
 PAD = 80
+FLAT = 40
 VMEM_LIMIT = 16 << 20
 
 A, B, S = 0, 1, 2
@@ -57,10 +58,9 @@
 def tile_pair(ref, first, second, planes, extent_x):
     one = row_of(ref, first // 2, planes, extent_x)
     two = row_of(ref, second // 2, planes, extent_x)
-    lane = lanes(one.shape)
-    one = jnp.where(first % 2 == 0, one, roll(one, TILE))
-    two = jnp.where(second % 2 == 1, two, roll(two, TILE))
-    return jnp.where(lane < TILE, one, two)
+    left = lanes(one.shape) < TILE
+    turned = roll(jnp.where(left, two, one), TILE)
+    return jnp.where(left, jnp.where(first % 2 == 0, one, turned), jnp.where(second % 2 == 1, two, turned))
 
 
 def add_tile_pair(ref, first, second, value, planes, extent_x):
@@ -200,13 +200,16 @@
 
 
 def begin_body(
-    heading, target, source, field, cotan, rate_x, rate_y, blocks, count,
+    heading, target, source, field, cotan, rate_y, blocks, cotan_cube, rate_cube, count,
     order, send_a, send_b, value_s, late_a, late_b, pairs, picked, field_out, cotan_out, rate_y_out,
-    rate_x_out, blocks_in, flat, square, heading_in, target_in, source_in, used, sems, *, planes, extent_x,
+    low_c, high_c, low_s, high_s, blocks_in, flat, square, heading_in, target_in, source_in, used, sems, *, planes, extent_x,
 ):
     moves = (
         (heading, heading_in), (target, target_in), (source, source_in),
-        (blocks, blocks_in), (field, field_out), (cotan, cotan_out), (rate_x, rate_x_out), (rate_y, rate_y_out),
+        (blocks, blocks_in), (field, field_out),
+        (cotan_cube.at[:, 0:8, :], low_c), (cotan_cube.at[:, extent_x - 8 : extent_x, :], high_c),
+        (rate_cube.at[:, 0:8, :], low_s), (rate_cube.at[:, extent_x - 8 : extent_x, :], high_s),
+        (cotan, cotan_out), (rate_y, rate_y_out),
     )
     copies = [pltpu.make_async_copy(a, b, sems.at[number]) for number, (a, b) in enumerate(moves)]
     for copy in copies:
@@ -215,7 +218,7 @@
     for label in range(9):
         used[label] = 0
     lane = lanes((8, 128))
-    for copy in copies[:3]:
+    for copy in copies[:4]:
         copy.wait()
     asked = jnp.zeros((8, 128), jnp.int32)
     slots = heading.shape[0]
@@ -234,20 +237,20 @@
         asked = jnp.where(lane == spot, target_in[slot], asked)
     for out in (send_a, send_b):
         out[0:8, :] = asked.astype(jnp.float32)
-    copies[3].wait()
     half = TILE // 2
     for row in range(half):
-        flat[pl.ds(row, slots, half), :] = blocks_in[:, row * 128 : (row + 1) * 128].astype(jnp.float32)
+        flat[pl.ds(row, slots, FLAT), :] = blocks_in[:, row * 128 : (row + 1) * 128].astype(jnp.float32)
     copies[4].wait()
     total = count[0, 0]
     size = 3 * planes
     first_half = lanes((half, 128)) < TILE
     for number, (lx, ly, side) in enumerate(LABELS):
-        one = flat[pl.ds(pl.multiple_of(order[0, 2 * number] * half, 8), half), :]
-        two = flat[pl.ds(pl.multiple_of(order[0, 2 * number + 1] * half, 8), half), :]
+        one = flat[pl.ds(pl.multiple_of(order[0, 2 * number] * FLAT, 8), half), :]
+        two = flat[pl.ds(pl.multiple_of(order[0, 2 * number + 1] * FLAT, 8), half), :]
+        turned = roll(jnp.where(first_half, two, one), TILE)
         square[number, pl.ds(0, half, 2), :] = jnp.where(first_half, one, 0.0)
-        square[number, pl.ds(1, half, 2), :] = jnp.where(first_half, roll(one, TILE), 0.0)
-        square[number, pl.ds(TILE, half, 2), :] = jnp.where(first_half, 0.0, roll(two, TILE))
+        square[number, pl.ds(1, half, 2), :] = jnp.where(first_half, turned, 0.0)
+        square[number, pl.ds(TILE, half, 2), :] = jnp.where(first_half, 0.0, turned)
         square[number, pl.ds(TILE + 1, half, 2), :] = jnp.where(first_half, 0.0, two)
         joined = square[number].astype(jnp.bfloat16)
         pairs[number] = joined
@@ -257,23 +260,40 @@
         first = (0 if lx == S else 8 + 2 * size) + (ly * 2 + side) * planes
         (send_a, send_b, value_s)[lx][first : first + planes, :] = value
     even = parity_x == 0
+    for copy in copies[5:9]:
+        copy.wait()
+    for number, (low, high) in enumerate(((low_c, high_c), (low_s, high_s))):
+        low = jnp.concatenate([low[:, j, :] for j in range(3)], axis=0)
+        high = jnp.concatenate([high[:, 5 + j, :] for j in range(3)], axis=0)
+        spot = slice(8 + number * size, 8 + (number + 1) * size)
+        send_a[spot, :] = jnp.where(even, low, high)
+        send_b[spot, :] = jnp.where(even, high, low)
     high = extent_x - 3
-    for number, ref in enumerate((cotan_out, rate_x_out, field_out)):
-        if number < 2:
-            copies[5 + number].wait()
-        to_a = edge_rows(ref, jnp.where(even, 0, high), planes, extent_x)
-        to_b = edge_rows(ref, jnp.where(even, high, 0), planes, extent_x)
-        if number < 2:
-            spot = slice(8 + number * size, 8 + (number + 1) * size)
-            send_a[spot, :], send_b[spot, :] = to_a, to_b
-        else:
-            late_a[...], late_b[...] = to_a, to_b
-    copies[7].wait()
-
-
-def edges_body(field, cotan, rate_y, packs, *, planes, extent_x):
+    late_a[...] = edge_rows(field_out, jnp.where(even, 0, high), planes, extent_x)
+    late_b[...] = edge_rows(field_out, jnp.where(even, high, 0), planes, extent_x)
+    copies[9].wait()
+    copies[10].wait()
+
+
+def local_body(field, cotan, rate_y, packs, early, section, *, planes, extent_x):
     for number, ref in enumerate((rate_y, field, cotan)):
         packs[number * extent_x : (number + 1) * extent_x, :] = edge_pack(ref, planes, extent_x)
+    rows = 4 * extent_x
+    for chunk, pulled in enumerate(adjoint_y(cotan, rate_y, planes, extent_x)):
+        spot = slice(chunk * rows, (chunk + 1) * rows)
+        early[spot, :] = 0.5 * cotan[spot, :] + (0.5 * TIME_STEP / 60.0) * pulled
+    both = jnp.concatenate(
+        [band({k: WEIGHTS[k + 2] for k in range(-2, 3)}, 128), band({k: WEIGHTS[3 - k] for k in range(-1, 4)}, 128)], axis=1
+    )
+    both = jnp.concatenate([both, both], axis=0)
+    first_lane = lanes((rows, 128)) == 0
+    for chunk in range(planes // 4):
+        spot = slice(chunk * rows, (chunk + 1) * rows)
+        parts = mix(jnp.concatenate(split(field[spot, :]), axis=1), both)
+        rate_up, rate_down = upwind(rate_y[spot, :])
+        flux = rate_up * parts[:, :128] + rate_down * parts[:, 128:]
+        change = jnp.where(first_lane, 0.0, roll(flux, 1)) - flux
+        section[spot, :] = field[spot, :] + (TIME_STEP / 60.0) * change
 
 
 def merge_lists(a, b, s):
@@ -297,21 +317,18 @@
         (out_a, out_b, out_s)[lx][first : first + planes, :] = tiles
 
 
-def gather_tiles(asked, field, outs, first, planes, extent_x):
-    for ly in range(3):
-        for inner in range(6):
-            at = ly * 12 + 2 * inner
-            tiles = tile_pair(field, asked[ly, at], asked[ly, at + 1], planes, extent_x)
-            outs[ly][first + inner * planes : first + (inner + 1) * planes, :] = tiles
-
-
 def rows_at(ref, first, planes):
     return ref[first : first + planes, :]
 
 
-def pull_y_body(
-    cotan, cotan_a, cotan_b, rate_y, packs, request, got_a, got_b, from_a, from_b, grad, edge_rate, asked, list_ref, joined, sem,
-    *, planes, extent_x,
+def give_back(back, number, scale, order, pairs, field, planes, extent_x):
+    pulled = scale * pair_dot(back, pairs[number], 0)
+    add_tile_pair(field, order[1, 2 * number], order[1, 2 * number + 1], pulled, planes, extent_x)
+
+
+def pull_body(
+    order, count, early, cotan, cotan_a, cotan_b, rate_x, packs, request, rows_a, rows_b, from_a, from_b, own, pairs,
+    grad, edge_rate, asked, pad_rate, returned, list_ref, joined, pad, up_ref, down_ref, sem, *, planes, extent_x,
 ):
     row = lax.broadcasted_iota(jnp.int32, (8, 128), 0)
     spread = [
@@ -319,13 +336,17 @@
         for a, b, c in (
             (from_a[8:16], from_a[16:24], from_a[0:8]),
             (from_b[8:16], from_b[16:24], from_b[0:8]),
-            (got_a[0:8], got_b[0:8], request[0:8]),
+            (rows_a[0:8], rows_b[0:8], request[0:8]),
         )
     ]
     list_ref[...] = jnp.where(row == 0, spread[0], jnp.where(row == 1, spread[1], spread[2]))
     copy = pltpu.make_async_copy(list_ref, asked, sem)
     copy.start()
-    even_y = parities()[1] == 0
+    parity_x, parity_y = parities()
+    even_x, even_y = parity_x == 0, parity_y == 0
+    size = 3 * planes
+    fill_padded(pad, cotan, rows_a[8 : 8 + size], rows_b[8 : 8 + size], even_x, planes, extent_x)
+    fill_padded(pad_rate, rate_x, rows_a[8 + size : 8 + 2 * size], rows_b[8 + size : 8 + 2 * size], even_x, planes, extent_x)
     lane = lanes((extent_x, 128))
     upper = jnp.where(even_y, lane, 127 - lane) >= TILE
     for z in range(planes):
@@ -335,27 +356,21 @@
     halo_rate = edge_join(from_a[24 : 24 + extent_x], from_b[24 : 24 + extent_x], even_y)
     edge_rate[...] = halo_rate
     edges = adjoint_edges(part(packs, 2, extent_x), halo, part(packs, 0, extent_x), halo_rate)
-    pulled = adjoint_y(cotan, rate_y, planes, extent_x)
     for z in range(planes):
         spot = pl.ds(z * extent_x, extent_x)
         rim = roll(edges, 125 - 8 * z)
         rim = jnp.where((lane < 3) | (lane >= 125), rim, 0.0)
-        main = pulled[z // 4][z % 4 * extent_x : (z % 4 + 1) * extent_x]
-        grad[spot, :] = 0.5 * cotan[spot, :] + (0.5 * TIME_STEP) * (main * (1.0 / 60.0) + rim)
+        along_x = adjoint_x(z, pad, pad_rate, up_ref, down_ref, extent_x)
+        grad[spot, :] = early[spot, :] + (0.5 * TIME_STEP) * (along_x + rim)
+    for number, (lx, ly, half) in enumerate(LABELS):
+        if lx == S:
+            back = alive_lanes(rows_at(own, (ly * 2 + half) * planes, planes), order, number, count[0, 0])
+            returned[number] = back
+            give_back(back, number, 0.5 * TIME_STEP, order, pairs, grad, planes, extent_x)
     copy.wait()
 
 
-def pull_x_body(early, cotan, rate_x, rows_a, rows_b, grad, pad_rate, pad, up_ref, down_ref, *, planes, extent_x):
-    even_x = parities()[0] == 0
-    size = 3 * planes
-    fill_padded(pad, cotan, rows_a[8 : 8 + size], rows_b[8 : 8 + size], even_x, planes, extent_x)
-    fill_padded(pad_rate, rate_x, rows_a[8 + size : 8 + 2 * size], rows_b[8 + size : 8 + 2 * size], even_x, planes, extent_x)
-    for z in range(planes):
-        spot = pl.ds(z * extent_x, extent_x)
-        grad[spot, :] = early[spot, :] + (0.5 * TIME_STEP) * adjoint_x(z, pad, pad_rate, up_ref, down_ref, extent_x)
-
-
-def push_body(field, pad_rate, rate_y, edge_rate, rows_a, rows_b, packs, packs_a, packs_b, section, pad, flux_ref, *, planes, extent_x):
+def push_body(early, field, pad_rate, edge_rate, rows_a, rows_b, packs, packs_a, packs_b, section, pad, flux_ref, *, planes, extent_x):
     parity_x, parity_y = parities()
     even_x, even_y = parity_x == 0, parity_y == 0
     first = 6 * planes
@@ -384,15 +399,6 @@
     change_edge = roll(flux_high, 1) - flux_high
     before = jnp.where(lane8 == 3, flux_low, roll(flux_first, 1))
     change_edge = jnp.where(lane8 < 3, change_edge, jnp.where(lane8 < 6, before - flux_first, 0.0))
-    both = jnp.concatenate([band({k: WEIGHTS[k + 2] for k in range(-2, 3)}, 128), band({k: WEIGHTS[3 - k] for k in range(-1, 4)}, 128)], axis=1)
-    both = jnp.concatenate([both, both], axis=0)
-    chunk_rows = 4 * extent_x
-    fluxes = []
-    for chunk in range(planes // 4):
-        rows = slice(chunk * chunk_rows, (chunk + 1) * chunk_rows)
-        parts = mix(jnp.concatenate(split(field[rows, :]), axis=1), both) * (1.0 / 60.0)
-        rate_up, rate_down = upwind(rate_y[rows, :])
-        fluxes.append(rate_up * parts[:, :128] + rate_down * parts[:, 128:])
     for z in range(planes):
         base = z * PAD
         spot = pl.ds(z * extent_x, extent_x)
@@ -403,40 +409,72 @@
             WEIGHTS[j] * near[3 - j] for j in range(5)
         )
         change = flux_ref[pl.ds(base, extent_x), :] - flux_ref[pl.ds(base + 1, extent_x), :]
-        flux = fluxes[z // 4][z % 4 * extent_x : (z % 4 + 1) * extent_x]
-        lane = lanes(flux.shape)
+        lane = lanes(change.shape)
         rim = roll(change_edge, 125 - 8 * z)
         rim = jnp.where((lane < 3) | (lane >= 125), rim, 0.0)
-        change = change + jnp.where(lane == 0, 0.0, roll(flux, 1)) - flux + rim
-        section[spot, :] = field[spot, :] + TIME_STEP * change
-
-
-def middle_body(order, asked, count, early, pairs, x_a, x_b, own, grad, returned, send_a, send_b, send_s, rows_a, rows_b, *, planes, extent_x):
+        section[spot, :] = early[spot, :] + TIME_STEP * (change + rim)
+
+
+def compact(packed, low):
+    chosen = jnp.where(low, roll(packed, -3), packed)
+    half = packed.shape[0] // 2
+    return jnp.where(lanes((half, 128)) % 8 < 4, chosen[:half], roll(chosen[half:], 4))
+
+
+def expand_join(from_a, from_b, even):
+    from_a, from_b = (jnp.concatenate([v, roll(v, -4)], axis=0) for v in (from_a, from_b))
+    low = jnp.where(even, from_a, from_b)
+    high = jnp.where(even, from_b, from_a)
+    return jnp.where(lanes(low.shape) % 8 < 3, low, roll(high, 3))
+
+
+def gather_pair(asked, field, out, first, lx, ly, half, planes, extent_x):
+    at = ly * 12 + lx * ROUTE_MOST + 2 * half
+    out[first : first + planes, :] = tile_pair(field, asked[ly, at], asked[ly, at + 1], planes, extent_x)
+
+
+def middle_body(order, asked, count, early, returned_early, pairs, x_a, x_b, grad, returned, send_a, send_b, *, planes, extent_x):
+    for number, (lx, ly, half) in enumerate(LABELS):
+        if lx != S:
+            back = rows_at((x_a, x_b)[lx], (ly * 2 + half) * planes, planes)
+            back = alive_lanes(back, order, number, count[0, 0])
+            returned[number] = back
+            give_back(back, number, 0.5 * TIME_STEP, order, pairs, grad, planes, extent_x)
+    for lx, ly, half in LABELS:
+        if ly != S:
+            gather_pair(asked, grad, (send_a, send_b)[ly], (lx * 2 + half) * planes, lx, ly, half, planes, extent_x)
+    packed = edge_pack(grad, planes, extent_x)
+    even_y = parities()[1] == 0
+    send_a[6 * planes :, :] = compact(packed, even_y)
+    send_b[6 * planes :, :] = compact(packed, jnp.logical_not(even_y))
+
+
+def after_body(asked, grad, own, pack, rows_a, rows_b, *, planes, extent_x):
+    pack[...] = edge_pack(grad, planes, extent_x)
+    for lx, ly, half in LABELS:
+        if ly == S:
+            gather_pair(asked, grad, own, (lx * 2 + half) * planes, lx, ly, half, planes, extent_x)
     even_x = parities()[0] == 0
-    alive = count[0, 0]
-    for number, (lx, ly, half) in enumerate(LABELS):
-        back = rows_at((x_a, x_b, own)[lx], (ly * 2 + half) * planes, planes)
-        back = alive_lanes(back, order, number, alive)
-        returned[number] = back
-        pulled = (0.5 * TIME_STEP) * pair_dot(back, pairs[number], 0)
-        add_tile_pair(grad, order[1, 2 * number], order[1, 2 * number + 1], pulled, planes, extent_x)
-    packed = edge_pack(grad, planes, extent_x)
-    for out in (send_a, send_b, send_s):
-        out[0:extent_x, :] = packed
-    gather_tiles(asked, grad, (send_a, send_b, send_s), extent_x, planes, extent_x)
     high = extent_x - 3
     rows_a[...] = edge_rows(grad, jnp.where(even_x, 0, high), planes, extent_x)
     rows_b[...] = edge_rows(grad, jnp.where(even_x, high, 0), planes, extent_x)
 
 
-def inner_body(cotan, grad, pad_rate, rate_y, out, pad, up_ref, down_ref, *, planes, extent_x):
+def row_back(ly, half, y_a, y_b, own, planes, extent_x):
+    if ly == S:
+        return rows_at(own, (S * 2 + half) * planes, planes)
+    return rows_at((y_a, y_b)[ly], (S * 2 + half) * planes, planes)
+
+
+def inner_body(
+    cotan, grad, pad_rate, rate_y, out, pad, up_ref, down_ref, *, planes, extent_x,
+):
     high = 8 + extent_x
     for z in range(planes):
         pad[z * PAD + 8 : z * PAD + high, :] = grad[z * extent_x : (z + 1) * extent_x, :]
     for j in range(3):
         pad[pl.ds(5 + j, planes, PAD), :] = row_of(grad, 0, planes, extent_x)
         pad[pl.ds(high + j, planes, PAD), :] = row_of(grad, extent_x - 1, planes, extent_x)
-
     along_y = adjoint_y(grad, rate_y, planes, extent_x)
     for z in range(planes):
         spot = pl.ds(z * extent_x, extent_x)
@@ -456,59 +494,69 @@
     )
 
 
-def section_body(order, asked, early, returned, x_a, x_b, y_a, y_b, own, section, first_outer, *, planes, extent_x):
-    for number, (lx, ly, half) in enumerate(LABELS):
+def merge_blocks(value, number, work, blocks):
+    work[number] = value
+    half = TILE // 2
+    half_lane = lanes((half, 128)) < TILE
+    even_one, odd_one, even_two, odd_two = (work[number, pl.ds(first, half, 2), :] for first in (0, 1, TILE, TILE + 1))
+    turned = roll(jnp.where(half_lane, odd_one, even_two), TILE)
+    blocks[2 * number] = jnp.where(half_lane, even_one, turned)
+    blocks[2 * number + 1] = jnp.where(half_lane, turned, odd_two)
+
+
+def start_blocks(number, order, blocks, out_blocks, sems):
+    half = TILE // 2
+    copies = []
+    for which in range(2):
+        spot = pl.ds(pl.multiple_of(order[0, 2 * number + which] * half, 8), half)
+        copies.append(pltpu.make_async_copy(blocks.at[2 * number + which], out_blocks.at[spot, :], sems.at[2 * number + which]))
+        copies[-1].start()
+    return copies
+
+
+def section_body(
+    order, asked, early, returned, x_a, x_b, y_a, y_b, value_s, section, first_outer, *, planes, extent_x,
+):
+    for lx, ly, half in LABELS:
         if ly == S:
-            came = rows_at((x_a, x_b, own)[lx], (0 if lx == S else 8 + 6 * planes) + (S * 2 + half) * planes, planes)
+            came = rows_at((x_a, x_b, value_s)[lx], (0 if lx == S else 8 + 6 * planes) + (S * 2 + half) * planes, planes)
         else:
             came = rows_at((y_a, y_b)[ly], 24 + 2 * extent_x + ((1, 2, 0)[lx] * 2 + half) * planes, planes)
-        came = TIME_STEP * came
         at = ly * 12 + lx * ROUTE_MOST + 2 * half
-        add_tile_pair(section, asked[ly, at], asked[ly, at + 1], came, planes, extent_x)
-
+        add_tile_pair(section, asked[ly, at], asked[ly, at + 1], TIME_STEP * came, planes, extent_x)
     for number in range(first_outer.shape[0]):
-        picked = tile_pair(section, order[1, 2 * number], order[1, 2 * number + 1], planes, extent_x)
-        first_outer[number] = outer((0.5 * TIME_STEP) * returned[number], picked)
-
-
-def finish(number, back, order, pairs, first_outer, picked, total, work, blocks, planes, extent_x):
-    pulled = TIME_STEP * pair_dot(back, pairs[number], 0)
-    add_tile_pair(total, order[1, 2 * number], order[1, 2 * number + 1], pulled, planes, extent_x)
-    work[number] = first_outer[number] + outer(TIME_STEP * back, picked[number])
-    half_lane = lanes((TILE // 2, 128)) < TILE
-    for which in range(2):
-        slot = order[0, 2 * number + which]
-        even_rows = work[number, pl.ds(which * TILE, TILE // 2, 2), :]
-        odd_rows = work[number, pl.ds(which * TILE + 1, TILE // 2, 2), :]
-        if which == 0:
-            merged = jnp.where(half_lane, even_rows, roll(odd_rows, TILE))
-        else:
-            merged = jnp.where(half_lane, roll(even_rows, TILE), odd_rows)
-        blocks[pl.ds(pl.multiple_of(slot * (TILE // 2), 8), TILE // 2), :] = merged
+        found = tile_pair(section, order[1, 2 * number], order[1, 2 * number + 1], planes, extent_x)
+        first_outer[number] = outer((0.5 * TIME_STEP) * returned[number], found)
 
 
 def rest_body(
-    order, count, early, rate_edge, packs, own, y_a, y_b, pairs, first_outer, picked, total, blocks, work, *, planes, extent_x,
+    order, count, early, edge_rate, packs, pack, y_a, y_b, own, pairs, first_outer, picked, total, blocks, work, *, planes, extent_x,
 ):
-    even_y = parities()[1] == 0
-    halo = edge_join(y_a[0:extent_x], y_b[0:extent_x], even_y)
-    edges = adjoint_edges(own[0:extent_x], halo, part(packs, 0, extent_x), rate_edge[...])
+    halo = expand_join(y_a[6 * planes :], y_b[6 * planes :], parities()[1] == 0)
+    edges = adjoint_edges(pack[...], halo, part(packs, 0, extent_x), edge_rate[...])
     lane = lanes((extent_x, 128))
+    backs = {}
+    for number, (lx, ly, half) in enumerate(LABELS):
+        if lx == S:
+            backs[number] = alive_lanes(row_back(ly, half, y_a, y_b, own, planes, extent_x), order, number, count[0, 0])
+            value = first_outer[number] + outer(TIME_STEP * backs[number], picked[number])
+            merge_blocks(value, number, work, blocks)
     for z in range(planes):
         spot = pl.ds(z * extent_x, extent_x)
         rim = roll(edges, 125 - 8 * z)
         total[spot, :] = total[spot, :] + TIME_STEP * jnp.where((lane < 3) | (lane >= 125), rim, 0.0)
-    for number, (lx, ly, half) in enumerate(LABELS):
-        if lx == S:
-            back = rows_at((y_a, y_b, own)[ly], extent_x + (S * 2 + half) * planes, planes)
-            back = alive_lanes(back, order, number, count[0, 0])
-            finish(number, back, order, pairs, first_outer, picked, total, work, blocks, planes, extent_x)
+    for number, back in backs.items():
+        give_back(back, number, TIME_STEP, order, pairs, total, planes, extent_x)
 
 
 def last_body(
-    order, count, early, blocks_early, grad, pad_rate, x_b, x_a, pairs, first_outer, picked, out, out_blocks, total, blocks, work, sems,
+    order, count, early, blocks_early, grad, pad_rate, x_b, x_a, pairs, first_outer, picked, out, out_blocks, total, work, blocks, sems,
     *, planes, extent_x,
 ):
+    copies = []
+    for number, (lx, _, _) in enumerate(LABELS):
+        if lx == S:
+            copies += start_blocks(number, order, blocks_early, out_blocks, sems)
     even_x = parities()[0] == 0
     size = 3 * planes
     low_rows = [jnp.where(even_x, x_a[j * planes : (j + 1) * planes], x_b[j * planes : (j + 1) * planes]) for j in range(3)]
@@ -530,14 +578,17 @@
                     added = added + combine(*faces[j], k)
             spot = pl.ds(cell, planes, extent_x)
             total[spot, :] = total[spot, :] + TIME_STEP * added
+    backs = {}
     for number, (lx, ly, half) in enumerate(LABELS):
         if lx != S:
             back = rows_at((x_a, x_b)[lx], size + ((1, 2, 0)[ly] * 2 + half) * planes, planes)
-            back = alive_lanes(back, order, number, count[0, 0])
-            finish(number, back, order, pairs, first_outer, picked, total, work, blocks, planes, extent_x)
-    copies = [pltpu.make_async_copy(total, out, sems.at[0]), pltpu.make_async_copy(blocks, out_blocks, sems.at[1])]
-    for copy in copies:
-        copy.start()
+            backs[number] = alive_lanes(back, order, number, count[0, 0])
+            give_back(backs[number], number, TIME_STEP, order, pairs, total, planes, extent_x)
+    copies.append(pltpu.make_async_copy(total, out, sems.at[2 * len(LABELS)]))
+    copies[-1].start()
+    for number, back in backs.items():
+        merge_blocks(first_outer[number] + outer(TIME_STEP * back, picked[number]), number, work, blocks)
+        copies += start_blocks(number, order, blocks, out_blocks, sems)
     for copy in copies:
         copy.wait()
 
@@ -590,18 +641,20 @@
     tall = ((slots * TILE // 2, 128), f32)
     order, send_a, send_b, value_s, late_a, late_b, pairs, picked, field, cotan, rate_y = call(
         begin_body,
-        [("h", [v.reshape(slots) for v in (dest_offset, dest_tile, source_tile)] + [field, cotan, rate_x, rate_y, blocks.reshape(slots, TILE * TILE)]),
+        [("h", [v.reshape(slots) for v in (dest_offset, dest_tile, source_tile)] + [field, cotan, rate_y, blocks.reshape(slots, TILE * TILE), cotangent, speed_x]),
          ("r", [tile_count])],
         [((2, slots), i32, "s"), sent, sent, box] + [((size, 128), f32, "v")] * 2
         + [((pair_total, 128, 128), jnp.bfloat16, "v"), ((pair_total, planes, 128), f32, "v")] + [whole] * 3,
-        scratch=[pltpu.VMEM((cells, 128), f32), pltpu.VMEM((slots, TILE * TILE), jnp.bfloat16), pltpu.VMEM(*tall), pltpu.VMEM((pair_total, 128, 128), f32)]
-        + [pltpu.SMEM((slots,), i32)] * 3 + [pltpu.SMEM((9,), i32), pltpu.SemaphoreType.DMA((8,))],
+        scratch=[pltpu.VMEM((planes, 8, 128), f32)] * 4 + [pltpu.VMEM((slots, TILE * TILE), jnp.bfloat16), pltpu.VMEM((slots * FLAT, 128), f32), pltpu.VMEM((pair_total, 128, 128), f32)]
+        + [pltpu.SMEM((slots,), i32)] * 3 + [pltpu.SMEM((9,), i32), pltpu.SemaphoreType.DMA((11,))],
         **sizes,
     )
     request = send_a
     rows_a = exchange(send_a, "gx", A)
     rows_b = exchange(send_b, "gx", B)
-    (packs,) = call(edges_body, [("v", [field, cotan, rate_y])], [((3 * extent_x, 128), f32, "v")], **sizes)
+    packs, early, pushed = call(
+        local_body, [("v", [field, cotan, rate_y])], [((3 * extent_x, 128), f32, "v"), whole, whole], **sizes
+    )
 
     def onward(own, a, b, own_first, first, m):
         cut = lambda v, start: v[start + m * 2 * planes : start + (m + 1) * 2 * planes]
@@ -618,50 +671,50 @@
     )
     x_b = exchange(jnp.concatenate([tiles_b, late_b], axis=0), "gx", B)
     x_a = exchange(jnp.concatenate([tiles_a, late_a], axis=0), "gx", A)
-    early, edge_rate, asked = call(
-        pull_y_body, [("v", [cotan, cotan_a, cotan_b, rate_y, packs, request, rows_a, rows_b, packs_a, packs_b])],
-        [whole, ((extent_x, 128), f32, "v"), ((8, 128), i32, "s")],
-        scratch=(pltpu.VMEM((8, 128), i32), pltpu.VMEM((cells, 128), f32), pltpu.SemaphoreType.DMA(())), **sizes,
-    )
-    early, pad_rate = call(
-        pull_x_body, [("v", [early, cotan, rate_x, rows_a, rows_b])], [whole, padded + ("v",)],
-        scratch=(pad_scratch,) * 3, alias={0: 0}, **sizes,
-    )
-    grad, returned, send_a, send_b, send_s, edge_a, edge_b = call(
-        middle_body, [("s", [order, asked]), ("r", [tile_count]), ("v", [early, pairs, x_a, x_b, tiles_s])],
-        [whole, ((pair_total, planes, 128), f32, "v")] + [((extent_x + 2 * size, 128), f32, "v")] * 3 + [((size, 128), f32, "v")] * 2,
-        alias={3: 0}, **sizes,
-    )
-
-    send_a, send_b, field = lax.optimization_barrier((send_a, send_b, field))
+    small = ((extent_x, 128), f32, "v")
+    eighteen = ((pair_total, planes, 128), f32, "v")
+    early, edge_rate, asked, pad_rate, returned = call(
+        pull_body,
+        [("s", [order]), ("r", [tile_count]),
+         ("v", [early, cotan, cotan_a, cotan_b, rate_x, packs, request, rows_a, rows_b, packs_a, packs_b, tiles_s, pairs])],
+        [whole, small, ((8, 128), i32, "s"), padded + ("v",), eighteen],
+        scratch=(pltpu.VMEM((8, 128), i32), pltpu.VMEM((cells, 128), f32), pad_scratch, pad_scratch, pad_scratch, pltpu.SemaphoreType.DMA(())),
+        alias={2: 0}, **sizes,
+    )
+    grad, returned, send_a, send_b = call(
+        middle_body, [("s", [order, asked]), ("r", [tile_count]), ("v", [early, returned, pairs, x_a, x_b])],
+        [whole, eighteen] + [((6 * planes + extent_x // 2, 128), f32, "v")] * 2, alias={3: 0, 4: 1}, **sizes,
+    )
+    send_a, send_b, pushed, grad = lax.optimization_barrier((send_a, send_b, pushed, grad))
     last_y_b = exchange(send_b, "gy", B)
     last_y_a = exchange(send_a, "gy", A)
+    own, pack, edge_a, edge_b = call(
+        after_body, [("s", [asked]), ("v", [grad])], [box, small] + [((size, 128), f32, "v")] * 2, **sizes,
+    )
     (pushed,) = call(
-        push_body, [("v", [field, pad_rate, rate_y, edge_rate, x_a, x_b, packs, packs_a, packs_b])],
-        [whole], scratch=(pad_scratch,) * 2, **sizes,
+        push_body, [("v", [pushed, field, pad_rate, edge_rate, x_a, x_b, packs, packs_a, packs_b])],
+        [whole], scratch=(pad_scratch,) * 2, alias={0: 0}, **sizes,
     )
     last_y_a, last_y_b, pushed = lax.optimization_barrier((last_y_a, last_y_b, pushed))
-    last_x_a = exchange(jnp.concatenate([edge_a] + onward(send_s, last_y_a, last_y_b, extent_x, extent_x, A), axis=0), "gx", A)
-    last_x_b = exchange(jnp.concatenate([edge_b] + onward(send_s, last_y_a, last_y_b, extent_x, extent_x, B), axis=0), "gx", B)
-    (inner,) = call(
-        inner_body, [("v", [cotan, grad, pad_rate, rate_y])], [whole], scratch=(pad_scratch,) * 3, **sizes,
-    )
+    last_x_a = exchange(jnp.concatenate([edge_a] + onward(own, last_y_a, last_y_b, 0, 0, A), axis=0), "gx", A)
+    last_x_b = exchange(jnp.concatenate([edge_b] + onward(own, last_y_a, last_y_b, 0, 0, B), axis=0), "gx", B)
+    (inner,) = call(inner_body, [("v", [cotan, grad, pad_rate, rate_y])], [whole], scratch=(pad_scratch,) * 3, **sizes)
     section, first_outer = call(
         section_body, [("s", [order, asked]), ("v", [pushed, returned, rows_a, rows_b, packs_a, packs_b, value_s])],
         [whole, ((pair_total, 128, 128), f32, "v")], alias={2: 0}, **sizes,
     )
     work = pltpu.VMEM((pair_total, 128, 128), f32)
-    flat = ((slots * TILE // 2, 128), f32)
-    total, early_blocks = call(
+    blocks_out = pltpu.VMEM((slots, TILE // 2, 128), f32)
+    inner, early_blocks = call(
         rest_body,
-        [("s", [order]), ("r", [tile_count]), ("v", [inner, edge_rate, packs, send_s, last_y_a, last_y_b, pairs, first_outer, picked])],
-        [whole, flat + ("v",)], scratch=(work,), alias={2: 0}, **sizes,
-    )
-    grad_level_set, grad_blocks, _, _ = call(
+        [("s", [order]), ("r", [tile_count]), ("v", [inner, edge_rate, packs, pack, last_y_a, last_y_b, own, pairs, first_outer, picked])],
+        [whole, ((slots, TILE // 2, 128), f32, "v")], scratch=(work,), alias={2: 0}, **sizes,
+    )
+    grad_level_set, grad_blocks, _ = call(
         last_body,
-        [("s", [order]), ("r", [tile_count]), ("v", [total, early_blocks, grad, pad_rate, last_x_b, last_x_a, pairs, first_outer, picked])],
-        [((cells, 128), f32, "h"), flat + ("h",), whole, flat + ("v",)],
-        scratch=(work, pltpu.SemaphoreType.DMA((2,))), alias={2: 2, 3: 3}, **sizes,
+        [("s", [order]), ("r", [tile_count]), ("v", [inner, early_blocks, grad, pad_rate, last_x_b, last_x_a, pairs, first_outer, picked])],
+        [((cells, 128), f32, "h"), tall + ("h",), whole],
+        scratch=(work, blocks_out, pltpu.SemaphoreType.DMA((slots + 1,))), alias={2: 2}, **sizes,
     )
     return (grad_level_set.reshape(planes, extent_x, extent_y), grad_blocks.reshape(1, 1, slots, TILE * TILE))
 

time: 41.1 us -> 40.2 us (0.978)
  waiting for transfers between devices: 7.03 us -> 5.27 us
  starting transfers between devices: 18.6 us -> 19.4 us
    ppermute x12, waiting for transfers between devices: 7.03 us -> 5.27 us  [exchange(): return lax.ppermute(block, axis, matching(lax.axis_size(axis), which))]
    ppermute x12, starting transfers between devices: 18.6 us -> 19.4 us  [exchange(): return lax.ppermute(block, axis, matching(lax.axis_size(axis), which))]
  transfers between devices with their start and end apart: 12 -> 12, of which waited for: 4 -> 4; matrix products, arithmetic and copies ran while one was open for 0% -> 0% of each run, Pallas kernels for 26% -> 27%
where the time goes in v7:
time: 40.2 us; the launch traced here: 40 us
  starting transfers between devices  19.4 us (48%)
  Pallas kernels  13.8 us (34%)
  waiting for transfers between devices  5.27 us (13%)
  between operations  1.47 us (4%)
    ppermute x12, starting transfers between devices, exchange(): return lax.ppermute(block, axis, matching(lax.axis_size(axis), which))  19.4 us
    pallas_call x11, Pallas kernels, call(): pl.pallas_call(functools.partial(body, **sizes), out_shape=tuple(shapes),...  13.8 us
    ppermute x12, waiting for transfers between devices, exchange(): return lax.ppermute(block, axis, matching(lax.axis_size(axis), which))  5.27 us
  transfers between devices with their start and end apart: 12, of which 4 were waited for; matrix products, arithmetic and copies ran while one was open for 0% of the time, Pallas kernels for 27%

profile of v7, /device:TPU:0, one launch (start us, length us, event | category | flops | bytes accessed | tf_op | source)
XLA Modules:
  0.0 40.0 jit_solution(3822903819146442309)
XLA Ops:
  0.6 0.5 %collective-permute-start.1 = (f32[1024,128]{1,0:T(8,128)}, f32[1024,128]{1,0:T(8,128)S(1)}, u32[]{:S(2)}, u32[]{:S(2)}) collective-permute-start(f32[1024,128]{1,0:T(8,128)} %bitcast.11), channel_id=1, source_target_pairs={{0,1},{1,0},{2,3},{3,2},{4,5},{5,4},{6,7},{7,6},{8,9},{9,8},{10,11... | collective-permute-start | bytes 1572872 | tf_op jit(solution)/shard_map/ppermute | solution.py:26
  1.2 2.6 %collective-permute-start = (f32[1024,128]{1,0:T(8,128)}, f32[1024,128]{1,0:T(8,128)S(1)}, u32[]{:S(2)}, u32[]{:S(2)}) collective-permute-start(f32[1024,128]{1,0:T(8,128)} %bitcast.12), channel_id=1, source_target_pairs={{0,3},{1,2},{2,1},{3,0},{4,7},{5,6},{6,5},{7,4},{8,11},{9,10},{10,... | collective-permute-start | bytes 1572872 | tf_op jit(solution)/shard_map/ppermute | solution.py:26
  4.4 2.5 %begin_body.1 = (s32[2,36]{1,0:T(2,128)S(4)}, f32[200,128]{1,0:T(8,128)S(1)}, f32[200,128]{1,0:T(8,128)S(1)}, f32[96,128]{1,0:T(8,128)S(1)}, f32[48,128]{1,0:T(8...) custom-call(s32[36]{0:T(128)} %bitcast.17, ...), custom_call_target="tpu_custom_call" | custom-call | tf_op jit(solution)/shard_map/begin_body/pallas_call | solution.py:608
  6.9 1.6 %collective-permute-start.3 = (f32[200,128]{1,0:T(8,128)S(1)}, f32[200,128]{1,0:T(8,128)S(1)}, u32[]{:S(2)}, u32[]{:S(2)}) collective-permute-start(f32[200,128]{1,0:T(8,128)S(1)} %get-tuple-element.51), channel_id=1, source_target_pairs={{0,4},{4,0},{8,12},{12,8},{16,20},{20,16},{24,28},{28,24},{1,5},{5... | collective-permute-start | bytes 307208 | tf_op jit(solution)/shard_map/ppermute | solution.py:26
  8.5 3.5 %collective-permute-start.2 = (f32[200,128]{1,0:T(8,128)S(1)}, f32[200,128]{1,0:T(8,128)S(1)}, u32[]{:S(2)}, u32[]{:S(2)}) collective-permute-start(f32[200,128]{1,0:T(8,128)S(1)} %get-tuple-element.50.request), channel_id=1, source_target_pairs={{0,28},{4,8},{8,4},{12,16},{16,12},{20,24},{24,20},{28,0},{1,29},{... | collective-permute-start | bytes 307208 | tf_op jit(solution)/shard_map/ppermute | solution.py:26
  12.0 0.9 %local_body.1 = (f32[192,128]{1,0:T(8,128)S(1)}, f32[1024,128]{1,0:T(8,128)S(1)}, f32[1024,128]{1,0:T(8,128)S(1)}) custom-call(f32[1024,128]{1,0:T(8,128)S(1)} %get-tuple-element.46.field, f32[1024,128]{1,0:T(8,128)S(1)} %get-tuple-element.45.cotan, f32[1024,128]{1,0:T(8,128)S(1)} %get-tuple-element.47.rate_y), custom_call_target="tpu_custom_call" | custom-call | tf_op jit(solution)/shard_map/local_body/pallas_call | solution.py:608
  13.0 2.9 %collective-permute-done.2.got_a.rows_a.x_a = f32[200,128]{1,0:T(8,128)S(1)} collective-permute-done((f32[200,128]{1,0:T(8,128)S(1)}, f32[200,128]{1,0:T(8,128)S(1)}, u32[]{:S(2)}, u32[]{:S(2)}) %collective-permute-start.2) | collective-permute-done | bytes 102432 | tf_op jit(solution)/shard_map/ppermute | solution.py:26
  15.9 0.0 collective-permute-done.3.got_b.rows_b.x_b
  15.9 0.0 copy-start
  16.0 0.1 collective-permute-start.5
  16.0 0.6 %collective-permute-start.4 = (f32[248,128]{1,0:T(8,128)S(1)}, f32[248,128]{1,0:T(8,128)S(1)}, u32[]{:S(2)}, u32[]{:S(2)}) collective-permute-start(f32[248,128]{1,0:T(8,128)S(1)} %get-tuple-element.91), channel_id=1, source_target_pairs={{0,3},{1,2},{2,1},{3,0},{4,7},{5,6},{6,5},{7,4},{8,11},{9,10},{10,... | collective-permute-start | bytes 380936 | tf_op jit(solution)/shard_map/ppermute | solution.py:26
  16.7 0.0 collective-permute-done.1.cotan_b
  16.7 0.0 collective-permute-done.cotan_a
  16.7 1.0 %serve_body.1 = (f32[96,128]{1,0:T(8,128)S(1)}, f32[96,128]{1,0:T(8,128)S(1)}, f32[96,128]{1,0:T(8,128)S(1)}) custom-call(f32[200,128]{1,0:T(8,128)S(1)} %get-tuple-element.50.request, f32[200,128]{1,0:T(8,128)S(1)} %collective-permute-done.3.got_b.rows_b.x_b, f32[200,128]{1,0:T(8,128)S(1)} %collective-permute-done.2.got_a.rows_a.x_a, ...), custom_call_target="tpu_custom_call" | custom-call | tf_op jit(solution)/shard_map/serve_body/pallas_call | solution.py:608
  17.7 1.0 %collective-permute-start.7 = (f32[144,128]{1,0:T(8,128)S(1)}, f32[144,128]{1,0:T(8,128)S(1)}, u32[]{:S(2)}, u32[]{:S(2)}) collective-permute-start(f32[144,128]{1,0:T(8,128)S(1)} %pad_maximum_fusion.1), channel_id=1, source_target_pairs={{0,4},{4,0},{8,12},{12,8},{16,20},{20,16},{24,28},{28,24},{1,5},{5... | collective-permute-start | bytes 221192 | tf_op jit(solution)/shard_map/ppermute | solution.py:26
  18.7 3.5 %collective-permute-start.6 = (f32[144,128]{1,0:T(8,128)S(1)}, f32[144,128]{1,0:T(8,128)S(1)}, u32[]{:S(2)}, u32[]{:S(2)}) collective-permute-start(f32[144,128]{1,0:T(8,128)S(1)} %pad_maximum_fusion), channel_id=1, source_target_pairs={{0,28},{4,8},{8,4},{12,16},{16,12},{20,24},{24,20},{28,0},{1,29},{... | collective-permute-start | bytes 221192 | tf_op jit(solution)/shard_map/ppermute | solution.py:26
  22.3 0.0 collective-permute-done.5.from_b.packs_b.y_b
  22.3 0.0 collective-permute-done.4.from_a.packs_a.y_a
  22.3 0.0 copy-done
  22.3 2.0 %pull_body.1 = (f32[1024,128]{1,0:T(8,128)S(1)}, f32[64,128]{1,0:T(8,128)S(1)}, s32[8,128]{1,0:T(8,128)S(4)}, f32[1288,128]{1,0:T(8,128)S(1)}, f32[18,16,128]{2,1,0:T(8,128)S(1)}) custom-call(s32[2,36]{1,0:T(2,128)S(4)} %get-tuple-element.44.order, s32[1,1]{1,0:T(1,128)S(6)} %copy.36.count, ...), custom_call_target="tpu_custom_call", output_to_operand_aliasing={{0}: (2, {})} | custom-call | tf_op jit(solution)/shard_map/pull_body/pallas_call | solution.py:608
  24.2 0.0 collective-permute-done.7.x_b.rows_b
  24.2 1.5 %collective-permute-done.6.x_a.rows_a = f32[144,128]{1,0:T(8,128)S(1)} collective-permute-done((f32[144,128]{1,0:T(8,128)S(1)}, f32[144,128]{1,0:T(8,128)S(1)}, u32[]{:S(2)}, u32[]{:S(2)}) %collective-permute-start.6) | collective-permute-done | bytes 73760 | tf_op jit(solution)/shard_map/ppermute | solution.py:26
  25.8 1.0 %middle_body.1 = (f32[1024,128]{1,0:T(8,128)S(1)}, f32[18,16,128]{2,1,0:T(8,128)S(1)}, f32[128,128]{1,0:T(8,128)S(1)}, f32[128,128]{1,0:T(8,128)S(1)}) custom-call(s32[2,36]{1,0:T(2,128)S(4)} %get-tuple-element.44.order, s32[8,128]{1,0:T(8,128)S(4)} %get-tuple-element.55.asked, ...), custom_call_target="tpu_custom_call", output_to_operand_aliasing={{0}: (3, {}), {1}: (4, {})} | custom-call | tf_op jit(solution)/shard_map/middle_body/pallas_call | solution.py:608
  26.8 1.5 %collective-permute-start.8 = (f32[128,128]{1,0:T(8,128)S(1)}, f32[128,128]{1,0:T(8,128)S(1)}, u32[]{:S(2)}, u32[]{:S(2)}) collective-permute-start(f32[128,128]{1,0:T(8,128)S(1)} %get-tuple-element.70), channel_id=1, source_target_pairs={{0,3},{1,2},{2,1},{3,0},{4,7},{5,6},{6,5},{7,4},{8,11},{9,10},{10,... | collective-permute-start | bytes 196616 | tf_op jit(solution)/shard_map/ppermute | solution.py:26
  28.3 0.7 %collective-permute-start.9 = (f32[128,128]{1,0:T(8,128)S(1)}, f32[128,128]{1,0:T(8,128)S(1)}, u32[]{:S(2)}, u32[]{:S(2)}) collective-permute-start(f32[128,128]{1,0:T(8,128)S(1)} %get-tuple-element.71), channel_id=1, source_target_pairs={{0,1},{1,0},{2,3},{3,2},{4,5},{5,4},{6,7},{7,6},{8,9},{9,8},{10,11... | collective-permute-start | bytes 196616 | tf_op jit(solution)/shard_map/ppermute | solution.py:26
  29.0 0.3 after_body.1
  29.3 1.0 %push_body.1.early = f32[1024,128]{1,0:T(8,128)S(1)} custom-call(f32[1024,128]{1,0:T(8,128)S(1)} %get-tuple-element.72.early, f32[1024,128]{1,0:T(8,128)S(1)} %get-tuple-element.46.field, f32[1288,128]{1,0:T(8,128)S(1)} %get-tuple-element.67.pad_rate, f32[64,128]{1,0:T(8,128)S(1)} %get-tuple-element.68.edge_rate, ...), custom_call_target="tpu_custom_call", output_to_operand_aliasing={{}: (0, {})} | custom-call | tf_op jit(solution)/shard_map/push_body/pallas_call | solution.py:608
  30.3 0.5 %collective-permute-done.8.y_a = f32[128,128]{1,0:T(8,128)S(1)} collective-permute-done((f32[128,128]{1,0:T(8,128)S(1)}, f32[128,128]{1,0:T(8,128)S(1)}, u32[]{:S(2)}, u32[]{:S(2)}) %collective-permute-start.8) | collective-permute-done | bytes 65568 | tf_op jit(solution)/shard_map/ppermute | solution.py:26
  30.8 0.0 collective-permute-done.9.y_b
  30.8 0.1 collective-permute-start.10
  30.9 3.6 %collective-permute-start.11 = (f32[144,128]{1,0:T(8,128)S(1)}, f32[144,128]{1,0:T(8,128)S(1)}, u32[]{:S(2)}, u32[]{:S(2)}) collective-permute-start(f32[144,128]{1,0:T(8,128)S(1)} %pad_maximum_fusion.3), channel_id=1, source_target_pairs={{0,28},{4,8},{8,4},{12,16},{16,12},{20,24},{24,20},{28,0},{1,29},{... | collective-permute-start | bytes 221192 | tf_op jit(solution)/shard_map/ppermute | solution.py:26
  34.5 1.2 %inner_body.1.early = f32[1024,128]{1,0:T(8,128)S(1)} custom-call(f32[1024,128]{1,0:T(8,128)S(1)} %get-tuple-element.45.cotan, f32[1024,128]{1,0:T(8,128)S(1)} %get-tuple-element.66.grad, f32[1288,128]{1,0:T(8,128)S(1)} %get-tuple-element.67.pad_rate, f32[1024,128]{1,0:T(8,128)S(1)} %get-tuple-element.47.rate_y), custom_call_target="tpu_custom_call" | custom-call | tf_op jit(solution)/shard_map/inner_body/pallas_call | solution.py:608
  35.7 1.2 %section_body.1 = (f32[1024,128]{1,0:T(8,128)S(1)}, f32[18,128,128]{2,1,0:T(8,128)S(1)}) custom-call(s32[2,36]{1,0:T(2,128)S(4)} %get-tuple-element.44.order, s32[8,128]{1,0:T(8,128)S(4)} %get-tuple-element.55.asked, f32[1024,128]{1,0:T(8,128)S(1)} %push_body.1.early, ...), custom_call_target="tpu_custom_call", output_to_operand_aliasing={{0}: (2, {})} | custom-call | tf_op jit(solution)/shard_map/section_body/pallas_call | solution.py:608
  37.0 0.8 %rest_body.1 = (f32[1024,128]{1,0:T(8,128)S(1)}, f32[36,32,128]{2,1,0:T(8,128)S(1)}) custom-call(s32[2,36]{1,0:T(2,128)S(4)} %get-tuple-element.44.order, s32[1,1]{1,0:T(1,128)S(6)} %copy.36.count, f32[1024,128]{1,0:T(8,128)S(1)} %inner_body.1.early, f32[64,128]{1,0:T(8,128)S(1)} %get-tuple-element.68.edge_rate, ...), custom_call_target="tpu_custom_call", output_to_operand_aliasing={{0}: (2, {})} | custom-call | tf_op jit(solution)/shard_map/rest_body/pallas_call | solution.py:608
  37.7 0.0 collective-permute-done.10.x_b
  37.7 0.4 collective-permute-done.11.x_a
  38.1 1.9 %last_body.1 = (f32[1024,128]{1,0:T(8,128)}, f32[1152,128]{1,0:T(8,128)}, f32[1024,128]{1,0:T(8,128)S(1)}) custom-call(s32[2,36]{1,0:T(2,128)S(4)} %get-tuple-element.44.order, s32[1,1]{1,0:T(1,128)S(6)} %copy.36.count, f32[1024,128]{1,0:T(8,128)S(1)} %get-tuple-element.80.early, ...), custom_call_target="tpu_custom_call", output_to_operand_aliasing={{2}: (2, {})} | custom-call | tf_op jit(solution)/shard_map/last_body/pallas_call | solution.py:608
  (15 shorter events, 0.1 us)
Async XLA Ops:
  0.6 16.1 %collective-permute-start.1 = (f32[1024,128]{1,0:T(8,128)}, f32[1024,128]{1,0:T(8,128)S(1)}, u32[]{:S(2)}, u32[]{:S(2)}) collective-permute-start(f32[1024,128]{1,0:T(8,128)} %bitcast.11), channel_id=1, source_target_pairs={{0,1},{1,0},{2,3},{3,2},{4,5},{5,4},{6,7},{7,6},{8,9},{9,8},{10,11... | collective-permute-start | bytes 1572872 | tf_op jit(solution)/shard_map/ppermute | solution.py:26
  1.2 15.5 %collective-permute-start = (f32[1024,128]{1,0:T(8,128)}, f32[1024,128]{1,0:T(8,128)S(1)}, u32[]{:S(2)}, u32[]{:S(2)}) collective-permute-start(f32[1024,128]{1,0:T(8,128)} %bitcast.12), channel_id=1, source_target_pairs={{0,3},{1,2},{2,1},{3,0},{4,7},{5,6},{6,5},{7,4},{8,11},{9,10},{10,... | collective-permute-start | bytes 1572872 | tf_op jit(solution)/shard_map/ppermute | solution.py:26
  6.9 8.9 %collective-permute-start.3 = (f32[200,128]{1,0:T(8,128)S(1)}, f32[200,128]{1,0:T(8,128)S(1)}, u32[]{:S(2)}, u32[]{:S(2)}) collective-permute-start(f32[200,128]{1,0:T(8,128)S(1)} %get-tuple-element.51), channel_id=1, source_target_pairs={{0,4},{4,0},{8,12},{12,8},{16,20},{20,16},{24,28},{28,24},{1,5},{5... | collective-permute-start | bytes 307208 | tf_op jit(solution)/shard_map/ppermute | solution.py:26
  8.5 7.4 %collective-permute-start.2 = (f32[200,128]{1,0:T(8,128)S(1)}, f32[200,128]{1,0:T(8,128)S(1)}, u32[]{:S(2)}, u32[]{:S(2)}) collective-permute-start(f32[200,128]{1,0:T(8,128)S(1)} %get-tuple-element.50.request), channel_id=1, source_target_pairs={{0,28},{4,8},{8,4},{12,16},{16,12},{20,24},{24,20},{28,0},{1,29},{... | collective-permute-start | bytes 307208 | tf_op jit(solution)/shard_map/ppermute | solution.py:26
  15.9 6.4 %copy-start = (f32[16,64,128]{2,1,0:T(8,128)S(1)}, f32[16,64,128]{2,1,0:T(8,128)}, u32[]{:S(2)}) copy-start(f32[16,64,128]{2,1,0:T(8,128)} %rate_cube.1) | copy-start | bytes 1572868
  16.0 6.3 %collective-permute-start.5 = (f32[248,128]{1,0:T(8,128)S(1)}, f32[248,128]{1,0:T(8,128)S(1)}, u32[]{:S(2)}, u32[]{:S(2)}) collective-permute-start(f32[248,128]{1,0:T(8,128)S(1)} %get-tuple-element.90), channel_id=1, source_target_pairs={{0,1},{1,0},{2,3},{3,2},{4,5},{5,4},{6,7},{7,6},{8,9},{9,8},{10,11... | collective-permute-start | bytes 380936 | tf_op jit(solution)/shard_map/ppermute | solution.py:26
  16.0 6.2 %collective-permute-start.4 = (f32[248,128]{1,0:T(8,128)S(1)}, f32[248,128]{1,0:T(8,128)S(1)}, u32[]{:S(2)}, u32[]{:S(2)}) collective-permute-start(f32[248,128]{1,0:T(8,128)S(1)} %get-tuple-element.91), channel_id=1, source_target_pairs={{0,3},{1,2},{2,1},{3,0},{4,7},{5,6},{6,5},{7,4},{8,11},{9,10},{10,... | collective-permute-start | bytes 380936 | tf_op jit(solution)/shard_map/ppermute | solution.py:26
  17.7 6.5 %collective-permute-start.7 = (f32[144,128]{1,0:T(8,128)S(1)}, f32[144,128]{1,0:T(8,128)S(1)}, u32[]{:S(2)}, u32[]{:S(2)}) collective-permute-start(f32[144,128]{1,0:T(8,128)S(1)} %pad_maximum_fusion.1), channel_id=1, source_target_pairs={{0,4},{4,0},{8,12},{12,8},{16,20},{20,16},{24,28},{28,24},{1,5},{5... | collective-permute-start | bytes 221192 | tf_op jit(solution)/shard_map/ppermute | solution.py:26
  18.7 7.0 %collective-permute-start.6 = (f32[144,128]{1,0:T(8,128)S(1)}, f32[144,128]{1,0:T(8,128)S(1)}, u32[]{:S(2)}, u32[]{:S(2)}) collective-permute-start(f32[144,128]{1,0:T(8,128)S(1)} %pad_maximum_fusion), channel_id=1, source_target_pairs={{0,28},{4,8},{8,4},{12,16},{16,12},{20,24},{24,20},{28,0},{1,29},{... | collective-permute-start | bytes 221192 | tf_op jit(solution)/shard_map/ppermute | solution.py:26
  26.8 4.0 %collective-permute-start.8 = (f32[128,128]{1,0:T(8,128)S(1)}, f32[128,128]{1,0:T(8,128)S(1)}, u32[]{:S(2)}, u32[]{:S(2)}) collective-permute-start(f32[128,128]{1,0:T(8,128)S(1)} %get-tuple-element.70), channel_id=1, source_target_pairs={{0,3},{1,2},{2,1},{3,0},{4,7},{5,6},{6,5},{7,4},{8,11},{9,10},{10,... | collective-permute-start | bytes 196616 | tf_op jit(solution)/shard_map/ppermute | solution.py:26
  28.3 2.5 %collective-permute-start.9 = (f32[128,128]{1,0:T(8,128)S(1)}, f32[128,128]{1,0:T(8,128)S(1)}, u32[]{:S(2)}, u32[]{:S(2)}) collective-permute-start(f32[128,128]{1,0:T(8,128)S(1)} %get-tuple-element.71), channel_id=1, source_target_pairs={{0,1},{1,0},{2,3},{3,2},{4,5},{5,4},{6,7},{7,6},{8,9},{9,8},{10,11... | collective-permute-start | bytes 196616 | tf_op jit(solution)/shard_map/ppermute | solution.py:26
  30.8 6.9 %collective-permute-start.10 = (f32[144,128]{1,0:T(8,128)S(1)}, f32[144,128]{1,0:T(8,128)S(1)}, u32[]{:S(2)}, u32[]{:S(2)}) collective-permute-start(f32[144,128]{1,0:T(8,128)S(1)} %pad_maximum_fusion.2), channel_id=1, source_target_pairs={{0,4},{4,0},{8,12},{12,8},{16,20},{20,16},{24,28},{28,24},{1,5},{5... | collective-permute-start | bytes 221192 | tf_op jit(solution)/shard_map/ppermute | solution.py:26
  30.9 7.2 %collective-permute-start.11 = (f32[144,128]{1,0:T(8,128)S(1)}, f32[144,128]{1,0:T(8,128)S(1)}, u32[]{:S(2)}, u32[]{:S(2)}) collective-permute-start(f32[144,128]{1,0:T(8,128)S(1)} %pad_maximum_fusion.3), channel_id=1, source_target_pairs={{0,28},{4,8},{8,4},{12,16},{16,12},{20,24},{24,20},{28,0},{1,29},{... | collective-permute-start | bytes 221192 | tf_op jit(solution)/shard_map/ppermute | solution.py:26

commit v8 on v7

--- a/solution.py
+++ b/solution.py
@@ -202,7 +202,7 @@
 def begin_body(
     heading, target, source, field, cotan, rate_y, blocks, cotan_cube, rate_cube, count,
     order, send_a, send_b, value_s, late_a, late_b, pairs, picked, field_out, cotan_out, rate_y_out,
-    low_c, high_c, low_s, high_s, blocks_in, flat, square, heading_in, target_in, source_in, used, sems, *, planes, extent_x,
+    low_c, high_c, low_s, high_s, blocks_in, flat, square, heading_in, target_in, source_in, sems, *, planes, extent_x,
 ):
     moves = (
         (heading, heading_in), (target, target_in), (source, source_in),
@@ -215,8 +215,7 @@
     for copy in copies:
         copy.start()
     parity_x, parity_y = parities()
-    for label in range(9):
-        used[label] = 0
+    used = jnp.int32(0)
     lane = lanes((8, 128))
     for copy in copies[:4]:
         copy.wait()
@@ -227,11 +226,11 @@
         across = (toward >= 3).astype(jnp.int32) + (toward >= 6).astype(jnp.int32)
         ex = (across - 1) * (1 - 2 * parity_x)
         ey = (toward - 3 * across - 1) * (1 - 2 * parity_y)
-        lx = jnp.where(ex == 0, 2, (ex + 1) // 2)
-        ly = jnp.where(ey == 0, 2, (ey + 1) // 2)
+        lx = jnp.where(ex == 0, 2, (ex == 1).astype(jnp.int32))
+        ly = jnp.where(ey == 0, 2, (ey == 1).astype(jnp.int32))
         label = ly * 3 + lx
-        spot = label * ROUTE_MOST + used[label]
-        used[label] = used[label] + 1
+        spot = label * ROUTE_MOST + ((used >> (3 * label)) & 7)
+        used = used + (jnp.int32(1) << (3 * label))
         order[0, spot] = slot
         order[1, spot] = source_in[slot]
         asked = jnp.where(lane == spot, target_in[slot], asked)
@@ -308,13 +307,22 @@
     copy.wait()
 
 
-def serve_body(request, got_b, got_a, cotan_a, cotan_b, cotan, out_a, out_b, out_s, list_ref, asked, sem, *, planes, extent_x):
+def serve_body(request, got_b, got_a, cotan_b, cotan, asked, out_a, out_b, out_s, list_ref, sem, *, planes, extent_x):
     to_scalars(merge_lists(got_a[0:8], got_b[0:8], request[0:8]), list_ref, asked, sem)
+    serve_tiles(asked, (None, cotan_b, cotan), (out_a, out_b, out_s), planes, extent_x)
+
+
+def serve_tiles(asked, fields, outs, planes, extent_x):
     for lx, ly, half in LABELS:
-        at = ly * 12 + lx * ROUTE_MOST + 2 * half
-        tiles = tile_pair((cotan_a, cotan_b, cotan)[ly], asked[0, at], asked[0, at + 1], planes, extent_x)
-        first = (ly * 2 + half) * planes
-        (out_a, out_b, out_s)[lx][first : first + planes, :] = tiles
+        if fields[ly] is not None:
+            at = ly * 12 + lx * ROUTE_MOST + 2 * half
+            tiles = tile_pair(fields[ly], asked[0, at], asked[0, at + 1], planes, extent_x)
+            first = (ly * 2 + half) * planes
+            outs[lx][first : first + planes, :] = tiles
+
+
+def serve_late_body(asked, early_a, early_b, early_s, cotan_a, out_a, out_b, out_s, *, planes, extent_x):
+    serve_tiles(asked, (cotan_a, None, None), (out_a, out_b, out_s), planes, extent_x)
 
 
 def rows_at(ref, first, planes):
@@ -646,7 +654,7 @@
         [((2, slots), i32, "s"), sent, sent, box] + [((size, 128), f32, "v")] * 2
         + [((pair_total, 128, 128), jnp.bfloat16, "v"), ((pair_total, planes, 128), f32, "v")] + [whole] * 3,
         scratch=[pltpu.VMEM((planes, 8, 128), f32)] * 4 + [pltpu.VMEM((slots, TILE * TILE), jnp.bfloat16), pltpu.VMEM((slots * FLAT, 128), f32), pltpu.VMEM((pair_total, 128, 128), f32)]
-        + [pltpu.SMEM((slots,), i32)] * 3 + [pltpu.SMEM((9,), i32), pltpu.SemaphoreType.DMA((11,))],
+        + [pltpu.SMEM((slots,), i32)] * 3 + [pltpu.SemaphoreType.DMA((11,))],
         **sizes,
     )
     request = send_a
@@ -665,9 +673,12 @@
     )
     packs_b = exchange(wide(B), "gy", B)
     packs_a = exchange(wide(A), "gy", A)
+    column, tiles_a, tiles_b, tiles_s = call(
+        serve_body, [("v", [request, rows_b, rows_a, cotan_b, cotan])], [((8, 128), i32, "s"), box, box, box],
+        scratch=(pltpu.VMEM((8, 128), i32), pltpu.SemaphoreType.DMA(())), **sizes,
+    )
     tiles_a, tiles_b, tiles_s = call(
-        serve_body, [("v", [request, rows_b, rows_a, cotan_a, cotan_b, cotan])], [box, box, box],
-        scratch=(pltpu.VMEM((8, 128), i32), pltpu.SMEM((8, 128), i32), pltpu.SemaphoreType.DMA(())), **sizes,
+        serve_late_body, [("s", [column]), ("v", [tiles_a, tiles_b, tiles_s, cotan_a])], [box, box, box], alias={1: 0, 2: 1, 3: 2}, **sizes,
     )
     x_b = exchange(jnp.concatenate([tiles_b, late_b], axis=0), "gx", B)
     x_a = exchange(jnp.concatenate([tiles_a, late_a], axis=0), "gx", A)

time: 40.2 us -> 39.6 us (0.985)
  starting transfers between devices: 19.4 us -> 18.9 us
    ppermute x12, starting transfers between devices: 19.4 us -> 18.9 us  [exchange(): return lax.ppermute(block, axis, matching(lax.axis_size(axis), which))]
    pallas_call x11 -> x12, Pallas kernels: 13.8 us -> 13.7 us  [call(): pl.pallas_call(functools.partial(body, **sizes), out_shape=tuple(shapes),...]
where the time goes in v8:
time: 39.6 us; the launch traced here: 39.4 us
  starting transfers between devices  18.9 us (48%)
  Pallas kernels  13.7 us (35%)
  waiting for transfers between devices  5.28 us (13%)
  between operations  1.46 us (4%)
    ppermute x12, starting transfers between devices, exchange(): return lax.ppermute(block, axis, matching(lax.axis_size(axis), which))  18.9 us
    pallas_call x12, Pallas kernels, call(): pl.pallas_call(functools.partial(body, **sizes), out_shape=tuple(shapes),...  13.7 us
    ppermute x12, waiting for transfers between devices, exchange(): return lax.ppermute(block, axis, matching(lax.axis_size(axis), which))  5.28 us
  transfers between devices with their start and end apart: 12, of which 4 were waited for; matrix products, arithmetic and copies ran while one was open for 0% of the time, Pallas kernels for 27%

profile of v8, /device:TPU:0, one launch (start us, length us, event | category | flops | bytes accessed | tf_op | source)
XLA Modules:
  0.0 39.4 jit_solution(16229551003008662302)
XLA Ops:
  0.6 0.5 %collective-permute-start.1 = (f32[1024,128]{1,0:T(8,128)}, f32[1024,128]{1,0:T(8,128)S(1)}, u32[]{:S(2)}, u32[]{:S(2)}) collective-permute-start(f32[1024,128]{1,0:T(8,128)} %bitcast.11), channel_id=1, source_target_pairs={{0,1},{1,0},{2,3},{3,2},{4,5},{5,4},{6,7},{7,6},{8,9},{9,8},{10,11... | collective-permute-start | bytes 1572872 | tf_op jit(solution)/shard_map/ppermute | solution.py:26
  1.2 2.6 %collective-permute-start = (f32[1024,128]{1,0:T(8,128)}, f32[1024,128]{1,0:T(8,128)S(1)}, u32[]{:S(2)}, u32[]{:S(2)}) collective-permute-start(f32[1024,128]{1,0:T(8,128)} %bitcast.12), channel_id=1, source_target_pairs={{0,3},{1,2},{2,1},{3,0},{4,7},{5,6},{6,5},{7,4},{8,11},{9,10},{10,... | collective-permute-start | bytes 1572872 | tf_op jit(solution)/shard_map/ppermute | solution.py:26
  4.4 2.3 %begin_body.1 = (s32[2,36]{1,0:T(2,128)S(4)}, f32[200,128]{1,0:T(8,128)S(1)}, f32[200,128]{1,0:T(8,128)S(1)}, f32[96,128]{1,0:T(8,128)S(1)}, f32[48,128]{1,0:T(8...) custom-call(s32[36]{0:T(128)} %bitcast.17, ...), custom_call_target="tpu_custom_call" | custom-call | tf_op jit(solution)/shard_map/begin_body/pallas_call | solution.py:616
  6.7 1.6 %collective-permute-start.3 = (f32[200,128]{1,0:T(8,128)S(1)}, f32[200,128]{1,0:T(8,128)S(1)}, u32[]{:S(2)}, u32[]{:S(2)}) collective-permute-start(f32[200,128]{1,0:T(8,128)S(1)} %get-tuple-element.55), channel_id=1, source_target_pairs={{0,4},{4,0},{8,12},{12,8},{16,20},{20,16},{24,28},{28,24},{1,5},{5... | collective-permute-start | bytes 307208 | tf_op jit(solution)/shard_map/ppermute | solution.py:26
  8.3 3.5 %collective-permute-start.2 = (f32[200,128]{1,0:T(8,128)S(1)}, f32[200,128]{1,0:T(8,128)S(1)}, u32[]{:S(2)}, u32[]{:S(2)}) collective-permute-start(f32[200,128]{1,0:T(8,128)S(1)} %get-tuple-element.54.request), channel_id=1, source_target_pairs={{0,28},{4,8},{8,4},{12,16},{16,12},{20,24},{24,20},{28,0},{1,29},{... | collective-permute-start | bytes 307208 | tf_op jit(solution)/shard_map/ppermute | solution.py:26
  11.8 0.9 %local_body.1 = (f32[192,128]{1,0:T(8,128)S(1)}, f32[1024,128]{1,0:T(8,128)S(1)}, f32[1024,128]{1,0:T(8,128)S(1)}) custom-call(f32[1024,128]{1,0:T(8,128)S(1)} %get-tuple-element.50.field, f32[1024,128]{1,0:T(8,128)S(1)} %get-tuple-element.49.cotan, f32[1024,128]{1,0:T(8,128)S(1)} %get-tuple-element.51.rate_y), custom_call_target="tpu_custom_call" | custom-call | tf_op jit(solution)/shard_map/local_body/pallas_call | solution.py:616
  12.8 2.9 %collective-permute-done.2.got_a.rows_a.x_a = f32[200,128]{1,0:T(8,128)S(1)} collective-permute-done((f32[200,128]{1,0:T(8,128)S(1)}, f32[200,128]{1,0:T(8,128)S(1)}, u32[]{:S(2)}, u32[]{:S(2)}) %collective-permute-start.2) | collective-permute-done | bytes 102432 | tf_op jit(solution)/shard_map/ppermute | solution.py:26
  15.6 0.0 collective-permute-done.3.got_b.rows_b.x_b
  15.7 0.0 copy-start
  15.7 0.1 collective-permute-start.5
  15.8 0.6 %collective-permute-start.4 = (f32[248,128]{1,0:T(8,128)S(1)}, f32[248,128]{1,0:T(8,128)S(1)}, u32[]{:S(2)}, u32[]{:S(2)}) collective-permute-start(f32[248,128]{1,0:T(8,128)S(1)} %get-tuple-element.99), channel_id=1, source_target_pairs={{0,3},{1,2},{2,1},{3,0},{4,7},{5,6},{6,5},{7,4},{8,11},{9,10},{10,... | collective-permute-start | bytes 380936 | tf_op jit(solution)/shard_map/ppermute | solution.py:26
  16.5 0.0 collective-permute-done.1.cotan_b
  16.5 0.9 %serve_body.1 = (s32[8,128]{1,0:T(8,128)S(4)}, f32[96,128]{1,0:T(8,128)S(1)}, f32[96,128]{1,0:T(8,128)S(1)}, f32[96,128]{1,0:T(8,128)S(1)}) custom-call(f32[200,128]{1,0:T(8,128)S(1)} %get-tuple-element.54.request, f32[200,128]{1,0:T(8,128)S(1)} %collective-permute-done.3.got_b.rows_b.x_b, f32[200,128]{1,0:T(8,128)S(1)} %collective-permute-done.2.got_a.rows_a.x_a, ...), custom_call_target="tpu_custom_call" | custom-call | tf_op jit(solution)/shard_map/serve_body/pallas_call | solution.py:616
  17.4 0.0 collective-permute-done.cotan_a
  17.4 0.2 serve_late_body.1
  17.6 0.5 %collective-permute-start.7 = (f32[144,128]{1,0:T(8,128)S(1)}, f32[144,128]{1,0:T(8,128)S(1)}, u32[]{:S(2)}, u32[]{:S(2)}) collective-permute-start(f32[144,128]{1,0:T(8,128)S(1)} %pad_maximum_fusion.1), channel_id=1, source_target_pairs={{0,4},{4,0},{8,12},{12,8},{16,20},{20,16},{24,28},{28,24},{1,5},{5... | collective-permute-start | bytes 221192 | tf_op jit(solution)/shard_map/ppermute | solution.py:26
  18.1 3.5 %collective-permute-start.6 = (f32[144,128]{1,0:T(8,128)S(1)}, f32[144,128]{1,0:T(8,128)S(1)}, u32[]{:S(2)}, u32[]{:S(2)}) collective-permute-start(f32[144,128]{1,0:T(8,128)S(1)} %pad_maximum_fusion), channel_id=1, source_target_pairs={{0,28},{4,8},{8,4},{12,16},{16,12},{20,24},{24,20},{28,0},{1,29},{... | collective-permute-start | bytes 221192 | tf_op jit(solution)/shard_map/ppermute | solution.py:26
  21.6 0.0 collective-permute-done.5.from_b.packs_b.y_b
  21.6 0.0 collective-permute-done.4.from_a.packs_a.y_a
  21.6 0.0 copy-done
  21.6 2.0 %pull_body.1 = (f32[1024,128]{1,0:T(8,128)S(1)}, f32[64,128]{1,0:T(8,128)S(1)}, s32[8,128]{1,0:T(8,128)S(4)}, f32[1288,128]{1,0:T(8,128)S(1)}, f32[18,16,128]{2,1,0:T(8,128)S(1)}) custom-call(s32[2,36]{1,0:T(2,128)S(4)} %get-tuple-element.48.order, s32[1,1]{1,0:T(1,128)S(6)} %copy.42.count, ...), custom_call_target="tpu_custom_call", output_to_operand_aliasing={{0}: (2, {})} | custom-call | tf_op jit(solution)/shard_map/pull_body/pallas_call | solution.py:616
  23.6 0.0 collective-permute-done.7.x_b.rows_b
  23.6 1.6 %collective-permute-done.6.x_a.rows_a = f32[144,128]{1,0:T(8,128)S(1)} collective-permute-done((f32[144,128]{1,0:T(8,128)S(1)}, f32[144,128]{1,0:T(8,128)S(1)}, u32[]{:S(2)}, u32[]{:S(2)}) %collective-permute-start.6) | collective-permute-done | bytes 73760 | tf_op jit(solution)/shard_map/ppermute | solution.py:26
  25.2 1.0 %middle_body.1 = (f32[1024,128]{1,0:T(8,128)S(1)}, f32[18,16,128]{2,1,0:T(8,128)S(1)}, f32[128,128]{1,0:T(8,128)S(1)}, f32[128,128]{1,0:T(8,128)S(1)}) custom-call(s32[2,36]{1,0:T(2,128)S(4)} %get-tuple-element.48.order, s32[8,128]{1,0:T(8,128)S(4)} %get-tuple-element.63.asked, ...), custom_call_target="tpu_custom_call", output_to_operand_aliasing={{0}: (3, {}), {1}: (4, {})} | custom-call | tf_op jit(solution)/shard_map/middle_body/pallas_call | solution.py:616
  26.2 1.8 %collective-permute-start.8 = (f32[128,128]{1,0:T(8,128)S(1)}, f32[128,128]{1,0:T(8,128)S(1)}, u32[]{:S(2)}, u32[]{:S(2)}) collective-permute-start(f32[128,128]{1,0:T(8,128)S(1)} %get-tuple-element.78), channel_id=1, source_target_pairs={{0,3},{1,2},{2,1},{3,0},{4,7},{5,6},{6,5},{7,4},{8,11},{9,10},{10,... | collective-permute-start | bytes 196616 | tf_op jit(solution)/shard_map/ppermute | solution.py:26
  28.0 0.4 collective-permute-start.9
  28.4 0.3 after_body.1
  28.7 1.0 %push_body.1.early = f32[1024,128]{1,0:T(8,128)S(1)} custom-call(f32[1024,128]{1,0:T(8,128)S(1)} %get-tuple-element.80.early, f32[1024,128]{1,0:T(8,128)S(1)} %get-tuple-element.50.field, f32[1288,128]{1,0:T(8,128)S(1)} %get-tuple-element.75.pad_rate, f32[64,128]{1,0:T(8,128)S(1)} %get-tuple-element.76.edge_rate, ...), custom_call_target="tpu_custom_call", output_to_operand_aliasing={{}: (0, {})} | custom-call | tf_op jit(solution)/shard_map/push_body/pallas_call | solution.py:616
  29.7 0.5 %collective-permute-done.8.y_a = f32[128,128]{1,0:T(8,128)S(1)} collective-permute-done((f32[128,128]{1,0:T(8,128)S(1)}, f32[128,128]{1,0:T(8,128)S(1)}, u32[]{:S(2)}, u32[]{:S(2)}) %collective-permute-start.8) | collective-permute-done | bytes 65568 | tf_op jit(solution)/shard_map/ppermute | solution.py:26
  30.2 0.0 collective-permute-done.9.y_b
  30.2 0.3 collective-permute-start.10
  30.5 3.6 %collective-permute-start.11 = (f32[144,128]{1,0:T(8,128)S(1)}, f32[144,128]{1,0:T(8,128)S(1)}, u32[]{:S(2)}, u32[]{:S(2)}) collective-permute-start(f32[144,128]{1,0:T(8,128)S(1)} %pad_maximum_fusion.3), channel_id=1, source_target_pairs={{0,28},{4,8},{8,4},{12,16},{16,12},{20,24},{24,20},{28,0},{1,29},{... | collective-permute-start | bytes 221192 | tf_op jit(solution)/shard_map/ppermute | solution.py:26
  34.0 1.2 %inner_body.1.early = f32[1024,128]{1,0:T(8,128)S(1)} custom-call(f32[1024,128]{1,0:T(8,128)S(1)} %get-tuple-element.49.cotan, f32[1024,128]{1,0:T(8,128)S(1)} %get-tuple-element.74.grad, f32[1288,128]{1,0:T(8,128)S(1)} %get-tuple-element.75.pad_rate, f32[1024,128]{1,0:T(8,128)S(1)} %get-tuple-element.51.rate_y), custom_call_target="tpu_custom_call" | custom-call | tf_op jit(solution)/shard_map/inner_body/pallas_call | solution.py:616
  35.2 1.2 %section_body.1 = (f32[1024,128]{1,0:T(8,128)S(1)}, f32[18,128,128]{2,1,0:T(8,128)S(1)}) custom-call(s32[2,36]{1,0:T(2,128)S(4)} %get-tuple-element.48.order, s32[8,128]{1,0:T(8,128)S(4)} %get-tuple-element.63.asked, f32[1024,128]{1,0:T(8,128)S(1)} %push_body.1.early, ...), custom_call_target="tpu_custom_call", output_to_operand_aliasing={{0}: (2, {})} | custom-call | tf_op jit(solution)/shard_map/section_body/pallas_call | solution.py:616
  36.4 0.8 %rest_body.1 = (f32[1024,128]{1,0:T(8,128)S(1)}, f32[36,32,128]{2,1,0:T(8,128)S(1)}) custom-call(s32[2,36]{1,0:T(2,128)S(4)} %get-tuple-element.48.order, s32[1,1]{1,0:T(1,128)S(6)} %copy.42.count, f32[1024,128]{1,0:T(8,128)S(1)} %inner_body.1.early, f32[64,128]{1,0:T(8,128)S(1)} %get-tuple-element.76.edge_rate, ...), custom_call_target="tpu_custom_call", output_to_operand_aliasing={{0}: (2, {})} | custom-call | tf_op jit(solution)/shard_map/rest_body/pallas_call | solution.py:616
  37.2 0.0 collective-permute-done.10.x_b
  37.2 0.3 collective-permute-done.11.x_a
  37.5 1.9 %last_body.1 = (f32[1024,128]{1,0:T(8,128)}, f32[1152,128]{1,0:T(8,128)}, f32[1024,128]{1,0:T(8,128)S(1)}) custom-call(s32[2,36]{1,0:T(2,128)S(4)} %get-tuple-element.48.order, s32[1,1]{1,0:T(1,128)S(6)} %copy.42.count, f32[1024,128]{1,0:T(8,128)S(1)} %get-tuple-element.88.early, ...), custom_call_target="tpu_custom_call", output_to_operand_aliasing={{2}: (2, {})} | custom-call | tf_op jit(solution)/shard_map/last_body/pallas_call | solution.py:616
  (15 shorter events, 0.1 us)
Async XLA Ops:
  0.6 15.8 %collective-permute-start.1 = (f32[1024,128]{1,0:T(8,128)}, f32[1024,128]{1,0:T(8,128)S(1)}, u32[]{:S(2)}, u32[]{:S(2)}) collective-permute-start(f32[1024,128]{1,0:T(8,128)} %bitcast.11), channel_id=1, source_target_pairs={{0,1},{1,0},{2,3},{3,2},{4,5},{5,4},{6,7},{7,6},{8,9},{9,8},{10,11... | collective-permute-start | bytes 1572872 | tf_op jit(solution)/shard_map/ppermute | solution.py:26
  1.2 16.2 %collective-permute-start = (f32[1024,128]{1,0:T(8,128)}, f32[1024,128]{1,0:T(8,128)S(1)}, u32[]{:S(2)}, u32[]{:S(2)}) collective-permute-start(f32[1024,128]{1,0:T(8,128)} %bitcast.12), channel_id=1, source_target_pairs={{0,3},{1,2},{2,1},{3,0},{4,7},{5,6},{6,5},{7,4},{8,11},{9,10},{10,... | collective-permute-start | bytes 1572872 | tf_op jit(solution)/shard_map/ppermute | solution.py:26
  6.7 9.0 %collective-permute-start.3 = (f32[200,128]{1,0:T(8,128)S(1)}, f32[200,128]{1,0:T(8,128)S(1)}, u32[]{:S(2)}, u32[]{:S(2)}) collective-permute-start(f32[200,128]{1,0:T(8,128)S(1)} %get-tuple-element.55), channel_id=1, source_target_pairs={{0,4},{4,0},{8,12},{12,8},{16,20},{20,16},{24,28},{28,24},{1,5},{5... | collective-permute-start | bytes 307208 | tf_op jit(solution)/shard_map/ppermute | solution.py:26
  8.3 7.4 %collective-permute-start.2 = (f32[200,128]{1,0:T(8,128)S(1)}, f32[200,128]{1,0:T(8,128)S(1)}, u32[]{:S(2)}, u32[]{:S(2)}) collective-permute-start(f32[200,128]{1,0:T(8,128)S(1)} %get-tuple-element.54.request), channel_id=1, source_target_pairs={{0,28},{4,8},{8,4},{12,16},{16,12},{20,24},{24,20},{28,0},{1,29},{... | collective-permute-start | bytes 307208 | tf_op jit(solution)/shard_map/ppermute | solution.py:26
  15.7 5.9 %copy-start = (f32[16,64,128]{2,1,0:T(8,128)S(1)}, f32[16,64,128]{2,1,0:T(8,128)}, u32[]{:S(2)}) copy-start(f32[16,64,128]{2,1,0:T(8,128)} %rate_cube.1) | copy-start | bytes 1572868
  15.7 5.8 %collective-permute-start.5 = (f32[248,128]{1,0:T(8,128)S(1)}, f32[248,128]{1,0:T(8,128)S(1)}, u32[]{:S(2)}, u32[]{:S(2)}) collective-permute-start(f32[248,128]{1,0:T(8,128)S(1)} %get-tuple-element.98), channel_id=1, source_target_pairs={{0,1},{1,0},{2,3},{3,2},{4,5},{5,4},{6,7},{7,6},{8,9},{9,8},{10,11... | collective-permute-start | bytes 380936 | tf_op jit(solution)/shard_map/ppermute | solution.py:26
  15.8 5.8 %collective-permute-start.4 = (f32[248,128]{1,0:T(8,128)S(1)}, f32[248,128]{1,0:T(8,128)S(1)}, u32[]{:S(2)}, u32[]{:S(2)}) collective-permute-start(f32[248,128]{1,0:T(8,128)S(1)} %get-tuple-element.99), channel_id=1, source_target_pairs={{0,3},{1,2},{2,1},{3,0},{4,7},{5,6},{6,5},{7,4},{8,11},{9,10},{10,... | collective-permute-start | bytes 380936 | tf_op jit(solution)/shard_map/ppermute | solution.py:26
  17.6 6.0 %collective-permute-start.7 = (f32[144,128]{1,0:T(8,128)S(1)}, f32[144,128]{1,0:T(8,128)S(1)}, u32[]{:S(2)}, u32[]{:S(2)}) collective-permute-start(f32[144,128]{1,0:T(8,128)S(1)} %pad_maximum_fusion.1), channel_id=1, source_target_pairs={{0,4},{4,0},{8,12},{12,8},{16,20},{20,16},{24,28},{28,24},{1,5},{5... | collective-permute-start | bytes 221192 | tf_op jit(solution)/shard_map/ppermute | solution.py:26
  18.1 7.0 %collective-permute-start.6 = (f32[144,128]{1,0:T(8,128)S(1)}, f32[144,128]{1,0:T(8,128)S(1)}, u32[]{:S(2)}, u32[]{:S(2)}) collective-permute-start(f32[144,128]{1,0:T(8,128)S(1)} %pad_maximum_fusion), channel_id=1, source_target_pairs={{0,28},{4,8},{8,4},{12,16},{16,12},{20,24},{24,20},{28,0},{1,29},{... | collective-permute-start | bytes 221192 | tf_op jit(solution)/shard_map/ppermute | solution.py:26
  26.2 4.0 %collective-permute-start.8 = (f32[128,128]{1,0:T(8,128)S(1)}, f32[128,128]{1,0:T(8,128)S(1)}, u32[]{:S(2)}, u32[]{:S(2)}) collective-permute-start(f32[128,128]{1,0:T(8,128)S(1)} %get-tuple-element.78), channel_id=1, source_target_pairs={{0,3},{1,2},{2,1},{3,0},{4,7},{5,6},{6,5},{7,4},{8,11},{9,10},{10,... | collective-permute-start | bytes 196616 | tf_op jit(solution)/shard_map/ppermute | solution.py:26
  28.0 2.2 %collective-permute-start.9 = (f32[128,128]{1,0:T(8,128)S(1)}, f32[128,128]{1,0:T(8,128)S(1)}, u32[]{:S(2)}, u32[]{:S(2)}) collective-permute-start(f32[128,128]{1,0:T(8,128)S(1)} %get-tuple-element.79), channel_id=1, source_target_pairs={{0,1},{1,0},{2,3},{3,2},{4,5},{5,4},{6,7},{7,6},{8,9},{9,8},{10,11... | collective-permute-start | bytes 196616 | tf_op jit(solution)/shard_map/ppermute | solution.py:26
  30.2 7.0 %collective-permute-start.10 = (f32[144,128]{1,0:T(8,128)S(1)}, f32[144,128]{1,0:T(8,128)S(1)}, u32[]{:S(2)}, u32[]{:S(2)}) collective-permute-start(f32[144,128]{1,0:T(8,128)S(1)} %pad_maximum_fusion.2), channel_id=1, source_target_pairs={{0,4},{4,0},{8,12},{12,8},{16,20},{20,16},{24,28},{28,24},{1,5},{5... | collective-permute-start | bytes 221192 | tf_op jit(solution)/shard_map/ppermute | solution.py:26
  30.5 7.1 %collective-permute-start.11 = (f32[144,128]{1,0:T(8,128)S(1)}, f32[144,128]{1,0:T(8,128)S(1)}, u32[]{:S(2)}, u32[]{:S(2)}) collective-permute-start(f32[144,128]{1,0:T(8,128)S(1)} %pad_maximum_fusion.3), channel_id=1, source_target_pairs={{0,28},{4,8},{8,4},{12,16},{16,12},{20,24},{24,20},{28,0},{1,29},{... | collective-permute-start | bytes 221192 | tf_op jit(solution)/shard_map/ppermute | solution.py:26

commit v9 on v8

--- a/solution.py
+++ b/solution.py
@@ -502,24 +502,14 @@
     )
 
 
-def merge_blocks(value, number, work, blocks):
+def merge_blocks(value, number, order, work, blocks):
     work[number] = value
     half = TILE // 2
     half_lane = lanes((half, 128)) < TILE
     even_one, odd_one, even_two, odd_two = (work[number, pl.ds(first, half, 2), :] for first in (0, 1, TILE, TILE + 1))
     turned = roll(jnp.where(half_lane, odd_one, even_two), TILE)
-    blocks[2 * number] = jnp.where(half_lane, even_one, turned)
-    blocks[2 * number + 1] = jnp.where(half_lane, turned, odd_two)
-
-
-def start_blocks(number, order, blocks, out_blocks, sems):
-    half = TILE // 2
-    copies = []
-    for which in range(2):
-        spot = pl.ds(pl.multiple_of(order[0, 2 * number + which] * half, 8), half)
-        copies.append(pltpu.make_async_copy(blocks.at[2 * number + which], out_blocks.at[spot, :], sems.at[2 * number + which]))
-        copies[-1].start()
-    return copies
+    for which, rows in enumerate((jnp.where(half_lane, even_one, turned), jnp.where(half_lane, turned, odd_two))):
+        blocks[pl.ds(pl.multiple_of(order[0, 2 * number + which] * half, 8), half), :] = rows
 
 
 def section_body(
@@ -548,7 +538,7 @@
         if lx == S:
             backs[number] = alive_lanes(row_back(ly, half, y_a, y_b, own, planes, extent_x), order, number, count[0, 0])
             value = first_outer[number] + outer(TIME_STEP * backs[number], picked[number])
-            merge_blocks(value, number, work, blocks)
+            merge_blocks(value, number, order, work, blocks)
     for z in range(planes):
         spot = pl.ds(z * extent_x, extent_x)
         rim = roll(edges, 125 - 8 * z)
@@ -558,13 +548,9 @@
 
 
 def last_body(
-    order, count, early, blocks_early, grad, pad_rate, x_b, x_a, pairs, first_outer, picked, out, out_blocks, total, work, blocks, sems,
+    order, count, early, blocks_early, grad, pad_rate, x_b, x_a, pairs, first_outer, picked, out, out_blocks, total, blocks, work, sems,
     *, planes, extent_x,
 ):
-    copies = []
-    for number, (lx, _, _) in enumerate(LABELS):
-        if lx == S:
-            copies += start_blocks(number, order, blocks_early, out_blocks, sems)
     even_x = parities()[0] == 0
     size = 3 * planes
     low_rows = [jnp.where(even_x, x_a[j * planes : (j + 1) * planes], x_b[j * planes : (j + 1) * planes]) for j in range(3)]
@@ -592,11 +578,11 @@
             back = rows_at((x_a, x_b)[lx], size + ((1, 2, 0)[ly] * 2 + half) * planes, planes)
             backs[number] = alive_lanes(back, order, number, count[0, 0])
             give_back(backs[number], number, TIME_STEP, order, pairs, total, planes, extent_x)
-    copies.append(pltpu.make_async_copy(total, out, sems.at[2 * len(LABELS)]))
-    copies[-1].start()
+    copies = (pltpu.make_async_copy(total, out, sems.at[0]), pltpu.make_async_copy(blocks, out_blocks, sems.at[1]))
+    copies[0].start()
     for number, back in backs.items():
-        merge_blocks(first_outer[number] + outer(TIME_STEP * back, picked[number]), number, work, blocks)
-        copies += start_blocks(number, order, blocks, out_blocks, sems)
+        merge_blocks(first_outer[number] + outer(TIME_STEP * back, picked[number]), number, order, work, blocks)
+    copies[1].start()
     for copy in copies:
         copy.wait()
 
@@ -715,17 +701,16 @@
         [whole, ((pair_total, 128, 128), f32, "v")], alias={2: 0}, **sizes,
     )
     work = pltpu.VMEM((pair_total, 128, 128), f32)
-    blocks_out = pltpu.VMEM((slots, TILE // 2, 128), f32)
     inner, early_blocks = call(
         rest_body,
         [("s", [order]), ("r", [tile_count]), ("v", [inner, edge_rate, packs, pack, last_y_a, last_y_b, own, pairs, first_outer, picked])],
-        [whole, ((slots, TILE // 2, 128), f32, "v")], scratch=(work,), alias={2: 0}, **sizes,
-    )
-    grad_level_set, grad_blocks, _ = call(
+        [whole, tall + ("v",)], scratch=(work,), alias={2: 0}, **sizes,
+    )
+    grad_level_set, grad_blocks, _, _ = call(
         last_body,
         [("s", [order]), ("r", [tile_count]), ("v", [inner, early_blocks, grad, pad_rate, last_x_b, last_x_a, pairs, first_outer, picked])],
-        [((cells, 128), f32, "h"), tall + ("h",), whole],
-        scratch=(work, blocks_out, pltpu.SemaphoreType.DMA((slots + 1,))), alias={2: 2}, **sizes,
+        [((cells, 128), f32, "h"), tall + ("h",), whole, tall + ("v",)],
+        scratch=(work, pltpu.SemaphoreType.DMA((2,))), alias={2: 2, 3: 3}, **sizes,
     )
     return (grad_level_set.reshape(planes, extent_x, extent_y), grad_blocks.reshape(1, 1, slots, TILE * TILE))
 

time: 39.6 us -> 39.4 us (level)
  no operation moved by 1% of the time
where the time goes in v9:
time: 39.4 us; the launch traced here: 39.3 us
  starting transfers between devices  18.9 us (48%)
  Pallas kernels  13.5 us (34%)
  waiting for transfers between devices  5.27 us (13%)
  between operations  1.46 us (4%)
    ppermute x12, starting transfers between devices, exchange(): return lax.ppermute(block, axis, matching(lax.axis_size(axis), which))  18.9 us
    pallas_call x12, Pallas kernels, call(): pl.pallas_call(functools.partial(body, **sizes), out_shape=tuple(shapes),...  13.5 us
    ppermute x12, waiting for transfers between devices, exchange(): return lax.ppermute(block, axis, matching(lax.axis_size(axis), which))  5.27 us
  transfers between devices with their start and end apart: 12, of which 4 were waited for; matrix products, arithmetic and copies ran while one was open for 0% of the time, Pallas kernels for 27%

profile of v9, /device:TPU:0, one launch (start us, length us, event | category | flops | bytes accessed | tf_op | source)
XLA Modules:
  0.0 39.3 jit_solution(5447411346054249844)
XLA Ops:
  0.6 0.5 %collective-permute-start.1 = (f32[1024,128]{1,0:T(8,128)}, f32[1024,128]{1,0:T(8,128)S(1)}, u32[]{:S(2)}, u32[]{:S(2)}) collective-permute-start(f32[1024,128]{1,0:T(8,128)} %bitcast.11), channel_id=1, source_target_pairs={{0,1},{1,0},{2,3},{3,2},{4,5},{5,4},{6,7},{7,6},{8,9},{9,8},{10,11... | collective-permute-start | bytes 1572872 | tf_op jit(solution)/shard_map/ppermute | solution.py:26
  1.2 2.6 %collective-permute-start = (f32[1024,128]{1,0:T(8,128)}, f32[1024,128]{1,0:T(8,128)S(1)}, u32[]{:S(2)}, u32[]{:S(2)}) collective-permute-start(f32[1024,128]{1,0:T(8,128)} %bitcast.12), channel_id=1, source_target_pairs={{0,3},{1,2},{2,1},{3,0},{4,7},{5,6},{6,5},{7,4},{8,11},{9,10},{10,... | collective-permute-start | bytes 1572872 | tf_op jit(solution)/shard_map/ppermute | solution.py:26
  4.4 2.3 %begin_body.1 = (s32[2,36]{1,0:T(2,128)S(4)}, f32[200,128]{1,0:T(8,128)S(1)}, f32[200,128]{1,0:T(8,128)S(1)}, f32[96,128]{1,0:T(8,128)S(1)}, f32[48,128]{1,0:T(8...) custom-call(s32[36]{0:T(128)} %bitcast.17, ...), custom_call_target="tpu_custom_call" | custom-call | tf_op jit(solution)/shard_map/begin_body/pallas_call | solution.py:602
  6.7 1.6 %collective-permute-start.3 = (f32[200,128]{1,0:T(8,128)S(1)}, f32[200,128]{1,0:T(8,128)S(1)}, u32[]{:S(2)}, u32[]{:S(2)}) collective-permute-start(f32[200,128]{1,0:T(8,128)S(1)} %get-tuple-element.55), channel_id=1, source_target_pairs={{0,4},{4,0},{8,12},{12,8},{16,20},{20,16},{24,28},{28,24},{1,5},{5... | collective-permute-start | bytes 307208 | tf_op jit(solution)/shard_map/ppermute | solution.py:26
  8.3 3.5 %collective-permute-start.2 = (f32[200,128]{1,0:T(8,128)S(1)}, f32[200,128]{1,0:T(8,128)S(1)}, u32[]{:S(2)}, u32[]{:S(2)}) collective-permute-start(f32[200,128]{1,0:T(8,128)S(1)} %get-tuple-element.54.request), channel_id=1, source_target_pairs={{0,28},{4,8},{8,4},{12,16},{16,12},{20,24},{24,20},{28,0},{1,29},{... | collective-permute-start | bytes 307208 | tf_op jit(solution)/shard_map/ppermute | solution.py:26
  11.8 0.9 %local_body.1 = (f32[192,128]{1,0:T(8,128)S(1)}, f32[1024,128]{1,0:T(8,128)S(1)}, f32[1024,128]{1,0:T(8,128)S(1)}) custom-call(f32[1024,128]{1,0:T(8,128)S(1)} %get-tuple-element.50.field, f32[1024,128]{1,0:T(8,128)S(1)} %get-tuple-element.49.cotan, f32[1024,128]{1,0:T(8,128)S(1)} %get-tuple-element.51.rate_y), custom_call_target="tpu_custom_call" | custom-call | tf_op jit(solution)/shard_map/local_body/pallas_call | solution.py:602
  12.8 2.9 %collective-permute-done.2.got_a.rows_a.x_a = f32[200,128]{1,0:T(8,128)S(1)} collective-permute-done((f32[200,128]{1,0:T(8,128)S(1)}, f32[200,128]{1,0:T(8,128)S(1)}, u32[]{:S(2)}, u32[]{:S(2)}) %collective-permute-start.2) | collective-permute-done | bytes 102432 | tf_op jit(solution)/shard_map/ppermute | solution.py:26
  15.6 0.0 collective-permute-done.3.got_b.rows_b.x_b
  15.7 0.0 copy-start
  15.7 0.1 collective-permute-start.5
  15.8 0.6 %collective-permute-start.4 = (f32[248,128]{1,0:T(8,128)S(1)}, f32[248,128]{1,0:T(8,128)S(1)}, u32[]{:S(2)}, u32[]{:S(2)}) collective-permute-start(f32[248,128]{1,0:T(8,128)S(1)} %get-tuple-element.99), channel_id=1, source_target_pairs={{0,3},{1,2},{2,1},{3,0},{4,7},{5,6},{6,5},{7,4},{8,11},{9,10},{10,... | collective-permute-start | bytes 380936 | tf_op jit(solution)/shard_map/ppermute | solution.py:26
  16.5 0.0 collective-permute-done.1.cotan_b
  16.5 0.9 %serve_body.1 = (s32[8,128]{1,0:T(8,128)S(4)}, f32[96,128]{1,0:T(8,128)S(1)}, f32[96,128]{1,0:T(8,128)S(1)}, f32[96,128]{1,0:T(8,128)S(1)}) custom-call(f32[200,128]{1,0:T(8,128)S(1)} %get-tuple-element.54.request, f32[200,128]{1,0:T(8,128)S(1)} %collective-permute-done.3.got_b.rows_b.x_b, f32[200,128]{1,0:T(8,128)S(1)} %collective-permute-done.2.got_a.rows_a.x_a, ...), custom_call_target="tpu_custom_call" | custom-call | tf_op jit(solution)/shard_map/serve_body/pallas_call | solution.py:602
  17.4 0.0 collective-permute-done.cotan_a
  17.4 0.2 serve_late_body.1
  17.6 0.5 %collective-permute-start.7 = (f32[144,128]{1,0:T(8,128)S(1)}, f32[144,128]{1,0:T(8,128)S(1)}, u32[]{:S(2)}, u32[]{:S(2)}) collective-permute-start(f32[144,128]{1,0:T(8,128)S(1)} %pad_maximum_fusion.1), channel_id=1, source_target_pairs={{0,4},{4,0},{8,12},{12,8},{16,20},{20,16},{24,28},{28,24},{1,5},{5... | collective-permute-start | bytes 221192 | tf_op jit(solution)/shard_map/ppermute | solution.py:26
  18.1 3.5 %collective-permute-start.6 = (f32[144,128]{1,0:T(8,128)S(1)}, f32[144,128]{1,0:T(8,128)S(1)}, u32[]{:S(2)}, u32[]{:S(2)}) collective-permute-start(f32[144,128]{1,0:T(8,128)S(1)} %pad_maximum_fusion), channel_id=1, source_target_pairs={{0,28},{4,8},{8,4},{12,16},{16,12},{20,24},{24,20},{28,0},{1,29},{... | collective-permute-start | bytes 221192 | tf_op jit(solution)/shard_map/ppermute | solution.py:26
  21.6 0.0 collective-permute-done.5.from_b.packs_b.y_b
  21.6 0.0 collective-permute-done.4.from_a.packs_a.y_a
  21.6 0.0 copy-done
  21.6 2.0 %pull_body.1 = (f32[1024,128]{1,0:T(8,128)S(1)}, f32[64,128]{1,0:T(8,128)S(1)}, s32[8,128]{1,0:T(8,128)S(4)}, f32[1288,128]{1,0:T(8,128)S(1)}, f32[18,16,128]{2,1,0:T(8,128)S(1)}) custom-call(s32[2,36]{1,0:T(2,128)S(4)} %get-tuple-element.48.order, s32[1,1]{1,0:T(1,128)S(6)} %copy.44.count, ...), custom_call_target="tpu_custom_call", output_to_operand_aliasing={{0}: (2, {})} | custom-call | tf_op jit(solution)/shard_map/pull_body/pallas_call | solution.py:602
  23.6 0.0 collective-permute-done.7.x_b.rows_b
  23.6 1.6 %collective-permute-done.6.x_a.rows_a = f32[144,128]{1,0:T(8,128)S(1)} collective-permute-done((f32[144,128]{1,0:T(8,128)S(1)}, f32[144,128]{1,0:T(8,128)S(1)}, u32[]{:S(2)}, u32[]{:S(2)}) %collective-permute-start.6) | collective-permute-done | bytes 73760 | tf_op jit(solution)/shard_map/ppermute | solution.py:26
  25.2 1.0 %middle_body.1 = (f32[1024,128]{1,0:T(8,128)S(1)}, f32[18,16,128]{2,1,0:T(8,128)S(1)}, f32[128,128]{1,0:T(8,128)S(1)}, f32[128,128]{1,0:T(8,128)S(1)}) custom-call(s32[2,36]{1,0:T(2,128)S(4)} %get-tuple-element.48.order, s32[8,128]{1,0:T(8,128)S(4)} %get-tuple-element.63.asked, ...), custom_call_target="tpu_custom_call", output_to_operand_aliasing={{0}: (3, {}), {1}: (4, {})} | custom-call | tf_op jit(solution)/shard_map/middle_body/pallas_call | solution.py:602
  26.2 1.8 %collective-permute-start.8 = (f32[128,128]{1,0:T(8,128)S(1)}, f32[128,128]{1,0:T(8,128)S(1)}, u32[]{:S(2)}, u32[]{:S(2)}) collective-permute-start(f32[128,128]{1,0:T(8,128)S(1)} %get-tuple-element.78), channel_id=1, source_target_pairs={{0,3},{1,2},{2,1},{3,0},{4,7},{5,6},{6,5},{7,4},{8,11},{9,10},{10,... | collective-permute-start | bytes 196616 | tf_op jit(solution)/shard_map/ppermute | solution.py:26
  28.0 0.4 %collective-permute-start.9 = (f32[128,128]{1,0:T(8,128)S(1)}, f32[128,128]{1,0:T(8,128)S(1)}, u32[]{:S(2)}, u32[]{:S(2)}) collective-permute-start(f32[128,128]{1,0:T(8,128)S(1)} %get-tuple-element.79), channel_id=1, source_target_pairs={{0,1},{1,0},{2,3},{3,2},{4,5},{5,4},{6,7},{7,6},{8,9},{9,8},{10,11... | collective-permute-start | bytes 196616 | tf_op jit(solution)/shard_map/ppermute | solution.py:26
  28.4 0.3 after_body.1
  28.7 1.0 %push_body.1.early = f32[1024,128]{1,0:T(8,128)S(1)} custom-call(f32[1024,128]{1,0:T(8,128)S(1)} %get-tuple-element.80.early, f32[1024,128]{1,0:T(8,128)S(1)} %get-tuple-element.50.field, f32[1288,128]{1,0:T(8,128)S(1)} %get-tuple-element.75.pad_rate, f32[64,128]{1,0:T(8,128)S(1)} %get-tuple-element.76.edge_rate, ...), custom_call_target="tpu_custom_call", output_to_operand_aliasing={{}: (0, {})} | custom-call | tf_op jit(solution)/shard_map/push_body/pallas_call | solution.py:602
  29.7 0.5 %collective-permute-done.8.y_a = f32[128,128]{1,0:T(8,128)S(1)} collective-permute-done((f32[128,128]{1,0:T(8,128)S(1)}, f32[128,128]{1,0:T(8,128)S(1)}, u32[]{:S(2)}, u32[]{:S(2)}) %collective-permute-start.8) | collective-permute-done | bytes 65568 | tf_op jit(solution)/shard_map/ppermute | solution.py:26
  30.2 0.0 collective-permute-done.9.y_b
  30.2 0.3 collective-permute-start.10
  30.5 3.6 %collective-permute-start.11 = (f32[144,128]{1,0:T(8,128)S(1)}, f32[144,128]{1,0:T(8,128)S(1)}, u32[]{:S(2)}, u32[]{:S(2)}) collective-permute-start(f32[144,128]{1,0:T(8,128)S(1)} %pad_maximum_fusion.3), channel_id=1, source_target_pairs={{0,28},{4,8},{8,4},{12,16},{16,12},{20,24},{24,20},{28,0},{1,29},{... | collective-permute-start | bytes 221192 | tf_op jit(solution)/shard_map/ppermute | solution.py:26
  34.0 1.2 %inner_body.1.early = f32[1024,128]{1,0:T(8,128)S(1)} custom-call(f32[1024,128]{1,0:T(8,128)S(1)} %get-tuple-element.49.cotan, f32[1024,128]{1,0:T(8,128)S(1)} %get-tuple-element.74.grad, f32[1288,128]{1,0:T(8,128)S(1)} %get-tuple-element.75.pad_rate, f32[1024,128]{1,0:T(8,128)S(1)} %get-tuple-element.51.rate_y), custom_call_target="tpu_custom_call" | custom-call | tf_op jit(solution)/shard_map/inner_body/pallas_call | solution.py:602
  35.2 1.2 %section_body.1 = (f32[1024,128]{1,0:T(8,128)S(1)}, f32[18,128,128]{2,1,0:T(8,128)S(1)}) custom-call(s32[2,36]{1,0:T(2,128)S(4)} %get-tuple-element.48.order, s32[8,128]{1,0:T(8,128)S(4)} %get-tuple-element.63.asked, f32[1024,128]{1,0:T(8,128)S(1)} %push_body.1.early, ...), custom_call_target="tpu_custom_call", output_to_operand_aliasing={{0}: (2, {})} | custom-call | tf_op jit(solution)/shard_map/section_body/pallas_call | solution.py:602
  36.4 0.7 %rest_body.1 = (f32[1024,128]{1,0:T(8,128)S(1)}, f32[1152,128]{1,0:T(8,128)S(1)}) custom-call(s32[2,36]{1,0:T(2,128)S(4)} %get-tuple-element.48.order, s32[1,1]{1,0:T(1,128)S(6)} %copy.44.count, f32[1024,128]{1,0:T(8,128)S(1)} %inner_body.1.early, f32[64,128]{1,0:T(8,128)S(1)} %get-tuple-element.76.edge_rate, ...), custom_call_target="tpu_custom_call", output_to_operand_aliasing={{0}: (2, {})} | custom-call | tf_op jit(solution)/shard_map/rest_body/pallas_call | solution.py:602
  37.2 0.0 collective-permute-done.10.x_b
  37.2 0.3 collective-permute-done.11.x_a
  37.5 1.8 %last_body.1 = (f32[1024,128]{1,0:T(8,128)}, f32[1152,128]{1,0:T(8,128)}, f32[1024,128]{1,0:T(8,128)S(1)}, f32[1152,128]{1,0:T(8,128)S(1)}) custom-call(s32[2,36]{1,0:T(2,128)S(4)} %get-tuple-element.48.order, s32[1,1]{1,0:T(1,128)S(6)} %copy.44.count, f32[1024,128]{1,0:T(8,128)S(1)} %get-tuple-element.88.early, ...), custom_call_target="tpu_custom_call", output_to_operand_aliasing={{2}: (2, {}), {3}: (3, {})} | custom-call | tf_op jit(solution)/shard_map/last_body/pallas_call | solution.py:602
  (15 shorter events, 0.1 us)
Async XLA Ops:
  0.6 15.8 %collective-permute-start.1 = (f32[1024,128]{1,0:T(8,128)}, f32[1024,128]{1,0:T(8,128)S(1)}, u32[]{:S(2)}, u32[]{:S(2)}) collective-permute-start(f32[1024,128]{1,0:T(8,128)} %bitcast.11), channel_id=1, source_target_pairs={{0,1},{1,0},{2,3},{3,2},{4,5},{5,4},{6,7},{7,6},{8,9},{9,8},{10,11... | collective-permute-start | bytes 1572872 | tf_op jit(solution)/shard_map/ppermute | solution.py:26
  1.2 16.2 %collective-permute-start = (f32[1024,128]{1,0:T(8,128)}, f32[1024,128]{1,0:T(8,128)S(1)}, u32[]{:S(2)}, u32[]{:S(2)}) collective-permute-start(f32[1024,128]{1,0:T(8,128)} %bitcast.12), channel_id=1, source_target_pairs={{0,3},{1,2},{2,1},{3,0},{4,7},{5,6},{6,5},{7,4},{8,11},{9,10},{10,... | collective-permute-start | bytes 1572872 | tf_op jit(solution)/shard_map/ppermute | solution.py:26
  6.7 8.9 %collective-permute-start.3 = (f32[200,128]{1,0:T(8,128)S(1)}, f32[200,128]{1,0:T(8,128)S(1)}, u32[]{:S(2)}, u32[]{:S(2)}) collective-permute-start(f32[200,128]{1,0:T(8,128)S(1)} %get-tuple-element.55), channel_id=1, source_target_pairs={{0,4},{4,0},{8,12},{12,8},{16,20},{20,16},{24,28},{28,24},{1,5},{5... | collective-permute-start | bytes 307208 | tf_op jit(solution)/shard_map/ppermute | solution.py:26
  8.3 7.4 %collective-permute-start.2 = (f32[200,128]{1,0:T(8,128)S(1)}, f32[200,128]{1,0:T(8,128)S(1)}, u32[]{:S(2)}, u32[]{:S(2)}) collective-permute-start(f32[200,128]{1,0:T(8,128)S(1)} %get-tuple-element.54.request), channel_id=1, source_target_pairs={{0,28},{4,8},{8,4},{12,16},{16,12},{20,24},{24,20},{28,0},{1,29},{... | collective-permute-start | bytes 307208 | tf_op jit(solution)/shard_map/ppermute | solution.py:26
  15.7 5.9 %copy-start = (f32[16,64,128]{2,1,0:T(8,128)S(1)}, f32[16,64,128]{2,1,0:T(8,128)}, u32[]{:S(2)}) copy-start(f32[16,64,128]{2,1,0:T(8,128)} %rate_cube.1) | copy-start | bytes 1572868
  15.7 5.8 %collective-permute-start.5 = (f32[248,128]{1,0:T(8,128)S(1)}, f32[248,128]{1,0:T(8,128)S(1)}, u32[]{:S(2)}, u32[]{:S(2)}) collective-permute-start(f32[248,128]{1,0:T(8,128)S(1)} %get-tuple-element.98), channel_id=1, source_target_pairs={{0,1},{1,0},{2,3},{3,2},{4,5},{5,4},{6,7},{7,6},{8,9},{9,8},{10,11... | collective-permute-start | bytes 380936 | tf_op jit(solution)/shard_map/ppermute | solution.py:26
  15.8 5.8 %collective-permute-start.4 = (f32[248,128]{1,0:T(8,128)S(1)}, f32[248,128]{1,0:T(8,128)S(1)}, u32[]{:S(2)}, u32[]{:S(2)}) collective-permute-start(f32[248,128]{1,0:T(8,128)S(1)} %get-tuple-element.99), channel_id=1, source_target_pairs={{0,3},{1,2},{2,1},{3,0},{4,7},{5,6},{6,5},{7,4},{8,11},{9,10},{10,... | collective-permute-start | bytes 380936 | tf_op jit(solution)/shard_map/ppermute | solution.py:26
  17.6 6.0 %collective-permute-start.7 = (f32[144,128]{1,0:T(8,128)S(1)}, f32[144,128]{1,0:T(8,128)S(1)}, u32[]{:S(2)}, u32[]{:S(2)}) collective-permute-start(f32[144,128]{1,0:T(8,128)S(1)} %pad_maximum_fusion.1), channel_id=1, source_target_pairs={{0,4},{4,0},{8,12},{12,8},{16,20},{20,16},{24,28},{28,24},{1,5},{5... | collective-permute-start | bytes 221192 | tf_op jit(solution)/shard_map/ppermute | solution.py:26
  18.1 7.0 %collective-permute-start.6 = (f32[144,128]{1,0:T(8,128)S(1)}, f32[144,128]{1,0:T(8,128)S(1)}, u32[]{:S(2)}, u32[]{:S(2)}) collective-permute-start(f32[144,128]{1,0:T(8,128)S(1)} %pad_maximum_fusion), channel_id=1, source_target_pairs={{0,28},{4,8},{8,4},{12,16},{16,12},{20,24},{24,20},{28,0},{1,29},{... | collective-permute-start | bytes 221192 | tf_op jit(solution)/shard_map/ppermute | solution.py:26
  26.2 4.0 %collective-permute-start.8 = (f32[128,128]{1,0:T(8,128)S(1)}, f32[128,128]{1,0:T(8,128)S(1)}, u32[]{:S(2)}, u32[]{:S(2)}) collective-permute-start(f32[128,128]{1,0:T(8,128)S(1)} %get-tuple-element.78), channel_id=1, source_target_pairs={{0,3},{1,2},{2,1},{3,0},{4,7},{5,6},{6,5},{7,4},{8,11},{9,10},{10,... | collective-permute-start | bytes 196616 | tf_op jit(solution)/shard_map/ppermute | solution.py:26
  28.0 2.2 %collective-permute-start.9 = (f32[128,128]{1,0:T(8,128)S(1)}, f32[128,128]{1,0:T(8,128)S(1)}, u32[]{:S(2)}, u32[]{:S(2)}) collective-permute-start(f32[128,128]{1,0:T(8,128)S(1)} %get-tuple-element.79), channel_id=1, source_target_pairs={{0,1},{1,0},{2,3},{3,2},{4,5},{5,4},{6,7},{7,6},{8,9},{9,8},{10,11... | collective-permute-start | bytes 196616 | tf_op jit(solution)/shard_map/ppermute | solution.py:26
  30.2 7.0 %collective-permute-start.10 = (f32[144,128]{1,0:T(8,128)S(1)}, f32[144,128]{1,0:T(8,128)S(1)}, u32[]{:S(2)}, u32[]{:S(2)}) collective-permute-start(f32[144,128]{1,0:T(8,128)S(1)} %pad_maximum_fusion.2), channel_id=1, source_target_pairs={{0,4},{4,0},{8,12},{12,8},{16,20},{20,16},{24,28},{28,24},{1,5},{5... | collective-permute-start | bytes 221192 | tf_op jit(solution)/shard_map/ppermute | solution.py:26
  30.5 7.1 %collective-permute-start.11 = (f32[144,128]{1,0:T(8,128)S(1)}, f32[144,128]{1,0:T(8,128)S(1)}, u32[]{:S(2)}, u32[]{:S(2)}) collective-permute-start(f32[144,128]{1,0:T(8,128)S(1)} %pad_maximum_fusion.3), channel_id=1, source_target_pairs={{0,28},{4,8},{8,4},{12,16},{16,12},{20,24},{24,20},{28,0},{1,29},{... | collective-permute-start | bytes 221192 | tf_op jit(solution)/shard_map/ppermute | solution.py:26
